TPU v7x, 32 devices: a whole 2x2x4 slice. The times are simulated.
32 devices in a mesh: ctx: 8 (over z, y), mp: 4 (over x, core).
Axes of the slice: x: 2, y: 2, z: 4, core: 2. Of those that a mesh axis runs over, the one named last changes fastest.
Arguments:
- tokens: bfloat16 [3072, 6144], P('ctx', 'mp'), may hold values from -24 to 24, as said below
- qkv_weight: bfloat16 [6144, 3, 24, 128], P('ctx', None, 'mp'), may hold values from -1 to 1, as said below
Outputs:
- attended: bfloat16 [3072, 24, 128], P('ctx', 'mp')
Inputs may be any that keep to these rules, and one draw needn't show every extreme that they name: `tokens`: finite values. `qkv_weight`: entries lie within 8 / sqrt(6144) of zero.
All inputs are finite; a program needn't handle non-finite values.
Results may differ from a plain program's by a relative error of at most 0.0045.
The roundings to bfloat16 on the way count: a program that leaves them out, or rounds other values in their place, can miss the bound.
Values may be sent and summed in bfloat16 or wider, within the bound.
No kernel may reach another device: no remote copies, remote signals or barrier semaphores. Data moves between devices by JAX's collectives and lax.ppermute only.
A program may use at most 128 MiB of HBM per device.

v0:
```python
import math

import jax
import jax.numpy as jnp
from jax import lax
from jax.sharding import PartitionSpec as P

REACH = 4


def shifted(array, axis, by):
    devices = lax.axis_size(axis)
    return lax.ppermute(array, axis, [(i, (i + by) % devices) for i in range(devices)])


def collect_blocks(key_value):
    blocks = [key_value]
    current = key_value
    for step in range(1, REACH):
        current = shifted(current, "ctx", 1)
        blocks.append(current)
    return blocks


def on_device(tokens, qkv_weight):
    features = lax.all_gather(tokens, "mp", axis=1, tiled=True)
    rows_dev = features.shape[0]
    heads_local = qkv_weight.shape[2]
    head_size = qkv_weight.shape[3]
    scale = 1.0 / math.sqrt(head_size)
    piece = lax.all_gather(qkv_weight, "ctx", axis=0, tiled=True)
    flat_piece = piece.reshape(piece.shape[0], -1)
    full_total = jnp.dot(features, flat_piece, preferred_element_type=jnp.float32)
    projected = full_total.astype(jnp.bfloat16).reshape(rows_dev, 3, heads_local, head_size)
    queries = projected[:, 0]
    key_value = projected[:, 1:]
    blocks = collect_blocks(key_value)
    key_rows = jnp.concatenate([block[:, 0] for block in blocks], axis=0)
    value_rows = jnp.concatenate([block[:, 1] for block in blocks], axis=0)
    scores = (
        jnp.einsum("thd,shd->hts", queries, key_rows, preferred_element_type=jnp.float32) * scale
    )
    top = jnp.max(scores, axis=-1, keepdims=True)
    expo = jnp.exp(scores - top)
    totals = jnp.sum(expo, axis=-1, keepdims=True)
    probs = expo.astype(jnp.bfloat16)
    mixed = (
        jnp.einsum("hts,shd->htd", probs, value_rows, preferred_element_type=jnp.float32) / totals
    )
    return jnp.transpose(mixed, (1, 0, 2)).astype(jnp.bfloat16)


def solution(mesh):
    placed = (P("ctx", "mp"), P("ctx", None, "mp", None))
    return jax.shard_map(
        on_device, mesh=mesh, in_specs=placed, out_specs=P("ctx", "mp", None), check_vma=False
    )
```

profile of v0, /device:TPU:0, one launch (start us, length us, event | category | flops | bytes accessed | tf_op | source)
XLA Modules:
  0.0 727.5 jit_solution(14110665750935580521)
XLA Ops:
  6.5 0.7 all-gather.3.cloned.1.call-update
  7.3 0.0 all-gather.5.cloned.1.call-start
  7.3 6.1 copy.7
  13.4 0.0 all-gather.5.cloned.1.call-update
  13.4 35.7 %all-gather.3.cloned.1.call-done = bf16[384,6144]{1,0:T(8,128)(2,1)} async-done(((bf16[384,1536]{1,0:T(8,128)(2,1)}), bf16[384,6144]{1,0:T(8,128)(2,1)}) %all-gather.3.cloned.1.call-update) | async-done | bytes 4718608 | tf_op jit(solution)/shard_map/all_gather | solution.py:26
  49.1 541.0 %all-gather.5.cloned.1.call-done = bf16[6144,3,6,128]{0,3,2,1:T(8,128)(2,1)} async-done(((bf16[768,3,6,128]{0,3,2,1:T(8,128)(2,1)}), bf16[6144,3,6,128]{0,3,2,1:T(8,128)(2,1)}) %all-gather.5.cloned.1.call-update) | async-done | bytes 28311568 | tf_op jit(solution)/shard_map/all_gather | solution.py:31
  590.1 16.6 %convolution_convert_fusion = bf16[384,2304]{1,0:T(8,128)(2,1)S(1)} fusion(bf16[384,6144]{1,0:T(8,128)(2,1)} %all-gather.3.cloned.1.call-done, bf16[6144,2304]{0,1:T(8,128)(2,1)} %bitcast.35), kind=kOutput, calls=%fused_computation.7 | convolution fusion | flops 10872520704 | bytes 34799616 | tf_op jit(solution)/shard_map/dot_general | solution.py:33
  606.7 1.1 copy.8
  607.8 0.1 slice.44
  608.0 1.5 copy.15
  609.4 0.3 collective-permute-start
  609.8 30.3 %collective-permute-done = bf16[384,2,6,128]{3,0,2,1:T(8,128)(2,1)S(1)} collective-permute-done((bf16[384,2,6,128]{3,0,2,1:T(8,128)(2,1)}, bf16[384,2,6,128]{3,0,2,1:T(8,128)(2,1)S(1)}, u32[]{:S(2)}, u32[]{:S(2)}) %collective-permute-start) | collective-permute-done | bytes 1179680 | tf_op jit(solution)/shard_map/ppermute | solution.py:13
  640.0 0.0 collective-permute-start.1
  640.0 29.6 %collective-permute-done.1 = bf16[384,2,6,128]{3,0,2,1:T(8,128)(2,1)} collective-permute-done((bf16[384,2,6,128]{3,0,2,1:T(8,128)(2,1)S(1)}, bf16[384,2,6,128]{3,0,2,1:T(8,128)(2,1)}, u32[]{:S(2)}, u32[]{:S(2)}) %collective-permute-start.1) | collective-permute-done | bytes 1179680 | tf_op jit(solution)/shard_map/ppermute | solution.py:13
  669.7 0.1 fusion.33
  669.8 0.3 copy.14
  670.1 0.3 copy.16
  670.4 1.3 slice_bitcast_fusion.5
  671.8 1.3 slice_bitcast_fusion.4
  673.1 25.5 %collective-permute-done.2 = bf16[384,2,6,128]{3,0,2,1:T(8,128)(2,1)} collective-permute-done((bf16[384,2,6,128]{3,0,2,1:T(8,128)(2,1)}, bf16[384,2,6,128]{3,0,2,1:T(8,128)(2,1)}, u32[]{:S(2)}, u32[]{:S(2)}) %collective-permute-start.2) | collective-permute-done | bytes 1179680 | tf_op jit(solution)/shard_map/ppermute | solution.py:13
  698.6 1.3 slice_bitcast_fusion.3
  699.9 6.2 multiply_reduce_fusion
  706.1 7.5 %fusion = f32[6,384]{1,0:T(8,128)S(1)} fusion(f32[6,384,1536]{2,1,0:T(8,128)} %get-tuple-element.14, f32[6,384]{1,0:T(8,128)S(1)} %get-tuple-element.13), kind=kLoop, calls=%fused_computation.2 | loop fusion | flops 10614528 | bytes 14174208 | tf_op jit(solution)/shard_map/reduce_sum | solution.py:45
  713.6 7.1 divide_convert_fusion
  (4 shorter events, 0.0 us)
Async XLA Ops:
  6.5 42.6 %all-gather.3.cloned.1.call-start = ((), (), s32[]{:S(2)}) async-start(), calls=%async_computation | async-start | bytes 5898240 | tf_op jit(solution)/shard_map/all_gather | solution.py:26
  7.3 582.8 %all-gather.5.cloned.1.call-start = ((), (), s32[]{:S(2)}) async-start(), calls=%async_computation.1 | async-start | bytes 31850496 | tf_op jit(solution)/shard_map/all_gather | solution.py:31
  609.4 30.6 %collective-permute-start = (bf16[384,2,6,128]{3,0,2,1:T(8,128)(2,1)}, bf16[384,2,6,128]{3,0,2,1:T(8,128)(2,1)S(1)}, u32[]{:S(2)}, u32[]{:S(2)}) collective-permute-start(bf16[384,2,6,128]{3,0,2,1:T(8,128)(2,1)} %copy.15), channel_id=1, source_target_pairs={{0,4},{4,8},{8,12},{12,16},{16,20},{20,24},{24,28},{28,0},{1,5},{5... | collective-permute-start | bytes 3538952 | tf_op jit(solution)/shard_map/ppermute | solution.py:13
  640.0 29.6 %copy-start = (bf16[384,2,6,128]{3,0,2,1:T(8,128)(2,1)}, bf16[384,2,6,128]{3,0,2,1:T(8,128)(2,1)S(1)}, u32[]{:S(2)}) copy-start(bf16[384,2,6,128]{3,0,2,1:T(8,128)(2,1)S(1)} %collective-permute-done) | copy-start | bytes 3538948
  640.0 29.6 %collective-permute-start.1 = (bf16[384,2,6,128]{3,0,2,1:T(8,128)(2,1)S(1)}, bf16[384,2,6,128]{3,0,2,1:T(8,128)(2,1)}, u32[]{:S(2)}, u32[]{:S(2)}) collective-permute-start(bf16[384,2,6,128]{3,0,2,1:T(8,128)(2,1)S(1)} %collective-permute-done), channel_id=1, source_target_pairs={{0,4},{4,8},{8,12},{12,16},{16,20},{20,24},{24,28},{28,0},{1,5},{5... | collective-permute-start | bytes 3538952 | tf_op jit(solution)/shard_map/ppermute | solution.py:13
  669.7 28.9 %collective-permute-start.2 = (bf16[384,2,6,128]{3,0,2,1:T(8,128)(2,1)}, bf16[384,2,6,128]{3,0,2,1:T(8,128)(2,1)}, u32[]{:S(2)}, u32[]{:S(2)}) collective-permute-start(bf16[384,2,6,128]{3,0,2,1:T(8,128)(2,1)} %collective-permute-done.1), channel_id=1, source_target_pairs={{0,4},{4,8},{8,12},{12,16},{16,20},{20,24},{24,28},{28,0},{1,5},{5... | collective-permute-start | bytes 3538952 | tf_op jit(solution)/shard_map/ppermute | solution.py:13
Sparse Core Ops, SparseCore 0:
  8.9 40.1 all-gather.2
  50.6 539.4 all-gather.4
where the time goes:
time: 728 us
  waiting for transfers between devices  663 us (91%)
  matrix products  29.9 us (4%)
  local copies, waits for them, and re-layouts  13.4 us (2%)
  between operations  13.4 us (2%)
  other arithmetic  7.47 us (1%)
    all_gather x1, waiting for transfers between devices, on_device(): piece = lax.all_gather(qkv_weight, 'ctx', axis=0, tiled=True)  541 us
    ppermute x3, waiting for transfers between devices, shifted(): lax.ppermute(array, axis, [(i, (i + by) % devices) for i in range(devices)])  85.4 us
    all_gather x1, waiting for transfers between devices, on_device(): features = lax.all_gather(tokens, 'mp', axis=1, tiled=True)  35.7 us
    dot_general x1, matrix products, on_device(): jnp.dot(features, flat_piece, preferred_element_type=jnp.float32)  16.6 us
  transfers between devices with their start and end apart: 5, of which 5 were waited for; matrix products, arithmetic and copies ran while one was open for 1% of the time, Pallas kernels for 0%

commit v1 on v0

v1 whole, which is shorter than its diff:
```python
import math

import jax
import jax.numpy as jnp
from jax import lax
from jax.sharding import PartitionSpec as P

REACH = 4


def ring_order(mesh):
    n = mesh.shape["ctx"]
    order = list(range(n))
    try:
        axis = mesh.axis_names.index("ctx")
        devices = mesh.devices.transpose([axis] + [a for a in range(mesh.devices.ndim) if a != axis])
        devices = devices.reshape(n, -1)[:, 0]
        coords = [tuple(d.coords) for d in devices]
    except Exception:
        return order
    if len(set(coords)) != n:
        return order

    def near(a, b):
        return sum(abs(i - j) for i, j in zip(coords[a], coords[b])) == 1

    neighbours = [[b for b in range(n) if b != a and near(a, b)] for a in range(n)]
    path, seen, budget = [0], {0}, [20000]

    def search():
        budget[0] -= 1
        if budget[0] < 0:
            return False
        if len(path) == n:
            return near(path[-1], path[0]) or n <= 2
        for b in sorted(neighbours[path[-1]], key=lambda b: len([x for x in neighbours[b] if x not in seen])):
            if b in seen:
                continue
            path.append(b)
            seen.add(b)
            if search():
                return True
            path.pop()
            seen.discard(b)
        return False

    if search():
        return path
    return order


def shifted(array, axis, by):
    devices = lax.axis_size(axis)
    return lax.ppermute(array, axis, [(i, (i + by) % devices) for i in range(devices)])


def make_on_device(ring):
    n = len(ring)
    pos = [0] * n
    for i, c in enumerate(ring):
        pos[c] = i
    clockwise = [(ring[i], ring[(i + 1) % n]) for i in range(n)]
    counter = [(ring[i], ring[(i - 1) % n]) for i in range(n)]
    ring_arr = jnp.array(ring, jnp.int32)
    pos_arr = jnp.array(pos, jnp.int32)

    def on_device(tokens, qkv_weight):
        features = lax.all_gather(tokens, "mp", axis=1, tiled=True)
        rows_dev = features.shape[0]
        rows_w = qkv_weight.shape[0]
        heads_local = qkv_weight.shape[2]
        head_size = qkv_weight.shape[3]
        scale = 1.0 / math.sqrt(head_size)
        me = lax.axis_index("ctx")
        my_pos = pos_arr[me]

        def partial(block, piece, offset):
            start = block * rows_w + offset
            cols = lax.dynamic_slice_in_dim(features, start, piece.shape[0], axis=1)
            flat = piece.reshape(piece.shape[0], -1)
            return jnp.dot(cols, flat, preferred_element_type=jnp.float32)

        total = partial(me, qkv_weight, 0)
        going_cw = qkv_weight
        going_ccw = qkv_weight
        full_steps = (n - 1) // 2
        for step in range(1, full_steps + 1):
            going_cw = lax.ppermute(going_cw, "ctx", clockwise)
            going_ccw = lax.ppermute(going_ccw, "ctx", counter)
            total = total + partial(ring_arr[(my_pos - step) % n], going_cw, 0)
            total = total + partial(ring_arr[(my_pos + step) % n], going_ccw, 0)
        if n % 2 == 0 and n > 1:
            step = n // 2
            far = ring_arr[(my_pos + step) % n]
            if rows_w % 2 == 0:
                half = rows_w // 2
                last_cw = lax.ppermute(going_cw[:half], "ctx", clockwise)
                last_ccw = lax.ppermute(going_ccw[half:], "ctx", counter)
                total = total + partial(far, last_cw, 0)
                total = total + partial(far, last_ccw, half)
            else:
                last_cw = lax.ppermute(going_cw, "ctx", clockwise)
                total = total + partial(far, last_cw, 0)

        projected = total.astype(jnp.bfloat16).reshape(rows_dev, 3, heads_local, head_size)
        queries = projected[:, 0]
        key_value = projected[:, 1:]
        blocks = [key_value] + [shifted(key_value, "ctx", by) for by in range(1, REACH)]
        key_rows = jnp.concatenate([block[:, 0] for block in blocks], axis=0)
        value_rows = jnp.concatenate([block[:, 1] for block in blocks], axis=0)
        scores = (
            jnp.einsum("thd,shd->hts", queries, key_rows, preferred_element_type=jnp.float32) * scale
        )
        top = jnp.max(scores, axis=-1, keepdims=True)
        expo = jnp.exp(scores - top)
        totals = jnp.sum(expo, axis=-1, keepdims=True)
        probs = expo.astype(jnp.bfloat16)
        mixed = (
            jnp.einsum("hts,shd->htd", probs, value_rows, preferred_element_type=jnp.float32) / totals
        )
        return jnp.transpose(mixed, (1, 0, 2)).astype(jnp.bfloat16)

    return on_device


def solution(mesh):
    placed = (P("ctx", "mp"), P("ctx", None, "mp", None))
    return jax.shard_map(
        make_on_device(ring_order(mesh)),
        mesh=mesh,
        in_specs=placed,
        out_specs=P("ctx", "mp", None),
        check_vma=False,
    )
```

time: 728 us -> 434 us (0.60)
  waiting for transfers between devices: 663 us -> 330 us
  starting transfers between devices: 0.39 us -> 13.8 us
  matrix products: 29.9 us -> 40.4 us
  between operations: 13.4 us -> 22.7 us
    all_gather x1 -> x0, waiting for transfers between devices: 541 us -> none  [on_device(): piece = lax.all_gather(qkv_weight, 'ctx', axis=0, tiled=True)]
    ppermute x0 -> x8, waiting for transfers between devices: none -> 234 us  [the longest x3 210 us: on_device(): going_cw = lax.ppermute(going_cw, 'ctx', clockwise)]
    all_gather x1, waiting for transfers between devices: 35.7 us -> 0.02 us  [on_device(): features = lax.all_gather(tokens, 'mp', axis=1, tiled=True)]
    dot_general x1 -> x9, matrix products: 16.6 us -> 27.1 us  [partial(): return jnp.dot(cols, flat, preferred_element_type=jnp.float32)]
    ppermute x3, waiting for transfers between devices: 85.4 us -> 95.8 us  [shifted(): lax.ppermute(array, axis, [(i, (i + by) % devices) for i in range(devices)])]
    ppermute x0 -> x8, starting transfers between devices: none -> 9.26 us  [the longest x3 6.06 us: on_device(): going_cw = lax.ppermute(going_cw, 'ctx', clockwise)]
  transfers between devices with their start and end apart: 5 -> 12, of which waited for: 5 -> 6; matrix products, arithmetic and copies ran while one was open for 1% -> 7% of each run, Pallas kernels for 0% -> 0%
where the time goes in v1:
time: 434 us; the launch traced here: 433 us
  waiting for transfers between devices  330 us (76%)
  matrix products  40.4 us (9%)
  between operations  22.7 us (5%)
  local copies, waits for them, and re-layouts  18.6 us (4%)
  starting transfers between devices  13.8 us (3%)
  other arithmetic  7.53 us (2%)
    ppermute x3, waiting for transfers between devices, on_device(): going_cw = lax.ppermute(going_cw, 'ctx', clockwise)  210 us
    ppermute x3, waiting for transfers between devices, shifted(): lax.ppermute(array, axis, [(i, (i + by) % devices) for i in range(devices)])  95.8 us
    dot_general x9, matrix products, partial(): return jnp.dot(cols, flat, preferred_element_type=jnp.float32)  27.1 us
    ppermute x1, waiting for transfers between devices, on_device(): last_cw = lax.ppermute(going_cw[:half], 'ctx', clockwise)  18.5 us
  transfers between devices with their start and end apart: 12, of which 6 were waited for; matrix products, arithmetic and copies ran while one was open for 7% of the time, Pallas kernels for 0%

profile of v1, /device:TPU:0, one launch (start us, length us, event | category | flops | bytes accessed | tf_op | source)
XLA Modules:
  0.0 433.1 jit_solution(17646828614856767184)
XLA Ops:
  6.5 4.3 copy.9
  10.9 3.0 collective-permute-start
  14.0 76.5 %collective-permute-done = bf16[768,3,6,128]{0,3,2,1:T(8,128)(2,1)} collective-permute-done((bf16[768,3,6,128]{0,3,2,1:T(8,128)(2,1)S(1)}, bf16[768,3,6,128]{0,3,2,1:T(8,128)(2,1)}, u32[]{:S(2)}, u32[]{:S(2)}) %collective-permute-start) | collective-permute-done | bytes 3538976 | tf_op jit(solution)/shard_map/ppermute | solution.py:88
  90.6 1.7 collective-permute-start.2
  92.6 76.0 %collective-permute-done.2 = bf16[768,3,6,128]{0,3,2,1:T(8,128)(2,1)} collective-permute-done((bf16[768,3,6,128]{0,3,2,1:T(8,128)(2,1)}, bf16[768,3,6,128]{0,3,2,1:T(8,128)(2,1)}, u32[]{:S(2)}, u32[]{:S(2)}) %collective-permute-start.2) | collective-permute-done | bytes 3538976 | tf_op jit(solution)/shard_map/ppermute | solution.py:88
  181.1 3.9 fusion.43
  185.0 3.6 convolution_add_fusion.3
  188.6 57.0 %collective-permute-done.4 = bf16[768,3,6,128]{0,3,2,1:T(8,128)(2,1)S(1)} collective-permute-done((bf16[768,3,6,128]{0,3,2,1:T(8,128)(2,1)}, bf16[768,3,6,128]{0,3,2,1:T(8,128)(2,1)S(1)}, u32[]{:S(2)}, u32[]{:S(2)}) %collective-permute-start.4) | collective-permute-done | bytes 3538976 | tf_op jit(solution)/shard_map/ppermute | solution.py:88
  246.9 3.6 convolution_add_fusion.2
  250.5 3.0 slice.51
  254.5 3.6 fusion.38
  258.1 3.7 fusion.7
  261.8 3.6 fusion.35
  265.4 18.5 %collective-permute-done.6 = bf16[384,3,6,128]{0,3,2,1:T(8,128)(2,1)S(1)} collective-permute-done((bf16[384,3,6,128]{0,3,2,1:T(8,128)(2,1)S(1)}, bf16[384,3,6,128]{0,3,2,1:T(8,128)(2,1)S(1)}, u32[]{:S(2)}, u32[]{:S(2)}) %collective-permute-start.6) | collective-permute-done | bytes 1769504 | tf_op jit(solution)/shard_map/ppermute | solution.py:97
  285.0 6.2 %collective-permute-done.7 = bf16[384,3,6,128]{0,3,2,1:T(8,128)(2,1)S(1)} collective-permute-done((bf16[384,3,6,128]{0,3,2,1:T(8,128)(2,1)}, bf16[384,3,6,128]{0,3,2,1:T(8,128)(2,1)S(1)}, u32[]{:S(2)}, u32[]{:S(2)}) %collective-permute-start.7) | collective-permute-done | bytes 1769504 | tf_op jit(solution)/shard_map/ppermute | solution.py:98
  292.3 2.9 fusion.10
  295.2 2.8 copy.12
  298.1 1.5 copy.19
  299.6 2.6 collective-permute-start.10
  302.5 1.6 collective-permute-start.9
  305.6 95.8 %collective-permute-done.10 = bf16[384,2,6,128]{3,0,2,1:T(8,128)(2,1)} collective-permute-done((bf16[384,2,6,128]{3,0,2,1:T(8,128)(2,1)}, bf16[384,2,6,128]{3,0,2,1:T(8,128)(2,1)}, u32[]{:S(2)}, u32[]{:S(2)}) %collective-permute-start.10) | collective-permute-done | bytes 1179680 | tf_op jit(solution)/shard_map/ppermute | solution.py:54
  405.4 6.2 %multiply_reduce_fusion = (f32[6,384]{1,0:T(8,128)S(1)}, f32[6,384,1536]{2,1,0:T(8,128)}) fusion(bf16[384,6,128]{2,0,1:T(8,128)(2,1)S(1)} %get-tuple-element.11, bf16[384,6,128]{2,0,1:T(8,128)(2,1)S(1)} %get-tuple-element.9, bf16[384,6,128]{2,0,1:T(8,128)(2,1)S(1)} %get-tuple-element.7, bf16[384,6,128]{2,0,1:T(8,128)(2,1)S(1)} %bitcast.63, ...), kind=kOutput, calls=%fused_computation.1 | convolution fusion | flops 922482432 | bytes 17114112 | tf_op jit(solution)/shard_map/thd,shd->hts/dot_general | solution.py:112
  411.7 7.5 %fusion = f32[6,384]{1,0:T(8,128)S(1)} fusion(f32[6,384,1536]{2,1,0:T(8,128)} %get-tuple-element.21, f32[6,384]{1,0:T(8,128)S(1)} %get-tuple-element.20), kind=kLoop, calls=%fused_computation.2 | loop fusion | flops 10614528 | bytes 14174208 | tf_op jit(solution)/shard_map/reduce_sum | solution.py:116
  419.2 7.1 %divide_convert_fusion = bf16[384,6,128]{2,0,1:T(8,128)(2,1)} fusion(bf16[384,6,128]{2,0,1:T(8,128)(2,1)S(1)} %get-tuple-element.12, bf16[384,6,128]{2,0,1:T(8,128)(2,1)S(1)} %get-tuple-element.10, bf16[384,6,128]{2,0,1:T(8,128)(2,1)S(1)} %get-tuple-element.8, bf16[384,6,128]{2,0,1:T(8,128)(2,1)S(1)} %bitcast.66, f32[6,384,1536]{2,1,0:T(8,128)} %get-tuple-element.21, ...), kind=kOutput, calls=%fused_computation.32 | convolution fusion | flops 926613504 | bytes 17123328 | tf_op jit(solution)/shard_map/hts,shd->htd/dot_general | solution.py:119
  (37 shorter events, 14.3 us)
Async XLA Ops:
  6.5 174.5 %all-gather.2.cloned.1.call-start = ((), (), s32[]{:S(2)}) async-start(), calls=%async_computation | async-start | bytes 5898240 | tf_op jit(solution)/shard_map/all_gather | solution.py:68
  6.5 164.1 %copy-start.4 = (s32[8]{0:T(128)S(1)}, s32[8]{0:T(128)}, u32[]{:S(2)}) copy-start(s32[8]{0:T(128)} %constant.91.clone) | copy-start | bytes 100
  6.5 169.3 %copy-start.3 = (s32[8]{0:T(128)S(1)}, s32[8]{0:T(128)}, u32[]{:S(2)}) copy-start(s32[8]{0:T(128)} %constant.92.clone) | copy-start | bytes 100
  10.8 81.8 %copy-start = (bf16[768,3,6,128]{0,3,2,1:T(8,128)(2,1)}, bf16[768,3,6,128]{0,3,2,1:T(8,128)(2,1)S(1)}, u32[]{:S(2)}) copy-start(bf16[768,3,6,128]{0,3,2,1:T(8,128)(2,1)S(1)} %copy.9) | copy-start | bytes 10616836
  10.9 79.7 %collective-permute-start = (bf16[768,3,6,128]{0,3,2,1:T(8,128)(2,1)S(1)}, bf16[768,3,6,128]{0,3,2,1:T(8,128)(2,1)}, u32[]{:S(2)}, u32[]{:S(2)}) collective-permute-start(bf16[768,3,6,128]{0,3,2,1:T(8,128)(2,1)S(1)} %copy.9), channel_id=1, source_target_pairs={{0,4},{4,12},{12,20},{20,28},{28,24},{24,16},{16,8},{8,0},{1,5},{5... | collective-permute-start | bytes 10616840 | tf_op jit(solution)/shard_map/ppermute | solution.py:88
  13.9 78.4 %collective-permute-start.1 = (bf16[768,3,6,128]{0,3,2,1:T(8,128)(2,1)S(1)}, bf16[768,3,6,128]{0,3,2,1:T(8,128)(2,1)}, u32[]{:S(2)}, u32[]{:S(2)}) collective-permute-start(bf16[768,3,6,128]{0,3,2,1:T(8,128)(2,1)S(1)} %copy.9), channel_id=1, source_target_pairs={{0,8},{4,0},{12,4},{20,12},{28,20},{24,28},{16,24},{8,16},{1,9},{5... | collective-permute-start | bytes 10616840 | tf_op jit(solution)/shard_map/ppermute | solution.py:89
  90.6 78.0 %collective-permute-start.2 = (bf16[768,3,6,128]{0,3,2,1:T(8,128)(2,1)}, bf16[768,3,6,128]{0,3,2,1:T(8,128)(2,1)}, u32[]{:S(2)}, u32[]{:S(2)}) collective-permute-start(bf16[768,3,6,128]{0,3,2,1:T(8,128)(2,1)} %collective-permute-done), channel_id=1, source_target_pairs={{0,4},{4,12},{12,20},{20,28},{28,24},{24,16},{16,8},{8,0},{1,5},{5... | collective-permute-start | bytes 10616840 | tf_op jit(solution)/shard_map/ppermute | solution.py:88
  92.3 77.7 %collective-permute-start.3 = (bf16[768,3,6,128]{0,3,2,1:T(8,128)(2,1)}, bf16[768,3,6,128]{0,3,2,1:T(8,128)(2,1)}, u32[]{:S(2)}, u32[]{:S(2)}) collective-permute-start(bf16[768,3,6,128]{0,3,2,1:T(8,128)(2,1)} %collective-permute-done.1), channel_id=1, source_target_pairs={{0,8},{4,0},{12,4},{20,12},{28,20},{24,28},{16,24},{8,16},{1,9},{5... | collective-permute-start | bytes 10616840 | tf_op jit(solution)/shard_map/ppermute | solution.py:89
  168.6 77.0 %collective-permute-start.4 = (bf16[768,3,6,128]{0,3,2,1:T(8,128)(2,1)}, bf16[768,3,6,128]{0,3,2,1:T(8,128)(2,1)S(1)}, u32[]{:S(2)}, u32[]{:S(2)}) collective-permute-start(bf16[768,3,6,128]{0,3,2,1:T(8,128)(2,1)} %collective-permute-done.2), channel_id=1, source_target_pairs={{0,4},{4,12},{12,20},{20,28},{28,24},{24,16},{16,8},{8,0},{1,5},{5... | collective-permute-start | bytes 10616840 | tf_op jit(solution)/shard_map/ppermute | solution.py:88
  170.0 80.6 %collective-permute-start.5 = (bf16[768,3,6,128]{0,3,2,1:T(8,128)(2,1)}, bf16[768,3,6,128]{0,3,2,1:T(8,128)(2,1)}, u32[]{:S(2)}, u32[]{:S(2)}) collective-permute-start(bf16[768,3,6,128]{0,3,2,1:T(8,128)(2,1)} %collective-permute-done.3), channel_id=1, source_target_pairs={{0,8},{4,0},{12,4},{20,12},{28,20},{24,28},{16,24},{8,16},{1,9},{5... | collective-permute-start | bytes 10616840 | tf_op jit(solution)/shard_map/ppermute | solution.py:89
  181.0 3.9 copy-start.1
  245.8 38.1 %collective-permute-start.6 = (bf16[384,3,6,128]{0,3,2,1:T(8,128)(2,1)S(1)}, bf16[384,3,6,128]{0,3,2,1:T(8,128)(2,1)S(1)}, u32[]{:S(2)}, u32[]{:S(2)}) collective-permute-start(bf16[384,3,6,128]{0,3,2,1:T(8,128)(2,1)S(1)} %slice.50), channel_id=1, source_target_pairs={{0,4},{4,12},{12,20},{20,28},{28,24},{24,16},{16,8},{8,0},{1,5},{5... | collective-permute-start | bytes 5308424 | tf_op jit(solution)/shard_map/ppermute | solution.py:97
  253.5 37.7 %collective-permute-start.7 = (bf16[384,3,6,128]{0,3,2,1:T(8,128)(2,1)}, bf16[384,3,6,128]{0,3,2,1:T(8,128)(2,1)S(1)}, u32[]{:S(2)}, u32[]{:S(2)}) collective-permute-start(bf16[384,3,6,128]{0,3,2,1:T(8,128)(2,1)} %slice.51), channel_id=1, source_target_pairs={{0,8},{4,0},{12,4},{20,12},{28,20},{24,28},{16,24},{8,16},{1,9},{5... | collective-permute-start | bytes 5308424 | tf_op jit(solution)/shard_map/ppermute | solution.py:98
  299.6 101.9 %collective-permute-start.10 = (bf16[384,2,6,128]{3,0,2,1:T(8,128)(2,1)}, bf16[384,2,6,128]{3,0,2,1:T(8,128)(2,1)}, u32[]{:S(2)}, u32[]{:S(2)}) collective-permute-start(bf16[384,2,6,128]{3,0,2,1:T(8,128)(2,1)} %copy.19), channel_id=1, source_target_pairs={{0,12},{4,16},{8,20},{12,24},{16,28},{20,0},{24,4},{28,8},{1,13},{... | collective-permute-start | bytes 3538952 | tf_op jit(solution)/shard_map/ppermute | solution.py:54
  302.1 100.6 %collective-permute-start.8 = (bf16[384,2,6,128]{3,0,2,1:T(8,128)(2,1)}, bf16[384,2,6,128]{3,0,2,1:T(8,128)(2,1)}, u32[]{:S(2)}, u32[]{:S(2)}) collective-permute-start(bf16[384,2,6,128]{3,0,2,1:T(8,128)(2,1)} %copy.19), channel_id=1, source_target_pairs={{0,4},{4,8},{8,12},{12,16},{16,20},{20,24},{24,28},{28,0},{1,5},{5... | collective-permute-start | bytes 3538952 | tf_op jit(solution)/shard_map/ppermute | solution.py:54
  302.5 101.6 %collective-permute-start.9 = (bf16[384,2,6,128]{3,0,2,1:T(8,128)(2,1)}, bf16[384,2,6,128]{3,0,2,1:T(8,128)(2,1)}, u32[]{:S(2)}, u32[]{:S(2)}) collective-permute-start(bf16[384,2,6,128]{3,0,2,1:T(8,128)(2,1)} %copy.19), channel_id=1, source_target_pairs={{0,8},{4,12},{8,16},{12,20},{16,24},{20,28},{24,0},{28,4},{1,9},{5... | collective-permute-start | bytes 3538952 | tf_op jit(solution)/shard_map/ppermute | solution.py:54
  411.7 7.5 %copy-start.2 = (bf16[384,1,6,128]{3,0,2,1:T(8,128)(2,1)S(1)}, bf16[384,1,6,128]{3,0,2,1:T(8,128)(2,1)}, u32[]{:S(2)}) copy-start(bf16[384,1,6,128]{3,0,2,1:T(8,128)(2,1)} %copy.20) | copy-start | bytes 1769476
Sparse Core Ops, SparseCore 0:
  14.1 39.0 all-gather.1

commit v2 on v1

--- a/solution.py
+++ b/solution.py
@@ -64,34 +64,26 @@
     ring_arr = jnp.array(ring, jnp.int32)
     pos_arr = jnp.array(pos, jnp.int32)
 
-    def on_device(tokens, qkv_weight):
-        features = lax.all_gather(tokens, "mp", axis=1, tiled=True)
-        rows_dev = features.shape[0]
-        rows_w = qkv_weight.shape[0]
-        heads_local = qkv_weight.shape[2]
-        head_size = qkv_weight.shape[3]
-        scale = 1.0 / math.sqrt(head_size)
-        me = lax.axis_index("ctx")
+    def ring_project(features, piece, me):
+        rows_w = piece.shape[0]
         my_pos = pos_arr[me]
 
-        def partial(block, piece, offset):
+        def partial(block, part, offset):
             start = block * rows_w + offset
-            cols = lax.dynamic_slice_in_dim(features, start, piece.shape[0], axis=1)
-            flat = piece.reshape(piece.shape[0], -1)
+            cols = lax.dynamic_slice_in_dim(features, start, part.shape[0], axis=1)
+            flat = part.reshape(part.shape[0], -1)
             return jnp.dot(cols, flat, preferred_element_type=jnp.float32)
 
-        total = partial(me, qkv_weight, 0)
-        going_cw = qkv_weight
-        going_ccw = qkv_weight
-        full_steps = (n - 1) // 2
-        for step in range(1, full_steps + 1):
+        total = partial(me, piece, 0)
+        going_cw = piece
+        going_ccw = piece
+        for step in range(1, (n - 1) // 2 + 1):
             going_cw = lax.ppermute(going_cw, "ctx", clockwise)
             going_ccw = lax.ppermute(going_ccw, "ctx", counter)
             total = total + partial(ring_arr[(my_pos - step) % n], going_cw, 0)
             total = total + partial(ring_arr[(my_pos + step) % n], going_ccw, 0)
         if n % 2 == 0 and n > 1:
-            step = n // 2
-            far = ring_arr[(my_pos + step) % n]
+            far = ring_arr[(my_pos + n // 2) % n]
             if rows_w % 2 == 0:
                 half = rows_w // 2
                 last_cw = lax.ppermute(going_cw[:half], "ctx", clockwise)
@@ -101,11 +93,37 @@
             else:
                 last_cw = lax.ppermute(going_cw, "ctx", clockwise)
                 total = total + partial(far, last_cw, 0)
+        return total
 
-        projected = total.astype(jnp.bfloat16).reshape(rows_dev, 3, heads_local, head_size)
-        queries = projected[:, 0]
-        key_value = projected[:, 1:]
-        blocks = [key_value] + [shifted(key_value, "ctx", by) for by in range(1, REACH)]
+    def earlier_blocks(key_value, me):
+        if n % 2 or n < 4 or REACH != 4:
+            return [shifted(key_value, "ctx", by) for by in range(1, REACH)]
+        two_back = shifted(key_value, "ctx", 2)
+        to_odd = lax.ppermute(
+            jnp.stack([key_value, two_back]), "ctx", [(e, e + 1) for e in range(0, n, 2)]
+        )
+        to_even = lax.ppermute(two_back, "ctx", [(o, o - 1) for o in range(1, n, 2)])
+        three_back = lax.ppermute(to_even, "ctx", [(e, (e + 2) % n) for e in range(0, n, 2)])
+        odd = (me % 2) == 1
+        one_back = jnp.where(odd, to_odd[0], to_even)
+        three_back = jnp.where(odd, to_odd[1], three_back)
+        return [one_back, two_back, three_back]
+
+    def on_device(tokens, qkv_weight):
+        features = lax.all_gather(tokens, "mp", axis=1, tiled=True)
+        rows_dev = features.shape[0]
+        heads_local = qkv_weight.shape[2]
+        head_size = qkv_weight.shape[3]
+        scale = 1.0 / math.sqrt(head_size)
+        me = lax.axis_index("ctx")
+
+        kv_total = ring_project(features, qkv_weight[:, 1:], me)
+        key_value = kv_total.astype(jnp.bfloat16).reshape(rows_dev, 2, heads_local, head_size)
+        q_piece, key_value = lax.optimization_barrier((qkv_weight[:, 0], key_value))
+        blocks = [key_value] + earlier_blocks(key_value, me)
+        q_total = ring_project(features, q_piece, me)
+        queries = q_total.astype(jnp.bfloat16).reshape(rows_dev, heads_local, head_size)
+
         key_rows = jnp.concatenate([block[:, 0] for block in blocks], axis=0)
         value_rows = jnp.concatenate([block[:, 1] for block in blocks], axis=0)
         scores = (

time: 434 us -> 393 us (0.906)
  waiting for transfers between devices: 330 us -> 265 us
  starting transfers between devices: 13.8 us -> 29.2 us
  matrix products: 40.4 us -> 48.4 us
    ppermute x3 -> x1, waiting for transfers between devices: 95.8 us -> 3.14 us  [shifted(): lax.ppermute(array, axis, [(i, (i + by) % devices) for i in range(devices)])]
    ppermute x8 -> x19, waiting for transfers between devices: 234 us -> 262 us  [the longest x6 227 us: ring_project(): going_cw = lax.ppermute(going_cw, 'ctx', clockwise)]
    ppermute x8 -> x19, starting transfers between devices: 9.26 us -> 27.8 us  [the longest x6 7.93 us: ring_project(): going_cw = lax.ppermute(going_cw, 'ctx', clockwise)]
    dot_general x9 -> x18, matrix products: 27.1 us -> 33.1 us  [partial(): return jnp.dot(cols, flat, preferred_element_type=jnp.float32)]
  transfers between devices with their start and end apart: 12 -> 21, of which waited for: 6 -> 12; matrix products, arithmetic and copies ran while one was open for 7% -> 11% of each run, Pallas kernels for 0% -> 0%
where the time goes in v2:
time: 393 us; the launch traced here: 392 us
  waiting for transfers between devices  265 us (67%)
  matrix products  48.4 us (12%)
  starting transfers between devices  29.2 us (7%)
  between operations  22.8 us (6%)
  local copies, waits for them, and re-layouts  17.5 us (4%)
  other arithmetic  9.49 us (2%)
    ppermute x6, waiting for transfers between devices, ring_project(): going_cw = lax.ppermute(going_cw, 'ctx', clockwise)  227 us
    dot_general x18, matrix products, partial(): return jnp.dot(cols, flat, preferred_element_type=jnp.float32)  33.1 us
    ppermute x1, waiting for transfers between devices, earlier_blocks(): lax.ppermute(two_back, 'ctx', [(o, o - 1) for o in range(1, n, 2)])  20.9 us
    ppermute x2, waiting for transfers between devices, ring_project(): last_cw = lax.ppermute(going_cw[:half], 'ctx', clockwise)  10.6 us
    dot_general x1, matrix products, on_device(): jnp.einsum('thd,shd->hts', queries, key_rows, preferred_element_type=jnp....  8.27 us
    ppermute x6, starting transfers between devices, ring_project(): going_cw = lax.ppermute(going_cw, 'ctx', clockwise)  7.93 us
  transfers between devices with their start and end apart: 21, of which 12 were waited for; matrix products, arithmetic and copies ran while one was open for 11% of the time, Pallas kernels for 0%

profile of v2, /device:TPU:0, one launch (start us, length us, event | category | flops | bytes accessed | tf_op | source)
XLA Modules:
  0.0 392.1 jit_solution(12178070460761239656)
XLA Ops:
  8.2 2.4 copy.21
  10.6 3.0 collective-permute-start
  13.7 51.4 %collective-permute-done = bf16[768,2,6,128]{0,3,2,1:T(8,128)(2,1)S(1)} collective-permute-done((bf16[768,2,6,128]{0,3,2,1:T(8,128)(2,1)}, bf16[768,2,6,128]{0,3,2,1:T(8,128)(2,1)S(1)}, u32[]{:S(2)}, u32[]{:S(2)}) %collective-permute-start) | collective-permute-done | bytes 2359328 | tf_op jit(solution)/shard_map/ppermute | solution.py:81
  67.1 50.6 %collective-permute-done.2 = bf16[768,2,6,128]{0,3,2,1:T(8,128)(2,1)} collective-permute-done((bf16[768,2,6,128]{0,3,2,1:T(8,128)(2,1)S(1)}, bf16[768,2,6,128]{0,3,2,1:T(8,128)(2,1)}, u32[]{:S(2)}, u32[]{:S(2)}) %collective-permute-start.2) | collective-permute-done | bytes 2359328 | tf_op jit(solution)/shard_map/ppermute | solution.py:81
  131.6 38.0 %collective-permute-done.4 = bf16[768,2,6,128]{0,3,2,1:T(8,128)(2,1)S(1)} collective-permute-done((bf16[768,2,6,128]{0,3,2,1:T(8,128)(2,1)}, bf16[768,2,6,128]{0,3,2,1:T(8,128)(2,1)S(1)}, u32[]{:S(2)}, u32[]{:S(2)}) %collective-permute-start.4) | collective-permute-done | bytes 2359328 | tf_op jit(solution)/shard_map/ppermute | solution.py:81
  170.8 2.4 slice.65
  174.2 3.1 fusion.60
  177.4 2.9 fusion.50
  181.5 2.8 fusion.44
  184.3 2.8 convolution_add_fusion.2
  187.1 2.9 fusion.6
  190.0 5.4 %collective-permute-done.6 = bf16[384,2,6,128]{0,3,2,1:T(8,128)(2,1)} collective-permute-done((bf16[384,2,6,128]{0,3,2,1:T(8,128)(2,1)S(1)}, bf16[384,2,6,128]{0,3,2,1:T(8,128)(2,1)}, u32[]{:S(2)}, u32[]{:S(2)}) %collective-permute-start.6) | collective-permute-done | bytes 1179680 | tf_op jit(solution)/shard_map/ppermute | solution.py:89
  208.5 43.5 %collective-permute-done.8 = bf16[768,6,128]{0,2,1:T(8,128)(2,1)} collective-permute-done((bf16[768,6,128]{0,2,1:T(8,128)(2,1)S(1)}, bf16[768,6,128]{0,2,1:T(8,128)(2,1)}, u32[]{:S(2)}, u32[]{:S(2)}) %collective-permute-start.8) | collective-permute-done | bytes 1179680 | tf_op jit(solution)/shard_map/ppermute | solution.py:81
  251.9 3.5 collective-permute-start.11
  255.5 3.1 collective-permute-done.16
  260.3 5.2 %collective-permute-start.17 = (bf16[2,384,2,6,128]{4,1,3,2,0:T(8,128)(2,1)S(1)}, bf16[2,384,2,6,128]{4,1,3,2,0:T(8,128)(2,1)S(1)}, u32[]{:S(2)}, u32[]{:S(2)}) collective-permute-start(bf16[2,384,2,6,128]{4,1,3,2,0:T(8,128)(2,1)S(1)} %pad_maximum_fusion), channel_id=1, source_target_pairs={{0,4},{8,12},{16,20},{24,28},{1,5},{9,13},{17,21},{25,29},{2,6},{1... | collective-permute-start | bytes 7077896 | tf_op jit(solution)/shard_map/ppermute | solution.py:102
  271.6 8.6 %collective-permute-done.10 = bf16[768,6,128]{0,2,1:T(8,128)(2,1)} collective-permute-done((bf16[768,6,128]{0,2,1:T(8,128)(2,1)}, bf16[768,6,128]{0,2,1:T(8,128)(2,1)}, u32[]{:S(2)}, u32[]{:S(2)}) %collective-permute-start.10) | collective-permute-done | bytes 1179680 | tf_op jit(solution)/shard_map/ppermute | solution.py:81
  284.1 20.9 %collective-permute-done.18 = bf16[384,2,6,128]{3,0,2,1:T(8,128)(2,1)S(1)} collective-permute-done((bf16[384,2,6,128]{3,0,2,1:T(8,128)(2,1)}, bf16[384,2,6,128]{3,0,2,1:T(8,128)(2,1)S(1)}, u32[]{:S(2)}, u32[]{:S(2)}) %collective-permute-start.18) | collective-permute-done | bytes 1179680 | tf_op jit(solution)/shard_map/ppermute | solution.py:105
  313.2 34.9 %collective-permute-done.12 = bf16[768,6,128]{0,2,1:T(8,128)(2,1)S(1)} collective-permute-done((bf16[768,6,128]{0,2,1:T(8,128)(2,1)}, bf16[768,6,128]{0,2,1:T(8,128)(2,1)S(1)}, u32[]{:S(2)}, u32[]{:S(2)}) %collective-permute-start.12) | collective-permute-done | bytes 1179680 | tf_op jit(solution)/shard_map/ppermute | solution.py:81
  348.2 2.4 collective-permute-start.14
  352.9 5.2 %collective-permute-done.14 = bf16[384,6,128]{0,2,1:T(8,128)(2,1)S(1)} collective-permute-done((bf16[384,6,128]{0,2,1:T(8,128)(2,1)S(1)}, bf16[384,6,128]{0,2,1:T(8,128)(2,1)S(1)}, u32[]{:S(2)}, u32[]{:S(2)}) %collective-permute-start.14) | collective-permute-done | bytes 589856 | tf_op jit(solution)/shard_map/ppermute | solution.py:89
  362.2 8.3 %multiply_reduce_fusion = (f32[6,384]{1,0:T(8,128)S(1)}, f32[6,384,1536]{2,1,0:T(8,128)}) fusion(bf16[384,6,128]{0,2,1:T(8,128)(2,1)S(1)} %bitcast.93, bf16[384,6,128]{2,0,1:T(8,128)(2,1)S(1)} %get-tuple-element.17, bf16[384,6,128]{2,0,1:T(8,128)(2,1)} %get-tuple-element.15, bf16[384,6,128]{2,0,1:T(8,128)(2,1)S(1)} %get-tuple-element.29, ...), kind=kOutput, calls=%fused_computation.1 | convolution fusion | flops 922482432 | bytes 17114112 | tf_op jit(solution)/shard_map/thd,shd->hts/dot_general | solution.py:130
  370.5 7.6 %fusion = f32[6,384]{1,0:T(8,128)S(1)} fusion(f32[6,384,1536]{2,1,0:T(8,128)} %get-tuple-element.27, f32[6,384]{1,0:T(8,128)S(1)} %get-tuple-element.26), kind=kLoop, calls=%fused_computation.2 | loop fusion | flops 10614528 | bytes 14174208 | tf_op jit(solution)/shard_map/reduce_sum | solution.py:134
  378.2 7.1 %divide_convert_fusion = bf16[384,6,128]{2,0,1:T(8,128)(2,1)} fusion(bf16[384,6,128]{2,0,1:T(8,128)(2,1)S(1)} %copy-done.4, bf16[384,6,128]{2,0,1:T(8,128)(2,1)S(1)} %copy-done.7, bf16[384,6,128]{2,0,1:T(8,128)(2,1)S(1)} %copy-done.5, bf16[384,6,128]{2,0,1:T(8,128)(2,1)S(1)} %copy-done.6, f32[6,384,1536]{2,1,0:T(8,128)} %get-tuple-element.27, ...), kind=kOutput, calls=%fused_computation.46 | convolution fusion | flops 926613504 | bytes 17123328 | tf_op jit(solution)/shard_map/hts,shd->htd/dot_general | solution.py:137
  (85 shorter events, 51.3 us)
Async XLA Ops:
  6.5 167.7 %all-gather.2.cloned.1.call-start = ((), (), s32[]{:S(2)}) async-start(), calls=%async_computation | async-start | bytes 5898240 | tf_op jit(solution)/shard_map/all_gather | solution.py:113
  8.2 111.6 %copy-start.9 = (s32[8]{0:T(128)S(1)}, s32[8]{0:T(128)}, u32[]{:S(2)}) copy-start(s32[8]{0:T(128)} %constant.114.clone) | copy-start | bytes 100
  8.2 116.8 %copy-start.8 = (s32[8]{0:T(128)S(1)}, s32[8]{0:T(128)}, u32[]{:S(2)}) copy-start(s32[8]{0:T(128)} %constant.115.clone) | copy-start | bytes 100
  10.6 119.5 %slice-start.3 = ((bf16[768,3,6,128]{3,0,2,1:T(8,128)(2,1)}), bf16[768,1,6,128]{3,0,2,1:T(8,128)(2,1)S(1)}, s32[]{:S(2)}) async-start(bf16[768,3,6,128]{3,0,2,1:T(8,128)(2,1)} %param.5), calls=%async_computation.4 | async-start | bytes 2359296 | tf_op jit(solution)/shard_map/slice | solution.py:122
  10.6 54.5 %collective-permute-start = (bf16[768,2,6,128]{0,3,2,1:T(8,128)(2,1)}, bf16[768,2,6,128]{0,3,2,1:T(8,128)(2,1)S(1)}, u32[]{:S(2)}, u32[]{:S(2)}) collective-permute-start(bf16[768,2,6,128]{0,3,2,1:T(8,128)(2,1)} %copy.21), channel_id=1, source_target_pairs={{0,4},{4,12},{12,20},{20,28},{28,24},{24,16},{16,8},{8,0},{1,5},{5... | collective-permute-start | bytes 7077896 | tf_op jit(solution)/shard_map/ppermute | solution.py:81
  13.6 53.2 %collective-permute-start.1 = (bf16[768,2,6,128]{0,3,2,1:T(8,128)(2,1)}, bf16[768,2,6,128]{0,3,2,1:T(8,128)(2,1)}, u32[]{:S(2)}, u32[]{:S(2)}) collective-permute-start(bf16[768,2,6,128]{0,3,2,1:T(8,128)(2,1)} %copy.21), channel_id=1, source_target_pairs={{0,8},{4,0},{12,4},{20,12},{28,20},{24,28},{16,24},{8,16},{1,9},{5... | collective-permute-start | bytes 7077896 | tf_op jit(solution)/shard_map/ppermute | solution.py:82
  65.1 52.6 %collective-permute-start.2 = (bf16[768,2,6,128]{0,3,2,1:T(8,128)(2,1)S(1)}, bf16[768,2,6,128]{0,3,2,1:T(8,128)(2,1)}, u32[]{:S(2)}, u32[]{:S(2)}) collective-permute-start(bf16[768,2,6,128]{0,3,2,1:T(8,128)(2,1)S(1)} %collective-permute-done), channel_id=1, source_target_pairs={{0,4},{4,12},{12,20},{20,28},{28,24},{24,16},{16,8},{8,0},{1,5},{5... | collective-permute-start | bytes 7077896 | tf_op jit(solution)/shard_map/ppermute | solution.py:81
  66.8 52.3 %collective-permute-start.3 = (bf16[768,2,6,128]{0,3,2,1:T(8,128)(2,1)}, bf16[768,2,6,128]{0,3,2,1:T(8,128)(2,1)}, u32[]{:S(2)}, u32[]{:S(2)}) collective-permute-start(bf16[768,2,6,128]{0,3,2,1:T(8,128)(2,1)} %collective-permute-done.1), channel_id=1, source_target_pairs={{0,8},{4,0},{12,4},{20,12},{28,20},{24,28},{16,24},{8,16},{1,9},{5... | collective-permute-start | bytes 7077896 | tf_op jit(solution)/shard_map/ppermute | solution.py:82
  117.7 51.8 %collective-permute-start.4 = (bf16[768,2,6,128]{0,3,2,1:T(8,128)(2,1)}, bf16[768,2,6,128]{0,3,2,1:T(8,128)(2,1)S(1)}, u32[]{:S(2)}, u32[]{:S(2)}) collective-permute-start(bf16[768,2,6,128]{0,3,2,1:T(8,128)(2,1)} %collective-permute-done.2), channel_id=1, source_target_pairs={{0,4},{4,12},{12,20},{20,28},{28,24},{24,16},{16,8},{8,0},{1,5},{5... | collective-permute-start | bytes 7077896 | tf_op jit(solution)/shard_map/ppermute | solution.py:81
  119.1 51.7 %collective-permute-start.5 = (bf16[768,2,6,128]{0,3,2,1:T(8,128)(2,1)}, bf16[768,2,6,128]{0,3,2,1:T(8,128)(2,1)}, u32[]{:S(2)}, u32[]{:S(2)}) collective-permute-start(bf16[768,2,6,128]{0,3,2,1:T(8,128)(2,1)} %collective-permute-done.3), channel_id=1, source_target_pairs={{0,8},{4,0},{12,4},{20,12},{28,20},{24,28},{16,24},{8,16},{1,9},{5... | collective-permute-start | bytes 7077896 | tf_op jit(solution)/shard_map/ppermute | solution.py:82
  169.7 25.7 %collective-permute-start.6 = (bf16[384,2,6,128]{0,3,2,1:T(8,128)(2,1)S(1)}, bf16[384,2,6,128]{0,3,2,1:T(8,128)(2,1)}, u32[]{:S(2)}, u32[]{:S(2)}) collective-permute-start(bf16[384,2,6,128]{0,3,2,1:T(8,128)(2,1)S(1)} %slice.64), channel_id=1, source_target_pairs={{0,4},{4,12},{12,20},{20,28},{28,24},{24,16},{16,8},{8,0},{1,5},{5... | collective-permute-start | bytes 3538952 | tf_op jit(solution)/shard_map/ppermute | solution.py:89
  173.2 25.2 %collective-permute-start.7 = (bf16[384,2,6,128]{0,3,2,1:T(8,128)(2,1)}, bf16[384,2,6,128]{0,3,2,1:T(8,128)(2,1)}, u32[]{:S(2)}, u32[]{:S(2)}) collective-permute-start(bf16[384,2,6,128]{0,3,2,1:T(8,128)(2,1)} %slice.65), channel_id=1, source_target_pairs={{0,8},{4,0},{12,4},{20,12},{28,20},{24,28},{16,24},{8,16},{1,9},{5... | collective-permute-start | bytes 3538952 | tf_op jit(solution)/shard_map/ppermute | solution.py:90
  203.3 48.6 %collective-permute-start.8 = (bf16[768,6,128]{0,2,1:T(8,128)(2,1)S(1)}, bf16[768,6,128]{0,2,1:T(8,128)(2,1)}, u32[]{:S(2)}, u32[]{:S(2)}) collective-permute-start(bf16[768,6,128]{0,2,1:T(8,128)(2,1)S(1)} %bitcast.89), channel_id=1, source_target_pairs={{0,4},{4,12},{12,20},{20,28},{28,24},{24,16},{16,8},{8,0},{1,5},{5... | collective-permute-start | bytes 3538952 | tf_op jit(solution)/shard_map/ppermute | solution.py:81
  204.9 47.0 %collective-permute-start.9 = (bf16[768,6,128]{0,2,1:T(8,128)(2,1)S(1)}, bf16[768,6,128]{0,2,1:T(8,128)(2,1)}, u32[]{:S(2)}, u32[]{:S(2)}) collective-permute-start(bf16[768,6,128]{0,2,1:T(8,128)(2,1)S(1)} %bitcast.90), channel_id=1, source_target_pairs={{0,8},{4,0},{12,4},{20,12},{28,20},{24,28},{16,24},{8,16},{1,9},{5... | collective-permute-start | bytes 3538952 | tf_op jit(solution)/shard_map/ppermute | solution.py:82
  207.1 51.5 %collective-permute-start.16 = (bf16[384,2,6,128]{3,0,2,1:T(8,128)(2,1)S(1)}, bf16[384,2,6,128]{3,0,2,1:T(8,128)(2,1)}, u32[]{:S(2)}, u32[]{:S(2)}) collective-permute-start(bf16[384,2,6,128]{3,0,2,1:T(8,128)(2,1)S(1)} %copy.14), channel_id=1, source_target_pairs={{0,8},{4,12},{8,16},{12,20},{16,24},{20,28},{24,0},{28,4},{1,9},{5... | collective-permute-start | bytes 3538952 | tf_op jit(solution)/shard_map/ppermute | solution.py:54
  251.9 28.2 %collective-permute-start.10 = (bf16[768,6,128]{0,2,1:T(8,128)(2,1)}, bf16[768,6,128]{0,2,1:T(8,128)(2,1)}, u32[]{:S(2)}, u32[]{:S(2)}) collective-permute-start(bf16[768,6,128]{0,2,1:T(8,128)(2,1)} %collective-permute-done.8), channel_id=1, source_target_pairs={{0,4},{4,12},{12,20},{20,28},{28,24},{24,16},{16,8},{8,0},{1,5},{5... | collective-permute-start | bytes 3538952 | tf_op jit(solution)/shard_map/ppermute | solution.py:81
  251.9 28.5 %collective-permute-start.11 = (bf16[768,6,128]{0,2,1:T(8,128)(2,1)}, bf16[768,6,128]{0,2,1:T(8,128)(2,1)}, u32[]{:S(2)}, u32[]{:S(2)}) collective-permute-start(bf16[768,6,128]{0,2,1:T(8,128)(2,1)} %collective-permute-done.9), channel_id=1, source_target_pairs={{0,8},{4,0},{12,4},{20,12},{28,20},{24,28},{16,24},{8,16},{1,9},{5... | collective-permute-start | bytes 3538952 | tf_op jit(solution)/shard_map/ppermute | solution.py:82
  260.3 91.2 %collective-permute-start.17 = (bf16[2,384,2,6,128]{4,1,3,2,0:T(8,128)(2,1)S(1)}, bf16[2,384,2,6,128]{4,1,3,2,0:T(8,128)(2,1)S(1)}, u32[]{:S(2)}, u32[]{:S(2)}) collective-permute-start(bf16[2,384,2,6,128]{4,1,3,2,0:T(8,128)(2,1)S(1)} %pad_maximum_fusion), channel_id=1, source_target_pairs={{0,4},{8,12},{16,20},{24,28},{1,5},{9,13},{17,21},{25,29},{2,6},{1... | collective-permute-start | bytes 7077896 | tf_op jit(solution)/shard_map/ppermute | solution.py:102
  265.5 39.6 %collective-permute-start.18 = (bf16[384,2,6,128]{3,0,2,1:T(8,128)(2,1)}, bf16[384,2,6,128]{3,0,2,1:T(8,128)(2,1)S(1)}, u32[]{:S(2)}, u32[]{:S(2)}) collective-permute-start(bf16[384,2,6,128]{3,0,2,1:T(8,128)(2,1)} %collective-permute-done.16), channel_id=1, source_target_pairs={{4,0},{12,8},{20,16},{28,24},{5,1},{13,9},{21,17},{29,25},{6,2},{1... | collective-permute-start | bytes 3538952 | tf_op jit(solution)/shard_map/ppermute | solution.py:105
  280.1 68.0 %collective-permute-start.12 = (bf16[768,6,128]{0,2,1:T(8,128)(2,1)}, bf16[768,6,128]{0,2,1:T(8,128)(2,1)S(1)}, u32[]{:S(2)}, u32[]{:S(2)}) collective-permute-start(bf16[768,6,128]{0,2,1:T(8,128)(2,1)} %collective-permute-done.10), channel_id=1, source_target_pairs={{0,4},{4,12},{12,20},{20,28},{28,24},{24,16},{16,8},{8,0},{1,5},{5... | collective-permute-start | bytes 3538952 | tf_op jit(solution)/shard_map/ppermute | solution.py:81
  280.5 70.1 %collective-permute-start.13 = (bf16[768,6,128]{0,2,1:T(8,128)(2,1)}, bf16[768,6,128]{0,2,1:T(8,128)(2,1)S(1)}, u32[]{:S(2)}, u32[]{:S(2)}) collective-permute-start(bf16[768,6,128]{0,2,1:T(8,128)(2,1)} %collective-permute-done.11), channel_id=1, source_target_pairs={{0,8},{4,0},{12,4},{20,12},{28,20},{24,28},{16,24},{8,16},{1,9},{5... | collective-permute-start | bytes 3538952 | tf_op jit(solution)/shard_map/ppermute | solution.py:82
  305.0 46.4 %collective-permute-start.19 = (bf16[384,2,6,128]{3,0,2,1:T(8,128)(2,1)S(1)}, bf16[384,2,6,128]{3,0,2,1:T(8,128)(2,1)S(1)}, u32[]{:S(2)}, u32[]{:S(2)}) collective-permute-start(bf16[384,2,6,128]{3,0,2,1:T(8,128)(2,1)S(1)} %collective-permute-done.18), channel_id=1, source_target_pairs={{0,8},{8,16},{16,24},{24,0},{1,9},{9,17},{17,25},{25,1},{2,10},{10... | collective-permute-start | bytes 3538952 | tf_op jit(solution)/shard_map/ppermute | solution.py:106
  348.2 9.9 %collective-permute-start.14 = (bf16[384,6,128]{0,2,1:T(8,128)(2,1)S(1)}, bf16[384,6,128]{0,2,1:T(8,128)(2,1)S(1)}, u32[]{:S(2)}, u32[]{:S(2)}) collective-permute-start(bf16[384,6,128]{0,2,1:T(8,128)(2,1)S(1)} %slice.66), channel_id=1, source_target_pairs={{0,4},{4,12},{12,20},{20,28},{28,24},{24,16},{16,8},{8,0},{1,5},{5... | collective-permute-start | bytes 1769480 | tf_op jit(solution)/shard_map/ppermute | solution.py:89
  350.7 9.9 %collective-permute-start.15 = (bf16[384,6,128]{0,2,1:T(8,128)(2,1)S(1)}, bf16[384,6,128]{0,2,1:T(8,128)(2,1)S(1)}, u32[]{:S(2)}, u32[]{:S(2)}) collective-permute-start(bf16[384,6,128]{0,2,1:T(8,128)(2,1)S(1)} %slice.67), channel_id=1, source_target_pairs={{0,8},{4,0},{12,4},{20,12},{28,20},{24,28},{16,24},{8,16},{1,9},{5... | collective-permute-start | bytes 1769480 | tf_op jit(solution)/shard_map/ppermute | solution.py:90
  (11 other events, 117.1 us)
Sparse Core Ops, SparseCore 0:
  13.8 39.1 all-gather.1

commit v3 on v2

--- a/solution.py
+++ b/solution.py
@@ -1,11 +1,60 @@
+import functools
 import math
 
 import jax
 import jax.numpy as jnp
 from jax import lax
+from jax.experimental import pallas as pl
+from jax.experimental.pallas import tpu as pltpu
 from jax.sharding import PartitionSpec as P
 
 REACH = 4
+
+
+def attention_kernel(scale, reach, q_ref, *refs):
+    k_refs = refs[:reach]
+    v_refs = refs[reach : 2 * reach]
+    o_ref = refs[2 * reach]
+    q = q_ref[...]
+    scores = [
+        lax.dot_general(q, k_ref[...], (((1,), (1,)), ((), ())), preferred_element_type=jnp.float32) * scale
+        for k_ref in k_refs
+    ]
+    top = scores[0].max(axis=-1, keepdims=True)
+    for s in scores[1:]:
+        top = jnp.maximum(top, s.max(axis=-1, keepdims=True))
+    expos = [jnp.exp(s - top) for s in scores]
+    totals = expos[0].sum(axis=-1, keepdims=True)
+    for e in expos[1:]:
+        totals = totals + e.sum(axis=-1, keepdims=True)
+    mixed = jnp.dot(expos[0].astype(jnp.bfloat16), v_refs[0][...], preferred_element_type=jnp.float32)
+    for e, v_ref in zip(expos[1:], v_refs[1:]):
+        mixed = mixed + jnp.dot(e.astype(jnp.bfloat16), v_ref[...], preferred_element_type=jnp.float32)
+    o_ref[...] = (mixed / totals).astype(o_ref.dtype)
+
+
+def windowed_attention(queries, blocks, scale):
+    rows, heads, size = queries.shape
+    reach = len(blocks)
+    q2d = queries.reshape(rows, heads * size)
+    kv2d = [block.reshape(rows, 2 * heads * size) for block in blocks]
+    q_spec = pl.BlockSpec((rows, size), lambda h: (0, h))
+    v_spec = pl.BlockSpec((rows, size), lambda h: (0, h + heads))
+    keys = rows * reach
+    cost = pl.CostEstimate(
+        flops=4 * rows * keys * size * heads,
+        transcendentals=rows * keys * heads,
+        bytes_accessed=2 * (2 * rows * heads * size + 2 * keys * heads * size),
+    )
+    out = pl.pallas_call(
+        functools.partial(attention_kernel, scale, reach),
+        out_shape=jax.ShapeDtypeStruct((rows, heads * size), jnp.bfloat16),
+        grid=(heads,),
+        in_specs=[q_spec] + [q_spec] * reach + [v_spec] * reach,
+        out_specs=q_spec,
+        cost_estimate=cost,
+    )(q2d, *kv2d, *kv2d)
+    return out.reshape(rows, heads, size)
 
 
 def ring_order(mesh):
@@ -124,19 +173,7 @@
         q_total = ring_project(features, q_piece, me)
         queries = q_total.astype(jnp.bfloat16).reshape(rows_dev, heads_local, head_size)
 
-        key_rows = jnp.concatenate([block[:, 0] for block in blocks], axis=0)
-        value_rows = jnp.concatenate([block[:, 1] for block in blocks], axis=0)
-        scores = (
-            jnp.einsum("thd,shd->hts", queries, key_rows, preferred_element_type=jnp.float32) * scale
-        )
-        top = jnp.max(scores, axis=-1, keepdims=True)
-        expo = jnp.exp(scores - top)
-        totals = jnp.sum(expo, axis=-1, keepdims=True)
-        probs = expo.astype(jnp.bfloat16)
-        mixed = (
-            jnp.einsum("hts,shd->htd", probs, value_rows, preferred_element_type=jnp.float32) / totals
-        )
-        return jnp.transpose(mixed, (1, 0, 2)).astype(jnp.bfloat16)
+        return windowed_attention(queries, blocks, scale)
 
     return on_device
 

time: 393 us -> 388 us (0.987)
  Pallas kernels: 0 us -> 9.25 us
  matrix products: 48.4 us -> 41.3 us
  waiting for transfers between devices: 265 us -> 258 us
  other arithmetic: 9.49 us -> 4 us
  local copies, waits for them, and re-layouts: 17.5 us -> 21.6 us
    ppermute x6, waiting for transfers between devices: 227 us -> 195 us  [ring_project(): going_cw = lax.ppermute(going_cw, 'ctx', clockwise)]
    ppermute x6, waiting for transfers between devices: 0.02 us -> 28.1 us  [ring_project(): going_ccw = lax.ppermute(going_ccw, 'ctx', counter)]
    dot_general x2 -> x0, matrix products: 15.3 us -> none  [the longest x1 8.27 us: on_device(): jnp.einsum('thd,shd->hts', queries, key_rows, preferred_element_type=jnp....]
    pallas_call x0 -> x1, Pallas kernels: none -> 9.25 us  [windowed_attention(): pl.pallas_call(functools.partial(attention_kernel, scale, reach), out_sha...]
    dot_general x18, matrix products: 33.1 us -> 41.3 us  [partial(): return jnp.dot(cols, flat, preferred_element_type=jnp.float32)]
    reduce_sum x1 -> x0, other arithmetic: 7.62 us -> none  [on_device(): totals = jnp.sum(expo, axis=-1, keepdims=True)]
    reshape x0 -> x5, local copies, waits for them, and re-layouts: none -> 7.08 us  [the longest x4 6.02 us: windowed_attention(): kv2d = [block.reshape(rows, 2 * heads * size) for block in blocks]]
    ppermute x2, waiting for transfers between devices: 10.6 us -> 5.36 us  [ring_project(): last_cw = lax.ppermute(going_cw[:half], 'ctx', clockwise)]
  transfers between devices with their start and end apart: 21 -> 21, of which waited for: 12 -> 12; matrix products, arithmetic and copies ran while one was open for 11% -> 13% of each run, Pallas kernels for 0% -> 0%
where the time goes in v3:
time: 388 us; the launch traced here: 387 us
  waiting for transfers between devices  258 us (66%)
  matrix products  41.3 us (11%)
  starting transfers between devices  30.6 us (8%)
  between operations  22.8 us (6%)
  local copies, waits for them, and re-layouts  21.6 us (6%)
  Pallas kernels  9.25 us (2%)
  other arithmetic  4 us (1%)
    ppermute x6, waiting for transfers between devices, ring_project(): going_cw = lax.ppermute(going_cw, 'ctx', clockwise)  195 us
    dot_general x18, matrix products, partial(): return jnp.dot(cols, flat, preferred_element_type=jnp.float32)  41.3 us
    ppermute x6, waiting for transfers between devices, ring_project(): going_ccw = lax.ppermute(going_ccw, 'ctx', counter)  28.1 us
    ppermute x1, waiting for transfers between devices, earlier_blocks(): lax.ppermute(two_back, 'ctx', [(o, o - 1) for o in range(1, n, 2)])  20.2 us
    pallas_call x1, Pallas kernels, windowed_attention(): pl.pallas_call(functools.partial(attention_kernel, scale, reach), out_sha...  9.25 us
  transfers between devices with their start and end apart: 21, of which 12 were waited for; matrix products, arithmetic and copies ran while one was open for 13% of the time, Pallas kernels for 0%

profile of v3, /device:TPU:0, one launch (start us, length us, event | category | flops | bytes accessed | tf_op | source)
XLA Modules:
  0.0 387.3 jit_solution(6241964964723201074)
XLA Ops:
  8.2 2.4 copy.20
  10.6 3.0 collective-permute-start
  13.7 51.4 %collective-permute-done = bf16[768,2,6,128]{0,3,2,1:T(8,128)(2,1)S(1)} collective-permute-done((bf16[768,2,6,128]{0,3,2,1:T(8,128)(2,1)}, bf16[768,2,6,128]{0,3,2,1:T(8,128)(2,1)S(1)}, u32[]{:S(2)}, u32[]{:S(2)}) %collective-permute-start) | collective-permute-done | bytes 2359328 | tf_op jit(solution)/shard_map/ppermute | solution.py:130
  67.1 50.6 %collective-permute-done.2 = bf16[768,2,6,128]{0,3,2,1:T(8,128)(2,1)} collective-permute-done((bf16[768,2,6,128]{0,3,2,1:T(8,128)(2,1)S(1)}, bf16[768,2,6,128]{0,3,2,1:T(8,128)(2,1)}, u32[]{:S(2)}, u32[]{:S(2)}) %collective-permute-start.2) | collective-permute-done | bytes 2359328 | tf_op jit(solution)/shard_map/ppermute | solution.py:130
  131.7 37.9 %collective-permute-done.4 = bf16[768,2,6,128]{0,3,2,1:T(8,128)(2,1)S(1)} collective-permute-done((bf16[768,2,6,128]{0,3,2,1:T(8,128)(2,1)}, bf16[768,2,6,128]{0,3,2,1:T(8,128)(2,1)S(1)}, u32[]{:S(2)}, u32[]{:S(2)}) %collective-permute-start.4) | collective-permute-done | bytes 2359328 | tf_op jit(solution)/shard_map/ppermute | solution.py:130
  170.8 2.4 slice.33
  174.2 3.1 fusion.30
  177.5 2.9 fusion.20
  181.6 2.8 fusion.14
  184.4 2.8 convolution_add_fusion.2
  187.2 2.9 fusion
  190.0 5.4 %collective-permute-done.6 = bf16[384,2,6,128]{0,3,2,1:T(8,128)(2,1)} collective-permute-done((bf16[384,2,6,128]{0,3,2,1:T(8,128)(2,1)S(1)}, bf16[384,2,6,128]{0,3,2,1:T(8,128)(2,1)}, u32[]{:S(2)}, u32[]{:S(2)}) %collective-permute-start.6) | collective-permute-done | bytes 1179680 | tf_op jit(solution)/shard_map/ppermute | solution.py:138
  208.1 24.4 %collective-permute-done.9 = bf16[768,6,128]{0,2,1:T(8,128)(2,1)} collective-permute-done((bf16[768,6,128]{0,2,1:T(8,128)(2,1)S(1)}, bf16[768,6,128]{0,2,1:T(8,128)(2,1)}, u32[]{:S(2)}, u32[]{:S(2)}) %collective-permute-start.9) | collective-permute-done | bytes 1179680 | tf_op jit(solution)/shard_map/ppermute | solution.py:131
  232.5 2.6 collective-permute-start.11
  235.1 19.9 %collective-permute-done.8 = bf16[768,6,128]{0,2,1:T(8,128)(2,1)} collective-permute-done((bf16[768,6,128]{0,2,1:T(8,128)(2,1)S(1)}, bf16[768,6,128]{0,2,1:T(8,128)(2,1)}, u32[]{:S(2)}, u32[]{:S(2)}) %collective-permute-start.8) | collective-permute-done | bytes 1179680 | tf_op jit(solution)/shard_map/ppermute | solution.py:130
  255.1 6.5 %collective-permute-done.16 = bf16[384,2,6,128]{0,3,2,1:T(8,128)(2,1)S(1)} collective-permute-done((bf16[384,2,6,128]{0,3,2,1:T(8,128)(2,1)S(1)}, bf16[384,2,6,128]{0,3,2,1:T(8,128)(2,1)S(1)}, u32[]{:S(2)}, u32[]{:S(2)}) %collective-permute-start.16) | collective-permute-done | bytes 1179680 | tf_op jit(solution)/shard_map/ppermute | solution.py:103
  264.6 7.0 %collective-permute-start.17 = (bf16[2,384,2,6,128]{1,4,3,2,0:T(8,128)(2,1)}, bf16[2,384,2,6,128]{1,4,3,2,0:T(8,128)(2,1)}, u32[]{:S(2)}, u32[]{:S(2)}) collective-permute-start(bf16[2,384,2,6,128]{1,4,3,2,0:T(8,128)(2,1)} %pad_maximum_fusion), channel_id=1, source_target_pairs={{0,4},{8,12},{16,20},{24,28},{1,5},{9,13},{17,21},{25,29},{2,6},{1... | collective-permute-start | bytes 7077896 | tf_op jit(solution)/shard_map/ppermute | solution.py:151
  276.4 3.7 collective-permute-done.11
  280.1 2.5 collective-permute-start.13
  285.1 20.2 %collective-permute-done.18 = bf16[384,2,6,128]{0,3,2,1:T(8,128)(2,1)} collective-permute-done((bf16[384,2,6,128]{0,3,2,1:T(8,128)(2,1)S(1)}, bf16[384,2,6,128]{0,3,2,1:T(8,128)(2,1)}, u32[]{:S(2)}, u32[]{:S(2)}) %collective-permute-start.18) | collective-permute-done | bytes 1179680 | tf_op jit(solution)/shard_map/ppermute | solution.py:154
  311.5 3.2 fusion.7
  314.7 35.3 %collective-permute-done.12 = bf16[768,6,128]{0,2,1:T(8,128)(2,1)S(1)} collective-permute-done((bf16[768,6,128]{0,2,1:T(8,128)(2,1)}, bf16[768,6,128]{0,2,1:T(8,128)(2,1)S(1)}, u32[]{:S(2)}, u32[]{:S(2)}) %collective-permute-start.12) | collective-permute-done | bytes 1179680 | tf_op jit(solution)/shard_map/ppermute | solution.py:130
  366.1 2.7 fusion.9.q_ref
  368.8 9.3 %shard_map.46 = bf16[384,768]{1,0:T(8,128)(2,1)} custom-call(bf16[384,768]{1,0:T(8,128)(2,1)} %fusion.9.q_ref, bf16[384,1536]{1,0:T(8,128)(2,1)} %copy.9.refs_0_.refs_4_, bf16[384,1536]{1,0:T(8,128)(2,1)} %copy.10.refs_1_.refs_5_, bf16[384,1536]{1,0:T(8,128)(2,1)} %copy.11.refs_2_.refs_6_, bf16[384,1536]{1,0:T(8,128)(2,1)} %copy.12.refs_3_.refs_7_, ...), custom_call_target="tpu_custom_call" | custom-call | flops 1811939328 | bytes 5898240 | tf_op jit(solution)/shard_map/pallas_call | solution.py:49
  (77 shorter events, 59.6 us)
Async XLA Ops:
  6.5 167.7 %all-gather.2.cloned.1.call-start = ((), (), s32[]{:S(2)}) async-start(), calls=%async_computation | async-start | bytes 5898240 | tf_op jit(solution)/shard_map/all_gather | solution.py:162
  8.2 111.6 %copy-start.8 = (s32[8]{0:T(128)S(1)}, s32[8]{0:T(128)}, u32[]{:S(2)}) copy-start(s32[8]{0:T(128)} %constant.108.clone) | copy-start | bytes 100
  8.2 116.8 %copy-start.7 = (s32[8]{0:T(128)S(1)}, s32[8]{0:T(128)}, u32[]{:S(2)}) copy-start(s32[8]{0:T(128)} %constant.109.clone) | copy-start | bytes 100
  10.6 119.6 %slice-start.1 = ((bf16[768,3,6,128]{3,0,2,1:T(8,128)(2,1)}), bf16[768,1,6,128]{3,0,2,1:T(8,128)(2,1)S(1)}, s32[]{:S(2)}) async-start(bf16[768,3,6,128]{3,0,2,1:T(8,128)(2,1)} %param.5), calls=%async_computation.2 | async-start | bytes 2359296 | tf_op jit(solution)/shard_map/slice | solution.py:171
  10.6 54.5 %collective-permute-start = (bf16[768,2,6,128]{0,3,2,1:T(8,128)(2,1)}, bf16[768,2,6,128]{0,3,2,1:T(8,128)(2,1)S(1)}, u32[]{:S(2)}, u32[]{:S(2)}) collective-permute-start(bf16[768,2,6,128]{0,3,2,1:T(8,128)(2,1)} %copy.20), channel_id=1, source_target_pairs={{0,4},{4,12},{12,20},{20,28},{28,24},{24,16},{16,8},{8,0},{1,5},{5... | collective-permute-start | bytes 7077896 | tf_op jit(solution)/shard_map/ppermute | solution.py:130
  13.6 53.2 %collective-permute-start.1 = (bf16[768,2,6,128]{0,3,2,1:T(8,128)(2,1)}, bf16[768,2,6,128]{0,3,2,1:T(8,128)(2,1)}, u32[]{:S(2)}, u32[]{:S(2)}) collective-permute-start(bf16[768,2,6,128]{0,3,2,1:T(8,128)(2,1)} %copy.20), channel_id=1, source_target_pairs={{0,8},{4,0},{12,4},{20,12},{28,20},{24,28},{16,24},{8,16},{1,9},{5... | collective-permute-start | bytes 7077896 | tf_op jit(solution)/shard_map/ppermute | solution.py:131
  65.1 52.6 %collective-permute-start.2 = (bf16[768,2,6,128]{0,3,2,1:T(8,128)(2,1)S(1)}, bf16[768,2,6,128]{0,3,2,1:T(8,128)(2,1)}, u32[]{:S(2)}, u32[]{:S(2)}) collective-permute-start(bf16[768,2,6,128]{0,3,2,1:T(8,128)(2,1)S(1)} %collective-permute-done), channel_id=1, source_target_pairs={{0,4},{4,12},{12,20},{20,28},{28,24},{24,16},{16,8},{8,0},{1,5},{5... | collective-permute-start | bytes 7077896 | tf_op jit(solution)/shard_map/ppermute | solution.py:130
  66.8 52.3 %collective-permute-start.3 = (bf16[768,2,6,128]{0,3,2,1:T(8,128)(2,1)}, bf16[768,2,6,128]{0,3,2,1:T(8,128)(2,1)}, u32[]{:S(2)}, u32[]{:S(2)}) collective-permute-start(bf16[768,2,6,128]{0,3,2,1:T(8,128)(2,1)} %collective-permute-done.1), channel_id=1, source_target_pairs={{0,8},{4,0},{12,4},{20,12},{28,20},{24,28},{16,24},{8,16},{1,9},{5... | collective-permute-start | bytes 7077896 | tf_op jit(solution)/shard_map/ppermute | solution.py:131
  117.8 51.8 %collective-permute-start.4 = (bf16[768,2,6,128]{0,3,2,1:T(8,128)(2,1)}, bf16[768,2,6,128]{0,3,2,1:T(8,128)(2,1)S(1)}, u32[]{:S(2)}, u32[]{:S(2)}) collective-permute-start(bf16[768,2,6,128]{0,3,2,1:T(8,128)(2,1)} %collective-permute-done.2), channel_id=1, source_target_pairs={{0,4},{4,12},{12,20},{20,28},{28,24},{24,16},{16,8},{8,0},{1,5},{5... | collective-permute-start | bytes 7077896 | tf_op jit(solution)/shard_map/ppermute | solution.py:130
  119.1 51.7 %collective-permute-start.5 = (bf16[768,2,6,128]{0,3,2,1:T(8,128)(2,1)}, bf16[768,2,6,128]{0,3,2,1:T(8,128)(2,1)}, u32[]{:S(2)}, u32[]{:S(2)}) collective-permute-start(bf16[768,2,6,128]{0,3,2,1:T(8,128)(2,1)} %collective-permute-done.3), channel_id=1, source_target_pairs={{0,8},{4,0},{12,4},{20,12},{28,20},{24,28},{16,24},{8,16},{1,9},{5... | collective-permute-start | bytes 7077896 | tf_op jit(solution)/shard_map/ppermute | solution.py:131
  169.7 25.7 %collective-permute-start.6 = (bf16[384,2,6,128]{0,3,2,1:T(8,128)(2,1)S(1)}, bf16[384,2,6,128]{0,3,2,1:T(8,128)(2,1)}, u32[]{:S(2)}, u32[]{:S(2)}) collective-permute-start(bf16[384,2,6,128]{0,3,2,1:T(8,128)(2,1)S(1)} %slice.32), channel_id=1, source_target_pairs={{0,4},{4,12},{12,20},{20,28},{28,24},{24,16},{16,8},{8,0},{1,5},{5... | collective-permute-start | bytes 3538952 | tf_op jit(solution)/shard_map/ppermute | solution.py:138
  173.2 25.2 %collective-permute-start.7 = (bf16[384,2,6,128]{0,3,2,1:T(8,128)(2,1)}, bf16[384,2,6,128]{0,3,2,1:T(8,128)(2,1)}, u32[]{:S(2)}, u32[]{:S(2)}) collective-permute-start(bf16[384,2,6,128]{0,3,2,1:T(8,128)(2,1)} %slice.33), channel_id=1, source_target_pairs={{0,8},{4,0},{12,4},{20,12},{28,20},{24,28},{16,24},{8,16},{1,9},{5... | collective-permute-start | bytes 3538952 | tf_op jit(solution)/shard_map/ppermute | solution.py:139
  204.8 27.8 %collective-permute-start.9 = (bf16[768,6,128]{0,2,1:T(8,128)(2,1)S(1)}, bf16[768,6,128]{0,2,1:T(8,128)(2,1)}, u32[]{:S(2)}, u32[]{:S(2)}) collective-permute-start(bf16[768,6,128]{0,2,1:T(8,128)(2,1)S(1)} %bitcast.70), channel_id=1, source_target_pairs={{0,8},{4,0},{12,4},{20,12},{28,20},{24,28},{16,24},{8,16},{1,9},{5... | collective-permute-start | bytes 3538952 | tf_op jit(solution)/shard_map/ppermute | solution.py:131
  206.1 49.0 %collective-permute-start.8 = (bf16[768,6,128]{0,2,1:T(8,128)(2,1)S(1)}, bf16[768,6,128]{0,2,1:T(8,128)(2,1)}, u32[]{:S(2)}, u32[]{:S(2)}) collective-permute-start(bf16[768,6,128]{0,2,1:T(8,128)(2,1)S(1)} %bitcast.71), channel_id=1, source_target_pairs={{0,4},{4,12},{12,20},{20,28},{28,24},{24,16},{16,8},{8,0},{1,5},{5... | collective-permute-start | bytes 3538952 | tf_op jit(solution)/shard_map/ppermute | solution.py:130
  206.8 54.7 %collective-permute-start.16 = (bf16[384,2,6,128]{0,3,2,1:T(8,128)(2,1)S(1)}, bf16[384,2,6,128]{0,3,2,1:T(8,128)(2,1)S(1)}, u32[]{:S(2)}, u32[]{:S(2)}) collective-permute-start(bf16[384,2,6,128]{0,3,2,1:T(8,128)(2,1)S(1)} %bitcast.67), channel_id=1, source_target_pairs={{0,8},{4,12},{8,16},{12,20},{16,24},{20,28},{24,0},{28,4},{1,9},{5... | collective-permute-start | bytes 3538952 | tf_op jit(solution)/shard_map/ppermute | solution.py:103
  232.5 47.6 %collective-permute-start.11 = (bf16[768,6,128]{0,2,1:T(8,128)(2,1)}, bf16[768,6,128]{0,2,1:T(8,128)(2,1)}, u32[]{:S(2)}, u32[]{:S(2)}) collective-permute-start(bf16[768,6,128]{0,2,1:T(8,128)(2,1)} %collective-permute-done.9), channel_id=1, source_target_pairs={{0,8},{4,0},{12,4},{20,12},{28,20},{24,28},{16,24},{8,16},{1,9},{5... | collective-permute-start | bytes 3538952 | tf_op jit(solution)/shard_map/ppermute | solution.py:131
  255.1 27.5 %collective-permute-start.10 = (bf16[768,6,128]{0,2,1:T(8,128)(2,1)}, bf16[768,6,128]{0,2,1:T(8,128)(2,1)}, u32[]{:S(2)}, u32[]{:S(2)}) collective-permute-start(bf16[768,6,128]{0,2,1:T(8,128)(2,1)} %collective-permute-done.8), channel_id=1, source_target_pairs={{0,4},{4,12},{12,20},{20,28},{28,24},{24,16},{16,8},{8,0},{1,5},{5... | collective-permute-start | bytes 3538952 | tf_op jit(solution)/shard_map/ppermute | solution.py:130
  261.6 43.7 %collective-permute-start.18 = (bf16[384,2,6,128]{0,3,2,1:T(8,128)(2,1)S(1)}, bf16[384,2,6,128]{0,3,2,1:T(8,128)(2,1)}, u32[]{:S(2)}, u32[]{:S(2)}) collective-permute-start(bf16[384,2,6,128]{0,3,2,1:T(8,128)(2,1)S(1)} %collective-permute-done.16), channel_id=1, source_target_pairs={{4,0},{12,8},{20,16},{28,24},{5,1},{13,9},{21,17},{29,25},{6,2},{1... | collective-permute-start | bytes 3538952 | tf_op jit(solution)/shard_map/ppermute | solution.py:154
  264.6 91.3 %collective-permute-start.17 = (bf16[2,384,2,6,128]{1,4,3,2,0:T(8,128)(2,1)}, bf16[2,384,2,6,128]{1,4,3,2,0:T(8,128)(2,1)}, u32[]{:S(2)}, u32[]{:S(2)}) collective-permute-start(bf16[2,384,2,6,128]{1,4,3,2,0:T(8,128)(2,1)} %pad_maximum_fusion), channel_id=1, source_target_pairs={{0,4},{8,12},{16,20},{24,28},{1,5},{9,13},{17,21},{25,29},{2,6},{1... | collective-permute-start | bytes 7077896 | tf_op jit(solution)/shard_map/ppermute | solution.py:151
  280.1 73.2 %collective-permute-start.13 = (bf16[768,6,128]{0,2,1:T(8,128)(2,1)}, bf16[768,6,128]{0,2,1:T(8,128)(2,1)S(1)}, u32[]{:S(2)}, u32[]{:S(2)}) collective-permute-start(bf16[768,6,128]{0,2,1:T(8,128)(2,1)} %collective-permute-done.11), channel_id=1, source_target_pairs={{0,8},{4,0},{12,4},{20,12},{28,20},{24,28},{16,24},{8,16},{1,9},{5... | collective-permute-start | bytes 3538952 | tf_op jit(solution)/shard_map/ppermute | solution.py:131
  282.6 67.4 %collective-permute-start.12 = (bf16[768,6,128]{0,2,1:T(8,128)(2,1)}, bf16[768,6,128]{0,2,1:T(8,128)(2,1)S(1)}, u32[]{:S(2)}, u32[]{:S(2)}) collective-permute-start(bf16[768,6,128]{0,2,1:T(8,128)(2,1)} %collective-permute-done.10), channel_id=1, source_target_pairs={{0,4},{4,12},{12,20},{20,28},{28,24},{24,16},{16,8},{8,0},{1,5},{5... | collective-permute-start | bytes 3538952 | tf_op jit(solution)/shard_map/ppermute | solution.py:130
  305.3 50.7 %collective-permute-start.19 = (bf16[384,2,6,128]{0,3,2,1:T(8,128)(2,1)}, bf16[384,2,6,128]{0,3,2,1:T(8,128)(2,1)S(1)}, u32[]{:S(2)}, u32[]{:S(2)}) collective-permute-start(bf16[384,2,6,128]{0,3,2,1:T(8,128)(2,1)} %collective-permute-done.18), channel_id=1, source_target_pairs={{0,8},{8,16},{16,24},{24,0},{1,9},{9,17},{17,25},{25,1},{2,10},{10... | collective-permute-start | bytes 3538952 | tf_op jit(solution)/shard_map/ppermute | solution.py:155
  350.9 10.3 %collective-permute-start.14 = (bf16[384,6,128]{0,2,1:T(8,128)(2,1)}, bf16[384,6,128]{0,2,1:T(8,128)(2,1)}, u32[]{:S(2)}, u32[]{:S(2)}) collective-permute-start(bf16[384,6,128]{0,2,1:T(8,128)(2,1)} %slice.34), channel_id=1, source_target_pairs={{0,4},{4,12},{12,20},{20,28},{28,24},{24,16},{16,8},{8,0},{1,5},{5... | collective-permute-start | bytes 1769480 | tf_op jit(solution)/shard_map/ppermute | solution.py:138
  354.2 10.2 %collective-permute-start.15 = (bf16[384,6,128]{0,2,1:T(8,128)(2,1)}, bf16[384,6,128]{0,2,1:T(8,128)(2,1)}, u32[]{:S(2)}, u32[]{:S(2)}) collective-permute-start(bf16[384,6,128]{0,2,1:T(8,128)(2,1)} %slice.35), channel_id=1, source_target_pairs={{0,8},{4,0},{12,4},{20,12},{28,20},{24,28},{16,24},{8,16},{1,9},{5... | collective-permute-start | bytes 1769480 | tf_op jit(solution)/shard_map/ppermute | solution.py:139
  (8 other events, 27.3 us)
Sparse Core Ops, SparseCore 0:
  13.8 39.1 all-gather.1

commit v4 on v3

--- a/solution.py
+++ b/solution.py
@@ -57,6 +57,38 @@
     return out.reshape(rows, heads, size)
 
 
+def ctx_coords(mesh):
+    n = mesh.shape["ctx"]
+    axis = mesh.axis_names.index("ctx")
+    devices = mesh.devices.transpose([axis] + [a for a in range(mesh.devices.ndim) if a != axis])
+    return [tuple(d.coords) for d in devices.reshape(n, -1)[:, 0]]
+
+
+def grid_layout(mesh):
+    try:
+        coords = ctx_coords(mesh)
+    except Exception:
+        return None
+    n = len(coords)
+    if n != 8 or len(set(coords)) != n:
+        return None
+    varying = [a for a in range(len(coords[0])) if len({c[a] for c in coords}) > 1]
+    if len(varying) != 2:
+        return None
+    sizes = {a: sorted({c[a] for c in coords}) for a in varying}
+    line = [a for a in varying if len(sizes[a]) == 4]
+    pair = [a for a in varying if len(sizes[a]) == 2]
+    if len(line) != 1 or len(pair) != 1:
+        return None
+    lin = [sizes[line[0]].index(c[line[0]]) for c in coords]
+    pr = [sizes[pair[0]].index(c[pair[0]]) for c in coords]
+    if sizes[line[0]] != list(range(sizes[line[0]][0], sizes[line[0]][0] + 4)):
+        return None
+    if sizes[pair[0]][1] - sizes[pair[0]][0] != 1:
+        return None
+    return lin, pr
+
+
 def ring_order(mesh):
     n = mesh.shape["ctx"]
     order = list(range(n))
@@ -103,7 +135,7 @@
     return lax.ppermute(array, axis, [(i, (i + by) % devices) for i in range(devices)])
 
 
-def make_on_device(ring):
+def make_on_device(ring, layout):
     n = len(ring)
     pos = [0] * n
     for i, c in enumerate(ring):
@@ -144,6 +176,55 @@
                 total = total + partial(far, last_cw, 0)
         return total
 
+
+    def spoke_project(tokens, features, piece, me, layout):
+        lin, pr = layout
+        at = {(lin[c], pr[c]): c for c in range(n)}
+        ends = [c for c in range(n) if lin[c] in (0, 3)]
+        middles = [c for c in range(n) if lin[c] in (1, 2)]
+        spoke = {e: at[(1 if lin[e] == 0 else 2, pr[e])] for e in ends}
+        end_of = {m: e for e, m in spoke.items()}
+        ynbr = {c: at[(lin[c], 1 - pr[c])] for c in range(n)}
+        znbr = {m: at[(3 - lin[m], pr[m])] for m in middles}
+        rows_w = piece.shape[0]
+
+        def table(values):
+            return jnp.array([values.get(c, c) for c in range(n)], jnp.int32)[me]
+
+        def partial(feats, block, part):
+            cols = lax.dynamic_slice_in_dim(feats, block * rows_w, rows_w, axis=1)
+            return jnp.dot(cols, part.reshape(rows_w, -1), preferred_element_type=jnp.float32)
+
+        end_y = lax.ppermute(piece, "ctx", [(e, ynbr[e]) for e in ends])
+        from_end = lax.ppermute(piece, "ctx", [(e, spoke[e]) for e in ends])
+        relayed = lax.ppermute(end_y, "ctx", [(e, spoke[e]) for e in ends])
+        mid_y = lax.ppermute(piece, "ctx", [(m, ynbr[m]) for m in middles])
+        mid_z = lax.ppermute(piece, "ctx", [(m, znbr[m]) for m in middles])
+        far_pair = lax.ppermute(jnp.stack([from_end, relayed]), "ctx", [(m, znbr[m]) for m in middles])
+        far_y = lax.ppermute(mid_z, "ctx", [(m, ynbr[m]) for m in middles])
+        end_tokens = lax.ppermute(tokens, "ctx", [(e, spoke[e]) for e in ends])
+        end_features = lax.all_gather(end_tokens, "mp", axis=1, tiled=True)
+
+        e_of = table(end_of)
+        shared = [
+            (me, piece),
+            (table(ynbr), mid_y),
+            (table(znbr), mid_z),
+            (table({m: end_of[znbr[m]] for m in middles}), far_pair[0]),
+            (table({m: ynbr[end_of[znbr[m]]] for m in middles}), far_pair[1]),
+            (table({m: znbr[ynbr[m]] for m in middles}), far_y),
+        ]
+        end_partial = partial(end_features, *shared[0])
+        for block, part in shared[1:]:
+            end_partial = end_partial + partial(end_features, block, part)
+        mid_total = partial(features, e_of, from_end) + partial(features, table({m: ynbr[end_of[m]] for m in middles}), relayed)
+        for block, part in shared:
+            mid_total = mid_total + partial(features, block, part)
+        returned = lax.ppermute(end_partial, "ctx", [(m, end_of[m]) for m in middles])
+        end_total = partial(features, me, piece) + partial(features, table(ynbr), end_y) + returned
+        is_end = jnp.array([c in ends for c in range(n)])[me]
+        return jnp.where(is_end, end_total, mid_total)
+
     def earlier_blocks(key_value, me):
         if n % 2 or n < 4 or REACH != 4:
             return [shifted(key_value, "ctx", by) for by in range(1, REACH)]
@@ -166,11 +247,15 @@
         scale = 1.0 / math.sqrt(head_size)
         me = lax.axis_index("ctx")
 
-        kv_total = ring_project(features, qkv_weight[:, 1:], me)
+        if layout is None:
+            project = lambda piece: ring_project(features, piece, me)
+        else:
+            project = lambda piece: spoke_project(tokens, features, piece, me, layout)
+        kv_total = project(qkv_weight[:, 1:])
         key_value = kv_total.astype(jnp.bfloat16).reshape(rows_dev, 2, heads_local, head_size)
         q_piece, key_value = lax.optimization_barrier((qkv_weight[:, 0], key_value))
         blocks = [key_value] + earlier_blocks(key_value, me)
-        q_total = ring_project(features, q_piece, me)
+        q_total = project(q_piece)
         queries = q_total.astype(jnp.bfloat16).reshape(rows_dev, heads_local, head_size)
 
         return windowed_attention(queries, blocks, scale)
@@ -181,7 +266,7 @@
 def solution(mesh):
     placed = (P("ctx", "mp"), P("ctx", None, "mp", None))
     return jax.shard_map(
-        make_on_device(ring_order(mesh)),
+        make_on_device(ring_order(mesh), grid_layout(mesh)),
         mesh=mesh,
         in_specs=placed,
         out_specs=P("ctx", "mp", None),

time: 388 us -> 630 us (1.62)
  waiting for transfers between devices: 258 us -> 445 us
  matrix products: 41.3 us -> 67.1 us
  starting transfers between devices: 30.6 us -> 48.5 us
  local copies, waits for them, and re-layouts: 21.6 us -> 29.8 us
  other arithmetic: 4 us -> 10.8 us
    ppermute x16 -> x17, waiting for transfers between devices: 231 us -> 406 us  [the longest x2 236 us: spoke_project(): lax.ppermute(end_partial, 'ctx', [(m, end_of[m]) for m in middles])]
    dot_general x18 -> x30, matrix products: 41.3 us -> 67.1 us  [partial(): jnp.dot(cols, part.reshape(rows_w, -1), preferred_element_type=jnp.float32)]
    ppermute x16 -> x17, starting transfers between devices: 19 us -> 36.9 us  [the longest x2 7.93 us: spoke_project(): end_y = lax.ppermute(piece, 'ctx', [(e, ynbr[e]) for e in ends])]
    ppermute x1, waiting for transfers between devices: 20.2 us -> 9.85 us  [earlier_blocks(): lax.ppermute(two_back, 'ctx', [(o, o - 1) for o in range(1, n, 2)])]
    ppermute x1, waiting for transfers between devices: 6.51 us -> 16.3 us  [shifted(): lax.ppermute(array, axis, [(i, (i + by) % devices) for i in range(devices)])]
    ppermute x1, waiting for transfers between devices: 0.01 us -> 7.8 us  [earlier_blocks(): lax.ppermute(to_even, 'ctx', [(e, (e + 2) % n) for e in range(0, n, 2)])]
  transfers between devices with their start and end apart: 21 -> 23, of which waited for: 12 -> 12; matrix products, arithmetic and copies ran while one was open for 13% -> 14% of each run, Pallas kernels for 0% -> 0%
where the time goes in v4:
time: 630 us; the launch traced here: 629 us
  waiting for transfers between devices  445 us (71%)
  matrix products  67.1 us (11%)
  starting transfers between devices  48.5 us (8%)
  local copies, waits for them, and re-layouts  29.8 us (5%)
  between operations  18.6 us (3%)
  other arithmetic  10.8 us (2%)
  Pallas kernels  9.25 us (1%)
    ppermute x2, waiting for transfers between devices, spoke_project(): lax.ppermute(end_partial, 'ctx', [(m, end_of[m]) for m in middles])  236 us
    ppermute x2, waiting for transfers between devices, spoke_project(): relayed = lax.ppermute(end_y, 'ctx', [(e, spoke[e]) for e in ends])  73.9 us
    dot_general x30, matrix products, partial(): jnp.dot(cols, part.reshape(rows_w, -1), preferred_element_type=jnp.float32)  67.1 us
    ppermute x2, waiting for transfers between devices, spoke_project(): end_y = lax.ppermute(piece, 'ctx', [(e, ynbr[e]) for e in ends])  39.7 us
    ppermute x2, waiting for transfers between devices, spoke_project(): from_end = lax.ppermute(piece, 'ctx', [(e, spoke[e]) for e in ends])  31.9 us
    ppermute x1, waiting for transfers between devices, spoke_project(): end_tokens = lax.ppermute(tokens, 'ctx', [(e, spoke[e]) for e in ends])  25.1 us
    ppermute x1, waiting for transfers between devices, shifted(): lax.ppermute(array, axis, [(i, (i + by) % devices) for i in range(devices)])  16.3 us
  transfers between devices with their start and end apart: 23, of which 12 were waited for; matrix products, arithmetic and copies ran while one was open for 14% of the time, Pallas kernels for 0%

profile of v4, /device:TPU:0, one launch (start us, length us, event | category | flops | bytes accessed | tf_op | source)
XLA Modules:
  0.0 628.5 jit_solution(6237555350994681950)
XLA Ops:
  11.4 4.9 collective-permute-start
  18.5 25.1 %collective-permute-done.1 = bf16[384,1536]{1,0:T(8,128)(2,1)S(1)} collective-permute-done((bf16[384,1536]{1,0:T(8,128)(2,1)S(1)}, bf16[384,1536]{1,0:T(8,128)(2,1)S(1)}, u32[]{:S(2)}, u32[]{:S(2)}) %collective-permute-start.1) | collective-permute-done | bytes 1179680 | tf_op jit(solution)/shard_map/ppermute | solution.py:205
  44.7 4.6 collective-permute-start.4
  49.2 18.6 %collective-permute-done = bf16[768,2,6,128]{0,3,2,1:T(8,128)(2,1)} collective-permute-done((bf16[768,2,6,128]{0,3,2,1:T(8,128)(2,1)}, bf16[768,2,6,128]{0,3,2,1:T(8,128)(2,1)}, u32[]{:S(2)}, u32[]{:S(2)}) %collective-permute-start) | collective-permute-done | bytes 2359328 | tf_op jit(solution)/shard_map/ppermute | solution.py:198
  69.3 31.8 %collective-permute-done.4 = bf16[768,2,6,128]{0,3,2,1:T(8,128)(2,1)S(1)} collective-permute-done((bf16[768,2,6,128]{0,3,2,1:T(8,128)(2,1)}, bf16[768,2,6,128]{0,3,2,1:T(8,128)(2,1)S(1)}, u32[]{:S(2)}, u32[]{:S(2)}) %collective-permute-start.4) | collective-permute-done | bytes 2359328 | tf_op jit(solution)/shard_map/ppermute | solution.py:199
  101.1 48.6 %collective-permute-done.5 = bf16[768,2,6,128]{0,3,2,1:T(8,128)(2,1)S(1)} collective-permute-done((bf16[768,2,6,128]{0,3,2,1:T(8,128)(2,1)}, bf16[768,2,6,128]{0,3,2,1:T(8,128)(2,1)S(1)}, u32[]{:S(2)}, u32[]{:S(2)}) %collective-permute-start.5) | collective-permute-done | bytes 2359328 | tf_op jit(solution)/shard_map/ppermute | solution.py:200
  173.9 4.4 fusion.32
  178.3 4.4 fusion.62
  193.8 3.2 fusion.7
  212.9 201.6 %collective-permute-done.8 = f32[384,1536]{1,0:T(8,128)S(1)} collective-permute-done((f32[384,1536]{1,0:T(8,128)S(1)}, f32[384,1536]{1,0:T(8,128)S(1)}, u32[]{:S(2)}, u32[]{:S(2)}) %collective-permute-start.8) | collective-permute-done | bytes 2359328 | tf_op jit(solution)/shard_map/ppermute | solution.py:223
  414.4 3.6 fusion.8
  423.2 21.1 %collective-permute-done.9 = bf16[768,6,128]{0,2,1:T(8,128)(2,1)S(1)} collective-permute-done((bf16[768,6,128]{0,2,1:T(8,128)(2,1)S(1)}, bf16[768,6,128]{0,2,1:T(8,128)(2,1)S(1)}, u32[]{:S(2)}, u32[]{:S(2)}) %collective-permute-start.9) | collective-permute-done | bytes 1179680 | tf_op jit(solution)/shard_map/ppermute | solution.py:198
  447.5 25.3 %collective-permute-done.13 = bf16[768,6,128]{0,2,1:T(8,128)(2,1)S(1)} collective-permute-done((bf16[768,6,128]{0,2,1:T(8,128)(2,1)S(1)}, bf16[768,6,128]{0,2,1:T(8,128)(2,1)S(1)}, u32[]{:S(2)}, u32[]{:S(2)}) %collective-permute-start.13) | collective-permute-done | bytes 1179680 | tf_op jit(solution)/shard_map/ppermute | solution.py:200
  481.5 16.3 %collective-permute-done.17 = bf16[384,2,6,128]{0,3,2,1:T(8,128)(2,1)} collective-permute-done((bf16[384,2,6,128]{0,3,2,1:T(8,128)(2,1)S(1)}, bf16[384,2,6,128]{0,3,2,1:T(8,128)(2,1)}, u32[]{:S(2)}, u32[]{:S(2)}) %collective-permute-start.17) | collective-permute-done | bytes 1179680 | tf_op jit(solution)/shard_map/ppermute | solution.py:135
  500.8 4.1 collective-permute-start.18
  506.2 3.3 fusion.30
  521.7 9.9 %collective-permute-done.19 = bf16[384,2,6,128]{0,3,2,1:T(8,128)(2,1)} collective-permute-done((bf16[384,2,6,128]{0,3,2,1:T(8,128)(2,1)}, bf16[384,2,6,128]{0,3,2,1:T(8,128)(2,1)}, u32[]{:S(2)}, u32[]{:S(2)}) %collective-permute-start.19) | collective-permute-done | bytes 1179680 | tf_op jit(solution)/shard_map/ppermute | solution.py:235
  531.6 6.2 collective-permute-start.20
  547.6 3.7 collective-permute-done.18
  551.3 7.8 %collective-permute-done.20 = bf16[384,2,6,128]{0,3,2,1:T(8,128)(2,1)S(1)} collective-permute-done((bf16[384,2,6,128]{0,3,2,1:T(8,128)(2,1)}, bf16[384,2,6,128]{0,3,2,1:T(8,128)(2,1)S(1)}, u32[]{:S(2)}, u32[]{:S(2)}) %collective-permute-start.20) | collective-permute-done | bytes 1179680 | tf_op jit(solution)/shard_map/ppermute | solution.py:236
  559.1 3.3 fusion.18
  572.3 34.0 %collective-permute-done.16 = f32[384,768]{1,0:T(8,128)} collective-permute-done((f32[384,768]{1,0:T(8,128)}, f32[384,768]{1,0:T(8,128)}, u32[]{:S(2)}, u32[]{:S(2)}) %collective-permute-start.16) | collective-permute-done | bytes 1179680 | tf_op jit(solution)/shard_map/ppermute | solution.py:223
  606.3 3.7 fusion.17.q_ref
  610.0 9.3 %shard_map.190 = bf16[384,768]{1,0:T(8,128)(2,1)} custom-call(bf16[384,768]{1,0:T(8,128)(2,1)} %fusion.17.q_ref, bf16[384,1536]{1,0:T(8,128)(2,1)} %copy.25.refs_0_.refs_4_, bf16[384,1536]{1,0:T(8,128)(2,1)} %copy.26.refs_1_.refs_5_, bf16[384,1536]{1,0:T(8,128)(2,1)} %copy.27.refs_2_.refs_6_, bf16[384,1536]{1,0:T(8,128)(2,1)} %copy.28.refs_3_.refs_7_, ...), custom_call_target="tpu_custom_call" | custom-call | flops 1811939328 | bytes 5898240 | tf_op jit(solution)/shard_map/pallas_call | solution.py:49
  (145 shorter events, 111.5 us)
Async XLA Ops:
  6.5 167.3 %all-gather.3.cloned.1.call-start = ((), (), s32[]{:S(2)}) async-start(), calls=%async_computation | async-start | bytes 5898240 | tf_op jit(solution)/shard_map/all_gather | solution.py:243
  7.3 175.4 %all-gather.5.cloned.1.call-start = ((), (), s32[]{:S(2)}) async-start(), calls=%async_computation.1 | async-start | bytes 5898240 | tf_op jit(solution)/shard_map/all_gather | solution.py:206
  11.4 56.4 %collective-permute-start = (bf16[768,2,6,128]{0,3,2,1:T(8,128)(2,1)}, bf16[768,2,6,128]{0,3,2,1:T(8,128)(2,1)}, u32[]{:S(2)}, u32[]{:S(2)}) collective-permute-start(bf16[768,2,6,128]{0,3,2,1:T(8,128)(2,1)} %copy.36), channel_id=1, source_target_pairs={{0,4},{4,0},{24,28},{28,24},{1,5},{5,1},{25,29},{29,25},{2,6},{6,2... | collective-permute-start | bytes 7077896 | tf_op jit(solution)/shard_map/ppermute | solution.py:198
  16.3 27.4 %collective-permute-start.1 = (bf16[384,1536]{1,0:T(8,128)(2,1)S(1)}, bf16[384,1536]{1,0:T(8,128)(2,1)S(1)}, u32[]{:S(2)}, u32[]{:S(2)}) collective-permute-start(bf16[384,1536]{1,0:T(8,128)(2,1)S(1)} %copy-done.15), channel_id=1, source_target_pairs={{0,8},{4,12},{24,16},{28,20},{1,9},{5,13},{25,17},{29,21},{2,10},{... | collective-permute-start | bytes 3538952 | tf_op jit(solution)/shard_map/ppermute | solution.py:205
  44.7 56.4 %collective-permute-start.4 = (bf16[768,2,6,128]{0,3,2,1:T(8,128)(2,1)}, bf16[768,2,6,128]{0,3,2,1:T(8,128)(2,1)S(1)}, u32[]{:S(2)}, u32[]{:S(2)}) collective-permute-start(bf16[768,2,6,128]{0,3,2,1:T(8,128)(2,1)} %copy.36), channel_id=1, source_target_pairs={{0,8},{4,12},{24,16},{28,20},{1,9},{5,13},{25,17},{29,21},{2,10},{... | collective-permute-start | bytes 7077896 | tf_op jit(solution)/shard_map/ppermute | solution.py:199
  67.8 81.8 %collective-permute-start.5 = (bf16[768,2,6,128]{0,3,2,1:T(8,128)(2,1)}, bf16[768,2,6,128]{0,3,2,1:T(8,128)(2,1)S(1)}, u32[]{:S(2)}, u32[]{:S(2)}) collective-permute-start(bf16[768,2,6,128]{0,3,2,1:T(8,128)(2,1)} %collective-permute-done), channel_id=1, source_target_pairs={{0,8},{4,12},{24,16},{28,20},{1,9},{5,13},{25,17},{29,21},{2,10},{... | collective-permute-start | bytes 7077896 | tf_op jit(solution)/shard_map/ppermute | solution.py:200
  101.1 51.3 %copy-start.12 = (bf16[768,2,6,128]{0,3,2,1:T(8,128)(2,1)}, bf16[768,2,6,128]{0,3,2,1:T(8,128)(2,1)S(1)}, u32[]{:S(2)}) copy-start(bf16[768,2,6,128]{0,3,2,1:T(8,128)(2,1)S(1)} %collective-permute-done.4) | copy-start | bytes 7077892
  152.5 36.2 %collective-permute-start.6 = (bf16[2,768,2,6,128]{1,4,3,2,0:T(8,128)(2,1)}, bf16[2,768,2,6,128]{1,4,3,2,0:T(8,128)(2,1)}, u32[]{:S(2)}, u32[]{:S(2)}) collective-permute-start(bf16[2,768,2,6,128]{1,4,3,2,0:T(8,128)(2,1)} %pad_maximum_fusion), channel_id=1, source_target_pairs={{8,16},{12,20},{16,8},{20,12},{9,17},{13,21},{17,9},{21,13},{10,18... | collective-permute-start | bytes 14155784 | tf_op jit(solution)/shard_map/ppermute | solution.py:203
  155.4 16.4 %collective-permute-start.3 = (bf16[768,2,6,128]{0,3,2,1:T(8,128)(2,1)}, bf16[768,2,6,128]{0,3,2,1:T(8,128)(2,1)}, u32[]{:S(2)}, u32[]{:S(2)}) collective-permute-start(bf16[768,2,6,128]{0,3,2,1:T(8,128)(2,1)} %copy.36), channel_id=1, source_target_pairs={{8,16},{12,20},{16,8},{20,12},{9,17},{13,21},{17,9},{21,13},{10,18... | collective-permute-start | bytes 7077896 | tf_op jit(solution)/shard_map/ppermute | solution.py:202
  157.5 28.3 %collective-permute-start.2 = (bf16[768,2,6,128]{0,3,2,1:T(8,128)(2,1)}, bf16[768,2,6,128]{0,3,2,1:T(8,128)(2,1)}, u32[]{:S(2)}, u32[]{:S(2)}) collective-permute-start(bf16[768,2,6,128]{0,3,2,1:T(8,128)(2,1)} %copy.36), channel_id=1, source_target_pairs={{8,12},{12,8},{16,20},{20,16},{9,13},{13,9},{17,21},{21,17},{10,14... | collective-permute-start | bytes 7077896 | tf_op jit(solution)/shard_map/ppermute | solution.py:201
  171.8 25.1 %collective-permute-start.7 = (bf16[768,2,6,128]{0,3,2,1:T(8,128)(2,1)}, bf16[768,2,6,128]{0,3,2,1:T(8,128)(2,1)}, u32[]{:S(2)}, u32[]{:S(2)}) collective-permute-start(bf16[768,2,6,128]{0,3,2,1:T(8,128)(2,1)} %collective-permute-done.3), channel_id=1, source_target_pairs={{8,12},{12,8},{16,20},{20,16},{9,13},{13,9},{17,21},{21,17},{10,14... | collective-permute-start | bytes 7077896 | tf_op jit(solution)/shard_map/ppermute | solution.py:204
  199.9 214.5 %collective-permute-start.8 = (f32[384,1536]{1,0:T(8,128)S(1)}, f32[384,1536]{1,0:T(8,128)S(1)}, u32[]{:S(2)}, u32[]{:S(2)}) collective-permute-start(f32[384,1536]{1,0:T(8,128)S(1)} %convolution_add_fusion.3), channel_id=1, source_target_pairs={{8,0},{12,4},{16,24},{20,28},{9,1},{13,5},{17,25},{21,29},{10,2},{... | collective-permute-start | bytes 7077896 | tf_op jit(solution)/shard_map/ppermute | solution.py:223
  418.8 25.5 %collective-permute-start.9 = (bf16[768,6,128]{0,2,1:T(8,128)(2,1)S(1)}, bf16[768,6,128]{0,2,1:T(8,128)(2,1)S(1)}, u32[]{:S(2)}, u32[]{:S(2)}) collective-permute-start(bf16[768,6,128]{0,2,1:T(8,128)(2,1)S(1)} %bitcast.85), channel_id=1, source_target_pairs={{0,4},{4,0},{24,28},{28,24},{1,5},{5,1},{25,29},{29,25},{2,6},{6,2... | collective-permute-start | bytes 3538952 | tf_op jit(solution)/shard_map/ppermute | solution.py:198
  421.8 25.6 %collective-permute-start.12 = (bf16[768,6,128]{0,2,1:T(8,128)(2,1)S(1)}, bf16[768,6,128]{0,2,1:T(8,128)(2,1)S(1)}, u32[]{:S(2)}, u32[]{:S(2)}) collective-permute-start(bf16[768,6,128]{0,2,1:T(8,128)(2,1)S(1)} %bitcast.86), channel_id=1, source_target_pairs={{0,8},{4,12},{24,16},{28,20},{1,9},{5,13},{25,17},{29,21},{2,10},{... | collective-permute-start | bytes 3538952 | tf_op jit(solution)/shard_map/ppermute | solution.py:199
  444.3 28.5 %collective-permute-start.13 = (bf16[768,6,128]{0,2,1:T(8,128)(2,1)S(1)}, bf16[768,6,128]{0,2,1:T(8,128)(2,1)S(1)}, u32[]{:S(2)}, u32[]{:S(2)}) collective-permute-start(bf16[768,6,128]{0,2,1:T(8,128)(2,1)S(1)} %collective-permute-done.9), channel_id=1, source_target_pairs={{0,8},{4,12},{24,16},{28,20},{1,9},{5,13},{25,17},{29,21},{2,10},{... | collective-permute-start | bytes 3538952 | tf_op jit(solution)/shard_map/ppermute | solution.py:200
  445.7 52.2 %collective-permute-start.17 = (bf16[384,2,6,128]{0,3,2,1:T(8,128)(2,1)S(1)}, bf16[384,2,6,128]{0,3,2,1:T(8,128)(2,1)}, u32[]{:S(2)}, u32[]{:S(2)}) collective-permute-start(bf16[384,2,6,128]{0,3,2,1:T(8,128)(2,1)S(1)} %bitcast.83), channel_id=1, source_target_pairs={{0,8},{4,12},{8,16},{12,20},{16,24},{20,28},{24,0},{28,4},{1,9},{5... | collective-permute-start | bytes 3538952 | tf_op jit(solution)/shard_map/ppermute | solution.py:135
  445.7 60.4 %collective-permute-start.11 = (bf16[768,6,128]{0,2,1:T(8,128)(2,1)S(1)}, bf16[768,6,128]{0,2,1:T(8,128)(2,1)}, u32[]{:S(2)}, u32[]{:S(2)}) collective-permute-start(bf16[768,6,128]{0,2,1:T(8,128)(2,1)S(1)} %bitcast.87), channel_id=1, source_target_pairs={{8,16},{12,20},{16,8},{20,12},{9,17},{13,21},{17,9},{21,13},{10,18... | collective-permute-start | bytes 3538952 | tf_op jit(solution)/shard_map/ppermute | solution.py:202
  474.6 66.1 %collective-permute-start.14 = (bf16[2,768,6,128]{1,3,2,0:T(8,128)(2,1)}, bf16[2,768,6,128]{1,3,2,0:T(8,128)(2,1)}, u32[]{:S(2)}, u32[]{:S(2)}) collective-permute-start(bf16[2,768,6,128]{1,3,2,0:T(8,128)(2,1)} %pad_maximum_fusion.1), channel_id=1, source_target_pairs={{8,16},{12,20},{16,8},{20,12},{9,17},{13,21},{17,9},{21,13},{10,18... | collective-permute-start | bytes 7077896 | tf_op jit(solution)/shard_map/ppermute | solution.py:203
  476.6 40.0 %collective-permute-start.10 = (bf16[768,6,128]{0,2,1:T(8,128)(2,1)S(1)}, bf16[768,6,128]{0,2,1:T(8,128)(2,1)}, u32[]{:S(2)}, u32[]{:S(2)}) collective-permute-start(bf16[768,6,128]{0,2,1:T(8,128)(2,1)S(1)} %bitcast.88), channel_id=1, source_target_pairs={{8,12},{12,8},{16,20},{20,16},{9,13},{13,9},{17,21},{21,17},{10,14... | collective-permute-start | bytes 3538952 | tf_op jit(solution)/shard_map/ppermute | solution.py:201
  500.8 50.6 %collective-permute-start.18 = (bf16[2,384,2,6,128]{1,4,3,2,0:T(8,128)(2,1)}, bf16[2,384,2,6,128]{1,4,3,2,0:T(8,128)(2,1)}, u32[]{:S(2)}, u32[]{:S(2)}) collective-permute-start(bf16[2,384,2,6,128]{1,4,3,2,0:T(8,128)(2,1)} %pad_maximum_fusion.2), channel_id=1, source_target_pairs={{0,4},{8,12},{16,20},{24,28},{1,5},{9,13},{17,21},{25,29},{2,6},{1... | collective-permute-start | bytes 7077896 | tf_op jit(solution)/shard_map/ppermute | solution.py:232
  504.9 26.7 %collective-permute-start.19 = (bf16[384,2,6,128]{0,3,2,1:T(8,128)(2,1)}, bf16[384,2,6,128]{0,3,2,1:T(8,128)(2,1)}, u32[]{:S(2)}, u32[]{:S(2)}) collective-permute-start(bf16[384,2,6,128]{0,3,2,1:T(8,128)(2,1)} %collective-permute-done.17), channel_id=1, source_target_pairs={{4,0},{12,8},{20,16},{28,24},{5,1},{13,9},{21,17},{29,25},{6,2},{1... | collective-permute-start | bytes 3538952 | tf_op jit(solution)/shard_map/ppermute | solution.py:235
  511.9 32.6 %collective-permute-start.15 = (bf16[768,6,128]{0,2,1:T(8,128)(2,1)}, bf16[768,6,128]{0,2,1:T(8,128)(2,1)S(1)}, u32[]{:S(2)}, u32[]{:S(2)}) collective-permute-start(bf16[768,6,128]{0,2,1:T(8,128)(2,1)} %collective-permute-done.11), channel_id=1, source_target_pairs={{8,12},{12,8},{16,20},{20,16},{9,13},{13,9},{17,21},{21,17},{10,14... | collective-permute-start | bytes 3538952 | tf_op jit(solution)/shard_map/ppermute | solution.py:204
  531.6 27.6 %collective-permute-start.20 = (bf16[384,2,6,128]{0,3,2,1:T(8,128)(2,1)}, bf16[384,2,6,128]{0,3,2,1:T(8,128)(2,1)S(1)}, u32[]{:S(2)}, u32[]{:S(2)}) collective-permute-start(bf16[384,2,6,128]{0,3,2,1:T(8,128)(2,1)} %collective-permute-done.19), channel_id=1, source_target_pairs={{0,8},{8,16},{16,24},{24,0},{1,9},{9,17},{17,25},{25,1},{2,10},{10... | collective-permute-start | bytes 3538952 | tf_op jit(solution)/shard_map/ppermute | solution.py:236
  546.3 60.0 %collective-permute-start.16 = (f32[384,768]{1,0:T(8,128)}, f32[384,768]{1,0:T(8,128)}, u32[]{:S(2)}, u32[]{:S(2)}) collective-permute-start(f32[384,768]{1,0:T(8,128)} %convolution_add_fusion.9), channel_id=1, source_target_pairs={{8,0},{12,4},{16,24},{20,28},{9,1},{13,5},{17,25},{21,29},{10,2},{... | collective-permute-start | bytes 3538952 | tf_op jit(solution)/shard_map/ppermute | solution.py:223
  (31 other events, 351.7 us)
Sparse Core Ops, SparseCore 0:
  8.9 40.1 all-gather.2
  50.7 37.4 all-gather.4

commit v5 on v3

--- a/solution.py
+++ b/solution.py
@@ -17,7 +17,7 @@
     o_ref = refs[2 * reach]
     q = q_ref[...]
     scores = [
-        lax.dot_general(q, k_ref[...], (((1,), (1,)), ((), ())), preferred_element_type=jnp.float32) * scale
+        lax.dot_general(q, k_ref[...], (((0,), (0,)), ((), ())), preferred_element_type=jnp.float32) * scale
         for k_ref in k_refs
     ]
     top = scores[0].max(axis=-1, keepdims=True)
@@ -27,19 +27,22 @@
     totals = expos[0].sum(axis=-1, keepdims=True)
     for e in expos[1:]:
         totals = totals + e.sum(axis=-1, keepdims=True)
-    mixed = jnp.dot(expos[0].astype(jnp.bfloat16), v_refs[0][...], preferred_element_type=jnp.float32)
-    for e, v_ref in zip(expos[1:], v_refs[1:]):
-        mixed = mixed + jnp.dot(e.astype(jnp.bfloat16), v_ref[...], preferred_element_type=jnp.float32)
-    o_ref[...] = (mixed / totals).astype(o_ref.dtype)
+    mixed = None
+    for e, v_ref in zip(expos, v_refs):
+        term = lax.dot_general(
+            e.astype(jnp.bfloat16), v_ref[...], (((1,), (1,)), ((), ())), preferred_element_type=jnp.float32
+        )
+        mixed = term if mixed is None else mixed + term
+    o_ref[0] = (mixed / totals).astype(o_ref.dtype)
 
 
 def windowed_attention(queries, blocks, scale):
     rows, heads, size = queries.shape
     reach = len(blocks)
-    q2d = queries.reshape(rows, heads * size)
-    kv2d = [block.reshape(rows, 2 * heads * size) for block in blocks]
-    q_spec = pl.BlockSpec((rows, size), lambda h: (0, h))
-    v_spec = pl.BlockSpec((rows, size), lambda h: (0, h + heads))
+    q_t = queries.reshape(rows, heads * size).T
+    kv_t = [block.reshape(rows, 2 * heads * size).T for block in blocks]
+    q_spec = pl.BlockSpec((size, rows), lambda h: (h, 0))
+    v_spec = pl.BlockSpec((size, rows), lambda h: (h + heads, 0))
     keys = rows * reach
     cost = pl.CostEstimate(
         flops=4 * rows * keys * size * heads,
@@ -48,13 +51,13 @@
     )
     out = pl.pallas_call(
         functools.partial(attention_kernel, scale, reach),
-        out_shape=jax.ShapeDtypeStruct((rows, heads * size), jnp.bfloat16),
+        out_shape=jax.ShapeDtypeStruct((heads, rows, size), jnp.bfloat16),
         grid=(heads,),
         in_specs=[q_spec] + [q_spec] * reach + [v_spec] * reach,
-        out_specs=q_spec,
+        out_specs=pl.BlockSpec((1, rows, size), lambda h: (h, 0, 0)),
         cost_estimate=cost,
-    )(q2d, *kv2d, *kv2d)
-    return out.reshape(rows, heads, size)
+    )(q_t, *kv_t, *kv_t)
+    return jnp.transpose(out, (1, 0, 2))
 
 
 def ring_order(mesh):

time: 388 us -> 383 us (0.987)
  local copies, waits for them, and re-layouts: 21.6 us -> 11.4 us
  waiting for transfers between devices: 258 us -> 266 us
  matrix products: 41.3 us -> 36.5 us
    reshape x5 -> x0, local copies, waits for them, and re-layouts: 7.08 us -> none  [the longest x4 6.02 us: windowed_attention(): kv2d = [block.reshape(rows, 2 * heads * size) for block in blocks]]
    dot_general x18, matrix products: 41.3 us -> 36.5 us  [partial(): return jnp.dot(cols, flat, preferred_element_type=jnp.float32)]
  transfers between devices with their start and end apart: 21 -> 21, of which waited for: 12 -> 13; matrix products, arithmetic and copies ran while one was open for 13% -> 11% of each run, Pallas kernels for 0% -> 0%
where the time goes in v5:
time: 383 us; the launch traced here: 382 us
  waiting for transfers between devices  266 us (69%)
  matrix products  36.5 us (10%)
  starting transfers between devices  30.9 us (8%)
  between operations  22.9 us (6%)
  local copies, waits for them, and re-layouts  11.4 us (3%)
  Pallas kernels  9.3 us (2%)
  other arithmetic  5.45 us (1%)
    ppermute x6, waiting for transfers between devices, ring_project(): going_cw = lax.ppermute(going_cw, 'ctx', clockwise)  197 us
    dot_general x18, matrix products, partial(): return jnp.dot(cols, flat, preferred_element_type=jnp.float32)  36.5 us
    ppermute x6, waiting for transfers between devices, ring_project(): going_ccw = lax.ppermute(going_ccw, 'ctx', counter)  30.8 us
    ppermute x1, waiting for transfers between devices, earlier_blocks(): lax.ppermute(two_back, 'ctx', [(o, o - 1) for o in range(1, n, 2)])  20 us
    pallas_call x1, Pallas kernels, windowed_attention(): pl.pallas_call(functools.partial(attention_kernel, scale, reach), out_sha...  9.3 us
    ppermute x2, waiting for transfers between devices, ring_project(): last_cw = lax.ppermute(going_cw[:half], 'ctx', clockwise)  8.18 us
  transfers between devices with their start and end apart: 21, of which 13 were waited for; matrix products, arithmetic and copies ran while one was open for 11% of the time, Pallas kernels for 0%

profile of v5, /device:TPU:0, one launch (start us, length us, event | category | flops | bytes accessed | tf_op | source)
XLA Modules:
  0.0 382.0 jit_solution(17395476493224227004)
XLA Ops:
  8.2 2.4 copy.12
  10.6 3.0 collective-permute-start
  13.7 51.4 %collective-permute-done = bf16[768,2,6,128]{0,3,2,1:T(8,128)(2,1)S(1)} collective-permute-done((bf16[768,2,6,128]{0,3,2,1:T(8,128)(2,1)}, bf16[768,2,6,128]{0,3,2,1:T(8,128)(2,1)S(1)}, u32[]{:S(2)}, u32[]{:S(2)}) %collective-permute-start) | collective-permute-done | bytes 2359328 | tf_op jit(solution)/shard_map/ppermute | solution.py:133
  67.2 50.6 %collective-permute-done.2 = bf16[768,2,6,128]{0,3,2,1:T(8,128)(2,1)} collective-permute-done((bf16[768,2,6,128]{0,3,2,1:T(8,128)(2,1)S(1)}, bf16[768,2,6,128]{0,3,2,1:T(8,128)(2,1)}, u32[]{:S(2)}, u32[]{:S(2)}) %collective-permute-start.2) | collective-permute-done | bytes 2359328 | tf_op jit(solution)/shard_map/ppermute | solution.py:133
  131.7 37.9 %collective-permute-done.4 = bf16[768,2,6,128]{0,3,2,1:T(8,128)(2,1)S(1)} collective-permute-done((bf16[768,2,6,128]{0,3,2,1:T(8,128)(2,1)}, bf16[768,2,6,128]{0,3,2,1:T(8,128)(2,1)S(1)}, u32[]{:S(2)}, u32[]{:S(2)}) %collective-permute-start.4) | collective-permute-done | bytes 2359328 | tf_op jit(solution)/shard_map/ppermute | solution.py:133
  174.2 3.1 fusion.30
  177.5 2.9 fusion.20
  181.6 2.8 fusion.14
  184.4 2.8 convolution_add_fusion.2
  187.2 2.9 fusion
  190.0 5.4 %collective-permute-done.6 = bf16[384,2,6,128]{0,3,2,1:T(8,128)(2,1)} collective-permute-done((bf16[384,2,6,128]{0,3,2,1:T(8,128)(2,1)S(1)}, bf16[384,2,6,128]{0,3,2,1:T(8,128)(2,1)}, u32[]{:S(2)}, u32[]{:S(2)}) %collective-permute-start.6) | collective-permute-done | bytes 1179680 | tf_op jit(solution)/shard_map/ppermute | solution.py:141
  208.2 24.4 %collective-permute-done.9 = bf16[768,6,128]{0,2,1:T(8,128)(2,1)} collective-permute-done((bf16[768,6,128]{0,2,1:T(8,128)(2,1)S(1)}, bf16[768,6,128]{0,2,1:T(8,128)(2,1)}, u32[]{:S(2)}, u32[]{:S(2)}) %collective-permute-start.9) | collective-permute-done | bytes 1179680 | tf_op jit(solution)/shard_map/ppermute | solution.py:134
  232.6 2.6 collective-permute-start.11
  235.2 19.9 %collective-permute-done.8 = bf16[768,6,128]{0,2,1:T(8,128)(2,1)} collective-permute-done((bf16[768,6,128]{0,2,1:T(8,128)(2,1)S(1)}, bf16[768,6,128]{0,2,1:T(8,128)(2,1)}, u32[]{:S(2)}, u32[]{:S(2)}) %collective-permute-start.8) | collective-permute-done | bytes 1179680 | tf_op jit(solution)/shard_map/ppermute | solution.py:133
  255.1 6.5 %collective-permute-done.16 = bf16[384,2,6,128]{0,3,2,1:T(8,128)(2,1)S(1)} collective-permute-done((bf16[384,2,6,128]{0,3,2,1:T(8,128)(2,1)S(1)}, bf16[384,2,6,128]{0,3,2,1:T(8,128)(2,1)S(1)}, u32[]{:S(2)}, u32[]{:S(2)}) %collective-permute-start.16) | collective-permute-done | bytes 1179680 | tf_op jit(solution)/shard_map/ppermute | solution.py:106
  264.7 7.1 %collective-permute-start.17 = (bf16[2,384,2,6,128]{1,4,3,2,0:T(8,128)(2,1)}, bf16[2,384,2,6,128]{1,4,3,2,0:T(8,128)(2,1)}, u32[]{:S(2)}, u32[]{:S(2)}) collective-permute-start(bf16[2,384,2,6,128]{1,4,3,2,0:T(8,128)(2,1)} %pad_maximum_fusion), channel_id=1, source_target_pairs={{0,4},{8,12},{16,20},{24,28},{1,5},{9,13},{17,21},{25,29},{2,6},{1... | collective-permute-start | bytes 7077896 | tf_op jit(solution)/shard_map/ppermute | solution.py:154
  273.7 6.4 %collective-permute-done.11 = bf16[768,6,128]{0,2,1:T(8,128)(2,1)} collective-permute-done((bf16[768,6,128]{0,2,1:T(8,128)(2,1)}, bf16[768,6,128]{0,2,1:T(8,128)(2,1)}, u32[]{:S(2)}, u32[]{:S(2)}) %collective-permute-start.11) | collective-permute-done | bytes 1179680 | tf_op jit(solution)/shard_map/ppermute | solution.py:134
  280.2 2.5 collective-permute-start.13
  285.3 20.0 %collective-permute-done.18 = bf16[384,2,6,128]{0,3,2,1:T(8,128)(2,1)} collective-permute-done((bf16[384,2,6,128]{0,3,2,1:T(8,128)(2,1)S(1)}, bf16[384,2,6,128]{0,3,2,1:T(8,128)(2,1)}, u32[]{:S(2)}, u32[]{:S(2)}) %collective-permute-start.18) | collective-permute-done | bytes 1179680 | tf_op jit(solution)/shard_map/ppermute | solution.py:157
  313.8 37.2 %collective-permute-done.12 = bf16[768,6,128]{0,2,1:T(8,128)(2,1)S(1)} collective-permute-done((bf16[768,6,128]{0,2,1:T(8,128)(2,1)}, bf16[768,6,128]{0,2,1:T(8,128)(2,1)S(1)}, u32[]{:S(2)}, u32[]{:S(2)}) %collective-permute-start.12) | collective-permute-done | bytes 1179680 | tf_op jit(solution)/shard_map/ppermute | solution.py:133
  351.1 2.4 collective-permute-start.14
  354.5 3.7 fusion.10
  358.2 2.8 collective-permute-done.14
  365.8 9.3 %shard_map.46 = bf16[6,384,128]{2,1,0:T(8,128)(2,1)} custom-call(bf16[768,384]{1,0:T(8,128)(2,1)} %fusion.9.q_ref, bf16[1536,384]{1,0:T(8,128)(2,1)} %bitcast.77, bf16[1536,384]{1,0:T(8,128)(2,1)} %bitcast.83, bf16[1536,384]{1,0:T(8,128)(2,1)} %bitcast.86, bf16[1536,384]{1,0:T(8,128)(2,1)} %bitcast.81, bf16[1536,384]{1,0:T(8,128)(2,1)} %bitcast.78, ...), custom_call_target="tpu_custom_call" | custom-call | flops 1811939328 | bytes 5898240 | tf_op jit(solution)/shard_map/pallas_call | solution.py:52
  (74 shorter events, 49.1 us)
Async XLA Ops:
  6.5 167.7 %all-gather.2.cloned.1.call-start = ((), (), s32[]{:S(2)}) async-start(), calls=%async_computation | async-start | bytes 5898240 | tf_op jit(solution)/shard_map/all_gather | solution.py:165
  8.2 111.6 %copy-start.7 = (s32[8]{0:T(128)S(1)}, s32[8]{0:T(128)}, u32[]{:S(2)}) copy-start(s32[8]{0:T(128)} %constant.108.clone) | copy-start | bytes 100
  8.2 116.8 %copy-start.6 = (s32[8]{0:T(128)S(1)}, s32[8]{0:T(128)}, u32[]{:S(2)}) copy-start(s32[8]{0:T(128)} %constant.109.clone) | copy-start | bytes 100
  10.6 119.7 %slice-start.3 = ((bf16[768,3,6,128]{3,0,2,1:T(8,128)(2,1)}), bf16[768,1,6,128]{3,0,2,1:T(8,128)(2,1)S(1)}, s32[]{:S(2)}) async-start(bf16[768,3,6,128]{3,0,2,1:T(8,128)(2,1)} %param.5), calls=%async_computation.4 | async-start | bytes 2359296 | tf_op jit(solution)/shard_map/slice | solution.py:174
  10.6 54.5 %collective-permute-start = (bf16[768,2,6,128]{0,3,2,1:T(8,128)(2,1)}, bf16[768,2,6,128]{0,3,2,1:T(8,128)(2,1)S(1)}, u32[]{:S(2)}, u32[]{:S(2)}) collective-permute-start(bf16[768,2,6,128]{0,3,2,1:T(8,128)(2,1)} %copy.12), channel_id=1, source_target_pairs={{0,4},{4,12},{12,20},{20,28},{28,24},{24,16},{16,8},{8,0},{1,5},{5... | collective-permute-start | bytes 7077896 | tf_op jit(solution)/shard_map/ppermute | solution.py:133
  13.6 53.2 %collective-permute-start.1 = (bf16[768,2,6,128]{0,3,2,1:T(8,128)(2,1)}, bf16[768,2,6,128]{0,3,2,1:T(8,128)(2,1)}, u32[]{:S(2)}, u32[]{:S(2)}) collective-permute-start(bf16[768,2,6,128]{0,3,2,1:T(8,128)(2,1)} %copy.12), channel_id=1, source_target_pairs={{0,8},{4,0},{12,4},{20,12},{28,20},{24,28},{16,24},{8,16},{1,9},{5... | collective-permute-start | bytes 7077896 | tf_op jit(solution)/shard_map/ppermute | solution.py:134
  65.1 52.6 %collective-permute-start.2 = (bf16[768,2,6,128]{0,3,2,1:T(8,128)(2,1)S(1)}, bf16[768,2,6,128]{0,3,2,1:T(8,128)(2,1)}, u32[]{:S(2)}, u32[]{:S(2)}) collective-permute-start(bf16[768,2,6,128]{0,3,2,1:T(8,128)(2,1)S(1)} %collective-permute-done), channel_id=1, source_target_pairs={{0,4},{4,12},{12,20},{20,28},{28,24},{24,16},{16,8},{8,0},{1,5},{5... | collective-permute-start | bytes 7077896 | tf_op jit(solution)/shard_map/ppermute | solution.py:133
  66.8 52.3 %collective-permute-start.3 = (bf16[768,2,6,128]{0,3,2,1:T(8,128)(2,1)}, bf16[768,2,6,128]{0,3,2,1:T(8,128)(2,1)}, u32[]{:S(2)}, u32[]{:S(2)}) collective-permute-start(bf16[768,2,6,128]{0,3,2,1:T(8,128)(2,1)} %collective-permute-done.1), channel_id=1, source_target_pairs={{0,8},{4,0},{12,4},{20,12},{28,20},{24,28},{16,24},{8,16},{1,9},{5... | collective-permute-start | bytes 7077896 | tf_op jit(solution)/shard_map/ppermute | solution.py:134
  117.8 51.8 %collective-permute-start.4 = (bf16[768,2,6,128]{0,3,2,1:T(8,128)(2,1)}, bf16[768,2,6,128]{0,3,2,1:T(8,128)(2,1)S(1)}, u32[]{:S(2)}, u32[]{:S(2)}) collective-permute-start(bf16[768,2,6,128]{0,3,2,1:T(8,128)(2,1)} %collective-permute-done.2), channel_id=1, source_target_pairs={{0,4},{4,12},{12,20},{20,28},{28,24},{24,16},{16,8},{8,0},{1,5},{5... | collective-permute-start | bytes 7077896 | tf_op jit(solution)/shard_map/ppermute | solution.py:133
  119.1 51.7 %collective-permute-start.5 = (bf16[768,2,6,128]{0,3,2,1:T(8,128)(2,1)}, bf16[768,2,6,128]{0,3,2,1:T(8,128)(2,1)}, u32[]{:S(2)}, u32[]{:S(2)}) collective-permute-start(bf16[768,2,6,128]{0,3,2,1:T(8,128)(2,1)} %collective-permute-done.3), channel_id=1, source_target_pairs={{0,8},{4,0},{12,4},{20,12},{28,20},{24,28},{16,24},{8,16},{1,9},{5... | collective-permute-start | bytes 7077896 | tf_op jit(solution)/shard_map/ppermute | solution.py:134
  169.7 25.7 %collective-permute-start.6 = (bf16[384,2,6,128]{0,3,2,1:T(8,128)(2,1)S(1)}, bf16[384,2,6,128]{0,3,2,1:T(8,128)(2,1)}, u32[]{:S(2)}, u32[]{:S(2)}) collective-permute-start(bf16[384,2,6,128]{0,3,2,1:T(8,128)(2,1)S(1)} %slice.32), channel_id=1, source_target_pairs={{0,4},{4,12},{12,20},{20,28},{28,24},{24,16},{16,8},{8,0},{1,5},{5... | collective-permute-start | bytes 3538952 | tf_op jit(solution)/shard_map/ppermute | solution.py:141
  173.3 25.2 %collective-permute-start.7 = (bf16[384,2,6,128]{0,3,2,1:T(8,128)(2,1)}, bf16[384,2,6,128]{0,3,2,1:T(8,128)(2,1)}, u32[]{:S(2)}, u32[]{:S(2)}) collective-permute-start(bf16[384,2,6,128]{0,3,2,1:T(8,128)(2,1)} %slice.33), channel_id=1, source_target_pairs={{0,8},{4,0},{12,4},{20,12},{28,20},{24,28},{16,24},{8,16},{1,9},{5... | collective-permute-start | bytes 3538952 | tf_op jit(solution)/shard_map/ppermute | solution.py:142
  204.8 27.8 %collective-permute-start.9 = (bf16[768,6,128]{0,2,1:T(8,128)(2,1)S(1)}, bf16[768,6,128]{0,2,1:T(8,128)(2,1)}, u32[]{:S(2)}, u32[]{:S(2)}) collective-permute-start(bf16[768,6,128]{0,2,1:T(8,128)(2,1)S(1)} %bitcast.89), channel_id=1, source_target_pairs={{0,8},{4,0},{12,4},{20,12},{28,20},{24,28},{16,24},{8,16},{1,9},{5... | collective-permute-start | bytes 3538952 | tf_op jit(solution)/shard_map/ppermute | solution.py:134
  206.2 48.9 %collective-permute-start.8 = (bf16[768,6,128]{0,2,1:T(8,128)(2,1)S(1)}, bf16[768,6,128]{0,2,1:T(8,128)(2,1)}, u32[]{:S(2)}, u32[]{:S(2)}) collective-permute-start(bf16[768,6,128]{0,2,1:T(8,128)(2,1)S(1)} %bitcast.90), channel_id=1, source_target_pairs={{0,4},{4,12},{12,20},{20,28},{28,24},{24,16},{16,8},{8,0},{1,5},{5... | collective-permute-start | bytes 3538952 | tf_op jit(solution)/shard_map/ppermute | solution.py:133
  206.9 54.7 %collective-permute-start.16 = (bf16[384,2,6,128]{0,3,2,1:T(8,128)(2,1)S(1)}, bf16[384,2,6,128]{0,3,2,1:T(8,128)(2,1)S(1)}, u32[]{:S(2)}, u32[]{:S(2)}) collective-permute-start(bf16[384,2,6,128]{0,3,2,1:T(8,128)(2,1)S(1)} %bitcast.75), channel_id=1, source_target_pairs={{0,8},{4,12},{8,16},{12,20},{16,24},{20,28},{24,0},{28,4},{1,9},{5... | collective-permute-start | bytes 3538952 | tf_op jit(solution)/shard_map/ppermute | solution.py:106
  232.6 47.6 %collective-permute-start.11 = (bf16[768,6,128]{0,2,1:T(8,128)(2,1)}, bf16[768,6,128]{0,2,1:T(8,128)(2,1)}, u32[]{:S(2)}, u32[]{:S(2)}) collective-permute-start(bf16[768,6,128]{0,2,1:T(8,128)(2,1)} %collective-permute-done.9), channel_id=1, source_target_pairs={{0,8},{4,0},{12,4},{20,12},{28,20},{24,28},{16,24},{8,16},{1,9},{5... | collective-permute-start | bytes 3538952 | tf_op jit(solution)/shard_map/ppermute | solution.py:134
  255.1 27.5 %collective-permute-start.10 = (bf16[768,6,128]{0,2,1:T(8,128)(2,1)}, bf16[768,6,128]{0,2,1:T(8,128)(2,1)}, u32[]{:S(2)}, u32[]{:S(2)}) collective-permute-start(bf16[768,6,128]{0,2,1:T(8,128)(2,1)} %collective-permute-done.8), channel_id=1, source_target_pairs={{0,4},{4,12},{12,20},{20,28},{28,24},{24,16},{16,8},{8,0},{1,5},{5... | collective-permute-start | bytes 3538952 | tf_op jit(solution)/shard_map/ppermute | solution.py:133
  261.6 43.7 %collective-permute-start.18 = (bf16[384,2,6,128]{0,3,2,1:T(8,128)(2,1)S(1)}, bf16[384,2,6,128]{0,3,2,1:T(8,128)(2,1)}, u32[]{:S(2)}, u32[]{:S(2)}) collective-permute-start(bf16[384,2,6,128]{0,3,2,1:T(8,128)(2,1)S(1)} %collective-permute-done.16), channel_id=1, source_target_pairs={{4,0},{12,8},{20,16},{28,24},{5,1},{13,9},{21,17},{29,25},{6,2},{1... | collective-permute-start | bytes 3538952 | tf_op jit(solution)/shard_map/ppermute | solution.py:157
  264.7 89.8 %collective-permute-start.17 = (bf16[2,384,2,6,128]{1,4,3,2,0:T(8,128)(2,1)}, bf16[2,384,2,6,128]{1,4,3,2,0:T(8,128)(2,1)}, u32[]{:S(2)}, u32[]{:S(2)}) collective-permute-start(bf16[2,384,2,6,128]{1,4,3,2,0:T(8,128)(2,1)} %pad_maximum_fusion), channel_id=1, source_target_pairs={{0,4},{8,12},{16,20},{24,28},{1,5},{9,13},{17,21},{25,29},{2,6},{1... | collective-permute-start | bytes 7077896 | tf_op jit(solution)/shard_map/ppermute | solution.py:154
  280.2 73.3 %collective-permute-start.13 = (bf16[768,6,128]{0,2,1:T(8,128)(2,1)}, bf16[768,6,128]{0,2,1:T(8,128)(2,1)S(1)}, u32[]{:S(2)}, u32[]{:S(2)}) collective-permute-start(bf16[768,6,128]{0,2,1:T(8,128)(2,1)} %collective-permute-done.11), channel_id=1, source_target_pairs={{0,8},{4,0},{12,4},{20,12},{28,20},{24,28},{16,24},{8,16},{1,9},{5... | collective-permute-start | bytes 3538952 | tf_op jit(solution)/shard_map/ppermute | solution.py:134
  282.6 68.4 %collective-permute-start.12 = (bf16[768,6,128]{0,2,1:T(8,128)(2,1)}, bf16[768,6,128]{0,2,1:T(8,128)(2,1)S(1)}, u32[]{:S(2)}, u32[]{:S(2)}) collective-permute-start(bf16[768,6,128]{0,2,1:T(8,128)(2,1)} %collective-permute-done.10), channel_id=1, source_target_pairs={{0,4},{4,12},{12,20},{20,28},{28,24},{24,16},{16,8},{8,0},{1,5},{5... | collective-permute-start | bytes 3538952 | tf_op jit(solution)/shard_map/ppermute | solution.py:133
  305.3 49.1 %collective-permute-start.19 = (bf16[384,2,6,128]{0,3,2,1:T(8,128)(2,1)}, bf16[384,2,6,128]{0,3,2,1:T(8,128)(2,1)S(1)}, u32[]{:S(2)}, u32[]{:S(2)}) collective-permute-start(bf16[384,2,6,128]{0,3,2,1:T(8,128)(2,1)} %collective-permute-done.18), channel_id=1, source_target_pairs={{0,8},{8,16},{16,24},{24,0},{1,9},{9,17},{17,25},{25,1},{2,10},{10... | collective-permute-start | bytes 3538952 | tf_op jit(solution)/shard_map/ppermute | solution.py:158
  351.1 9.9 %collective-permute-start.14 = (bf16[384,6,128]{0,2,1:T(8,128)(2,1)S(1)}, bf16[384,6,128]{0,2,1:T(8,128)(2,1)S(1)}, u32[]{:S(2)}, u32[]{:S(2)}) collective-permute-start(bf16[384,6,128]{0,2,1:T(8,128)(2,1)S(1)} %slice.34), channel_id=1, source_target_pairs={{0,4},{4,12},{12,20},{20,28},{28,24},{24,16},{16,8},{8,0},{1,5},{5... | collective-permute-start | bytes 1769480 | tf_op jit(solution)/shard_map/ppermute | solution.py:141
  353.6 9.9 %collective-permute-start.15 = (bf16[384,6,128]{0,2,1:T(8,128)(2,1)S(1)}, bf16[384,6,128]{0,2,1:T(8,128)(2,1)S(1)}, u32[]{:S(2)}, u32[]{:S(2)}) collective-permute-start(bf16[384,6,128]{0,2,1:T(8,128)(2,1)S(1)} %slice.35), channel_id=1, source_target_pairs={{0,8},{4,0},{12,4},{20,12},{28,20},{24,28},{16,24},{8,16},{1,9},{5... | collective-permute-start | bytes 1769480 | tf_op jit(solution)/shard_map/ppermute | solution.py:142
  (9 other events, 139.1 us)
Sparse Core Ops, SparseCore 0:
  13.8 39.1 all-gather.1

commit v6 on v5

--- a/solution.py
+++ b/solution.py
@@ -142,10 +142,11 @@
                 last_ccw = lax.ppermute(going_ccw[half:], "ctx", counter)
                 total = total + partial(far, last_cw, 0)
                 total = total + partial(far, last_ccw, half)
-            else:
-                last_cw = lax.ppermute(going_cw, "ctx", clockwise)
-                total = total + partial(far, last_cw, 0)
-        return total
+                return total, (last_cw, last_ccw)
+            last_cw = lax.ppermute(going_cw, "ctx", clockwise)
+            total = total + partial(far, last_cw, 0)
+            return total, (last_cw,)
+        return total, (going_cw, going_ccw)
 
     def earlier_blocks(key_value, me):
         if n % 2 or n < 4 or REACH != 4:
@@ -169,11 +170,14 @@
         scale = 1.0 / math.sqrt(head_size)
         me = lax.axis_index("ctx")
 
-        kv_total = ring_project(features, qkv_weight[:, 1:], me)
+        kv_total, arrived = ring_project(features, qkv_weight[:, 1:], me)
         key_value = kv_total.astype(jnp.bfloat16).reshape(rows_dev, 2, heads_local, head_size)
-        q_piece, key_value = lax.optimization_barrier((qkv_weight[:, 0], key_value))
+        if n <= 8:
+            q_piece, _ = lax.optimization_barrier((qkv_weight[:, 0], arrived))
+        else:
+            q_piece, key_value = lax.optimization_barrier((qkv_weight[:, 0], key_value))
         blocks = [key_value] + earlier_blocks(key_value, me)
-        q_total = ring_project(features, q_piece, me)
+        q_total, _ = ring_project(features, q_piece, me)
         queries = q_total.astype(jnp.bfloat16).reshape(rows_dev, heads_local, head_size)
 
         return windowed_attention(queries, blocks, scale)

time: 383 us -> 377 us (0.984)
  waiting for transfers between devices: 266 us -> 260 us
    ppermute x6, waiting for transfers between devices: 197 us -> 51.2 us  [ring_project(): going_cw = lax.ppermute(going_cw, 'ctx', clockwise)]
    ppermute x6, waiting for transfers between devices: 30.8 us -> 168 us  [ring_project(): going_ccw = lax.ppermute(going_ccw, 'ctx', counter)]
    ppermute x6, starting transfers between devices: 7.47 us -> 12.5 us  [ring_project(): going_ccw = lax.ppermute(going_ccw, 'ctx', counter)]
  transfers between devices with their start and end apart: 21 -> 21, of which waited for: 13 -> 13; matrix products, arithmetic and copies ran while one was open for 11% -> 12% of each run, Pallas kernels for 0% -> 0%
where the time goes in v6:
time: 377 us; the launch traced here: 376 us
  waiting for transfers between devices  260 us (69%)
  matrix products  36.5 us (10%)
  starting transfers between devices  31.7 us (8%)
  between operations  22.7 us (6%)
  local copies, waits for them, and re-layouts  10.5 us (3%)
  Pallas kernels  9.3 us (2%)
  other arithmetic  5.09 us (1%)
    ppermute x6, waiting for transfers between devices, ring_project(): going_ccw = lax.ppermute(going_ccw, 'ctx', counter)  168 us
    ppermute x6, waiting for transfers between devices, ring_project(): going_cw = lax.ppermute(going_cw, 'ctx', clockwise)  51.2 us
    dot_general x18, matrix products, partial(): return jnp.dot(cols, flat, preferred_element_type=jnp.float32)  36.5 us
    ppermute x1, waiting for transfers between devices, earlier_blocks(): lax.ppermute(two_back, 'ctx', [(o, o - 1) for o in range(1, n, 2)])  20.6 us
    ppermute x6, starting transfers between devices, ring_project(): going_ccw = lax.ppermute(going_ccw, 'ctx', counter)  12.5 us
    pallas_call x1, Pallas kernels, windowed_attention(): pl.pallas_call(functools.partial(attention_kernel, scale, reach), out_sha...  9.3 us
  transfers between devices with their start and end apart: 21, of which 13 were waited for; matrix products, arithmetic and copies ran while one was open for 12% of the time, Pallas kernels for 0%

profile of v6, /device:TPU:0, one launch (start us, length us, event | category | flops | bytes accessed | tf_op | source)
XLA Modules:
  0.0 376.3 jit_solution(14208627266058997627)
XLA Ops:
  10.6 3.0 collective-permute-start.4
  13.7 51.4 %collective-permute-done.4 = bf16[768,2,6,128]{0,3,2,1:T(8,128)(2,1)S(1)} collective-permute-done((bf16[768,2,6,128]{0,3,2,1:T(8,128)(2,1)}, bf16[768,2,6,128]{0,3,2,1:T(8,128)(2,1)S(1)}, u32[]{:S(2)}, u32[]{:S(2)}) %collective-permute-start.4) | collective-permute-done | bytes 2359328 | tf_op jit(solution)/shard_map/ppermute | solution.py:134
  67.1 50.6 %collective-permute-done.5 = bf16[768,2,6,128]{0,3,2,1:T(8,128)(2,1)} collective-permute-done((bf16[768,2,6,128]{0,3,2,1:T(8,128)(2,1)S(1)}, bf16[768,2,6,128]{0,3,2,1:T(8,128)(2,1)}, u32[]{:S(2)}, u32[]{:S(2)}) %collective-permute-start.5) | collective-permute-done | bytes 2359328 | tf_op jit(solution)/shard_map/ppermute | solution.py:134
  131.5 38.1 %collective-permute-done.6 = bf16[768,2,6,128]{0,3,2,1:T(8,128)(2,1)} collective-permute-done((bf16[768,2,6,128]{0,3,2,1:T(8,128)(2,1)}, bf16[768,2,6,128]{0,3,2,1:T(8,128)(2,1)}, u32[]{:S(2)}, u32[]{:S(2)}) %collective-permute-start.6) | collective-permute-done | bytes 2359328 | tf_op jit(solution)/shard_map/ppermute | solution.py:134
  169.6 2.4 slice.33
  175.3 3.4 fusion.29
  178.7 3.1 fusion.18
  181.8 3.1 convolution_add_fusion.3
  184.9 3.2 fusion.12
  189.7 3.3 fusion
  192.9 4.7 %collective-permute-done.7 = bf16[384,2,6,128]{0,3,2,1:T(8,128)(2,1)S(1)} collective-permute-done((bf16[384,2,6,128]{0,3,2,1:T(8,128)(2,1)}, bf16[384,2,6,128]{0,3,2,1:T(8,128)(2,1)S(1)}, u32[]{:S(2)}, u32[]{:S(2)}) %collective-permute-start.7) | collective-permute-done | bytes 1179680 | tf_op jit(solution)/shard_map/ppermute | solution.py:142
  197.7 3.0 collective-permute-done.3
  209.0 20.2 %collective-permute-done.9 = bf16[768,6,128]{0,2,1:T(8,128)(2,1)} collective-permute-done((bf16[768,6,128]{0,2,1:T(8,128)(2,1)S(1)}, bf16[768,6,128]{0,2,1:T(8,128)(2,1)}, u32[]{:S(2)}, u32[]{:S(2)}) %collective-permute-start.9) | collective-permute-done | bytes 1179680 | tf_op jit(solution)/shard_map/ppermute | solution.py:134
  229.2 2.6 collective-permute-start.11
  231.8 16.0 %collective-permute-done.8 = bf16[768,6,128]{0,2,1:T(8,128)(2,1)} collective-permute-done((bf16[768,6,128]{0,2,1:T(8,128)(2,1)S(1)}, bf16[768,6,128]{0,2,1:T(8,128)(2,1)}, u32[]{:S(2)}, u32[]{:S(2)}) %collective-permute-start.8) | collective-permute-done | bytes 1179680 | tf_op jit(solution)/shard_map/ppermute | solution.py:133
  249.7 7.2 %collective-permute-done.16 = bf16[384,2,6,128]{0,3,2,1:T(8,128)(2,1)S(1)} collective-permute-done((bf16[384,2,6,128]{0,3,2,1:T(8,128)(2,1)S(1)}, bf16[384,2,6,128]{0,3,2,1:T(8,128)(2,1)S(1)}, u32[]{:S(2)}, u32[]{:S(2)}) %collective-permute-start.16) | collective-permute-done | bytes 1179680 | tf_op jit(solution)/shard_map/ppermute | solution.py:106
  260.0 6.2 %collective-permute-start.17 = (bf16[2,384,2,6,128]{1,4,3,2,0:T(8,128)(2,1)}, bf16[2,384,2,6,128]{1,4,3,2,0:T(8,128)(2,1)}, u32[]{:S(2)}, u32[]{:S(2)}) collective-permute-start(bf16[2,384,2,6,128]{1,4,3,2,0:T(8,128)(2,1)} %pad_maximum_fusion), channel_id=1, source_target_pairs={{0,4},{8,12},{16,20},{24,28},{1,5},{9,13},{17,21},{25,29},{2,6},{1... | collective-permute-start | bytes 7077896 | tf_op jit(solution)/shard_map/ppermute | solution.py:155
  268.6 8.2 %collective-permute-done.11 = bf16[768,6,128]{0,2,1:T(8,128)(2,1)} collective-permute-done((bf16[768,6,128]{0,2,1:T(8,128)(2,1)}, bf16[768,6,128]{0,2,1:T(8,128)(2,1)}, u32[]{:S(2)}, u32[]{:S(2)}) %collective-permute-start.11) | collective-permute-done | bytes 1179680 | tf_op jit(solution)/shard_map/ppermute | solution.py:134
  276.8 2.5 collective-permute-start.13
  281.2 20.6 %collective-permute-done.18 = bf16[384,2,6,128]{0,3,2,1:T(8,128)(2,1)S(1)} collective-permute-done((bf16[384,2,6,128]{0,3,2,1:T(8,128)(2,1)S(1)}, bf16[384,2,6,128]{0,3,2,1:T(8,128)(2,1)S(1)}, u32[]{:S(2)}, u32[]{:S(2)}) %collective-permute-start.18) | collective-permute-done | bytes 1179680 | tf_op jit(solution)/shard_map/ppermute | solution.py:158
  310.2 35.2 %collective-permute-done.12 = bf16[768,6,128]{0,2,1:T(8,128)(2,1)S(1)} collective-permute-done((bf16[768,6,128]{0,2,1:T(8,128)(2,1)}, bf16[768,6,128]{0,2,1:T(8,128)(2,1)S(1)}, u32[]{:S(2)}, u32[]{:S(2)}) %collective-permute-start.12) | collective-permute-done | bytes 1179680 | tf_op jit(solution)/shard_map/ppermute | solution.py:133
  348.8 3.4 fusion.10
  352.1 3.2 collective-permute-done.14
  360.1 9.3 %shard_map.46 = bf16[6,384,128]{2,1,0:T(8,128)(2,1)} custom-call(bf16[768,384]{1,0:T(8,128)(2,1)} %fusion.9.q_ref, bf16[1536,384]{1,0:T(8,128)(2,1)} %bitcast.75, bf16[1536,384]{1,0:T(8,128)(2,1)} %bitcast.81, bf16[1536,384]{1,0:T(8,128)(2,1)} %bitcast.84, bf16[1536,384]{1,0:T(8,128)(2,1)} %bitcast.79, bf16[1536,384]{1,0:T(8,128)(2,1)} %bitcast.76, ...), custom_call_target="tpu_custom_call" | custom-call | flops 1811939328 | bytes 5898240 | tf_op jit(solution)/shard_map/pallas_call | solution.py:52
  (75 shorter events, 49.6 us)
Async XLA Ops:
  6.5 168.7 %all-gather.2.cloned.1.call-start = ((), (), s32[]{:S(2)}) async-start(), calls=%async_computation | async-start | bytes 5898240 | tf_op jit(solution)/shard_map/all_gather | solution.py:166
  8.2 111.5 %copy-start.8 = (s32[8]{0:T(128)S(1)}, s32[8]{0:T(128)}, u32[]{:S(2)}) copy-start(s32[8]{0:T(128)} %constant.108.clone) | copy-start | bytes 100
  8.2 116.8 %copy-start.7 = (s32[8]{0:T(128)S(1)}, s32[8]{0:T(128)}, u32[]{:S(2)}) copy-start(s32[8]{0:T(128)} %constant.109.clone) | copy-start | bytes 100
  10.6 119.5 %slice-start.3 = ((bf16[768,3,6,128]{3,0,2,1:T(8,128)(2,1)}), bf16[768,1,6,128]{3,0,2,1:T(8,128)(2,1)S(1)}, s32[]{:S(2)}) async-start(bf16[768,3,6,128]{3,0,2,1:T(8,128)(2,1)} %param.5), calls=%async_computation.4 | async-start | bytes 2359296 | tf_op jit(solution)/shard_map/slice | solution.py:176
  10.6 54.4 %collective-permute-start.4 = (bf16[768,2,6,128]{0,3,2,1:T(8,128)(2,1)}, bf16[768,2,6,128]{0,3,2,1:T(8,128)(2,1)S(1)}, u32[]{:S(2)}, u32[]{:S(2)}) collective-permute-start(bf16[768,2,6,128]{0,3,2,1:T(8,128)(2,1)} %copy.35), channel_id=1, source_target_pairs={{0,8},{4,0},{12,4},{20,12},{28,20},{24,28},{16,24},{8,16},{1,9},{5... | collective-permute-start | bytes 7077896 | tf_op jit(solution)/shard_map/ppermute | solution.py:134
  13.6 53.2 %collective-permute-start = (bf16[768,2,6,128]{0,3,2,1:T(8,128)(2,1)}, bf16[768,2,6,128]{0,3,2,1:T(8,128)(2,1)}, u32[]{:S(2)}, u32[]{:S(2)}) collective-permute-start(bf16[768,2,6,128]{0,3,2,1:T(8,128)(2,1)} %copy.35), channel_id=1, source_target_pairs={{0,4},{4,12},{12,20},{20,28},{28,24},{24,16},{16,8},{8,0},{1,5},{5... | collective-permute-start | bytes 7077896 | tf_op jit(solution)/shard_map/ppermute | solution.py:133
  65.0 52.6 %collective-permute-start.5 = (bf16[768,2,6,128]{0,3,2,1:T(8,128)(2,1)S(1)}, bf16[768,2,6,128]{0,3,2,1:T(8,128)(2,1)}, u32[]{:S(2)}, u32[]{:S(2)}) collective-permute-start(bf16[768,2,6,128]{0,3,2,1:T(8,128)(2,1)S(1)} %collective-permute-done.4), channel_id=1, source_target_pairs={{0,8},{4,0},{12,4},{20,12},{28,20},{24,28},{16,24},{8,16},{1,9},{5... | collective-permute-start | bytes 7077896 | tf_op jit(solution)/shard_map/ppermute | solution.py:134
  66.8 52.3 %collective-permute-start.1 = (bf16[768,2,6,128]{0,3,2,1:T(8,128)(2,1)}, bf16[768,2,6,128]{0,3,2,1:T(8,128)(2,1)}, u32[]{:S(2)}, u32[]{:S(2)}) collective-permute-start(bf16[768,2,6,128]{0,3,2,1:T(8,128)(2,1)} %collective-permute-done), channel_id=1, source_target_pairs={{0,4},{4,12},{12,20},{20,28},{28,24},{24,16},{16,8},{8,0},{1,5},{5... | collective-permute-start | bytes 7077896 | tf_op jit(solution)/shard_map/ppermute | solution.py:133
  117.7 51.9 %collective-permute-start.6 = (bf16[768,2,6,128]{0,3,2,1:T(8,128)(2,1)}, bf16[768,2,6,128]{0,3,2,1:T(8,128)(2,1)}, u32[]{:S(2)}, u32[]{:S(2)}) collective-permute-start(bf16[768,2,6,128]{0,3,2,1:T(8,128)(2,1)} %collective-permute-done.5), channel_id=1, source_target_pairs={{0,8},{4,0},{12,4},{20,12},{28,20},{24,28},{16,24},{8,16},{1,9},{5... | collective-permute-start | bytes 7077896 | tf_op jit(solution)/shard_map/ppermute | solution.py:134
  119.2 54.0 %collective-permute-start.2 = (bf16[768,2,6,128]{0,3,2,1:T(8,128)(2,1)}, bf16[768,2,6,128]{0,3,2,1:T(8,128)(2,1)S(1)}, u32[]{:S(2)}, u32[]{:S(2)}) collective-permute-start(bf16[768,2,6,128]{0,3,2,1:T(8,128)(2,1)} %collective-permute-done.1), channel_id=1, source_target_pairs={{0,4},{4,12},{12,20},{20,28},{28,24},{24,16},{16,8},{8,0},{1,5},{5... | collective-permute-start | bytes 7077896 | tf_op jit(solution)/shard_map/ppermute | solution.py:133
  172.1 25.6 %collective-permute-start.7 = (bf16[384,2,6,128]{0,3,2,1:T(8,128)(2,1)}, bf16[384,2,6,128]{0,3,2,1:T(8,128)(2,1)S(1)}, u32[]{:S(2)}, u32[]{:S(2)}) collective-permute-start(bf16[384,2,6,128]{0,3,2,1:T(8,128)(2,1)} %slice.33), channel_id=1, source_target_pairs={{0,8},{4,0},{12,4},{20,12},{28,20},{24,28},{16,24},{8,16},{1,9},{5... | collective-permute-start | bytes 3538952 | tf_op jit(solution)/shard_map/ppermute | solution.py:142
  174.4 26.3 %collective-permute-start.3 = (bf16[384,2,6,128]{0,3,2,1:T(8,128)(2,1)}, bf16[384,2,6,128]{0,3,2,1:T(8,128)(2,1)}, u32[]{:S(2)}, u32[]{:S(2)}) collective-permute-start(bf16[384,2,6,128]{0,3,2,1:T(8,128)(2,1)} %slice.32), channel_id=1, source_target_pairs={{0,4},{4,12},{12,20},{20,28},{28,24},{24,16},{16,8},{8,0},{1,5},{5... | collective-permute-start | bytes 3538952 | tf_op jit(solution)/shard_map/ppermute | solution.py:141
  200.7 47.0 %collective-permute-start.8 = (bf16[768,6,128]{0,2,1:T(8,128)(2,1)S(1)}, bf16[768,6,128]{0,2,1:T(8,128)(2,1)}, u32[]{:S(2)}, u32[]{:S(2)}) collective-permute-start(bf16[768,6,128]{0,2,1:T(8,128)(2,1)S(1)} %bitcast.87), channel_id=1, source_target_pairs={{0,4},{4,12},{12,20},{20,28},{28,24},{24,16},{16,8},{8,0},{1,5},{5... | collective-permute-start | bytes 3538952 | tf_op jit(solution)/shard_map/ppermute | solution.py:133
  201.6 27.6 %collective-permute-start.9 = (bf16[768,6,128]{0,2,1:T(8,128)(2,1)S(1)}, bf16[768,6,128]{0,2,1:T(8,128)(2,1)}, u32[]{:S(2)}, u32[]{:S(2)}) collective-permute-start(bf16[768,6,128]{0,2,1:T(8,128)(2,1)S(1)} %bitcast.88), channel_id=1, source_target_pairs={{0,8},{4,0},{12,4},{20,12},{28,20},{24,28},{16,24},{8,16},{1,9},{5... | collective-permute-start | bytes 3538952 | tf_op jit(solution)/shard_map/ppermute | solution.py:134
  207.4 49.6 %collective-permute-start.16 = (bf16[384,2,6,128]{0,3,2,1:T(8,128)(2,1)S(1)}, bf16[384,2,6,128]{0,3,2,1:T(8,128)(2,1)S(1)}, u32[]{:S(2)}, u32[]{:S(2)}) collective-permute-start(bf16[384,2,6,128]{0,3,2,1:T(8,128)(2,1)S(1)} %bitcast.73), channel_id=1, source_target_pairs={{0,8},{4,12},{8,16},{12,20},{16,24},{20,28},{24,0},{28,4},{1,9},{5... | collective-permute-start | bytes 3538952 | tf_op jit(solution)/shard_map/ppermute | solution.py:106
  229.2 47.6 %collective-permute-start.11 = (bf16[768,6,128]{0,2,1:T(8,128)(2,1)}, bf16[768,6,128]{0,2,1:T(8,128)(2,1)}, u32[]{:S(2)}, u32[]{:S(2)}) collective-permute-start(bf16[768,6,128]{0,2,1:T(8,128)(2,1)} %collective-permute-done.9), channel_id=1, source_target_pairs={{0,8},{4,0},{12,4},{20,12},{28,20},{24,28},{16,24},{8,16},{1,9},{5... | collective-permute-start | bytes 3538952 | tf_op jit(solution)/shard_map/ppermute | solution.py:134
  247.8 31.5 %collective-permute-start.10 = (bf16[768,6,128]{0,2,1:T(8,128)(2,1)}, bf16[768,6,128]{0,2,1:T(8,128)(2,1)}, u32[]{:S(2)}, u32[]{:S(2)}) collective-permute-start(bf16[768,6,128]{0,2,1:T(8,128)(2,1)} %collective-permute-done.8), channel_id=1, source_target_pairs={{0,4},{4,12},{12,20},{20,28},{28,24},{24,16},{16,8},{8,0},{1,5},{5... | collective-permute-start | bytes 3538952 | tf_op jit(solution)/shard_map/ppermute | solution.py:133
  257.0 44.8 %collective-permute-start.18 = (bf16[384,2,6,128]{0,3,2,1:T(8,128)(2,1)S(1)}, bf16[384,2,6,128]{0,3,2,1:T(8,128)(2,1)S(1)}, u32[]{:S(2)}, u32[]{:S(2)}) collective-permute-start(bf16[384,2,6,128]{0,3,2,1:T(8,128)(2,1)S(1)} %collective-permute-done.16), channel_id=1, source_target_pairs={{4,0},{12,8},{20,16},{28,24},{5,1},{13,9},{21,17},{29,25},{6,2},{1... | collective-permute-start | bytes 3538952 | tf_op jit(solution)/shard_map/ppermute | solution.py:158
  260.0 88.8 %collective-permute-start.17 = (bf16[2,384,2,6,128]{1,4,3,2,0:T(8,128)(2,1)}, bf16[2,384,2,6,128]{1,4,3,2,0:T(8,128)(2,1)}, u32[]{:S(2)}, u32[]{:S(2)}) collective-permute-start(bf16[2,384,2,6,128]{1,4,3,2,0:T(8,128)(2,1)} %pad_maximum_fusion), channel_id=1, source_target_pairs={{0,4},{8,12},{16,20},{24,28},{1,5},{9,13},{17,21},{25,29},{2,6},{1... | collective-permute-start | bytes 7077896 | tf_op jit(solution)/shard_map/ppermute | solution.py:155
  276.8 71.1 %collective-permute-start.13 = (bf16[768,6,128]{0,2,1:T(8,128)(2,1)}, bf16[768,6,128]{0,2,1:T(8,128)(2,1)S(1)}, u32[]{:S(2)}, u32[]{:S(2)}) collective-permute-start(bf16[768,6,128]{0,2,1:T(8,128)(2,1)} %collective-permute-done.11), channel_id=1, source_target_pairs={{0,8},{4,0},{12,4},{20,12},{28,20},{24,28},{16,24},{8,16},{1,9},{5... | collective-permute-start | bytes 3538952 | tf_op jit(solution)/shard_map/ppermute | solution.py:134
  279.2 66.1 %collective-permute-start.12 = (bf16[768,6,128]{0,2,1:T(8,128)(2,1)}, bf16[768,6,128]{0,2,1:T(8,128)(2,1)S(1)}, u32[]{:S(2)}, u32[]{:S(2)}) collective-permute-start(bf16[768,6,128]{0,2,1:T(8,128)(2,1)} %collective-permute-done.10), channel_id=1, source_target_pairs={{0,4},{4,12},{12,20},{20,28},{28,24},{24,16},{16,8},{8,0},{1,5},{5... | collective-permute-start | bytes 3538952 | tf_op jit(solution)/shard_map/ppermute | solution.py:133
  301.8 46.9 %collective-permute-start.19 = (bf16[384,2,6,128]{0,3,2,1:T(8,128)(2,1)S(1)}, bf16[384,2,6,128]{0,3,2,1:T(8,128)(2,1)S(1)}, u32[]{:S(2)}, u32[]{:S(2)}) collective-permute-start(bf16[384,2,6,128]{0,3,2,1:T(8,128)(2,1)S(1)} %collective-permute-done.18), channel_id=1, source_target_pairs={{0,8},{8,16},{16,24},{24,0},{1,9},{9,17},{17,25},{25,1},{2,10},{10... | collective-permute-start | bytes 3538952 | tf_op jit(solution)/shard_map/ppermute | solution.py:159
  345.4 9.9 %collective-permute-start.14 = (bf16[384,6,128]{0,2,1:T(8,128)(2,1)S(1)}, bf16[384,6,128]{0,2,1:T(8,128)(2,1)S(1)}, u32[]{:S(2)}, u32[]{:S(2)}) collective-permute-start(bf16[384,6,128]{0,2,1:T(8,128)(2,1)S(1)} %slice.34), channel_id=1, source_target_pairs={{0,4},{4,12},{12,20},{20,28},{28,24},{24,16},{16,8},{8,0},{1,5},{5... | collective-permute-start | bytes 1769480 | tf_op jit(solution)/shard_map/ppermute | solution.py:141
  347.9 9.9 %collective-permute-start.15 = (bf16[384,6,128]{0,2,1:T(8,128)(2,1)S(1)}, bf16[384,6,128]{0,2,1:T(8,128)(2,1)S(1)}, u32[]{:S(2)}, u32[]{:S(2)}) collective-permute-start(bf16[384,6,128]{0,2,1:T(8,128)(2,1)S(1)} %slice.35), channel_id=1, source_target_pairs={{0,8},{4,0},{12,4},{20,12},{28,20},{24,28},{16,24},{8,16},{1,9},{5... | collective-permute-start | bytes 1769480 | tf_op jit(solution)/shard_map/ppermute | solution.py:142
  (10 other events, 215.0 us)
Sparse Core Ops, SparseCore 0:
  13.8 39.1 all-gather.1

commit v7 on v6

--- a/solution.py
+++ b/solution.py
@@ -15,11 +15,8 @@
     k_refs = refs[:reach]
     v_refs = refs[reach : 2 * reach]
     o_ref = refs[2 * reach]
-    q = q_ref[...]
-    scores = [
-        lax.dot_general(q, k_ref[...], (((0,), (0,)), ((), ())), preferred_element_type=jnp.float32) * scale
-        for k_ref in k_refs
-    ]
+    q = q_ref[...].T
+    scores = [jnp.dot(q, k_ref[...], preferred_element_type=jnp.float32) * scale for k_ref in k_refs]
     top = scores[0].max(axis=-1, keepdims=True)
     for s in scores[1:]:
         top = jnp.maximum(top, s.max(axis=-1, keepdims=True))

time: 377 us -> 377 us (level)
  no operation moved by 1% of the time
where the time goes in v7:
time: 377 us; the launch traced here: 376 us
  waiting for transfers between devices  260 us (69%)
  matrix products  36.5 us (10%)
  starting transfers between devices  31.7 us (8%)
  between operations  22.7 us (6%)
  local copies, waits for them, and re-layouts  10.5 us (3%)
  Pallas kernels  9.3 us (2%)
  other arithmetic  5.09 us (1%)
    ppermute x6, waiting for transfers between devices, ring_project(): going_ccw = lax.ppermute(going_ccw, 'ctx', counter)  168 us
    ppermute x6, waiting for transfers between devices, ring_project(): going_cw = lax.ppermute(going_cw, 'ctx', clockwise)  51.2 us
    dot_general x18, matrix products, partial(): return jnp.dot(cols, flat, preferred_element_type=jnp.float32)  36.5 us
    ppermute x1, waiting for transfers between devices, earlier_blocks(): lax.ppermute(two_back, 'ctx', [(o, o - 1) for o in range(1, n, 2)])  20.6 us
    ppermute x6, starting transfers between devices, ring_project(): going_ccw = lax.ppermute(going_ccw, 'ctx', counter)  12.5 us
    pallas_call x1, Pallas kernels, windowed_attention(): pl.pallas_call(functools.partial(attention_kernel, scale, reach), out_sha...  9.3 us
  transfers between devices with their start and end apart: 21, of which 13 were waited for; matrix products, arithmetic and copies ran while one was open for 12% of the time, Pallas kernels for 0%

profile of v7, /device:TPU:0, one launch (start us, length us, event | category | flops | bytes accessed | tf_op | source)
XLA Modules:
  0.0 376.3 jit_solution(14208627266058997627)
XLA Ops:
  10.6 3.0 collective-permute-start.4
  13.7 51.4 %collective-permute-done.4 = bf16[768,2,6,128]{0,3,2,1:T(8,128)(2,1)S(1)} collective-permute-done((bf16[768,2,6,128]{0,3,2,1:T(8,128)(2,1)}, bf16[768,2,6,128]{0,3,2,1:T(8,128)(2,1)S(1)}, u32[]{:S(2)}, u32[]{:S(2)}) %collective-permute-start.4) | collective-permute-done | bytes 2359328 | tf_op jit(solution)/shard_map/ppermute | solution.py:131
  67.1 50.6 %collective-permute-done.5 = bf16[768,2,6,128]{0,3,2,1:T(8,128)(2,1)} collective-permute-done((bf16[768,2,6,128]{0,3,2,1:T(8,128)(2,1)S(1)}, bf16[768,2,6,128]{0,3,2,1:T(8,128)(2,1)}, u32[]{:S(2)}, u32[]{:S(2)}) %collective-permute-start.5) | collective-permute-done | bytes 2359328 | tf_op jit(solution)/shard_map/ppermute | solution.py:131
  131.5 38.1 %collective-permute-done.6 = bf16[768,2,6,128]{0,3,2,1:T(8,128)(2,1)} collective-permute-done((bf16[768,2,6,128]{0,3,2,1:T(8,128)(2,1)}, bf16[768,2,6,128]{0,3,2,1:T(8,128)(2,1)}, u32[]{:S(2)}, u32[]{:S(2)}) %collective-permute-start.6) | collective-permute-done | bytes 2359328 | tf_op jit(solution)/shard_map/ppermute | solution.py:131
  169.6 2.4 slice.33
  175.3 3.4 fusion.29
  178.7 3.1 fusion.18
  181.8 3.1 convolution_add_fusion.3
  184.9 3.2 fusion.12
  189.7 3.3 fusion
  192.9 4.7 %collective-permute-done.7 = bf16[384,2,6,128]{0,3,2,1:T(8,128)(2,1)S(1)} collective-permute-done((bf16[384,2,6,128]{0,3,2,1:T(8,128)(2,1)}, bf16[384,2,6,128]{0,3,2,1:T(8,128)(2,1)S(1)}, u32[]{:S(2)}, u32[]{:S(2)}) %collective-permute-start.7) | collective-permute-done | bytes 1179680 | tf_op jit(solution)/shard_map/ppermute | solution.py:139
  197.7 3.0 collective-permute-done.3
  209.0 20.2 %collective-permute-done.9 = bf16[768,6,128]{0,2,1:T(8,128)(2,1)} collective-permute-done((bf16[768,6,128]{0,2,1:T(8,128)(2,1)S(1)}, bf16[768,6,128]{0,2,1:T(8,128)(2,1)}, u32[]{:S(2)}, u32[]{:S(2)}) %collective-permute-start.9) | collective-permute-done | bytes 1179680 | tf_op jit(solution)/shard_map/ppermute | solution.py:131
  229.2 2.6 collective-permute-start.11
  231.8 16.0 %collective-permute-done.8 = bf16[768,6,128]{0,2,1:T(8,128)(2,1)} collective-permute-done((bf16[768,6,128]{0,2,1:T(8,128)(2,1)S(1)}, bf16[768,6,128]{0,2,1:T(8,128)(2,1)}, u32[]{:S(2)}, u32[]{:S(2)}) %collective-permute-start.8) | collective-permute-done | bytes 1179680 | tf_op jit(solution)/shard_map/ppermute | solution.py:130
  249.7 7.2 %collective-permute-done.16 = bf16[384,2,6,128]{0,3,2,1:T(8,128)(2,1)S(1)} collective-permute-done((bf16[384,2,6,128]{0,3,2,1:T(8,128)(2,1)S(1)}, bf16[384,2,6,128]{0,3,2,1:T(8,128)(2,1)S(1)}, u32[]{:S(2)}, u32[]{:S(2)}) %collective-permute-start.16) | collective-permute-done | bytes 1179680 | tf_op jit(solution)/shard_map/ppermute | solution.py:103
  260.0 6.2 %collective-permute-start.17 = (bf16[2,384,2,6,128]{1,4,3,2,0:T(8,128)(2,1)}, bf16[2,384,2,6,128]{1,4,3,2,0:T(8,128)(2,1)}, u32[]{:S(2)}, u32[]{:S(2)}) collective-permute-start(bf16[2,384,2,6,128]{1,4,3,2,0:T(8,128)(2,1)} %pad_maximum_fusion), channel_id=1, source_target_pairs={{0,4},{8,12},{16,20},{24,28},{1,5},{9,13},{17,21},{25,29},{2,6},{1... | collective-permute-start | bytes 7077896 | tf_op jit(solution)/shard_map/ppermute | solution.py:152
  268.6 8.2 %collective-permute-done.11 = bf16[768,6,128]{0,2,1:T(8,128)(2,1)} collective-permute-done((bf16[768,6,128]{0,2,1:T(8,128)(2,1)}, bf16[768,6,128]{0,2,1:T(8,128)(2,1)}, u32[]{:S(2)}, u32[]{:S(2)}) %collective-permute-start.11) | collective-permute-done | bytes 1179680 | tf_op jit(solution)/shard_map/ppermute | solution.py:131
  276.8 2.5 collective-permute-start.13
  281.2 20.6 %collective-permute-done.18 = bf16[384,2,6,128]{0,3,2,1:T(8,128)(2,1)S(1)} collective-permute-done((bf16[384,2,6,128]{0,3,2,1:T(8,128)(2,1)S(1)}, bf16[384,2,6,128]{0,3,2,1:T(8,128)(2,1)S(1)}, u32[]{:S(2)}, u32[]{:S(2)}) %collective-permute-start.18) | collective-permute-done | bytes 1179680 | tf_op jit(solution)/shard_map/ppermute | solution.py:155
  310.2 35.2 %collective-permute-done.12 = bf16[768,6,128]{0,2,1:T(8,128)(2,1)S(1)} collective-permute-done((bf16[768,6,128]{0,2,1:T(8,128)(2,1)}, bf16[768,6,128]{0,2,1:T(8,128)(2,1)S(1)}, u32[]{:S(2)}, u32[]{:S(2)}) %collective-permute-start.12) | collective-permute-done | bytes 1179680 | tf_op jit(solution)/shard_map/ppermute | solution.py:130
  348.8 3.4 fusion.10
  352.1 3.2 collective-permute-done.14
  360.1 9.3 %shard_map.46 = bf16[6,384,128]{2,1,0:T(8,128)(2,1)} custom-call(bf16[768,384]{1,0:T(8,128)(2,1)} %fusion.9.q_ref, bf16[1536,384]{1,0:T(8,128)(2,1)} %bitcast.75, bf16[1536,384]{1,0:T(8,128)(2,1)} %bitcast.81, bf16[1536,384]{1,0:T(8,128)(2,1)} %bitcast.84, bf16[1536,384]{1,0:T(8,128)(2,1)} %bitcast.79, bf16[1536,384]{1,0:T(8,128)(2,1)} %bitcast.76, ...), custom_call_target="tpu_custom_call" | custom-call | flops 1811939328 | bytes 5898240 | tf_op jit(solution)/shard_map/pallas_call | solution.py:49
  (75 shorter events, 49.6 us)
Async XLA Ops:
  6.5 168.7 %all-gather.2.cloned.1.call-start = ((), (), s32[]{:S(2)}) async-start(), calls=%async_computation | async-start | bytes 5898240 | tf_op jit(solution)/shard_map/all_gather | solution.py:163
  8.2 111.5 %copy-start.8 = (s32[8]{0:T(128)S(1)}, s32[8]{0:T(128)}, u32[]{:S(2)}) copy-start(s32[8]{0:T(128)} %constant.108.clone) | copy-start | bytes 100
  8.2 116.8 %copy-start.7 = (s32[8]{0:T(128)S(1)}, s32[8]{0:T(128)}, u32[]{:S(2)}) copy-start(s32[8]{0:T(128)} %constant.109.clone) | copy-start | bytes 100
  10.6 119.5 %slice-start.3 = ((bf16[768,3,6,128]{3,0,2,1:T(8,128)(2,1)}), bf16[768,1,6,128]{3,0,2,1:T(8,128)(2,1)S(1)}, s32[]{:S(2)}) async-start(bf16[768,3,6,128]{3,0,2,1:T(8,128)(2,1)} %param.5), calls=%async_computation.4 | async-start | bytes 2359296 | tf_op jit(solution)/shard_map/slice | solution.py:173
  10.6 54.4 %collective-permute-start.4 = (bf16[768,2,6,128]{0,3,2,1:T(8,128)(2,1)}, bf16[768,2,6,128]{0,3,2,1:T(8,128)(2,1)S(1)}, u32[]{:S(2)}, u32[]{:S(2)}) collective-permute-start(bf16[768,2,6,128]{0,3,2,1:T(8,128)(2,1)} %copy.35), channel_id=1, source_target_pairs={{0,8},{4,0},{12,4},{20,12},{28,20},{24,28},{16,24},{8,16},{1,9},{5... | collective-permute-start | bytes 7077896 | tf_op jit(solution)/shard_map/ppermute | solution.py:131
  13.6 53.2 %collective-permute-start = (bf16[768,2,6,128]{0,3,2,1:T(8,128)(2,1)}, bf16[768,2,6,128]{0,3,2,1:T(8,128)(2,1)}, u32[]{:S(2)}, u32[]{:S(2)}) collective-permute-start(bf16[768,2,6,128]{0,3,2,1:T(8,128)(2,1)} %copy.35), channel_id=1, source_target_pairs={{0,4},{4,12},{12,20},{20,28},{28,24},{24,16},{16,8},{8,0},{1,5},{5... | collective-permute-start | bytes 7077896 | tf_op jit(solution)/shard_map/ppermute | solution.py:130
  65.0 52.6 %collective-permute-start.5 = (bf16[768,2,6,128]{0,3,2,1:T(8,128)(2,1)S(1)}, bf16[768,2,6,128]{0,3,2,1:T(8,128)(2,1)}, u32[]{:S(2)}, u32[]{:S(2)}) collective-permute-start(bf16[768,2,6,128]{0,3,2,1:T(8,128)(2,1)S(1)} %collective-permute-done.4), channel_id=1, source_target_pairs={{0,8},{4,0},{12,4},{20,12},{28,20},{24,28},{16,24},{8,16},{1,9},{5... | collective-permute-start | bytes 7077896 | tf_op jit(solution)/shard_map/ppermute | solution.py:131
  66.8 52.3 %collective-permute-start.1 = (bf16[768,2,6,128]{0,3,2,1:T(8,128)(2,1)}, bf16[768,2,6,128]{0,3,2,1:T(8,128)(2,1)}, u32[]{:S(2)}, u32[]{:S(2)}) collective-permute-start(bf16[768,2,6,128]{0,3,2,1:T(8,128)(2,1)} %collective-permute-done), channel_id=1, source_target_pairs={{0,4},{4,12},{12,20},{20,28},{28,24},{24,16},{16,8},{8,0},{1,5},{5... | collective-permute-start | bytes 7077896 | tf_op jit(solution)/shard_map/ppermute | solution.py:130
  117.7 51.9 %collective-permute-start.6 = (bf16[768,2,6,128]{0,3,2,1:T(8,128)(2,1)}, bf16[768,2,6,128]{0,3,2,1:T(8,128)(2,1)}, u32[]{:S(2)}, u32[]{:S(2)}) collective-permute-start(bf16[768,2,6,128]{0,3,2,1:T(8,128)(2,1)} %collective-permute-done.5), channel_id=1, source_target_pairs={{0,8},{4,0},{12,4},{20,12},{28,20},{24,28},{16,24},{8,16},{1,9},{5... | collective-permute-start | bytes 7077896 | tf_op jit(solution)/shard_map/ppermute | solution.py:131
  119.2 54.0 %collective-permute-start.2 = (bf16[768,2,6,128]{0,3,2,1:T(8,128)(2,1)}, bf16[768,2,6,128]{0,3,2,1:T(8,128)(2,1)S(1)}, u32[]{:S(2)}, u32[]{:S(2)}) collective-permute-start(bf16[768,2,6,128]{0,3,2,1:T(8,128)(2,1)} %collective-permute-done.1), channel_id=1, source_target_pairs={{0,4},{4,12},{12,20},{20,28},{28,24},{24,16},{16,8},{8,0},{1,5},{5... | collective-permute-start | bytes 7077896 | tf_op jit(solution)/shard_map/ppermute | solution.py:130
  172.1 25.6 %collective-permute-start.7 = (bf16[384,2,6,128]{0,3,2,1:T(8,128)(2,1)}, bf16[384,2,6,128]{0,3,2,1:T(8,128)(2,1)S(1)}, u32[]{:S(2)}, u32[]{:S(2)}) collective-permute-start(bf16[384,2,6,128]{0,3,2,1:T(8,128)(2,1)} %slice.33), channel_id=1, source_target_pairs={{0,8},{4,0},{12,4},{20,12},{28,20},{24,28},{16,24},{8,16},{1,9},{5... | collective-permute-start | bytes 3538952 | tf_op jit(solution)/shard_map/ppermute | solution.py:139
  174.4 26.3 %collective-permute-start.3 = (bf16[384,2,6,128]{0,3,2,1:T(8,128)(2,1)}, bf16[384,2,6,128]{0,3,2,1:T(8,128)(2,1)}, u32[]{:S(2)}, u32[]{:S(2)}) collective-permute-start(bf16[384,2,6,128]{0,3,2,1:T(8,128)(2,1)} %slice.32), channel_id=1, source_target_pairs={{0,4},{4,12},{12,20},{20,28},{28,24},{24,16},{16,8},{8,0},{1,5},{5... | collective-permute-start | bytes 3538952 | tf_op jit(solution)/shard_map/ppermute | solution.py:138
  200.7 47.0 %collective-permute-start.8 = (bf16[768,6,128]{0,2,1:T(8,128)(2,1)S(1)}, bf16[768,6,128]{0,2,1:T(8,128)(2,1)}, u32[]{:S(2)}, u32[]{:S(2)}) collective-permute-start(bf16[768,6,128]{0,2,1:T(8,128)(2,1)S(1)} %bitcast.87), channel_id=1, source_target_pairs={{0,4},{4,12},{12,20},{20,28},{28,24},{24,16},{16,8},{8,0},{1,5},{5... | collective-permute-start | bytes 3538952 | tf_op jit(solution)/shard_map/ppermute | solution.py:130
  201.6 27.6 %collective-permute-start.9 = (bf16[768,6,128]{0,2,1:T(8,128)(2,1)S(1)}, bf16[768,6,128]{0,2,1:T(8,128)(2,1)}, u32[]{:S(2)}, u32[]{:S(2)}) collective-permute-start(bf16[768,6,128]{0,2,1:T(8,128)(2,1)S(1)} %bitcast.88), channel_id=1, source_target_pairs={{0,8},{4,0},{12,4},{20,12},{28,20},{24,28},{16,24},{8,16},{1,9},{5... | collective-permute-start | bytes 3538952 | tf_op jit(solution)/shard_map/ppermute | solution.py:131
  207.4 49.6 %collective-permute-start.16 = (bf16[384,2,6,128]{0,3,2,1:T(8,128)(2,1)S(1)}, bf16[384,2,6,128]{0,3,2,1:T(8,128)(2,1)S(1)}, u32[]{:S(2)}, u32[]{:S(2)}) collective-permute-start(bf16[384,2,6,128]{0,3,2,1:T(8,128)(2,1)S(1)} %bitcast.73), channel_id=1, source_target_pairs={{0,8},{4,12},{8,16},{12,20},{16,24},{20,28},{24,0},{28,4},{1,9},{5... | collective-permute-start | bytes 3538952 | tf_op jit(solution)/shard_map/ppermute | solution.py:103
  229.2 47.6 %collective-permute-start.11 = (bf16[768,6,128]{0,2,1:T(8,128)(2,1)}, bf16[768,6,128]{0,2,1:T(8,128)(2,1)}, u32[]{:S(2)}, u32[]{:S(2)}) collective-permute-start(bf16[768,6,128]{0,2,1:T(8,128)(2,1)} %collective-permute-done.9), channel_id=1, source_target_pairs={{0,8},{4,0},{12,4},{20,12},{28,20},{24,28},{16,24},{8,16},{1,9},{5... | collective-permute-start | bytes 3538952 | tf_op jit(solution)/shard_map/ppermute | solution.py:131
  247.8 31.5 %collective-permute-start.10 = (bf16[768,6,128]{0,2,1:T(8,128)(2,1)}, bf16[768,6,128]{0,2,1:T(8,128)(2,1)}, u32[]{:S(2)}, u32[]{:S(2)}) collective-permute-start(bf16[768,6,128]{0,2,1:T(8,128)(2,1)} %collective-permute-done.8), channel_id=1, source_target_pairs={{0,4},{4,12},{12,20},{20,28},{28,24},{24,16},{16,8},{8,0},{1,5},{5... | collective-permute-start | bytes 3538952 | tf_op jit(solution)/shard_map/ppermute | solution.py:130
  257.0 44.8 %collective-permute-start.18 = (bf16[384,2,6,128]{0,3,2,1:T(8,128)(2,1)S(1)}, bf16[384,2,6,128]{0,3,2,1:T(8,128)(2,1)S(1)}, u32[]{:S(2)}, u32[]{:S(2)}) collective-permute-start(bf16[384,2,6,128]{0,3,2,1:T(8,128)(2,1)S(1)} %collective-permute-done.16), channel_id=1, source_target_pairs={{4,0},{12,8},{20,16},{28,24},{5,1},{13,9},{21,17},{29,25},{6,2},{1... | collective-permute-start | bytes 3538952 | tf_op jit(solution)/shard_map/ppermute | solution.py:155
  260.0 88.8 %collective-permute-start.17 = (bf16[2,384,2,6,128]{1,4,3,2,0:T(8,128)(2,1)}, bf16[2,384,2,6,128]{1,4,3,2,0:T(8,128)(2,1)}, u32[]{:S(2)}, u32[]{:S(2)}) collective-permute-start(bf16[2,384,2,6,128]{1,4,3,2,0:T(8,128)(2,1)} %pad_maximum_fusion), channel_id=1, source_target_pairs={{0,4},{8,12},{16,20},{24,28},{1,5},{9,13},{17,21},{25,29},{2,6},{1... | collective-permute-start | bytes 7077896 | tf_op jit(solution)/shard_map/ppermute | solution.py:152
  276.8 71.1 %collective-permute-start.13 = (bf16[768,6,128]{0,2,1:T(8,128)(2,1)}, bf16[768,6,128]{0,2,1:T(8,128)(2,1)S(1)}, u32[]{:S(2)}, u32[]{:S(2)}) collective-permute-start(bf16[768,6,128]{0,2,1:T(8,128)(2,1)} %collective-permute-done.11), channel_id=1, source_target_pairs={{0,8},{4,0},{12,4},{20,12},{28,20},{24,28},{16,24},{8,16},{1,9},{5... | collective-permute-start | bytes 3538952 | tf_op jit(solution)/shard_map/ppermute | solution.py:131
  279.2 66.1 %collective-permute-start.12 = (bf16[768,6,128]{0,2,1:T(8,128)(2,1)}, bf16[768,6,128]{0,2,1:T(8,128)(2,1)S(1)}, u32[]{:S(2)}, u32[]{:S(2)}) collective-permute-start(bf16[768,6,128]{0,2,1:T(8,128)(2,1)} %collective-permute-done.10), channel_id=1, source_target_pairs={{0,4},{4,12},{12,20},{20,28},{28,24},{24,16},{16,8},{8,0},{1,5},{5... | collective-permute-start | bytes 3538952 | tf_op jit(solution)/shard_map/ppermute | solution.py:130
  301.8 46.9 %collective-permute-start.19 = (bf16[384,2,6,128]{0,3,2,1:T(8,128)(2,1)S(1)}, bf16[384,2,6,128]{0,3,2,1:T(8,128)(2,1)S(1)}, u32[]{:S(2)}, u32[]{:S(2)}) collective-permute-start(bf16[384,2,6,128]{0,3,2,1:T(8,128)(2,1)S(1)} %collective-permute-done.18), channel_id=1, source_target_pairs={{0,8},{8,16},{16,24},{24,0},{1,9},{9,17},{17,25},{25,1},{2,10},{10... | collective-permute-start | bytes 3538952 | tf_op jit(solution)/shard_map/ppermute | solution.py:156
  345.4 9.9 %collective-permute-start.14 = (bf16[384,6,128]{0,2,1:T(8,128)(2,1)S(1)}, bf16[384,6,128]{0,2,1:T(8,128)(2,1)S(1)}, u32[]{:S(2)}, u32[]{:S(2)}) collective-permute-start(bf16[384,6,128]{0,2,1:T(8,128)(2,1)S(1)} %slice.34), channel_id=1, source_target_pairs={{0,4},{4,12},{12,20},{20,28},{28,24},{24,16},{16,8},{8,0},{1,5},{5... | collective-permute-start | bytes 1769480 | tf_op jit(solution)/shard_map/ppermute | solution.py:138
  347.9 9.9 %collective-permute-start.15 = (bf16[384,6,128]{0,2,1:T(8,128)(2,1)S(1)}, bf16[384,6,128]{0,2,1:T(8,128)(2,1)S(1)}, u32[]{:S(2)}, u32[]{:S(2)}) collective-permute-start(bf16[384,6,128]{0,2,1:T(8,128)(2,1)S(1)} %slice.35), channel_id=1, source_target_pairs={{0,8},{4,0},{12,4},{20,12},{28,20},{24,28},{16,24},{8,16},{1,9},{5... | collective-permute-start | bytes 1769480 | tf_op jit(solution)/shard_map/ppermute | solution.py:139
  (10 other events, 215.0 us)
Sparse Core Ops, SparseCore 0:
  13.8 39.1 all-gather.1

commit v8 on v7

--- a/solution.py
+++ b/solution.py
@@ -149,14 +149,14 @@
         if n % 2 or n < 4 or REACH != 4:
             return [shifted(key_value, "ctx", by) for by in range(1, REACH)]
         two_back = shifted(key_value, "ctx", 2)
-        to_odd = lax.ppermute(
-            jnp.stack([key_value, two_back]), "ctx", [(e, e + 1) for e in range(0, n, 2)]
-        )
+        evens_up = [(e, e + 1) for e in range(0, n, 2)]
+        own_up = lax.ppermute(key_value, "ctx", evens_up)
+        two_back_up = lax.ppermute(two_back, "ctx", evens_up)
         to_even = lax.ppermute(two_back, "ctx", [(o, o - 1) for o in range(1, n, 2)])
         three_back = lax.ppermute(to_even, "ctx", [(e, (e + 2) % n) for e in range(0, n, 2)])
         odd = (me % 2) == 1
-        one_back = jnp.where(odd, to_odd[0], to_even)
-        three_back = jnp.where(odd, to_odd[1], three_back)
+        one_back = jnp.where(odd, own_up, to_even)
+        three_back = jnp.where(odd, two_back_up, three_back)
         return [one_back, two_back, three_back]
 
     def on_device(tokens, qkv_weight):

time: 377 us -> 378 us (level)
  transfers between devices with their start and end apart: 21 -> 22, of which waited for: 13 -> 13; matrix products, arithmetic and copies ran while one was open for 12% -> 12% of each run, Pallas kernels for 0% -> 0%
where the time goes in v8:
time: 378 us; the launch traced here: 377 us
  waiting for transfers between devices  261 us (69%)
  matrix products  36.5 us (10%)
  starting transfers between devices  32.5 us (9%)
  between operations  22.8 us (6%)
  local copies, waits for them, and re-layouts  10.5 us (3%)
  Pallas kernels  9.3 us (2%)
    ppermute x6, waiting for transfers between devices, ring_project(): going_ccw = lax.ppermute(going_ccw, 'ctx', counter)  167 us
    ppermute x6, waiting for transfers between devices, ring_project(): going_cw = lax.ppermute(going_cw, 'ctx', clockwise)  51.3 us
    dot_general x18, matrix products, partial(): return jnp.dot(cols, flat, preferred_element_type=jnp.float32)  36.5 us
    ppermute x1, waiting for transfers between devices, earlier_blocks(): lax.ppermute(two_back, 'ctx', [(o, o - 1) for o in range(1, n, 2)])  20.4 us
    ppermute x6, starting transfers between devices, ring_project(): going_ccw = lax.ppermute(going_ccw, 'ctx', counter)  12.5 us
    pallas_call x1, Pallas kernels, windowed_attention(): pl.pallas_call(functools.partial(attention_kernel, scale, reach), out_sha...  9.3 us
    ppermute x2, waiting for transfers between devices, ring_project(): last_cw = lax.ppermute(going_cw[:half], 'ctx', clockwise)  8.32 us
  transfers between devices with their start and end apart: 22, of which 13 were waited for; matrix products, arithmetic and copies ran while one was open for 12% of the time, Pallas kernels for 0%

profile of v8, /device:TPU:0, one launch (start us, length us, event | category | flops | bytes accessed | tf_op | source)
XLA Modules:
  0.0 376.8 jit_solution(36046691041028759)
XLA Ops:
  10.6 3.0 collective-permute-start.4
  13.7 51.4 %collective-permute-done.4 = bf16[768,2,6,128]{0,3,2,1:T(8,128)(2,1)S(1)} collective-permute-done((bf16[768,2,6,128]{0,3,2,1:T(8,128)(2,1)}, bf16[768,2,6,128]{0,3,2,1:T(8,128)(2,1)S(1)}, u32[]{:S(2)}, u32[]{:S(2)}) %collective-permute-start.4) | collective-permute-done | bytes 2359328 | tf_op jit(solution)/shard_map/ppermute | solution.py:131
  67.1 50.6 %collective-permute-done.5 = bf16[768,2,6,128]{0,3,2,1:T(8,128)(2,1)} collective-permute-done((bf16[768,2,6,128]{0,3,2,1:T(8,128)(2,1)S(1)}, bf16[768,2,6,128]{0,3,2,1:T(8,128)(2,1)}, u32[]{:S(2)}, u32[]{:S(2)}) %collective-permute-start.5) | collective-permute-done | bytes 2359328 | tf_op jit(solution)/shard_map/ppermute | solution.py:131
  131.5 38.1 %collective-permute-done.6 = bf16[768,2,6,128]{0,3,2,1:T(8,128)(2,1)} collective-permute-done((bf16[768,2,6,128]{0,3,2,1:T(8,128)(2,1)}, bf16[768,2,6,128]{0,3,2,1:T(8,128)(2,1)}, u32[]{:S(2)}, u32[]{:S(2)}) %collective-permute-start.6) | collective-permute-done | bytes 2359328 | tf_op jit(solution)/shard_map/ppermute | solution.py:131
  169.6 2.4 slice.25
  175.3 3.4 fusion.27
  178.7 3.1 fusion.16
  181.8 3.1 convolution_add_fusion.3
  184.9 3.2 fusion.10
  189.7 3.3 fusion
  192.9 4.7 %collective-permute-done.7 = bf16[384,2,6,128]{0,3,2,1:T(8,128)(2,1)S(1)} collective-permute-done((bf16[384,2,6,128]{0,3,2,1:T(8,128)(2,1)}, bf16[384,2,6,128]{0,3,2,1:T(8,128)(2,1)S(1)}, u32[]{:S(2)}, u32[]{:S(2)}) %collective-permute-start.7) | collective-permute-done | bytes 1179680 | tf_op jit(solution)/shard_map/ppermute | solution.py:139
  197.7 3.0 collective-permute-done.3
  209.0 20.2 %collective-permute-done.9 = bf16[768,6,128]{0,2,1:T(8,128)(2,1)} collective-permute-done((bf16[768,6,128]{0,2,1:T(8,128)(2,1)S(1)}, bf16[768,6,128]{0,2,1:T(8,128)(2,1)}, u32[]{:S(2)}, u32[]{:S(2)}) %collective-permute-start.9) | collective-permute-done | bytes 1179680 | tf_op jit(solution)/shard_map/ppermute | solution.py:131
  229.2 2.6 collective-permute-start.11
  231.8 16.0 %collective-permute-done.8 = bf16[768,6,128]{0,2,1:T(8,128)(2,1)} collective-permute-done((bf16[768,6,128]{0,2,1:T(8,128)(2,1)S(1)}, bf16[768,6,128]{0,2,1:T(8,128)(2,1)}, u32[]{:S(2)}, u32[]{:S(2)}) %collective-permute-start.8) | collective-permute-done | bytes 1179680 | tf_op jit(solution)/shard_map/ppermute | solution.py:130
  249.7 7.2 %collective-permute-done.17 = bf16[384,2,6,128]{0,3,2,1:T(8,128)(2,1)S(1)} collective-permute-done((bf16[384,2,6,128]{0,3,2,1:T(8,128)(2,1)S(1)}, bf16[384,2,6,128]{0,3,2,1:T(8,128)(2,1)S(1)}, u32[]{:S(2)}, u32[]{:S(2)}) %collective-permute-start.17) | collective-permute-done | bytes 1179680 | tf_op jit(solution)/shard_map/ppermute | solution.py:103
  258.3 5.7 %collective-permute-start.16 = (bf16[384,2,6,128]{0,3,2,1:T(8,128)(2,1)S(1)}, bf16[384,2,6,128]{0,3,2,1:T(8,128)(2,1)S(1)}, u32[]{:S(2)}, u32[]{:S(2)}) collective-permute-start(bf16[384,2,6,128]{0,3,2,1:T(8,128)(2,1)S(1)} %bitcast.66), channel_id=1, source_target_pairs={{0,4},{8,12},{16,20},{24,28},{1,5},{9,13},{17,21},{25,29},{2,6},{1... | collective-permute-start | bytes 3538952 | tf_op jit(solution)/shard_map/ppermute | solution.py:153
  269.7 7.1 %collective-permute-done.11 = bf16[768,6,128]{0,2,1:T(8,128)(2,1)} collective-permute-done((bf16[768,6,128]{0,2,1:T(8,128)(2,1)}, bf16[768,6,128]{0,2,1:T(8,128)(2,1)}, u32[]{:S(2)}, u32[]{:S(2)}) %collective-permute-start.11) | collective-permute-done | bytes 1179680 | tf_op jit(solution)/shard_map/ppermute | solution.py:131
  276.8 2.5 collective-permute-start.13
  281.5 20.4 %collective-permute-done.18 = bf16[384,2,6,128]{0,3,2,1:T(8,128)(2,1)} collective-permute-done((bf16[384,2,6,128]{0,3,2,1:T(8,128)(2,1)S(1)}, bf16[384,2,6,128]{0,3,2,1:T(8,128)(2,1)}, u32[]{:S(2)}, u32[]{:S(2)}) %collective-permute-start.18) | collective-permute-done | bytes 1179680 | tf_op jit(solution)/shard_map/ppermute | solution.py:155
  306.0 2.5 broadcast_select_fusion.1
  310.6 35.3 %collective-permute-done.12 = bf16[768,6,128]{0,2,1:T(8,128)(2,1)S(1)} collective-permute-done((bf16[768,6,128]{0,2,1:T(8,128)(2,1)}, bf16[768,6,128]{0,2,1:T(8,128)(2,1)S(1)}, u32[]{:S(2)}, u32[]{:S(2)}) %collective-permute-start.12) | collective-permute-done | bytes 1179680 | tf_op jit(solution)/shard_map/ppermute | solution.py:130
  350.7 5.3 %collective-permute-done.14 = bf16[384,6,128]{0,2,1:T(8,128)(2,1)S(1)} collective-permute-done((bf16[384,6,128]{0,2,1:T(8,128)(2,1)S(1)}, bf16[384,6,128]{0,2,1:T(8,128)(2,1)S(1)}, u32[]{:S(2)}, u32[]{:S(2)}) %collective-permute-start.14) | collective-permute-done | bytes 589856 | tf_op jit(solution)/shard_map/ppermute | solution.py:138
  360.7 9.3 %shard_map.46 = bf16[6,384,128]{2,1,0:T(8,128)(2,1)} custom-call(bf16[768,384]{1,0:T(8,128)(2,1)} %fusion.9.q_ref, bf16[1536,384]{1,0:T(8,128)(2,1)} %bitcast.67, bf16[1536,384]{1,0:T(8,128)(2,1)} %bitcast.69, bf16[1536,384]{1,0:T(8,128)(2,1)} %bitcast.77, bf16[1536,384]{1,0:T(8,128)(2,1)} %bitcast.71, bf16[1536,384]{1,0:T(8,128)(2,1)} %bitcast.68, ...), custom_call_target="tpu_custom_call" | custom-call | flops 1811939328 | bytes 5898240 | tf_op jit(solution)/shard_map/pallas_call | solution.py:49
  (77 shorter events, 50.4 us)
Async XLA Ops:
  6.5 168.7 %all-gather.2.cloned.1.call-start = ((), (), s32[]{:S(2)}) async-start(), calls=%async_computation | async-start | bytes 5898240 | tf_op jit(solution)/shard_map/all_gather | solution.py:163
  8.2 116.8 %copy-start.7 = (s32[8]{0:T(128)S(1)}, s32[8]{0:T(128)}, u32[]{:S(2)}) copy-start(s32[8]{0:T(128)} %constant.109.clone) | copy-start | bytes 100
  10.6 119.5 %slice-start.3 = ((bf16[768,3,6,128]{3,0,2,1:T(8,128)(2,1)}), bf16[768,1,6,128]{3,0,2,1:T(8,128)(2,1)S(1)}, s32[]{:S(2)}) async-start(bf16[768,3,6,128]{3,0,2,1:T(8,128)(2,1)} %param.5), calls=%async_computation.4 | async-start | bytes 2359296 | tf_op jit(solution)/shard_map/slice | solution.py:173
  10.6 54.4 %collective-permute-start.4 = (bf16[768,2,6,128]{0,3,2,1:T(8,128)(2,1)}, bf16[768,2,6,128]{0,3,2,1:T(8,128)(2,1)S(1)}, u32[]{:S(2)}, u32[]{:S(2)}) collective-permute-start(bf16[768,2,6,128]{0,3,2,1:T(8,128)(2,1)} %copy.35), channel_id=1, source_target_pairs={{0,8},{4,0},{12,4},{20,12},{28,20},{24,28},{16,24},{8,16},{1,9},{5... | collective-permute-start | bytes 7077896 | tf_op jit(solution)/shard_map/ppermute | solution.py:131
  13.6 53.2 %collective-permute-start = (bf16[768,2,6,128]{0,3,2,1:T(8,128)(2,1)}, bf16[768,2,6,128]{0,3,2,1:T(8,128)(2,1)}, u32[]{:S(2)}, u32[]{:S(2)}) collective-permute-start(bf16[768,2,6,128]{0,3,2,1:T(8,128)(2,1)} %copy.35), channel_id=1, source_target_pairs={{0,4},{4,12},{12,20},{20,28},{28,24},{24,16},{16,8},{8,0},{1,5},{5... | collective-permute-start | bytes 7077896 | tf_op jit(solution)/shard_map/ppermute | solution.py:130
  65.0 52.6 %collective-permute-start.5 = (bf16[768,2,6,128]{0,3,2,1:T(8,128)(2,1)S(1)}, bf16[768,2,6,128]{0,3,2,1:T(8,128)(2,1)}, u32[]{:S(2)}, u32[]{:S(2)}) collective-permute-start(bf16[768,2,6,128]{0,3,2,1:T(8,128)(2,1)S(1)} %collective-permute-done.4), channel_id=1, source_target_pairs={{0,8},{4,0},{12,4},{20,12},{28,20},{24,28},{16,24},{8,16},{1,9},{5... | collective-permute-start | bytes 7077896 | tf_op jit(solution)/shard_map/ppermute | solution.py:131
  66.8 52.3 %collective-permute-start.1 = (bf16[768,2,6,128]{0,3,2,1:T(8,128)(2,1)}, bf16[768,2,6,128]{0,3,2,1:T(8,128)(2,1)}, u32[]{:S(2)}, u32[]{:S(2)}) collective-permute-start(bf16[768,2,6,128]{0,3,2,1:T(8,128)(2,1)} %collective-permute-done), channel_id=1, source_target_pairs={{0,4},{4,12},{12,20},{20,28},{28,24},{24,16},{16,8},{8,0},{1,5},{5... | collective-permute-start | bytes 7077896 | tf_op jit(solution)/shard_map/ppermute | solution.py:130
  117.7 51.9 %collective-permute-start.6 = (bf16[768,2,6,128]{0,3,2,1:T(8,128)(2,1)}, bf16[768,2,6,128]{0,3,2,1:T(8,128)(2,1)}, u32[]{:S(2)}, u32[]{:S(2)}) collective-permute-start(bf16[768,2,6,128]{0,3,2,1:T(8,128)(2,1)} %collective-permute-done.5), channel_id=1, source_target_pairs={{0,8},{4,0},{12,4},{20,12},{28,20},{24,28},{16,24},{8,16},{1,9},{5... | collective-permute-start | bytes 7077896 | tf_op jit(solution)/shard_map/ppermute | solution.py:131
  119.2 54.0 %collective-permute-start.2 = (bf16[768,2,6,128]{0,3,2,1:T(8,128)(2,1)}, bf16[768,2,6,128]{0,3,2,1:T(8,128)(2,1)S(1)}, u32[]{:S(2)}, u32[]{:S(2)}) collective-permute-start(bf16[768,2,6,128]{0,3,2,1:T(8,128)(2,1)} %collective-permute-done.1), channel_id=1, source_target_pairs={{0,4},{4,12},{12,20},{20,28},{28,24},{24,16},{16,8},{8,0},{1,5},{5... | collective-permute-start | bytes 7077896 | tf_op jit(solution)/shard_map/ppermute | solution.py:130
  172.1 25.6 %collective-permute-start.7 = (bf16[384,2,6,128]{0,3,2,1:T(8,128)(2,1)}, bf16[384,2,6,128]{0,3,2,1:T(8,128)(2,1)S(1)}, u32[]{:S(2)}, u32[]{:S(2)}) collective-permute-start(bf16[384,2,6,128]{0,3,2,1:T(8,128)(2,1)} %slice.25), channel_id=1, source_target_pairs={{0,8},{4,0},{12,4},{20,12},{28,20},{24,28},{16,24},{8,16},{1,9},{5... | collective-permute-start | bytes 3538952 | tf_op jit(solution)/shard_map/ppermute | solution.py:139
  174.4 26.3 %collective-permute-start.3 = (bf16[384,2,6,128]{0,3,2,1:T(8,128)(2,1)}, bf16[384,2,6,128]{0,3,2,1:T(8,128)(2,1)}, u32[]{:S(2)}, u32[]{:S(2)}) collective-permute-start(bf16[384,2,6,128]{0,3,2,1:T(8,128)(2,1)} %slice.24), channel_id=1, source_target_pairs={{0,4},{4,12},{12,20},{20,28},{28,24},{24,16},{16,8},{8,0},{1,5},{5... | collective-permute-start | bytes 3538952 | tf_op jit(solution)/shard_map/ppermute | solution.py:138
  200.7 47.0 %collective-permute-start.8 = (bf16[768,6,128]{0,2,1:T(8,128)(2,1)S(1)}, bf16[768,6,128]{0,2,1:T(8,128)(2,1)}, u32[]{:S(2)}, u32[]{:S(2)}) collective-permute-start(bf16[768,6,128]{0,2,1:T(8,128)(2,1)S(1)} %bitcast.74), channel_id=1, source_target_pairs={{0,4},{4,12},{12,20},{20,28},{28,24},{24,16},{16,8},{8,0},{1,5},{5... | collective-permute-start | bytes 3538952 | tf_op jit(solution)/shard_map/ppermute | solution.py:130
  201.6 27.6 %collective-permute-start.9 = (bf16[768,6,128]{0,2,1:T(8,128)(2,1)S(1)}, bf16[768,6,128]{0,2,1:T(8,128)(2,1)}, u32[]{:S(2)}, u32[]{:S(2)}) collective-permute-start(bf16[768,6,128]{0,2,1:T(8,128)(2,1)S(1)} %bitcast.75), channel_id=1, source_target_pairs={{0,8},{4,0},{12,4},{20,12},{28,20},{24,28},{16,24},{8,16},{1,9},{5... | collective-permute-start | bytes 3538952 | tf_op jit(solution)/shard_map/ppermute | solution.py:131
  207.4 49.6 %collective-permute-start.17 = (bf16[384,2,6,128]{0,3,2,1:T(8,128)(2,1)S(1)}, bf16[384,2,6,128]{0,3,2,1:T(8,128)(2,1)S(1)}, u32[]{:S(2)}, u32[]{:S(2)}) collective-permute-start(bf16[384,2,6,128]{0,3,2,1:T(8,128)(2,1)S(1)} %bitcast.65), channel_id=1, source_target_pairs={{0,8},{4,12},{8,16},{12,20},{16,24},{20,28},{24,0},{28,4},{1,9},{5... | collective-permute-start | bytes 3538952 | tf_op jit(solution)/shard_map/ppermute | solution.py:103
  229.2 47.6 %collective-permute-start.11 = (bf16[768,6,128]{0,2,1:T(8,128)(2,1)}, bf16[768,6,128]{0,2,1:T(8,128)(2,1)}, u32[]{:S(2)}, u32[]{:S(2)}) collective-permute-start(bf16[768,6,128]{0,2,1:T(8,128)(2,1)} %collective-permute-done.9), channel_id=1, source_target_pairs={{0,8},{4,0},{12,4},{20,12},{28,20},{24,28},{16,24},{8,16},{1,9},{5... | collective-permute-start | bytes 3538952 | tf_op jit(solution)/shard_map/ppermute | solution.py:131
  247.8 31.5 %collective-permute-start.10 = (bf16[768,6,128]{0,2,1:T(8,128)(2,1)}, bf16[768,6,128]{0,2,1:T(8,128)(2,1)}, u32[]{:S(2)}, u32[]{:S(2)}) collective-permute-start(bf16[768,6,128]{0,2,1:T(8,128)(2,1)} %collective-permute-done.8), channel_id=1, source_target_pairs={{0,4},{4,12},{12,20},{20,28},{28,24},{24,16},{16,8},{8,0},{1,5},{5... | collective-permute-start | bytes 3538952 | tf_op jit(solution)/shard_map/ppermute | solution.py:130
  257.0 44.9 %collective-permute-start.18 = (bf16[384,2,6,128]{0,3,2,1:T(8,128)(2,1)S(1)}, bf16[384,2,6,128]{0,3,2,1:T(8,128)(2,1)}, u32[]{:S(2)}, u32[]{:S(2)}) collective-permute-start(bf16[384,2,6,128]{0,3,2,1:T(8,128)(2,1)S(1)} %collective-permute-done.17), channel_id=1, source_target_pairs={{4,0},{12,8},{20,16},{28,24},{5,1},{13,9},{21,17},{29,25},{6,2},{1... | collective-permute-start | bytes 3538952 | tf_op jit(solution)/shard_map/ppermute | solution.py:155
  258.3 47.7 %collective-permute-start.16 = (bf16[384,2,6,128]{0,3,2,1:T(8,128)(2,1)S(1)}, bf16[384,2,6,128]{0,3,2,1:T(8,128)(2,1)S(1)}, u32[]{:S(2)}, u32[]{:S(2)}) collective-permute-start(bf16[384,2,6,128]{0,3,2,1:T(8,128)(2,1)S(1)} %bitcast.66), channel_id=1, source_target_pairs={{0,4},{8,12},{16,20},{24,28},{1,5},{9,13},{17,21},{25,29},{2,6},{1... | collective-permute-start | bytes 3538952 | tf_op jit(solution)/shard_map/ppermute | solution.py:153
  264.0 85.4 %collective-permute-start.19 = (bf16[384,2,6,128]{0,3,2,1:T(8,128)(2,1)S(1)}, bf16[384,2,6,128]{0,3,2,1:T(8,128)(2,1)S(1)}, u32[]{:S(2)}, u32[]{:S(2)}) collective-permute-start(bf16[384,2,6,128]{0,3,2,1:T(8,128)(2,1)S(1)} %collective-permute-done.17), channel_id=1, source_target_pairs={{0,4},{8,12},{16,20},{24,28},{1,5},{9,13},{17,21},{25,29},{2,6},{1... | collective-permute-start | bytes 3538952 | tf_op jit(solution)/shard_map/ppermute | solution.py:154
  276.8 71.7 %collective-permute-start.13 = (bf16[768,6,128]{0,2,1:T(8,128)(2,1)}, bf16[768,6,128]{0,2,1:T(8,128)(2,1)S(1)}, u32[]{:S(2)}, u32[]{:S(2)}) collective-permute-start(bf16[768,6,128]{0,2,1:T(8,128)(2,1)} %collective-permute-done.11), channel_id=1, source_target_pairs={{0,8},{4,0},{12,4},{20,12},{28,20},{24,28},{16,24},{8,16},{1,9},{5... | collective-permute-start | bytes 3538952 | tf_op jit(solution)/shard_map/ppermute | solution.py:131
  279.2 66.7 %collective-permute-start.12 = (bf16[768,6,128]{0,2,1:T(8,128)(2,1)}, bf16[768,6,128]{0,2,1:T(8,128)(2,1)S(1)}, u32[]{:S(2)}, u32[]{:S(2)}) collective-permute-start(bf16[768,6,128]{0,2,1:T(8,128)(2,1)} %collective-permute-done.10), channel_id=1, source_target_pairs={{0,4},{4,12},{12,20},{20,28},{28,24},{24,16},{16,8},{8,0},{1,5},{5... | collective-permute-start | bytes 3538952 | tf_op jit(solution)/shard_map/ppermute | solution.py:130
  301.9 47.4 %collective-permute-start.20 = (bf16[384,2,6,128]{0,3,2,1:T(8,128)(2,1)}, bf16[384,2,6,128]{0,3,2,1:T(8,128)(2,1)S(1)}, u32[]{:S(2)}, u32[]{:S(2)}) collective-permute-start(bf16[384,2,6,128]{0,3,2,1:T(8,128)(2,1)} %collective-permute-done.18), channel_id=1, source_target_pairs={{0,8},{8,16},{16,24},{24,0},{1,9},{9,17},{17,25},{25,1},{2,10},{10... | collective-permute-start | bytes 3538952 | tf_op jit(solution)/shard_map/ppermute | solution.py:156
  346.0 9.9 %collective-permute-start.14 = (bf16[384,6,128]{0,2,1:T(8,128)(2,1)S(1)}, bf16[384,6,128]{0,2,1:T(8,128)(2,1)S(1)}, u32[]{:S(2)}, u32[]{:S(2)}) collective-permute-start(bf16[384,6,128]{0,2,1:T(8,128)(2,1)S(1)} %slice.26), channel_id=1, source_target_pairs={{0,4},{4,12},{12,20},{20,28},{28,24},{24,16},{16,8},{8,0},{1,5},{5... | collective-permute-start | bytes 1769480 | tf_op jit(solution)/shard_map/ppermute | solution.py:138
  348.5 9.9 %collective-permute-start.15 = (bf16[384,6,128]{0,2,1:T(8,128)(2,1)S(1)}, bf16[384,6,128]{0,2,1:T(8,128)(2,1)S(1)}, u32[]{:S(2)}, u32[]{:S(2)}) collective-permute-start(bf16[384,6,128]{0,2,1:T(8,128)(2,1)S(1)} %slice.27), channel_id=1, source_target_pairs={{0,8},{4,0},{12,4},{20,12},{28,20},{24,28},{16,24},{8,16},{1,9},{5... | collective-permute-start | bytes 1769480 | tf_op jit(solution)/shard_map/ppermute | solution.py:139
  (11 other events, 395.1 us)
Sparse Core Ops, SparseCore 0:
  13.8 39.1 all-gather.1

commit v9 on v8

--- a/solution.py
+++ b/solution.py
@@ -160,7 +160,14 @@
         return [one_back, two_back, three_back]
 
     def on_device(tokens, qkv_weight):
-        features = lax.all_gather(tokens, "mp", axis=1, tiled=True)
+        parts = lax.axis_size("mp")
+        me_mp = lax.axis_index("mp")
+        width = tokens.shape[1]
+        features = jnp.zeros((tokens.shape[0], width * parts), tokens.dtype)
+        features = lax.dynamic_update_slice(features, tokens, (0, me_mp * width))
+        for by in range(1, parts):
+            piece = shifted(tokens, "mp", by)
+            features = lax.dynamic_update_slice(features, piece, (0, ((me_mp - by) % parts) * width))
         rows_dev = features.shape[0]
         heads_local = qkv_weight.shape[2]
         head_size = qkv_weight.shape[3]

time: 378 us -> 365 us (0.966)
  between operations: 22.8 us -> 9.34 us
  local copies, waits for them, and re-layouts: 10.5 us -> 19.4 us
  waiting for transfers between devices: 261 us -> 254 us
  matrix products: 36.5 us -> 32.1 us
    ppermute x6, waiting for transfers between devices: 167 us -> 152 us  [ring_project(): going_ccw = lax.ppermute(going_ccw, 'ctx', counter)]
    ppermute x2, waiting for transfers between devices: 6.71 us -> 12.8 us  [ring_project(): last_ccw = lax.ppermute(going_ccw[half:], 'ctx', counter)]
    dynamic_update_slice x0 -> x4, local copies, waits for them, and re-layouts: none -> 4.47 us  [the longest x3 4.35 us: on_device(): lax.dynamic_update_slice(features, piece, (0, (me_mp - by) % parts * width))]
    dot_general x18, matrix products: 36.5 us -> 32.1 us  [partial(): return jnp.dot(cols, flat, preferred_element_type=jnp.float32)]
  transfers between devices with their start and end apart: 22 -> 24, of which waited for: 13 -> 13; matrix products, arithmetic and copies ran while one was open for 12% -> 12% of each run, Pallas kernels for 0% -> 0%
where the time goes in v9:
time: 365 us; the launch traced here: 364 us
  waiting for transfers between devices  254 us (70%)
  starting transfers between devices  36.2 us (10%)
  matrix products  32.1 us (9%)
  local copies, waits for them, and re-layouts  19.4 us (5%)
  between operations  9.34 us (3%)
  Pallas kernels  9.3 us (3%)
  other arithmetic  3.65 us (1%)
    ppermute x6, waiting for transfers between devices, ring_project(): going_ccw = lax.ppermute(going_ccw, 'ctx', counter)  152 us
    ppermute x6, waiting for transfers between devices, ring_project(): going_cw = lax.ppermute(going_cw, 'ctx', clockwise)  51.5 us
    dot_general x18, matrix products, partial(): return jnp.dot(cols, flat, preferred_element_type=jnp.float32)  32.1 us
    ppermute x1, waiting for transfers between devices, earlier_blocks(): lax.ppermute(two_back, 'ctx', [(o, o - 1) for o in range(1, n, 2)])  21.7 us
    ppermute x2, waiting for transfers between devices, ring_project(): last_ccw = lax.ppermute(going_ccw[half:], 'ctx', counter)  12.8 us
    ppermute x6, starting transfers between devices, ring_project(): going_ccw = lax.ppermute(going_ccw, 'ctx', counter)  12.6 us
    pallas_call x1, Pallas kernels, windowed_attention(): pl.pallas_call(functools.partial(attention_kernel, scale, reach), out_sha...  9.3 us
    ppermute x2, waiting for transfers between devices, ring_project(): last_cw = lax.ppermute(going_cw[:half], 'ctx', clockwise)  8.81 us
  transfers between devices with their start and end apart: 24, of which 13 were waited for; matrix products, arithmetic and copies ran while one was open for 12% of the time, Pallas kernels for 0%

profile of v9, /device:TPU:0, one launch (start us, length us, event | category | flops | bytes accessed | tf_op | source)
XLA Modules:
  0.0 364.3 jit_solution(3629259757617625111)
XLA Ops:
  0.0 3.2 slice.19
  3.2 2.9 copy.35
  6.1 3.1 collective-permute-start.4
  9.2 51.2 %collective-permute-done.4 = bf16[768,2,6,128]{0,3,2,1:T(8,128)(2,1)S(1)} collective-permute-done((bf16[768,2,6,128]{0,3,2,1:T(8,128)(2,1)S(1)}, bf16[768,2,6,128]{0,3,2,1:T(8,128)(2,1)S(1)}, u32[]{:S(2)}, u32[]{:S(2)}) %collective-permute-start.4) | collective-permute-done | bytes 2359328 | tf_op jit(solution)/shard_map/ppermute | solution.py:131
  65.1 47.8 %collective-permute-done.5 = bf16[768,2,6,128]{0,3,2,1:T(8,128)(2,1)} collective-permute-done((bf16[768,2,6,128]{0,3,2,1:T(8,128)(2,1)S(1)}, bf16[768,2,6,128]{0,3,2,1:T(8,128)(2,1)}, u32[]{:S(2)}, u32[]{:S(2)}) %collective-permute-start.5) | collective-permute-done | bytes 2359328 | tf_op jit(solution)/shard_map/ppermute | solution.py:131
  138.1 26.6 %collective-permute-done.6 = bf16[768,2,6,128]{0,3,2,1:T(8,128)(2,1)} collective-permute-done((bf16[768,2,6,128]{0,3,2,1:T(8,128)(2,1)}, bf16[768,2,6,128]{0,3,2,1:T(8,128)(2,1)}, u32[]{:S(2)}, u32[]{:S(2)}) %collective-permute-start.6) | collective-permute-done | bytes 2359328 | tf_op jit(solution)/shard_map/ppermute | solution.py:131
  171.2 3.1 fusion.18
  174.3 3.2 fusion.1
  177.5 3.2 fusion.12
  180.7 10.8 %collective-permute-done.7 = bf16[384,2,6,128]{0,3,2,1:T(8,128)(2,1)S(1)} collective-permute-done((bf16[384,2,6,128]{0,3,2,1:T(8,128)(2,1)S(1)}, bf16[384,2,6,128]{0,3,2,1:T(8,128)(2,1)S(1)}, u32[]{:S(2)}, u32[]{:S(2)}) %collective-permute-start.7) | collective-permute-done | bytes 1179680 | tf_op jit(solution)/shard_map/ppermute | solution.py:139
  191.5 3.4 collective-permute-done.3
  198.8 3.2 fusion.5
  203.7 19.8 %collective-permute-done.12 = bf16[768,6,128]{0,2,1:T(8,128)(2,1)} collective-permute-done((bf16[768,6,128]{0,2,1:T(8,128)(2,1)S(1)}, bf16[768,6,128]{0,2,1:T(8,128)(2,1)}, u32[]{:S(2)}, u32[]{:S(2)}) %collective-permute-start.12) | collective-permute-done | bytes 1179680 | tf_op jit(solution)/shard_map/ppermute | solution.py:131
  223.4 2.6 collective-permute-start.14
  226.0 16.0 %collective-permute-done.11 = bf16[768,6,128]{0,2,1:T(8,128)(2,1)} collective-permute-done((bf16[768,6,128]{0,2,1:T(8,128)(2,1)S(1)}, bf16[768,6,128]{0,2,1:T(8,128)(2,1)}, u32[]{:S(2)}, u32[]{:S(2)}) %collective-permute-start.11) | collective-permute-done | bytes 1179680 | tf_op jit(solution)/shard_map/ppermute | solution.py:130
  244.0 7.4 %collective-permute-done.20 = bf16[384,2,6,128]{0,3,2,1:T(8,128)(2,1)} collective-permute-done((bf16[384,2,6,128]{0,3,2,1:T(8,128)(2,1)S(1)}, bf16[384,2,6,128]{0,3,2,1:T(8,128)(2,1)}, u32[]{:S(2)}, u32[]{:S(2)}) %collective-permute-start.20) | collective-permute-done | bytes 1179680 | tf_op jit(solution)/shard_map/ppermute | solution.py:103
  252.6 5.7 %collective-permute-start.19 = (bf16[384,2,6,128]{0,3,2,1:T(8,128)(2,1)S(1)}, bf16[384,2,6,128]{0,3,2,1:T(8,128)(2,1)S(1)}, u32[]{:S(2)}, u32[]{:S(2)}) collective-permute-start(bf16[384,2,6,128]{0,3,2,1:T(8,128)(2,1)S(1)} %bitcast.64), channel_id=1, source_target_pairs={{0,4},{8,12},{16,20},{24,28},{1,5},{9,13},{17,21},{25,29},{2,6},{1... | collective-permute-start | bytes 3538952 | tf_op jit(solution)/shard_map/ppermute | solution.py:153
  264.3 6.7 %collective-permute-done.14 = bf16[768,6,128]{0,2,1:T(8,128)(2,1)} collective-permute-done((bf16[768,6,128]{0,2,1:T(8,128)(2,1)}, bf16[768,6,128]{0,2,1:T(8,128)(2,1)}, u32[]{:S(2)}, u32[]{:S(2)}) %collective-permute-start.14) | collective-permute-done | bytes 1179680 | tf_op jit(solution)/shard_map/ppermute | solution.py:131
  271.0 2.5 collective-permute-start.16
  274.4 21.7 %collective-permute-done.21 = bf16[384,2,6,128]{0,3,2,1:T(8,128)(2,1)} collective-permute-done((bf16[384,2,6,128]{0,3,2,1:T(8,128)(2,1)}, bf16[384,2,6,128]{0,3,2,1:T(8,128)(2,1)}, u32[]{:S(2)}, u32[]{:S(2)}) %collective-permute-start.21) | collective-permute-done | bytes 1179680 | tf_op jit(solution)/shard_map/ppermute | solution.py:155
  300.1 2.5 broadcast_select_fusion.1
  304.7 35.5 %collective-permute-done.15 = bf16[768,6,128]{0,2,1:T(8,128)(2,1)S(1)} collective-permute-done((bf16[768,6,128]{0,2,1:T(8,128)(2,1)}, bf16[768,6,128]{0,2,1:T(8,128)(2,1)S(1)}, u32[]{:S(2)}, u32[]{:S(2)}) %collective-permute-start.15) | collective-permute-done | bytes 1179680 | tf_op jit(solution)/shard_map/ppermute | solution.py:130
  344.8 5.4 %collective-permute-done.17 = bf16[384,6,128]{0,2,1:T(8,128)(2,1)S(1)} collective-permute-done((bf16[384,6,128]{0,2,1:T(8,128)(2,1)S(1)}, bf16[384,6,128]{0,2,1:T(8,128)(2,1)S(1)}, u32[]{:S(2)}, u32[]{:S(2)}) %collective-permute-start.17) | collective-permute-done | bytes 589856 | tf_op jit(solution)/shard_map/ppermute | solution.py:138
  355.0 9.3 %shard_map.46 = bf16[6,384,128]{2,1,0:T(8,128)(2,1)} custom-call(bf16[768,384]{1,0:T(8,128)(2,1)} %fusion.11.q_ref, bf16[1536,384]{1,0:T(8,128)(2,1)} %bitcast.65, bf16[1536,384]{1,0:T(8,128)(2,1)} %bitcast.67, bf16[1536,384]{1,0:T(8,128)(2,1)} %bitcast.38.refs_2_.refs_6_, bf16[1536,384]{1,0:T(8,128)(2,1)} %bitcast.69, bf16[1536,384]{1,0:T(8,128)(2,1)} %bitcast.66, ...), custom_call_target="tpu_custom_call" | custom-call | flops 1811939328 | bytes 5898240 | tf_op jit(solution)/shard_map/pallas_call | solution.py:49
  (83 shorter events, 58.3 us)
Async XLA Ops:
  6.1 54.3 %collective-permute-start.4 = (bf16[768,2,6,128]{0,3,2,1:T(8,128)(2,1)S(1)}, bf16[768,2,6,128]{0,3,2,1:T(8,128)(2,1)S(1)}, u32[]{:S(2)}, u32[]{:S(2)}) collective-permute-start(bf16[768,2,6,128]{0,3,2,1:T(8,128)(2,1)S(1)} %copy.35), channel_id=1, source_target_pairs={{0,8},{4,0},{12,4},{20,12},{28,20},{24,28},{16,24},{8,16},{1,9},{5... | collective-permute-start | bytes 7077896 | tf_op jit(solution)/shard_map/ppermute | solution.py:131
  9.2 53.0 %collective-permute-start = (bf16[768,2,6,128]{0,3,2,1:T(8,128)(2,1)S(1)}, bf16[768,2,6,128]{0,3,2,1:T(8,128)(2,1)S(1)}, u32[]{:S(2)}, u32[]{:S(2)}) collective-permute-start(bf16[768,2,6,128]{0,3,2,1:T(8,128)(2,1)S(1)} %copy.35), channel_id=1, source_target_pairs={{0,4},{4,12},{12,20},{20,28},{28,24},{24,16},{16,8},{8,0},{1,5},{5... | collective-permute-start | bytes 7077896 | tf_op jit(solution)/shard_map/ppermute | solution.py:130
  60.4 52.5 %collective-permute-start.5 = (bf16[768,2,6,128]{0,3,2,1:T(8,128)(2,1)S(1)}, bf16[768,2,6,128]{0,3,2,1:T(8,128)(2,1)}, u32[]{:S(2)}, u32[]{:S(2)}) collective-permute-start(bf16[768,2,6,128]{0,3,2,1:T(8,128)(2,1)S(1)} %collective-permute-done.4), channel_id=1, source_target_pairs={{0,8},{4,0},{12,4},{20,12},{28,20},{24,28},{16,24},{8,16},{1,9},{5... | collective-permute-start | bytes 7077896 | tf_op jit(solution)/shard_map/ppermute | solution.py:131
  62.2 52.2 %collective-permute-start.1 = (bf16[768,2,6,128]{0,3,2,1:T(8,128)(2,1)S(1)}, bf16[768,2,6,128]{0,3,2,1:T(8,128)(2,1)}, u32[]{:S(2)}, u32[]{:S(2)}) collective-permute-start(bf16[768,2,6,128]{0,3,2,1:T(8,128)(2,1)S(1)} %collective-permute-done), channel_id=1, source_target_pairs={{0,4},{4,12},{12,20},{20,28},{28,24},{24,16},{16,8},{8,0},{1,5},{5... | collective-permute-start | bytes 7077896 | tf_op jit(solution)/shard_map/ppermute | solution.py:130
  63.6 65.3 %collective-permute-start.8 = (bf16[384,1536]{1,0:T(8,128)(2,1)}, bf16[384,1536]{1,0:T(8,128)(2,1)}, u32[]{:S(2)}, u32[]{:S(2)}) collective-permute-start(bf16[384,1536]{1,0:T(8,128)(2,1)} %param.4), channel_id=1, source_target_pairs={{0,1},{1,2},{2,3},{3,0},{4,5},{5,6},{6,7},{7,4},{8,9},{9,10},{10,1... | collective-permute-start | bytes 3538952 | tf_op jit(solution)/shard_map/ppermute | solution.py:103
  63.6 66.7 %collective-permute-start.9 = (bf16[384,1536]{1,0:T(8,128)(2,1)}, bf16[384,1536]{1,0:T(8,128)(2,1)}, u32[]{:S(2)}, u32[]{:S(2)}) collective-permute-start(bf16[384,1536]{1,0:T(8,128)(2,1)} %param.4), channel_id=1, source_target_pairs={{0,2},{1,3},{2,0},{3,1},{4,6},{5,7},{6,4},{7,5},{8,10},{9,11},{10,... | collective-permute-start | bytes 3538952 | tf_op jit(solution)/shard_map/ppermute | solution.py:103
  112.9 51.8 %collective-permute-start.6 = (bf16[768,2,6,128]{0,3,2,1:T(8,128)(2,1)}, bf16[768,2,6,128]{0,3,2,1:T(8,128)(2,1)}, u32[]{:S(2)}, u32[]{:S(2)}) collective-permute-start(bf16[768,2,6,128]{0,3,2,1:T(8,128)(2,1)} %collective-permute-done.5), channel_id=1, source_target_pairs={{0,8},{4,0},{12,4},{20,12},{28,20},{24,28},{16,24},{8,16},{1,9},{5... | collective-permute-start | bytes 7077896 | tf_op jit(solution)/shard_map/ppermute | solution.py:131
  114.4 53.0 %collective-permute-start.2 = (bf16[768,2,6,128]{0,3,2,1:T(8,128)(2,1)}, bf16[768,2,6,128]{0,3,2,1:T(8,128)(2,1)}, u32[]{:S(2)}, u32[]{:S(2)}) collective-permute-start(bf16[768,2,6,128]{0,3,2,1:T(8,128)(2,1)} %collective-permute-done.1), channel_id=1, source_target_pairs={{0,4},{4,12},{12,20},{20,28},{28,24},{24,16},{16,8},{8,0},{1,5},{5... | collective-permute-start | bytes 7077896 | tf_op jit(solution)/shard_map/ppermute | solution.py:130
  115.8 16.1 %collective-permute-start.10 = (bf16[384,1536]{1,0:T(8,128)(2,1)}, bf16[384,1536]{1,0:T(8,128)(2,1)}, u32[]{:S(2)}, u32[]{:S(2)}) collective-permute-start(bf16[384,1536]{1,0:T(8,128)(2,1)} %param.4), channel_id=1, source_target_pairs={{0,3},{1,0},{2,1},{3,2},{4,7},{5,4},{6,5},{7,6},{8,11},{9,8},{10,9... | collective-permute-start | bytes 3538952 | tf_op jit(solution)/shard_map/ppermute | solution.py:103
  166.2 25.4 %collective-permute-start.7 = (bf16[384,2,6,128]{0,3,2,1:T(8,128)(2,1)S(1)}, bf16[384,2,6,128]{0,3,2,1:T(8,128)(2,1)S(1)}, u32[]{:S(2)}, u32[]{:S(2)}) collective-permute-start(bf16[384,2,6,128]{0,3,2,1:T(8,128)(2,1)S(1)} %slice.25), channel_id=1, source_target_pairs={{0,8},{4,0},{12,4},{20,12},{28,20},{24,28},{16,24},{8,16},{1,9},{5... | collective-permute-start | bytes 3538952 | tf_op jit(solution)/shard_map/ppermute | solution.py:139
  168.8 26.2 %collective-permute-start.3 = (bf16[384,2,6,128]{0,3,2,1:T(8,128)(2,1)S(1)}, bf16[384,2,6,128]{0,3,2,1:T(8,128)(2,1)S(1)}, u32[]{:S(2)}, u32[]{:S(2)}) collective-permute-start(bf16[384,2,6,128]{0,3,2,1:T(8,128)(2,1)S(1)} %slice.24), channel_id=1, source_target_pairs={{0,4},{4,12},{12,20},{20,28},{28,24},{24,16},{16,8},{8,0},{1,5},{5... | collective-permute-start | bytes 3538952 | tf_op jit(solution)/shard_map/ppermute | solution.py:138
  195.0 47.0 %collective-permute-start.11 = (bf16[768,6,128]{0,2,1:T(8,128)(2,1)S(1)}, bf16[768,6,128]{0,2,1:T(8,128)(2,1)}, u32[]{:S(2)}, u32[]{:S(2)}) collective-permute-start(bf16[768,6,128]{0,2,1:T(8,128)(2,1)S(1)} %bitcast.72), channel_id=1, source_target_pairs={{0,4},{4,12},{12,20},{20,28},{28,24},{24,16},{16,8},{8,0},{1,5},{5... | collective-permute-start | bytes 3538952 | tf_op jit(solution)/shard_map/ppermute | solution.py:130
  195.8 27.6 %collective-permute-start.12 = (bf16[768,6,128]{0,2,1:T(8,128)(2,1)S(1)}, bf16[768,6,128]{0,2,1:T(8,128)(2,1)}, u32[]{:S(2)}, u32[]{:S(2)}) collective-permute-start(bf16[768,6,128]{0,2,1:T(8,128)(2,1)S(1)} %bitcast.73), channel_id=1, source_target_pairs={{0,8},{4,0},{12,4},{20,12},{28,20},{24,28},{16,24},{8,16},{1,9},{5... | collective-permute-start | bytes 3538952 | tf_op jit(solution)/shard_map/ppermute | solution.py:131
  202.0 49.3 %collective-permute-start.20 = (bf16[384,2,6,128]{0,3,2,1:T(8,128)(2,1)S(1)}, bf16[384,2,6,128]{0,3,2,1:T(8,128)(2,1)}, u32[]{:S(2)}, u32[]{:S(2)}) collective-permute-start(bf16[384,2,6,128]{0,3,2,1:T(8,128)(2,1)S(1)} %bitcast.63), channel_id=1, source_target_pairs={{0,8},{4,12},{8,16},{12,20},{16,24},{20,28},{24,0},{28,4},{1,9},{5... | collective-permute-start | bytes 3538952 | tf_op jit(solution)/shard_map/ppermute | solution.py:103
  223.4 47.6 %collective-permute-start.14 = (bf16[768,6,128]{0,2,1:T(8,128)(2,1)}, bf16[768,6,128]{0,2,1:T(8,128)(2,1)}, u32[]{:S(2)}, u32[]{:S(2)}) collective-permute-start(bf16[768,6,128]{0,2,1:T(8,128)(2,1)} %collective-permute-done.12), channel_id=1, source_target_pairs={{0,8},{4,0},{12,4},{20,12},{28,20},{24,28},{16,24},{8,16},{1,9},{5... | collective-permute-start | bytes 3538952 | tf_op jit(solution)/shard_map/ppermute | solution.py:131
  242.0 31.5 %collective-permute-start.13 = (bf16[768,6,128]{0,2,1:T(8,128)(2,1)}, bf16[768,6,128]{0,2,1:T(8,128)(2,1)}, u32[]{:S(2)}, u32[]{:S(2)}) collective-permute-start(bf16[768,6,128]{0,2,1:T(8,128)(2,1)} %collective-permute-done.11), channel_id=1, source_target_pairs={{0,4},{4,12},{12,20},{20,28},{28,24},{24,16},{16,8},{8,0},{1,5},{5... | collective-permute-start | bytes 3538952 | tf_op jit(solution)/shard_map/ppermute | solution.py:130
  251.3 44.7 %collective-permute-start.21 = (bf16[384,2,6,128]{0,3,2,1:T(8,128)(2,1)}, bf16[384,2,6,128]{0,3,2,1:T(8,128)(2,1)}, u32[]{:S(2)}, u32[]{:S(2)}) collective-permute-start(bf16[384,2,6,128]{0,3,2,1:T(8,128)(2,1)} %collective-permute-done.20), channel_id=1, source_target_pairs={{4,0},{12,8},{20,16},{28,24},{5,1},{13,9},{21,17},{29,25},{6,2},{1... | collective-permute-start | bytes 3538952 | tf_op jit(solution)/shard_map/ppermute | solution.py:155
  252.6 47.4 %collective-permute-start.19 = (bf16[384,2,6,128]{0,3,2,1:T(8,128)(2,1)S(1)}, bf16[384,2,6,128]{0,3,2,1:T(8,128)(2,1)S(1)}, u32[]{:S(2)}, u32[]{:S(2)}) collective-permute-start(bf16[384,2,6,128]{0,3,2,1:T(8,128)(2,1)S(1)} %bitcast.64), channel_id=1, source_target_pairs={{0,4},{8,12},{16,20},{24,28},{1,5},{9,13},{17,21},{25,29},{2,6},{1... | collective-permute-start | bytes 3538952 | tf_op jit(solution)/shard_map/ppermute | solution.py:153
  258.3 85.3 %collective-permute-start.22 = (bf16[384,2,6,128]{0,3,2,1:T(8,128)(2,1)}, bf16[384,2,6,128]{0,3,2,1:T(8,128)(2,1)S(1)}, u32[]{:S(2)}, u32[]{:S(2)}) collective-permute-start(bf16[384,2,6,128]{0,3,2,1:T(8,128)(2,1)} %collective-permute-done.20), channel_id=1, source_target_pairs={{0,4},{8,12},{16,20},{24,28},{1,5},{9,13},{17,21},{25,29},{2,6},{1... | collective-permute-start | bytes 3538952 | tf_op jit(solution)/shard_map/ppermute | solution.py:154
  271.0 71.7 %collective-permute-start.16 = (bf16[768,6,128]{0,2,1:T(8,128)(2,1)}, bf16[768,6,128]{0,2,1:T(8,128)(2,1)S(1)}, u32[]{:S(2)}, u32[]{:S(2)}) collective-permute-start(bf16[768,6,128]{0,2,1:T(8,128)(2,1)} %collective-permute-done.14), channel_id=1, source_target_pairs={{0,8},{4,0},{12,4},{20,12},{28,20},{24,28},{16,24},{8,16},{1,9},{5... | collective-permute-start | bytes 3538952 | tf_op jit(solution)/shard_map/ppermute | solution.py:131
  273.5 66.7 %collective-permute-start.15 = (bf16[768,6,128]{0,2,1:T(8,128)(2,1)}, bf16[768,6,128]{0,2,1:T(8,128)(2,1)S(1)}, u32[]{:S(2)}, u32[]{:S(2)}) collective-permute-start(bf16[768,6,128]{0,2,1:T(8,128)(2,1)} %collective-permute-done.13), channel_id=1, source_target_pairs={{0,4},{4,12},{12,20},{20,28},{28,24},{24,16},{16,8},{8,0},{1,5},{5... | collective-permute-start | bytes 3538952 | tf_op jit(solution)/shard_map/ppermute | solution.py:130
  296.1 47.6 %collective-permute-start.23 = (bf16[384,2,6,128]{0,3,2,1:T(8,128)(2,1)}, bf16[384,2,6,128]{0,3,2,1:T(8,128)(2,1)S(1)}, u32[]{:S(2)}, u32[]{:S(2)}) collective-permute-start(bf16[384,2,6,128]{0,3,2,1:T(8,128)(2,1)} %collective-permute-done.21), channel_id=1, source_target_pairs={{0,8},{8,16},{16,24},{24,0},{1,9},{9,17},{17,25},{25,1},{2,10},{10... | collective-permute-start | bytes 3538952 | tf_op jit(solution)/shard_map/ppermute | solution.py:156
  340.2 9.9 %collective-permute-start.17 = (bf16[384,6,128]{0,2,1:T(8,128)(2,1)S(1)}, bf16[384,6,128]{0,2,1:T(8,128)(2,1)S(1)}, u32[]{:S(2)}, u32[]{:S(2)}) collective-permute-start(bf16[384,6,128]{0,2,1:T(8,128)(2,1)S(1)} %slice.26), channel_id=1, source_target_pairs={{0,4},{4,12},{12,20},{20,28},{28,24},{24,16},{16,8},{8,0},{1,5},{5... | collective-permute-start | bytes 1769480 | tf_op jit(solution)/shard_map/ppermute | solution.py:138
  342.7 9.9 %collective-permute-start.18 = (bf16[384,6,128]{0,2,1:T(8,128)(2,1)S(1)}, bf16[384,6,128]{0,2,1:T(8,128)(2,1)S(1)}, u32[]{:S(2)}, u32[]{:S(2)}) collective-permute-start(bf16[384,6,128]{0,2,1:T(8,128)(2,1)S(1)} %slice.27), channel_id=1, source_target_pairs={{0,8},{4,0},{12,4},{20,12},{28,20},{24,28},{16,24},{8,16},{1,9},{5... | collective-permute-start | bytes 1769480 | tf_op jit(solution)/shard_map/ppermute | solution.py:139
  (12 other events, 569.6 us)

commit v10 on v9

--- a/solution.py
+++ b/solution.py
@@ -111,15 +111,19 @@
     clockwise = [(ring[i], ring[(i + 1) % n]) for i in range(n)]
     counter = [(ring[i], ring[(i - 1) % n]) for i in range(n)]
     ring_arr = jnp.array(ring, jnp.int32)
+    head_major = n <= 8
     pos_arr = jnp.array(pos, jnp.int32)
 
     def ring_project(features, piece, me):
-        rows_w = piece.shape[0]
+        axis = -2 if head_major else 0
+        rows_w = piece.shape[axis]
         my_pos = pos_arr[me]
 
         def partial(block, part, offset):
             start = block * rows_w + offset
-            cols = lax.dynamic_slice_in_dim(features, start, part.shape[0], axis=1)
+            cols = lax.dynamic_slice_in_dim(features, start, part.shape[axis], axis=1)
+            if head_major:
+                return jnp.einsum("tr,...rd->t...d", cols, part, preferred_element_type=jnp.float32)
             flat = part.reshape(part.shape[0], -1)
             return jnp.dot(cols, flat, preferred_element_type=jnp.float32)
 
@@ -135,8 +139,10 @@
             far = ring_arr[(my_pos + n // 2) % n]
             if rows_w % 2 == 0:
                 half = rows_w // 2
-                last_cw = lax.ppermute(going_cw[:half], "ctx", clockwise)
-                last_ccw = lax.ppermute(going_ccw[half:], "ctx", counter)
+                first = lax.slice_in_dim(going_cw, 0, half, axis=axis % going_cw.ndim)
+                second = lax.slice_in_dim(going_ccw, half, rows_w, axis=axis % going_ccw.ndim)
+                last_cw = lax.ppermute(first, "ctx", clockwise)
+                last_ccw = lax.ppermute(second, "ctx", counter)
                 total = total + partial(far, last_cw, 0)
                 total = total + partial(far, last_ccw, half)
                 return total, (last_cw, last_ccw)
@@ -174,12 +180,17 @@
         scale = 1.0 / math.sqrt(head_size)
         me = lax.axis_index("ctx")
 
-        kv_total, arrived = ring_project(features, qkv_weight[:, 1:], me)
+        if head_major:
+            by_head = jnp.transpose(qkv_weight, (1, 2, 0, 3))
+            kv_piece, q_piece = by_head[1:], by_head[0]
+        else:
+            kv_piece, q_piece = qkv_weight[:, 1:], qkv_weight[:, 0]
+        kv_total, arrived = ring_project(features, kv_piece, me)
         key_value = kv_total.astype(jnp.bfloat16).reshape(rows_dev, 2, heads_local, head_size)
         if n <= 8:
-            q_piece, _ = lax.optimization_barrier((qkv_weight[:, 0], arrived))
+            q_piece, _ = lax.optimization_barrier((q_piece, arrived))
         else:
-            q_piece, key_value = lax.optimization_barrier((qkv_weight[:, 0], key_value))
+            q_piece, key_value = lax.optimization_barrier((q_piece, key_value))
         blocks = [key_value] + earlier_blocks(key_value, me)
         q_total, _ = ring_project(features, q_piece, me)
         queries = q_total.astype(jnp.bfloat16).reshape(rows_dev, heads_local, head_size)

time: 365 us -> 356 us (0.975)
  waiting for transfers between devices: 254 us -> 241 us
    ppermute x6, waiting for transfers between devices: 152 us -> 125 us  [ring_project(): going_ccw = lax.ppermute(going_ccw, 'ctx', counter)]
    ppermute x1, waiting for transfers between devices: 0.01 us -> 15.2 us  [earlier_blocks(): two_back_up = lax.ppermute(two_back, 'ctx', evens_up)]
    unnamed x0 -> x9, matrix products: none -> 13.2 us
    dot_general x18 -> x9, matrix products: 32.1 us -> 19.3 us  [partial(): jnp.einsum('tr,...rd->t...d', cols, part, preferred_element_type=jnp.floa...]
    ppermute x6, waiting for transfers between devices: 51.5 us -> 59.4 us  [ring_project(): going_cw = lax.ppermute(going_cw, 'ctx', clockwise)]
    ppermute x1, waiting for transfers between devices: 21.7 us -> 16.5 us  [earlier_blocks(): lax.ppermute(two_back, 'ctx', [(o, o - 1) for o in range(1, n, 2)])]
    ppermute x4, starting transfers between devices: 4.62 us -> 8.77 us  [the longest x2 5.43 us: ring_project(): last_ccw = lax.ppermute(second, 'ctx', counter)]
    unnamed x24 -> x25, local copies, waits for them, and re-layouts: 6.96 us -> 7.62 us
  transfers between devices with their start and end apart: 24 -> 24, of which waited for: 13 -> 13; matrix products, arithmetic and copies ran while one was open for 12% -> 13% of each run, Pallas kernels for 0% -> 0%
where the time goes in v10:
time: 356 us; the launch traced here: 355 us
  waiting for transfers between devices  241 us (68%)
  starting transfers between devices  38.2 us (11%)
  matrix products  32.5 us (9%)
  local copies, waits for them, and re-layouts  18.6 us (5%)
  between operations  9.51 us (3%)
  Pallas kernels  9.3 us (3%)
  other arithmetic  5.31 us (1%)
    ppermute x6, waiting for transfers between devices, ring_project(): going_ccw = lax.ppermute(going_ccw, 'ctx', counter)  125 us
    ppermute x6, waiting for transfers between devices, ring_project(): going_cw = lax.ppermute(going_cw, 'ctx', clockwise)  59.4 us
    dot_general x9, matrix products, partial(): jnp.einsum('tr,...rd->t...d', cols, part, preferred_element_type=jnp.floa...  19.3 us
    ppermute x1, waiting for transfers between devices, earlier_blocks(): lax.ppermute(two_back, 'ctx', [(o, o - 1) for o in range(1, n, 2)])  16.5 us
    ppermute x1, waiting for transfers between devices, earlier_blocks(): two_back_up = lax.ppermute(two_back, 'ctx', evens_up)  15.2 us
    unnamed x9, matrix products  13.2 us
    ppermute x6, starting transfers between devices, ring_project(): going_ccw = lax.ppermute(going_ccw, 'ctx', counter)  13.1 us
    ppermute x2, waiting for transfers between devices, ring_project(): last_ccw = lax.ppermute(second, 'ctx', counter)  11.1 us
  transfers between devices with their start and end apart: 24, of which 13 were waited for; matrix products, arithmetic and copies ran while one was open for 13% of the time, Pallas kernels for 0%

profile of v10, /device:TPU:0, one launch (start us, length us, event | category | flops | bytes accessed | tf_op | source)
XLA Modules:
  0.0 354.7 jit_solution(13696630409301751900)
XLA Ops:
  0.0 4.3 %copy.5 = bf16[768,3,6,128]{0,3,2,1:T(8,128)(2,1)S(1)} copy(bf16[768,3,6,128]{3,0,2,1:T(8,128)(2,1)} %param.5) | data formatting | bytes 7077888 | tf_op args[1]
  4.5 3.1 collective-permute-start.7
  7.6 51.2 %collective-permute-done.7 = bf16[2,6,768,128]{2,3,1,0:T(8,128)(2,1)S(1)} collective-permute-done((bf16[2,6,768,128]{2,3,1,0:T(8,128)(2,1)S(1)}, bf16[2,6,768,128]{2,3,1,0:T(8,128)(2,1)S(1)}, u32[]{:S(2)}, u32[]{:S(2)}) %collective-permute-start.7) | collective-permute-done | bytes 2359328 | tf_op jit(solution)/shard_map/ppermute | solution.py:135
  64.1 47.2 %collective-permute-done.8 = bf16[2,6,768,128]{2,3,1,0:T(8,128)(2,1)} collective-permute-done((bf16[2,6,768,128]{2,3,1,0:T(8,128)(2,1)S(1)}, bf16[2,6,768,128]{2,3,1,0:T(8,128)(2,1)}, u32[]{:S(2)}, u32[]{:S(2)}) %collective-permute-start.8) | collective-permute-done | bytes 2359328 | tf_op jit(solution)/shard_map/ppermute | solution.py:135
  136.6 26.5 %collective-permute-done.9 = bf16[2,6,768,128]{2,3,1,0:T(8,128)(2,1)} collective-permute-done((bf16[2,6,768,128]{2,3,1,0:T(8,128)(2,1)}, bf16[2,6,768,128]{2,3,1,0:T(8,128)(2,1)}, u32[]{:S(2)}, u32[]{:S(2)}) %collective-permute-start.9) | collective-permute-done | bytes 2359328 | tf_op jit(solution)/shard_map/ppermute | solution.py:135
  169.5 3.1 fusion.6
  172.6 3.1 fusion.8
  175.7 3.1 fusion.4
  178.8 11.1 %collective-permute-done.10 = bf16[2,6,384,128]{2,3,1,0:T(8,128)(2,1)S(1)} collective-permute-done((bf16[2,6,384,128]{2,3,1,0:T(8,128)(2,1)S(1)}, bf16[2,6,384,128]{2,3,1,0:T(8,128)(2,1)S(1)}, u32[]{:S(2)}, u32[]{:S(2)}) %collective-permute-start.10) | collective-permute-done | bytes 1179680 | tf_op jit(solution)/shard_map/ppermute | solution.py:145
  189.9 3.4 collective-permute-done.6
  197.2 4.0 %add_convert_fusion = bf16[384,2,6,128]{0,3,2,1:T(8,128)(2,1)S(1)} fusion(f32[384,2,6,128]{0,3,2,1:T(8,128)S(1)} %fusion.37, f32[384,2,6,128]{0,3,2,1:T(8,128)S(1)} %fusion.39, f32[384,2,6,128]{0,3,2,1:T(8,128)S(1)} %fusion.4, f32[384,2,6,128]{0,3,2,1:T(8,128)S(1)} %fusion.6, f32[384,2,6,128]{0,3,2,1:T(8,128)S(1)} %fusion.8, ...), kind=kOutput, calls=%fused_computation | convolution fusion | flops 911278080 | bytes 23003140 | tf_op jit(solution)/shard_map/tr,...rd->t...d/dot_general | solution.py:126
  202.8 37.5 %collective-permute-done.11 = bf16[6,768,128]{1,2,0:T(8,128)(2,1)} collective-permute-done((bf16[6,768,128]{1,2,0:T(8,128)(2,1)S(1)}, bf16[6,768,128]{1,2,0:T(8,128)(2,1)}, u32[]{:S(2)}, u32[]{:S(2)}) %collective-permute-start.11) | collective-permute-done | bytes 1179680 | tf_op jit(solution)/shard_map/ppermute | solution.py:134
  240.3 3.6 %collective-permute-start.14 = (bf16[6,768,128]{1,2,0:T(8,128)(2,1)}, bf16[6,768,128]{1,2,0:T(8,128)(2,1)}, u32[]{:S(2)}, u32[]{:S(2)}) collective-permute-start(bf16[6,768,128]{1,2,0:T(8,128)(2,1)} %collective-permute-done.12), channel_id=1, source_target_pairs={{0,8},{4,0},{12,4},{20,12},{28,20},{24,28},{16,24},{8,16},{1,9},{5... | collective-permute-start | bytes 3538952 | tf_op jit(solution)/shard_map/ppermute | solution.py:135
  243.9 5.6 %collective-permute-done.20 = bf16[384,2,6,128]{0,3,2,1:T(8,128)(2,1)S(1)} collective-permute-done((bf16[384,2,6,128]{0,3,2,1:T(8,128)(2,1)S(1)}, bf16[384,2,6,128]{0,3,2,1:T(8,128)(2,1)S(1)}, u32[]{:S(2)}, u32[]{:S(2)}) %collective-permute-start.20) | collective-permute-done | bytes 1179680 | tf_op jit(solution)/shard_map/ppermute | solution.py:103
  250.9 5.7 %collective-permute-start.19 = (bf16[384,2,6,128]{0,3,2,1:T(8,128)(2,1)S(1)}, bf16[384,2,6,128]{0,3,2,1:T(8,128)(2,1)S(1)}, u32[]{:S(2)}, u32[]{:S(2)}) collective-permute-start(bf16[384,2,6,128]{0,3,2,1:T(8,128)(2,1)S(1)} %add_convert_fusion), channel_id=1, source_target_pairs={{0,4},{8,12},{16,20},{24,28},{1,5},{9,13},{17,21},{25,29},{2,6},{1... | collective-permute-start | bytes 3538952 | tf_op jit(solution)/shard_map/ppermute | solution.py:159
  258.6 11.3 %collective-permute-done.13 = bf16[6,768,128]{1,2,0:T(8,128)(2,1)} collective-permute-done((bf16[6,768,128]{1,2,0:T(8,128)(2,1)}, bf16[6,768,128]{1,2,0:T(8,128)(2,1)}, u32[]{:S(2)}, u32[]{:S(2)}) %collective-permute-start.13) | collective-permute-done | bytes 1179680 | tf_op jit(solution)/shard_map/ppermute | solution.py:134
  278.2 16.5 %collective-permute-done.21 = bf16[384,2,6,128]{0,3,2,1:T(8,128)(2,1)} collective-permute-done((bf16[384,2,6,128]{0,3,2,1:T(8,128)(2,1)S(1)}, bf16[384,2,6,128]{0,3,2,1:T(8,128)(2,1)}, u32[]{:S(2)}, u32[]{:S(2)}) %collective-permute-start.21) | collective-permute-done | bytes 1179680 | tf_op jit(solution)/shard_map/ppermute | solution.py:161
  300.8 2.5 broadcast_select_fusion.1
  303.3 9.5 %collective-permute-done.15 = bf16[6,768,128]{1,2,0:T(8,128)(2,1)S(1)} collective-permute-done((bf16[6,768,128]{1,2,0:T(8,128)(2,1)}, bf16[6,768,128]{1,2,0:T(8,128)(2,1)S(1)}, u32[]{:S(2)}, u32[]{:S(2)}) %collective-permute-start.15) | collective-permute-done | bytes 1179680 | tf_op jit(solution)/shard_map/ppermute | solution.py:134
  312.9 2.4 collective-permute-start.17
  315.4 4.2 %collective-permute-start.18 = (bf16[6,384,128]{1,2,0:T(8,128)(2,1)S(1)}, bf16[6,384,128]{1,2,0:T(8,128)(2,1)S(1)}, u32[]{:S(2)}, u32[]{:S(2)}) collective-permute-start(bf16[6,384,128]{1,2,0:T(8,128)(2,1)S(1)} %slice.29), channel_id=1, source_target_pairs={{0,8},{4,0},{12,4},{20,12},{28,20},{24,28},{16,24},{8,16},{1,9},{5... | collective-permute-start | bytes 1769480 | tf_op jit(solution)/shard_map/ppermute | solution.py:145
  321.2 15.2 %collective-permute-done.22 = bf16[384,2,6,128]{0,3,2,1:T(8,128)(2,1)S(1)} collective-permute-done((bf16[384,2,6,128]{0,3,2,1:T(8,128)(2,1)S(1)}, bf16[384,2,6,128]{0,3,2,1:T(8,128)(2,1)S(1)}, u32[]{:S(2)}, u32[]{:S(2)}) %collective-permute-start.22) | collective-permute-done | bytes 1179680 | tf_op jit(solution)/shard_map/ppermute | solution.py:160
  337.7 5.0 %collective-permute-done.17 = bf16[6,384,128]{1,2,0:T(8,128)(2,1)S(1)} collective-permute-done((bf16[6,384,128]{1,2,0:T(8,128)(2,1)S(1)}, bf16[6,384,128]{1,2,0:T(8,128)(2,1)S(1)}, u32[]{:S(2)}, u32[]{:S(2)}) %collective-permute-start.17) | collective-permute-done | bytes 589856 | tf_op jit(solution)/shard_map/ppermute | solution.py:144
  345.4 9.3 %shard_map.46 = bf16[6,384,128]{2,1,0:T(8,128)(2,1)} custom-call(bf16[768,384]{1,0:T(8,128)(2,1)} %bitcast.156, bf16[1536,384]{1,0:T(8,128)(2,1)} %bitcast.136, bf16[1536,384]{1,0:T(8,128)(2,1)} %bitcast.138, bf16[1536,384]{1,0:T(8,128)(2,1)} %bitcast.152, bf16[1536,384]{1,0:T(8,128)(2,1)} %bitcast.140, bf16[1536,384]{1,0:T(8,128)(2,1)} %bitcast.137, ...), custom_call_target="tpu_custom_call" | custom-call | flops 1811939328 | bytes 5898240 | tf_op jit(solution)/shard_map/pallas_call | solution.py:49
  (84 shorter events, 56.8 us)
Async XLA Ops:
  4.5 54.3 %collective-permute-start.7 = (bf16[2,6,768,128]{2,3,1,0:T(8,128)(2,1)S(1)}, bf16[2,6,768,128]{2,3,1,0:T(8,128)(2,1)S(1)}, u32[]{:S(2)}, u32[]{:S(2)}) collective-permute-start(bf16[2,6,768,128]{2,3,1,0:T(8,128)(2,1)S(1)} %slice.25), channel_id=1, source_target_pairs={{0,8},{4,0},{12,4},{20,12},{28,20},{24,28},{16,24},{8,16},{1,9},{5... | collective-permute-start | bytes 7077896 | tf_op jit(solution)/shard_map/ppermute | solution.py:135
  7.5 53.0 %collective-permute-start.3 = (bf16[2,6,768,128]{2,3,1,0:T(8,128)(2,1)S(1)}, bf16[2,6,768,128]{2,3,1,0:T(8,128)(2,1)S(1)}, u32[]{:S(2)}, u32[]{:S(2)}) collective-permute-start(bf16[2,6,768,128]{2,3,1,0:T(8,128)(2,1)S(1)} %slice.25), channel_id=1, source_target_pairs={{0,4},{4,12},{12,20},{20,28},{28,24},{24,16},{16,8},{8,0},{1,5},{5... | collective-permute-start | bytes 7077896 | tf_op jit(solution)/shard_map/ppermute | solution.py:134
  58.7 52.5 %collective-permute-start.8 = (bf16[2,6,768,128]{2,3,1,0:T(8,128)(2,1)S(1)}, bf16[2,6,768,128]{2,3,1,0:T(8,128)(2,1)}, u32[]{:S(2)}, u32[]{:S(2)}) collective-permute-start(bf16[2,6,768,128]{2,3,1,0:T(8,128)(2,1)S(1)} %collective-permute-done.7), channel_id=1, source_target_pairs={{0,8},{4,0},{12,4},{20,12},{28,20},{24,28},{16,24},{8,16},{1,9},{5... | collective-permute-start | bytes 7077896 | tf_op jit(solution)/shard_map/ppermute | solution.py:135
  61.9 51.9 %collective-permute-start.4 = (bf16[2,6,768,128]{2,3,1,0:T(8,128)(2,1)S(1)}, bf16[2,6,768,128]{2,3,1,0:T(8,128)(2,1)}, u32[]{:S(2)}, u32[]{:S(2)}) collective-permute-start(bf16[2,6,768,128]{2,3,1,0:T(8,128)(2,1)S(1)} %collective-permute-done.3), channel_id=1, source_target_pairs={{0,4},{4,12},{12,20},{20,28},{28,24},{24,16},{16,8},{8,0},{1,5},{5... | collective-permute-start | bytes 7077896 | tf_op jit(solution)/shard_map/ppermute | solution.py:134
  62.3 64.8 %collective-permute-start = (bf16[384,1536]{1,0:T(8,128)(2,1)}, bf16[384,1536]{1,0:T(8,128)(2,1)}, u32[]{:S(2)}, u32[]{:S(2)}) collective-permute-start(bf16[384,1536]{1,0:T(8,128)(2,1)} %param.4), channel_id=1, source_target_pairs={{0,1},{1,2},{2,3},{3,0},{4,5},{5,6},{6,7},{7,4},{8,9},{9,10},{10,1... | collective-permute-start | bytes 3538952 | tf_op jit(solution)/shard_map/ppermute | solution.py:103
  62.4 66.6 %collective-permute-start.1 = (bf16[384,1536]{1,0:T(8,128)(2,1)}, bf16[384,1536]{1,0:T(8,128)(2,1)}, u32[]{:S(2)}, u32[]{:S(2)}) collective-permute-start(bf16[384,1536]{1,0:T(8,128)(2,1)} %param.4), channel_id=1, source_target_pairs={{0,2},{1,3},{2,0},{3,1},{4,6},{5,7},{6,4},{7,5},{8,10},{9,11},{10,... | collective-permute-start | bytes 3538952 | tf_op jit(solution)/shard_map/ppermute | solution.py:103
  111.3 51.8 %collective-permute-start.9 = (bf16[2,6,768,128]{2,3,1,0:T(8,128)(2,1)}, bf16[2,6,768,128]{2,3,1,0:T(8,128)(2,1)}, u32[]{:S(2)}, u32[]{:S(2)}) collective-permute-start(bf16[2,6,768,128]{2,3,1,0:T(8,128)(2,1)} %collective-permute-done.8), channel_id=1, source_target_pairs={{0,8},{4,0},{12,4},{20,12},{28,20},{24,28},{16,24},{8,16},{1,9},{5... | collective-permute-start | bytes 7077896 | tf_op jit(solution)/shard_map/ppermute | solution.py:135
  113.9 51.9 %collective-permute-start.5 = (bf16[2,6,768,128]{2,3,1,0:T(8,128)(2,1)}, bf16[2,6,768,128]{2,3,1,0:T(8,128)(2,1)}, u32[]{:S(2)}, u32[]{:S(2)}) collective-permute-start(bf16[2,6,768,128]{2,3,1,0:T(8,128)(2,1)} %collective-permute-done.4), channel_id=1, source_target_pairs={{0,4},{4,12},{12,20},{20,28},{28,24},{24,16},{16,8},{8,0},{1,5},{5... | collective-permute-start | bytes 7077896 | tf_op jit(solution)/shard_map/ppermute | solution.py:134
  114.6 15.7 %collective-permute-start.2 = (bf16[384,1536]{1,0:T(8,128)(2,1)}, bf16[384,1536]{1,0:T(8,128)(2,1)}, u32[]{:S(2)}, u32[]{:S(2)}) collective-permute-start(bf16[384,1536]{1,0:T(8,128)(2,1)} %param.4), channel_id=1, source_target_pairs={{0,3},{1,0},{2,1},{3,2},{4,7},{5,4},{6,5},{7,6},{8,11},{9,8},{10,9... | collective-permute-start | bytes 3538952 | tf_op jit(solution)/shard_map/ppermute | solution.py:103
  164.5 25.4 %collective-permute-start.10 = (bf16[2,6,384,128]{2,3,1,0:T(8,128)(2,1)S(1)}, bf16[2,6,384,128]{2,3,1,0:T(8,128)(2,1)S(1)}, u32[]{:S(2)}, u32[]{:S(2)}) collective-permute-start(bf16[2,6,384,128]{2,3,1,0:T(8,128)(2,1)S(1)} %slice.27), channel_id=1, source_target_pairs={{0,8},{4,0},{12,4},{20,12},{28,20},{24,28},{16,24},{8,16},{1,9},{5... | collective-permute-start | bytes 3538952 | tf_op jit(solution)/shard_map/ppermute | solution.py:145
  167.1 26.2 %collective-permute-start.6 = (bf16[2,6,384,128]{2,3,1,0:T(8,128)(2,1)S(1)}, bf16[2,6,384,128]{2,3,1,0:T(8,128)(2,1)S(1)}, u32[]{:S(2)}, u32[]{:S(2)}) collective-permute-start(bf16[2,6,384,128]{2,3,1,0:T(8,128)(2,1)S(1)} %slice.26), channel_id=1, source_target_pairs={{0,4},{4,12},{12,20},{20,28},{28,24},{24,16},{16,8},{8,0},{1,5},{5... | collective-permute-start | bytes 3538952 | tf_op jit(solution)/shard_map/ppermute | solution.py:144
  193.3 47.0 %collective-permute-start.11 = (bf16[6,768,128]{1,2,0:T(8,128)(2,1)S(1)}, bf16[6,768,128]{1,2,0:T(8,128)(2,1)}, u32[]{:S(2)}, u32[]{:S(2)}) collective-permute-start(bf16[6,768,128]{1,2,0:T(8,128)(2,1)S(1)} %slice_bitcast_fusion), channel_id=1, source_target_pairs={{0,4},{4,12},{12,20},{20,28},{28,24},{24,16},{16,8},{8,0},{1,5},{5... | collective-permute-start | bytes 3538952 | tf_op jit(solution)/shard_map/ppermute | solution.py:134
  194.2 46.2 %collective-permute-start.12 = (bf16[6,768,128]{1,2,0:T(8,128)(2,1)S(1)}, bf16[6,768,128]{1,2,0:T(8,128)(2,1)}, u32[]{:S(2)}, u32[]{:S(2)}) collective-permute-start(bf16[6,768,128]{1,2,0:T(8,128)(2,1)S(1)} %slice_bitcast_fusion), channel_id=1, source_target_pairs={{0,8},{4,0},{12,4},{20,12},{28,20},{24,28},{16,24},{8,16},{1,9},{5... | collective-permute-start | bytes 3538952 | tf_op jit(solution)/shard_map/ppermute | solution.py:135
  201.2 48.4 %collective-permute-start.20 = (bf16[384,2,6,128]{0,3,2,1:T(8,128)(2,1)S(1)}, bf16[384,2,6,128]{0,3,2,1:T(8,128)(2,1)S(1)}, u32[]{:S(2)}, u32[]{:S(2)}) collective-permute-start(bf16[384,2,6,128]{0,3,2,1:T(8,128)(2,1)S(1)} %add_convert_fusion), channel_id=1, source_target_pairs={{0,8},{4,12},{8,16},{12,20},{16,24},{20,28},{24,0},{28,4},{1,9},{5... | collective-permute-start | bytes 3538952 | tf_op jit(solution)/shard_map/ppermute | solution.py:103
  240.3 29.5 %collective-permute-start.13 = (bf16[6,768,128]{1,2,0:T(8,128)(2,1)}, bf16[6,768,128]{1,2,0:T(8,128)(2,1)}, u32[]{:S(2)}, u32[]{:S(2)}) collective-permute-start(bf16[6,768,128]{1,2,0:T(8,128)(2,1)} %collective-permute-done.11), channel_id=1, source_target_pairs={{0,4},{4,12},{12,20},{20,28},{28,24},{24,16},{16,8},{8,0},{1,5},{5... | collective-permute-start | bytes 3538952 | tf_op jit(solution)/shard_map/ppermute | solution.py:134
  240.3 29.5 %collective-permute-start.14 = (bf16[6,768,128]{1,2,0:T(8,128)(2,1)}, bf16[6,768,128]{1,2,0:T(8,128)(2,1)}, u32[]{:S(2)}, u32[]{:S(2)}) collective-permute-start(bf16[6,768,128]{1,2,0:T(8,128)(2,1)} %collective-permute-done.12), channel_id=1, source_target_pairs={{0,8},{4,0},{12,4},{20,12},{28,20},{24,28},{16,24},{8,16},{1,9},{5... | collective-permute-start | bytes 3538952 | tf_op jit(solution)/shard_map/ppermute | solution.py:135
  249.6 45.2 %collective-permute-start.21 = (bf16[384,2,6,128]{0,3,2,1:T(8,128)(2,1)S(1)}, bf16[384,2,6,128]{0,3,2,1:T(8,128)(2,1)}, u32[]{:S(2)}, u32[]{:S(2)}) collective-permute-start(bf16[384,2,6,128]{0,3,2,1:T(8,128)(2,1)S(1)} %collective-permute-done.20), channel_id=1, source_target_pairs={{4,0},{12,8},{20,16},{28,24},{5,1},{13,9},{21,17},{29,25},{6,2},{1... | collective-permute-start | bytes 3538952 | tf_op jit(solution)/shard_map/ppermute | solution.py:161
  250.9 49.9 %collective-permute-start.19 = (bf16[384,2,6,128]{0,3,2,1:T(8,128)(2,1)S(1)}, bf16[384,2,6,128]{0,3,2,1:T(8,128)(2,1)S(1)}, u32[]{:S(2)}, u32[]{:S(2)}) collective-permute-start(bf16[384,2,6,128]{0,3,2,1:T(8,128)(2,1)S(1)} %add_convert_fusion), channel_id=1, source_target_pairs={{0,4},{8,12},{16,20},{24,28},{1,5},{9,13},{17,21},{25,29},{2,6},{1... | collective-permute-start | bytes 3538952 | tf_op jit(solution)/shard_map/ppermute | solution.py:159
  269.9 43.0 %collective-permute-start.15 = (bf16[6,768,128]{1,2,0:T(8,128)(2,1)}, bf16[6,768,128]{1,2,0:T(8,128)(2,1)S(1)}, u32[]{:S(2)}, u32[]{:S(2)}) collective-permute-start(bf16[6,768,128]{1,2,0:T(8,128)(2,1)} %collective-permute-done.13), channel_id=1, source_target_pairs={{0,4},{4,12},{12,20},{20,28},{28,24},{24,16},{16,8},{8,0},{1,5},{5... | collective-permute-start | bytes 3538952 | tf_op jit(solution)/shard_map/ppermute | solution.py:134
  269.9 45.4 %collective-permute-start.16 = (bf16[6,768,128]{1,2,0:T(8,128)(2,1)}, bf16[6,768,128]{1,2,0:T(8,128)(2,1)S(1)}, u32[]{:S(2)}, u32[]{:S(2)}) collective-permute-start(bf16[6,768,128]{1,2,0:T(8,128)(2,1)} %collective-permute-done.14), channel_id=1, source_target_pairs={{0,8},{4,0},{12,4},{20,12},{28,20},{24,28},{16,24},{8,16},{1,9},{5... | collective-permute-start | bytes 3538952 | tf_op jit(solution)/shard_map/ppermute | solution.py:135
  274.2 62.3 %collective-permute-start.22 = (bf16[384,2,6,128]{0,3,2,1:T(8,128)(2,1)S(1)}, bf16[384,2,6,128]{0,3,2,1:T(8,128)(2,1)S(1)}, u32[]{:S(2)}, u32[]{:S(2)}) collective-permute-start(bf16[384,2,6,128]{0,3,2,1:T(8,128)(2,1)S(1)} %collective-permute-done.20), channel_id=1, source_target_pairs={{0,4},{8,12},{16,20},{24,28},{1,5},{9,13},{17,21},{25,29},{2,6},{1... | collective-permute-start | bytes 3538952 | tf_op jit(solution)/shard_map/ppermute | solution.py:160
  294.7 41.7 %collective-permute-start.23 = (bf16[384,2,6,128]{0,3,2,1:T(8,128)(2,1)}, bf16[384,2,6,128]{0,3,2,1:T(8,128)(2,1)S(1)}, u32[]{:S(2)}, u32[]{:S(2)}) collective-permute-start(bf16[384,2,6,128]{0,3,2,1:T(8,128)(2,1)} %collective-permute-done.21), channel_id=1, source_target_pairs={{0,8},{8,16},{16,24},{24,0},{1,9},{9,17},{17,25},{25,1},{2,10},{10... | collective-permute-start | bytes 3538952 | tf_op jit(solution)/shard_map/ppermute | solution.py:162
  312.9 29.9 %collective-permute-start.17 = (bf16[6,384,128]{1,2,0:T(8,128)(2,1)S(1)}, bf16[6,384,128]{1,2,0:T(8,128)(2,1)S(1)}, u32[]{:S(2)}, u32[]{:S(2)}) collective-permute-start(bf16[6,384,128]{1,2,0:T(8,128)(2,1)S(1)} %slice.28), channel_id=1, source_target_pairs={{0,4},{4,12},{12,20},{20,28},{28,24},{24,16},{16,8},{8,0},{1,5},{5... | collective-permute-start | bytes 1769480 | tf_op jit(solution)/shard_map/ppermute | solution.py:144
  315.4 27.9 %collective-permute-start.18 = (bf16[6,384,128]{1,2,0:T(8,128)(2,1)S(1)}, bf16[6,384,128]{1,2,0:T(8,128)(2,1)S(1)}, u32[]{:S(2)}, u32[]{:S(2)}) collective-permute-start(bf16[6,384,128]{1,2,0:T(8,128)(2,1)S(1)} %slice.29), channel_id=1, source_target_pairs={{0,8},{4,0},{12,4},{20,12},{28,20},{24,28},{16,24},{8,16},{1,9},{5... | collective-permute-start | bytes 1769480 | tf_op jit(solution)/shard_map/ppermute | solution.py:145
  (12 other events, 626.3 us)

commit v11 on v10

--- a/solution.py
+++ b/solution.py
@@ -33,11 +33,10 @@
     o_ref[0] = (mixed / totals).astype(o_ref.dtype)
 
 
-def windowed_attention(queries, blocks, scale):
-    rows, heads, size = queries.shape
-    reach = len(blocks)
-    q_t = queries.reshape(rows, heads * size).T
-    kv_t = [block.reshape(rows, 2 * heads * size).T for block in blocks]
+def windowed_attention(q_t, kv_t, scale, size):
+    rows = q_t.shape[1]
+    heads = q_t.shape[0] // size
+    reach = len(kv_t)
     q_spec = pl.BlockSpec((size, rows), lambda h: (h, 0))
     v_spec = pl.BlockSpec((size, rows), lambda h: (h + heads, 0))
     keys = rows * reach
@@ -57,6 +56,37 @@
     return jnp.transpose(out, (1, 0, 2))
 
 
+def accumulate_kernel(block_ref, feat_ref, w_ref, acc_ref, out_ref):
+    out_ref[...] = acc_ref[...] + lax.dot_general(
+        w_ref[0], feat_ref[...], (((0,), (1,)), ((), ())), preferred_element_type=jnp.float32
+    )
+
+
+def accumulate(total_t, features, part, column_block):
+    groups, rows, size = part.shape
+    tokens = features.shape[0]
+    return pl.pallas_call(
+        accumulate_kernel,
+        out_shape=jax.ShapeDtypeStruct(total_t.shape, jnp.float32),
+        grid_spec=pltpu.PrefetchScalarGridSpec(
+            num_scalar_prefetch=1,
+            grid=(groups,),
+            in_specs=[
+                pl.BlockSpec((tokens, rows), lambda g, b: (0, b[0])),
+                pl.BlockSpec((1, rows, size), lambda g, b: (g, 0, 0)),
+                pl.BlockSpec((size, tokens), lambda g, b: (g, 0)),
+            ],
+            out_specs=pl.BlockSpec((size, tokens), lambda g, b: (g, 0)),
+        ),
+        input_output_aliases={3: 0},
+        cost_estimate=pl.CostEstimate(
+            flops=2 * tokens * rows * groups * size,
+            transcendentals=0,
+            bytes_accessed=2 * tokens * rows + 2 * groups * rows * size + 8 * groups * size * tokens,
+        ),
+    )(jnp.reshape(column_block, (1,)).astype(jnp.int32), features, part, total_t)
+
+
 def ring_order(mesh):
     n = mesh.shape["ctx"]
     order = list(range(n))
@@ -127,14 +157,33 @@
             flat = part.reshape(part.shape[0], -1)
             return jnp.dot(cols, flat, preferred_element_type=jnp.float32)
 
-        total = partial(me, piece, 0)
+        if head_major:
+            size = piece.shape[-1]
+            piece = piece.reshape(-1, rows_w, size)
+            empty = jnp.zeros((piece.shape[0] * size, features.shape[0]), jnp.float32)
+
+            def partial(block, part, offset):
+                return lambda total_t: accumulate(
+                    total_t, features, part, (block * rows_w + offset) // part.shape[1]
+                )
+
+            def combine(total, term):
+                return term(total)
+
+            total = combine(empty, partial(me, piece, 0))
+        else:
+            total = partial(me, piece, 0).T
+
+            def combine(total, term):
+                return total + term.T
+
         going_cw = piece
         going_ccw = piece
         for step in range(1, (n - 1) // 2 + 1):
             going_cw = lax.ppermute(going_cw, "ctx", clockwise)
             going_ccw = lax.ppermute(going_ccw, "ctx", counter)
-            total = total + partial(ring_arr[(my_pos - step) % n], going_cw, 0)
-            total = total + partial(ring_arr[(my_pos + step) % n], going_ccw, 0)
+            total = combine(total, partial(ring_arr[(my_pos - step) % n], going_cw, 0))
+            total = combine(total, partial(ring_arr[(my_pos + step) % n], going_ccw, 0))
         if n % 2 == 0 and n > 1:
             far = ring_arr[(my_pos + n // 2) % n]
             if rows_w % 2 == 0:
@@ -143,11 +192,11 @@
                 second = lax.slice_in_dim(going_ccw, half, rows_w, axis=axis % going_ccw.ndim)
                 last_cw = lax.ppermute(first, "ctx", clockwise)
                 last_ccw = lax.ppermute(second, "ctx", counter)
-                total = total + partial(far, last_cw, 0)
-                total = total + partial(far, last_ccw, half)
+                total = combine(total, partial(far, last_cw, 0))
+                total = combine(total, partial(far, last_ccw, half))
                 return total, (last_cw, last_ccw)
             last_cw = lax.ppermute(going_cw, "ctx", clockwise)
-            total = total + partial(far, last_cw, 0)
+            total = combine(total, partial(far, last_cw, 0))
             return total, (last_cw,)
         return total, (going_cw, going_ccw)
 
@@ -186,16 +235,16 @@
         else:
             kv_piece, q_piece = qkv_weight[:, 1:], qkv_weight[:, 0]
         kv_total, arrived = ring_project(features, kv_piece, me)
-        key_value = kv_total.astype(jnp.bfloat16).reshape(rows_dev, 2, heads_local, head_size)
+        key_value = kv_total.astype(jnp.bfloat16)
         if n <= 8:
             q_piece, _ = lax.optimization_barrier((q_piece, arrived))
         else:
             q_piece, key_value = lax.optimization_barrier((q_piece, key_value))
         blocks = [key_value] + earlier_blocks(key_value, me)
         q_total, _ = ring_project(features, q_piece, me)
-        queries = q_total.astype(jnp.bfloat16).reshape(rows_dev, heads_local, head_size)
-
-        return windowed_attention(queries, blocks, scale)
+        queries = q_total.astype(jnp.bfloat16)
+
+        return windowed_attention(queries, blocks, scale, head_size)
 
     return on_device
 

time: 356 us -> 417 us (1.17)
  Pallas kernels: 9.3 us -> 151 us
  waiting for transfers between devices: 241 us -> 166 us
  matrix products: 32.5 us -> 0 us
  starting transfers between devices: 38.2 us -> 53.9 us
  local copies, waits for them, and re-layouts: 18.6 us -> 23.6 us
    pallas_call x0 -> x18, Pallas kernels: none -> 142 us  [accumulate(): pl.pallas_call(accumulate_kernel, out_shape=jax.ShapeDtypeStruct(total_t....]
    ppermute x6, waiting for transfers between devices: 125 us -> 3.46 us  [ring_project(): going_ccw = lax.ppermute(going_ccw, 'ctx', counter)]
    ppermute x6, waiting for transfers between devices: 59.4 us -> 140 us  [ring_project(): going_cw = lax.ppermute(going_cw, 'ctx', clockwise)]
    dot_general x9 -> x0, matrix products: 19.3 us -> none  [partial(): jnp.einsum('tr,...rd->t...d', cols, part, preferred_element_type=jnp.floa...]
    ppermute x4, waiting for transfers between devices: 5.62 us -> 22.8 us  [shifted(): lax.ppermute(array, axis, [(i, (i + by) % devices) for i in range(devices)])]
    ppermute x1, waiting for transfers between devices: 16.5 us -> 0.01 us  [earlier_blocks(): lax.ppermute(two_back, 'ctx', [(o, o - 1) for o in range(1, n, 2)])]
    ppermute x1, waiting for transfers between devices: 15.2 us -> 0.01 us  [earlier_blocks(): two_back_up = lax.ppermute(two_back, 'ctx', evens_up)]
    unnamed x9 -> x0, matrix products: 13.2 us -> none
  transfers between devices with their start and end apart: 24 -> 24, of which waited for: 13 -> 8; matrix products, arithmetic and copies ran while one was open for 13% -> 7% of each run, Pallas kernels for 0% -> 33%
where the time goes in v11:
time: 417 us; the launch traced here: 414 us
  waiting for transfers between devices  166 us (40%)
  Pallas kernels  151 us (36%)
  starting transfers between devices  53.9 us (13%)
  local copies, waits for them, and re-layouts  23.6 us (6%)
  between operations  9.39 us (2%)
  other arithmetic  9.09 us (2%)
    pallas_call x18, Pallas kernels, accumulate(): pl.pallas_call(accumulate_kernel, out_shape=jax.ShapeDtypeStruct(total_t....  142 us
    ppermute x6, waiting for transfers between devices, ring_project(): going_cw = lax.ppermute(going_cw, 'ctx', clockwise)  140 us
    ppermute x4, waiting for transfers between devices, shifted(): lax.ppermute(array, axis, [(i, (i + by) % devices) for i in range(devices)])  22.8 us
    ppermute x2, starting transfers between devices, ring_project(): last_ccw = lax.ppermute(second, 'ctx', counter)  10.4 us
    ppermute x6, starting transfers between devices, ring_project(): going_cw = lax.ppermute(going_cw, 'ctx', clockwise)  9.74 us
    ppermute x1, starting transfers between devices, earlier_blocks(): own_up = lax.ppermute(key_value, 'ctx', evens_up)  9.32 us
    pallas_call x1, Pallas kernels, windowed_attention(): pl.pallas_call(functools.partial(attention_kernel, scale, reach), out_sha...  9.3 us
    ppermute x6, starting transfers between devices, ring_project(): going_ccw = lax.ppermute(going_ccw, 'ctx', counter)  9.07 us
  transfers between devices with their start and end apart: 24, of which 8 were waited for; matrix products, arithmetic and copies ran while one was open for 7% of the time, Pallas kernels for 33%

profile of v11, /device:TPU:0, one launch (start us, length us, event | category | flops | bytes accessed | tf_op | source)
XLA Modules:
  0.0 413.6 jit_solution(2586679478538757043)
XLA Ops:
  5.1 51.2 %collective-permute-done.3.w_ref = bf16[12,768,128]{2,1,0:T(8,128)(2,1)S(1)} collective-permute-done((bf16[12,768,128]{2,1,0:T(8,128)(2,1)S(1)}, bf16[12,768,128]{2,1,0:T(8,128)(2,1)S(1)}, u32[]{:S(2)}, u32[]{:S(2)}) %collective-permute-start.3) | collective-permute-done | bytes 2359328 | tf_op jit(solution)/shard_map/ppermute | solution.py:183
  59.4 49.4 %collective-permute-done.4.w_ref = bf16[12,768,128]{2,1,0:T(8,128)(2,1)} collective-permute-done((bf16[12,768,128]{2,1,0:T(8,128)(2,1)S(1)}, bf16[12,768,128]{2,1,0:T(8,128)(2,1)}, u32[]{:S(2)}, u32[]{:S(2)}) %collective-permute-start.4) | collective-permute-done | bytes 2359328 | tf_op jit(solution)/shard_map/ppermute | solution.py:183
  130.3 30.3 %collective-permute-done.5.w_ref = bf16[12,768,128]{2,1,0:T(8,128)(2,1)} collective-permute-done((bf16[12,768,128]{2,1,0:T(8,128)(2,1)}, bf16[12,768,128]{2,1,0:T(8,128)(2,1)}, u32[]{:S(2)}, u32[]{:S(2)}) %collective-permute-start.5) | collective-permute-done | bytes 2359328 | tf_op jit(solution)/shard_map/ppermute | solution.py:183
  175.4 10.2 %shard_map.55.acc_ref = f32[1536,384]{1,0:T(8,128)} custom-call(s32[1]{0:T(128)} %bitcast.34.block_ref, bf16[384,6144]{1,0:T(8,128)(2,1)} %constant_dynamic-update-slice_fusion.feat_ref, bf16[12,768,128]{2,1,0:T(8,128)(2,1)} %bitcast.39, f32[1536,384]{1,0:T(8,128)} %broadcast_in_dim.11.acc_ref), custom_call_target="tpu_custom_call", output_to_operand_aliasing={{}: (3, {})} | custom-call | flops 905969664 | bytes 7667712 | tf_op jit(solution)/shard_map/pallas_call | solution.py:68
  185.6 10.2 %shard_map.56.acc_ref = f32[1536,384]{1,0:T(8,128)} custom-call(s32[1]{0:T(128)} %bitcast.33.block_ref, bf16[384,6144]{1,0:T(8,128)(2,1)} %constant_dynamic-update-slice_fusion.feat_ref, bf16[12,768,128]{2,1,0:T(8,128)(2,1)} %copy-done.5, f32[1536,384]{1,0:T(8,128)} %shard_map.55.acc_ref), custom_call_target="tpu_custom_call", output_to_operand_aliasing={{}: (3, {})} | custom-call | flops 905969664 | bytes 7667712 | tf_op jit(solution)/shard_map/pallas_call | solution.py:68
  195.8 10.2 %shard_map.57.acc_ref = f32[1536,384]{1,0:T(8,128)} custom-call(s32[1]{0:T(128)} %bitcast.29.block_ref, bf16[384,6144]{1,0:T(8,128)(2,1)} %constant_dynamic-update-slice_fusion.feat_ref, bf16[12,768,128]{2,1,0:T(8,128)(2,1)} %copy-done.6, f32[1536,384]{1,0:T(8,128)} %shard_map.56.acc_ref), custom_call_target="tpu_custom_call", output_to_operand_aliasing={{}: (3, {})} | custom-call | flops 905969664 | bytes 7667712 | tf_op jit(solution)/shard_map/pallas_call | solution.py:68
  206.1 10.2 %shard_map.58.acc_ref = f32[1536,384]{1,0:T(8,128)} custom-call(s32[1]{0:T(128)} %bitcast.25.block_ref, bf16[384,6144]{1,0:T(8,128)(2,1)} %constant_dynamic-update-slice_fusion.feat_ref, bf16[12,768,128]{2,1,0:T(8,128)(2,1)} %collective-permute-done.4.w_ref, f32[1536,384]{1,0:T(8,128)} %shard_map.57.acc_ref), custom_call_target="tpu_custom_call", output_to_operand_aliasing={{}: (3, {})} | custom-call | flops 905969664 | bytes 7667712 | tf_op jit(solution)/shard_map/pallas_call | solution.py:68
  216.3 10.2 %shard_map.59.acc_ref = f32[1536,384]{1,0:T(8,128)} custom-call(s32[1]{0:T(128)} %bitcast.21.block_ref, bf16[384,6144]{1,0:T(8,128)(2,1)} %constant_dynamic-update-slice_fusion.feat_ref, bf16[12,768,128]{2,1,0:T(8,128)(2,1)} %collective-permute-done.8.w_ref, f32[1536,384]{1,0:T(8,128)} %shard_map.58.acc_ref), custom_call_target="tpu_custom_call", output_to_operand_aliasing={{}: (3, {})} | custom-call | flops 905969664 | bytes 7667712 | tf_op jit(solution)/shard_map/pallas_call | solution.py:68
  226.6 10.2 %shard_map.60.acc_ref = f32[1536,384]{1,0:T(8,128)} custom-call(s32[1]{0:T(128)} %bitcast.17.block_ref, bf16[384,6144]{1,0:T(8,128)(2,1)} %constant_dynamic-update-slice_fusion.feat_ref, bf16[12,768,128]{2,1,0:T(8,128)(2,1)} %collective-permute-done.5.w_ref, f32[1536,384]{1,0:T(8,128)} %shard_map.59.acc_ref), custom_call_target="tpu_custom_call", output_to_operand_aliasing={{}: (3, {})} | custom-call | flops 905969664 | bytes 7667712 | tf_op jit(solution)/shard_map/pallas_call | solution.py:68
  237.9 10.2 %shard_map.61.acc_ref = f32[1536,384]{1,0:T(8,128)} custom-call(s32[1]{0:T(128)} %bitcast.13.block_ref, bf16[384,6144]{1,0:T(8,128)(2,1)} %constant_dynamic-update-slice_fusion.feat_ref, bf16[12,768,128]{2,1,0:T(8,128)(2,1)} %collective-permute-done.9.w_ref, f32[1536,384]{1,0:T(8,128)} %shard_map.60.acc_ref), custom_call_target="tpu_custom_call", output_to_operand_aliasing={{}: (3, {})} | custom-call | flops 905969664 | bytes 7667712 | tf_op jit(solution)/shard_map/pallas_call | solution.py:68
  249.2 9.4 %shard_map.62.acc_ref = f32[1536,384]{1,0:T(8,128)} custom-call(s32[1]{0:T(128)} %bitcast.9.block_ref, bf16[384,6144]{1,0:T(8,128)(2,1)} %constant_dynamic-update-slice_fusion.feat_ref, bf16[12,384,128]{2,1,0:T(8,128)(2,1)} %collective-permute-done.6.w_ref, f32[1536,384]{1,0:T(8,128)} %shard_map.61.acc_ref), custom_call_target="tpu_custom_call", output_to_operand_aliasing={{}: (3, {})} | custom-call | flops 452984832 | bytes 6193152 | tf_op jit(solution)/shard_map/pallas_call | solution.py:68
  258.6 9.4 %shard_map.63 = f32[1536,384]{1,0:T(8,128)} custom-call(s32[1]{0:T(128)} %bitcast.3.block_ref, bf16[384,6144]{1,0:T(8,128)(2,1)} %constant_dynamic-update-slice_fusion.feat_ref, bf16[12,384,128]{2,1,0:T(8,128)(2,1)} %collective-permute-done.10.w_ref, f32[1536,384]{1,0:T(8,128)} %shard_map.62.acc_ref), custom_call_target="tpu_custom_call", output_to_operand_aliasing={{}: (3, {})} | custom-call | flops 452984832 | bytes 6193152 | tf_op jit(solution)/shard_map/pallas_call | solution.py:68
  277.8 22.7 %collective-permute-done.20.refs_2_.refs_6_ = bf16[1536,384]{1,0:T(8,128)(2,1)S(1)} collective-permute-done((bf16[1536,384]{1,0:T(8,128)(2,1)S(1)}, bf16[1536,384]{1,0:T(8,128)(2,1)S(1)}, u32[]{:S(2)}, u32[]{:S(2)}) %collective-permute-start.20) | collective-permute-done | bytes 1179680 | tf_op jit(solution)/shard_map/ppermute | solution.py:133
  301.8 9.3 %collective-permute-start.19 = (bf16[1536,384]{1,0:T(8,128)(2,1)S(1)}, bf16[1536,384]{1,0:T(8,128)(2,1)}, u32[]{:S(2)}, u32[]{:S(2)}) collective-permute-start(bf16[1536,384]{1,0:T(8,128)(2,1)S(1)} %convert_element_type.7.refs_0_.refs_4_), channel_id=1, source_target_pairs={{0,4},{8,12},{16,20},{24,28},{1,5},{9,13},{17,21},{25,29},{2,6},{1... | collective-permute-start | bytes 3538952 | tf_op jit(solution)/shard_map/ppermute | solution.py:208
  311.2 9.0 %collective-permute-done.16.w_ref = bf16[6,768,128]{2,1,0:T(8,128)(2,1)} collective-permute-done((bf16[6,768,128]{2,1,0:T(8,128)(2,1)}, bf16[6,768,128]{2,1,0:T(8,128)(2,1)}, u32[]{:S(2)}, u32[]{:S(2)}) %collective-permute-start.16) | collective-permute-done | bytes 1179680 | tf_op jit(solution)/shard_map/ppermute | solution.py:183
  334.3 5.8 %shard_map.46.acc_ref = f32[768,384]{1,0:T(8,128)} custom-call(s32[1]{0:T(128)} %bitcast.34.block_ref, bf16[384,6144]{1,0:T(8,128)(2,1)} %constant_dynamic-update-slice_fusion.feat_ref, bf16[6,768,128]{2,1,0:T(8,128)(2,1)} %copy-done.2, f32[768,384]{1,0:T(8,128)} %broadcast_in_dim.10.acc_ref), custom_call_target="tpu_custom_call", output_to_operand_aliasing={{}: (3, {})} | custom-call | flops 452984832 | bytes 4128768 | tf_op jit(solution)/shard_map/pallas_call | solution.py:68
  340.1 5.9 %shard_map.47.acc_ref = f32[768,384]{1,0:T(8,128)} custom-call(s32[1]{0:T(128)} %bitcast.33.block_ref, bf16[384,6144]{1,0:T(8,128)(2,1)} %constant_dynamic-update-slice_fusion.feat_ref, bf16[6,768,128]{2,1,0:T(8,128)(2,1)} %collective-permute-done.15.w_ref, f32[768,384]{1,0:T(8,128)} %shard_map.46.acc_ref), custom_call_target="tpu_custom_call", output_to_operand_aliasing={{}: (3, {})} | custom-call | flops 452984832 | bytes 4128768 | tf_op jit(solution)/shard_map/pallas_call | solution.py:68
  346.0 5.8 %shard_map.48.acc_ref = f32[768,384]{1,0:T(8,128)} custom-call(s32[1]{0:T(128)} %bitcast.29.block_ref, bf16[384,6144]{1,0:T(8,128)(2,1)} %constant_dynamic-update-slice_fusion.feat_ref, bf16[6,768,128]{2,1,0:T(8,128)(2,1)} %collective-permute-done.11.w_ref, f32[768,384]{1,0:T(8,128)} %shard_map.47.acc_ref), custom_call_target="tpu_custom_call", output_to_operand_aliasing={{}: (3, {})} | custom-call | flops 452984832 | bytes 4128768 | tf_op jit(solution)/shard_map/pallas_call | solution.py:68
  351.8 5.8 %shard_map.49.acc_ref = f32[768,384]{1,0:T(8,128)} custom-call(s32[1]{0:T(128)} %bitcast.25.block_ref, bf16[384,6144]{1,0:T(8,128)(2,1)} %constant_dynamic-update-slice_fusion.feat_ref, bf16[6,768,128]{2,1,0:T(8,128)(2,1)} %collective-permute-done.16.w_ref, f32[768,384]{1,0:T(8,128)} %shard_map.48.acc_ref), custom_call_target="tpu_custom_call", output_to_operand_aliasing={{}: (3, {})} | custom-call | flops 452984832 | bytes 4128768 | tf_op jit(solution)/shard_map/pallas_call | solution.py:68
  357.7 5.8 %shard_map.50.acc_ref = f32[768,384]{1,0:T(8,128)} custom-call(s32[1]{0:T(128)} %bitcast.21.block_ref, bf16[384,6144]{1,0:T(8,128)(2,1)} %constant_dynamic-update-slice_fusion.feat_ref, bf16[6,768,128]{2,1,0:T(8,128)(2,1)} %collective-permute-done.12.w_ref, f32[768,384]{1,0:T(8,128)} %shard_map.49.acc_ref), custom_call_target="tpu_custom_call", output_to_operand_aliasing={{}: (3, {})} | custom-call | flops 452984832 | bytes 4128768 | tf_op jit(solution)/shard_map/pallas_call | solution.py:68
  367.5 9.5 %collective-permute-start.14 = (bf16[6,384,128]{2,1,0:T(8,128)(2,1)S(1)}, bf16[6,384,128]{2,1,0:T(8,128)(2,1)}, u32[]{:S(2)}, u32[]{:S(2)}) collective-permute-start(bf16[6,384,128]{2,1,0:T(8,128)(2,1)S(1)} %slice.28), channel_id=1, source_target_pairs={{0,8},{4,0},{12,4},{20,12},{28,20},{24,28},{16,24},{8,16},{1,9},{5... | collective-permute-start | bytes 1769480 | tf_op jit(solution)/shard_map/ppermute | solution.py:194
  377.0 5.8 %shard_map.51.acc_ref = f32[768,384]{1,0:T(8,128)} custom-call(s32[1]{0:T(128)} %bitcast.17.block_ref, bf16[384,6144]{1,0:T(8,128)(2,1)} %constant_dynamic-update-slice_fusion.feat_ref, bf16[6,768,128]{2,1,0:T(8,128)(2,1)} %copy-done.4, f32[768,384]{1,0:T(8,128)} %shard_map.50.acc_ref), custom_call_target="tpu_custom_call", output_to_operand_aliasing={{}: (3, {})} | custom-call | flops 452984832 | bytes 4128768 | tf_op jit(solution)/shard_map/pallas_call | solution.py:68
  382.9 5.8 %shard_map.52.acc_ref = f32[768,384]{1,0:T(8,128)} custom-call(s32[1]{0:T(128)} %bitcast.13.block_ref, bf16[384,6144]{1,0:T(8,128)(2,1)} %constant_dynamic-update-slice_fusion.feat_ref, bf16[6,768,128]{2,1,0:T(8,128)(2,1)} %collective-permute-done.13.w_ref, f32[768,384]{1,0:T(8,128)} %shard_map.51.acc_ref), custom_call_target="tpu_custom_call", output_to_operand_aliasing={{}: (3, {})} | custom-call | flops 452984832 | bytes 4128768 | tf_op jit(solution)/shard_map/pallas_call | solution.py:68
  404.3 9.3 %shard_map.64 = bf16[6,384,128]{2,1,0:T(8,128)(2,1)} custom-call(bf16[768,384]{1,0:T(8,128)(2,1)} %convert_element_type.6.q_ref, bf16[1536,384]{1,0:T(8,128)(2,1)} %copy-done, bf16[1536,384]{1,0:T(8,128)(2,1)} %broadcast_select_fusion.1.refs_1_.refs_5_, bf16[1536,384]{1,0:T(8,128)(2,1)} %copy-done.3, bf16[1536,384]{1,0:T(8,128)(2,1)} %broadcast_select_fusion.refs_3_.refs_7_, ...), custom_call_target="tpu_custom_call" | custom-call | flops 1811939328 | bytes 5898240 | tf_op jit(solution)/shard_map/pallas_call | solution.py:48
  (82 shorter events, 82.1 us)
Async XLA Ops:
  1.9 54.3 %collective-permute-start.3 = (bf16[12,768,128]{2,1,0:T(8,128)(2,1)S(1)}, bf16[12,768,128]{2,1,0:T(8,128)(2,1)S(1)}, u32[]{:S(2)}, u32[]{:S(2)}) collective-permute-start(bf16[12,768,128]{2,1,0:T(8,128)(2,1)S(1)} %bitcast.37), channel_id=1, source_target_pairs={{0,4},{4,12},{12,20},{20,28},{28,24},{24,16},{16,8},{8,0},{1,5},{5... | collective-permute-start | bytes 7077896 | tf_op jit(solution)/shard_map/ppermute | solution.py:183
  5.0 53.0 %collective-permute-start.7 = (bf16[12,768,128]{2,1,0:T(8,128)(2,1)S(1)}, bf16[12,768,128]{2,1,0:T(8,128)(2,1)S(1)}, u32[]{:S(2)}, u32[]{:S(2)}) collective-permute-start(bf16[12,768,128]{2,1,0:T(8,128)(2,1)S(1)} %bitcast.38), channel_id=1, source_target_pairs={{0,8},{4,0},{12,4},{20,12},{28,20},{24,28},{16,24},{8,16},{1,9},{5... | collective-permute-start | bytes 7077896 | tf_op jit(solution)/shard_map/ppermute | solution.py:184
  56.3 52.5 %collective-permute-start.4 = (bf16[12,768,128]{2,1,0:T(8,128)(2,1)S(1)}, bf16[12,768,128]{2,1,0:T(8,128)(2,1)}, u32[]{:S(2)}, u32[]{:S(2)}) collective-permute-start(bf16[12,768,128]{2,1,0:T(8,128)(2,1)S(1)} %collective-permute-done.3.w_ref), channel_id=1, source_target_pairs={{0,4},{4,12},{12,20},{20,28},{28,24},{24,16},{16,8},{8,0},{1,5},{5... | collective-permute-start | bytes 7077896 | tf_op jit(solution)/shard_map/ppermute | solution.py:183
  58.0 52.3 %collective-permute-start.8 = (bf16[12,768,128]{2,1,0:T(8,128)(2,1)S(1)}, bf16[12,768,128]{2,1,0:T(8,128)(2,1)}, u32[]{:S(2)}, u32[]{:S(2)}) collective-permute-start(bf16[12,768,128]{2,1,0:T(8,128)(2,1)S(1)} %collective-permute-done.7.w_ref), channel_id=1, source_target_pairs={{0,8},{4,0},{12,4},{20,12},{28,20},{24,28},{16,24},{8,16},{1,9},{5... | collective-permute-start | bytes 7077896 | tf_op jit(solution)/shard_map/ppermute | solution.py:184
  108.8 51.8 %collective-permute-start.5 = (bf16[12,768,128]{2,1,0:T(8,128)(2,1)}, bf16[12,768,128]{2,1,0:T(8,128)(2,1)}, u32[]{:S(2)}, u32[]{:S(2)}) collective-permute-start(bf16[12,768,128]{2,1,0:T(8,128)(2,1)} %collective-permute-done.4.w_ref), channel_id=1, source_target_pairs={{0,4},{4,12},{12,20},{20,28},{28,24},{24,16},{16,8},{8,0},{1,5},{5... | collective-permute-start | bytes 7077896 | tf_op jit(solution)/shard_map/ppermute | solution.py:183
  110.2 52.9 %collective-permute-start.9 = (bf16[12,768,128]{2,1,0:T(8,128)(2,1)}, bf16[12,768,128]{2,1,0:T(8,128)(2,1)}, u32[]{:S(2)}, u32[]{:S(2)}) collective-permute-start(bf16[12,768,128]{2,1,0:T(8,128)(2,1)} %collective-permute-done.8.w_ref), channel_id=1, source_target_pairs={{0,8},{4,0},{12,4},{20,12},{28,20},{24,28},{16,24},{8,16},{1,9},{5... | collective-permute-start | bytes 7077896 | tf_op jit(solution)/shard_map/ppermute | solution.py:184
  111.7 54.8 %collective-permute-start = (bf16[384,1536]{1,0:T(8,128)(2,1)S(1)}, bf16[384,1536]{1,0:T(8,128)(2,1)}, u32[]{:S(2)}, u32[]{:S(2)}) collective-permute-start(bf16[384,1536]{1,0:T(8,128)(2,1)S(1)} %copy-done.7), channel_id=1, source_target_pairs={{0,1},{1,2},{2,3},{3,0},{4,5},{5,6},{6,7},{7,4},{8,9},{9,10},{10,1... | collective-permute-start | bytes 3538952 | tf_op jit(solution)/shard_map/ppermute | solution.py:133
  111.7 57.3 %collective-permute-start.1 = (bf16[384,1536]{1,0:T(8,128)(2,1)S(1)}, bf16[384,1536]{1,0:T(8,128)(2,1)}, u32[]{:S(2)}, u32[]{:S(2)}) collective-permute-start(bf16[384,1536]{1,0:T(8,128)(2,1)S(1)} %copy-done.7), channel_id=1, source_target_pairs={{0,2},{1,3},{2,0},{3,1},{4,6},{5,7},{6,4},{7,5},{8,10},{9,11},{10,... | collective-permute-start | bytes 3538952 | tf_op jit(solution)/shard_map/ppermute | solution.py:133
  113.2 58.2 %collective-permute-start.2 = (bf16[384,1536]{1,0:T(8,128)(2,1)S(1)}, bf16[384,1536]{1,0:T(8,128)(2,1)}, u32[]{:S(2)}, u32[]{:S(2)}) collective-permute-start(bf16[384,1536]{1,0:T(8,128)(2,1)S(1)} %copy-done.7), channel_id=1, source_target_pairs={{0,3},{1,0},{2,1},{3,2},{4,7},{5,4},{6,5},{7,6},{8,11},{9,8},{10,9... | collective-permute-start | bytes 3538952 | tf_op jit(solution)/shard_map/ppermute | solution.py:133
  162.0 74.9 %collective-permute-start.6 = (bf16[12,384,128]{2,1,0:T(8,128)(2,1)S(1)}, bf16[12,384,128]{2,1,0:T(8,128)(2,1)}, u32[]{:S(2)}, u32[]{:S(2)}) collective-permute-start(bf16[12,384,128]{2,1,0:T(8,128)(2,1)S(1)} %slice.26), channel_id=1, source_target_pairs={{0,4},{4,12},{12,20},{20,28},{28,24},{24,16},{16,8},{8,0},{1,5},{5... | collective-permute-start | bytes 3538952 | tf_op jit(solution)/shard_map/ppermute | solution.py:193
  165.5 71.3 %collective-permute-start.10 = (bf16[12,384,128]{2,1,0:T(8,128)(2,1)}, bf16[12,384,128]{2,1,0:T(8,128)(2,1)}, u32[]{:S(2)}, u32[]{:S(2)}) collective-permute-start(bf16[12,384,128]{2,1,0:T(8,128)(2,1)} %slice.27), channel_id=1, source_target_pairs={{0,8},{4,0},{12,4},{20,12},{28,20},{24,28},{16,24},{8,16},{1,9},{5... | collective-permute-start | bytes 3538952 | tf_op jit(solution)/shard_map/ppermute | solution.py:194
  236.8 34.1 %collective-permute-start.15 = (bf16[6,768,128]{2,1,0:T(8,128)(2,1)S(1)}, bf16[6,768,128]{2,1,0:T(8,128)(2,1)}, u32[]{:S(2)}, u32[]{:S(2)}) collective-permute-start(bf16[6,768,128]{2,1,0:T(8,128)(2,1)S(1)} %slice_bitcast_fusion.w_ref), channel_id=1, source_target_pairs={{0,4},{4,12},{12,20},{20,28},{28,24},{24,16},{16,8},{8,0},{1,5},{5... | collective-permute-start | bytes 3538952 | tf_op jit(solution)/shard_map/ppermute | solution.py:183
  248.2 27.0 %collective-permute-start.11 = (bf16[6,768,128]{2,1,0:T(8,128)(2,1)S(1)}, bf16[6,768,128]{2,1,0:T(8,128)(2,1)}, u32[]{:S(2)}, u32[]{:S(2)}) collective-permute-start(bf16[6,768,128]{2,1,0:T(8,128)(2,1)S(1)} %slice_bitcast_fusion.w_ref), channel_id=1, source_target_pairs={{0,8},{4,0},{12,4},{20,12},{28,20},{24,28},{16,24},{8,16},{1,9},{5... | collective-permute-start | bytes 3538952 | tf_op jit(solution)/shard_map/ppermute | solution.py:184
  269.8 30.8 %collective-permute-start.20 = (bf16[1536,384]{1,0:T(8,128)(2,1)S(1)}, bf16[1536,384]{1,0:T(8,128)(2,1)S(1)}, u32[]{:S(2)}, u32[]{:S(2)}) collective-permute-start(bf16[1536,384]{1,0:T(8,128)(2,1)S(1)} %convert_element_type.7.refs_0_.refs_4_), channel_id=1, source_target_pairs={{0,8},{4,12},{8,16},{12,20},{16,24},{20,28},{24,0},{28,4},{1,9},{5... | collective-permute-start | bytes 3538952 | tf_op jit(solution)/shard_map/ppermute | solution.py:133
  270.9 49.2 %collective-permute-start.16 = (bf16[6,768,128]{2,1,0:T(8,128)(2,1)}, bf16[6,768,128]{2,1,0:T(8,128)(2,1)}, u32[]{:S(2)}, u32[]{:S(2)}) collective-permute-start(bf16[6,768,128]{2,1,0:T(8,128)(2,1)} %collective-permute-done.15.w_ref), channel_id=1, source_target_pairs={{0,4},{4,12},{12,20},{20,28},{28,24},{24,16},{16,8},{8,0},{1,5},{5... | collective-permute-start | bytes 3538952 | tf_op jit(solution)/shard_map/ppermute | solution.py:183
  275.2 46.6 %collective-permute-start.12 = (bf16[6,768,128]{2,1,0:T(8,128)(2,1)}, bf16[6,768,128]{2,1,0:T(8,128)(2,1)}, u32[]{:S(2)}, u32[]{:S(2)}) collective-permute-start(bf16[6,768,128]{2,1,0:T(8,128)(2,1)} %collective-permute-done.11.w_ref), channel_id=1, source_target_pairs={{0,8},{4,0},{12,4},{20,12},{28,20},{24,28},{16,24},{8,16},{1,9},{5... | collective-permute-start | bytes 3538952 | tf_op jit(solution)/shard_map/ppermute | solution.py:184
  300.5 28.7 %collective-permute-start.21 = (bf16[1536,384]{1,0:T(8,128)(2,1)S(1)}, bf16[1536,384]{1,0:T(8,128)(2,1)}, u32[]{:S(2)}, u32[]{:S(2)}) collective-permute-start(bf16[1536,384]{1,0:T(8,128)(2,1)S(1)} %collective-permute-done.20.refs_2_.refs_6_), channel_id=1, source_target_pairs={{4,0},{12,8},{20,16},{28,24},{5,1},{13,9},{21,17},{29,25},{6,2},{1... | collective-permute-start | bytes 3538952 | tf_op jit(solution)/shard_map/ppermute | solution.py:210
  301.8 61.7 %collective-permute-start.19 = (bf16[1536,384]{1,0:T(8,128)(2,1)S(1)}, bf16[1536,384]{1,0:T(8,128)(2,1)}, u32[]{:S(2)}, u32[]{:S(2)}) collective-permute-start(bf16[1536,384]{1,0:T(8,128)(2,1)S(1)} %convert_element_type.7.refs_0_.refs_4_), channel_id=1, source_target_pairs={{0,4},{8,12},{16,20},{24,28},{1,5},{9,13},{17,21},{25,29},{2,6},{1... | collective-permute-start | bytes 3538952 | tf_op jit(solution)/shard_map/ppermute | solution.py:208
  320.1 45.9 %collective-permute-start.17 = (bf16[6,768,128]{2,1,0:T(8,128)(2,1)}, bf16[6,768,128]{2,1,0:T(8,128)(2,1)S(1)}, u32[]{:S(2)}, u32[]{:S(2)}) collective-permute-start(bf16[6,768,128]{2,1,0:T(8,128)(2,1)} %collective-permute-done.16.w_ref), channel_id=1, source_target_pairs={{0,4},{4,12},{12,20},{20,28},{28,24},{24,16},{16,8},{8,0},{1,5},{5... | collective-permute-start | bytes 3538952 | tf_op jit(solution)/shard_map/ppermute | solution.py:183
  321.8 44.3 %collective-permute-start.13 = (bf16[6,768,128]{2,1,0:T(8,128)(2,1)}, bf16[6,768,128]{2,1,0:T(8,128)(2,1)}, u32[]{:S(2)}, u32[]{:S(2)}) collective-permute-start(bf16[6,768,128]{2,1,0:T(8,128)(2,1)} %collective-permute-done.12.w_ref), channel_id=1, source_target_pairs={{0,8},{4,0},{12,4},{20,12},{28,20},{24,28},{16,24},{8,16},{1,9},{5... | collective-permute-start | bytes 3538952 | tf_op jit(solution)/shard_map/ppermute | solution.py:184
  324.3 64.4 %collective-permute-start.22 = (bf16[1536,384]{1,0:T(8,128)(2,1)S(1)}, bf16[1536,384]{1,0:T(8,128)(2,1)}, u32[]{:S(2)}, u32[]{:S(2)}) collective-permute-start(bf16[1536,384]{1,0:T(8,128)(2,1)S(1)} %collective-permute-done.20.refs_2_.refs_6_), channel_id=1, source_target_pairs={{0,4},{8,12},{16,20},{24,28},{1,5},{9,13},{17,21},{25,29},{2,6},{1... | collective-permute-start | bytes 3538952 | tf_op jit(solution)/shard_map/ppermute | solution.py:209
  329.2 59.5 %collective-permute-start.23 = (bf16[1536,384]{1,0:T(8,128)(2,1)}, bf16[1536,384]{1,0:T(8,128)(2,1)}, u32[]{:S(2)}, u32[]{:S(2)}) collective-permute-start(bf16[1536,384]{1,0:T(8,128)(2,1)} %collective-permute-done.21), channel_id=1, source_target_pairs={{0,8},{8,16},{16,24},{24,0},{1,9},{9,17},{17,25},{25,1},{2,10},{10... | collective-permute-start | bytes 3538952 | tf_op jit(solution)/shard_map/ppermute | solution.py:211
  366.0 25.2 %collective-permute-start.18 = (bf16[6,384,128]{2,1,0:T(8,128)(2,1)S(1)}, bf16[6,384,128]{2,1,0:T(8,128)(2,1)}, u32[]{:S(2)}, u32[]{:S(2)}) collective-permute-start(bf16[6,384,128]{2,1,0:T(8,128)(2,1)S(1)} %slice.29), channel_id=1, source_target_pairs={{0,4},{4,12},{12,20},{20,28},{28,24},{24,16},{16,8},{8,0},{1,5},{5... | collective-permute-start | bytes 1769480 | tf_op jit(solution)/shard_map/ppermute | solution.py:193
  367.5 29.1 %collective-permute-start.14 = (bf16[6,384,128]{2,1,0:T(8,128)(2,1)S(1)}, bf16[6,384,128]{2,1,0:T(8,128)(2,1)}, u32[]{:S(2)}, u32[]{:S(2)}) collective-permute-start(bf16[6,384,128]{2,1,0:T(8,128)(2,1)S(1)} %slice.28), channel_id=1, source_target_pairs={{0,8},{4,0},{12,4},{20,12},{28,20},{24,28},{16,24},{8,16},{1,9},{5... | collective-permute-start | bytes 1769480 | tf_op jit(solution)/shard_map/ppermute | solution.py:194
  (10 other events, 763.4 us)

commit v12 on v10

--- a/solution.py
+++ b/solution.py
@@ -6,6 +6,7 @@
 from jax import lax
 from jax.experimental import pallas as pl
 from jax.experimental.pallas import tpu as pltpu
+from jax.experimental.layout import Layout, with_layout_constraint
 from jax.sharding import PartitionSpec as P
 
 REACH = 4
@@ -127,6 +128,8 @@
             flat = part.reshape(part.shape[0], -1)
             return jnp.dot(cols, flat, preferred_element_type=jnp.float32)
 
+        if head_major:
+            piece = with_layout_constraint(piece, Layout(major_to_minor=tuple(range(piece.ndim))))
         total = partial(me, piece, 0)
         going_cw = piece
         going_ccw = piece

time: 356 us -> 372 us (1.045)
  local copies, waits for them, and re-layouts: 18.6 us -> 33.2 us
  matrix products: 32.5 us -> 43.5 us
  waiting for transfers between devices: 241 us -> 232 us
    ppermute x0 -> x8, local copies, waits for them, and re-layouts: none -> 16.1 us  [the longest x3 6.33 us: ring_project(): going_ccw = lax.ppermute(going_ccw, 'ctx', counter)]
    ppermute x1, waiting for transfers between devices: 15.2 us -> 0.01 us  [earlier_blocks(): two_back_up = lax.ppermute(two_back, 'ctx', evens_up)]
    ppermute x6, waiting for transfers between devices: 59.4 us -> 71.4 us  [ring_project(): going_cw = lax.ppermute(going_cw, 'ctx', clockwise)]
    dot_general x9 -> x10, matrix products: 19.3 us -> 25.8 us  [partial(): jnp.einsum('tr,...rd->t...d', cols, part, preferred_element_type=jnp.floa...]
    ppermute x2, waiting for transfers between devices: 8.48 us -> 1.98 us  [ring_project(): last_cw = lax.ppermute(first, 'ctx', clockwise)]
    unnamed x9 -> x8, matrix products: 13.2 us -> 17.6 us
    unnamed x25 -> x28, local copies, waits for them, and re-layouts: 7.62 us -> 3.27 us
    ppermute x2, starting transfers between devices: 5.43 us -> 1.22 us  [ring_project(): last_ccw = lax.ppermute(second, 'ctx', counter)]
  transfers between devices with their start and end apart: 24 -> 24, of which waited for: 13 -> 10; matrix products, arithmetic and copies ran while one was open for 13% -> 20% of each run, Pallas kernels for 0% -> 0%
where the time goes in v12:
time: 372 us; the launch traced here: 370 us
  waiting for transfers between devices  232 us (62%)
  matrix products  43.5 us (12%)
  starting transfers between devices  35.5 us (10%)
  local copies, waits for them, and re-layouts  33.2 us (9%)
  between operations  9.39 us (3%)
  Pallas kernels  9.3 us (3%)
  other arithmetic  7.83 us (2%)
    ppermute x6, waiting for transfers between devices, ring_project(): going_ccw = lax.ppermute(going_ccw, 'ctx', counter)  128 us
    ppermute x6, waiting for transfers between devices, ring_project(): going_cw = lax.ppermute(going_cw, 'ctx', clockwise)  71.4 us
    dot_general x10, matrix products, partial(): jnp.einsum('tr,...rd->t...d', cols, part, preferred_element_type=jnp.floa...  25.8 us
    unnamed x8, matrix products  17.6 us
    ppermute x1, waiting for transfers between devices, earlier_blocks(): lax.ppermute(two_back, 'ctx', [(o, o - 1) for o in range(1, n, 2)])  16.3 us
    ppermute x6, starting transfers between devices, ring_project(): going_ccw = lax.ppermute(going_ccw, 'ctx', counter)  14.2 us
    pallas_call x1, Pallas kernels, windowed_attention(): pl.pallas_call(functools.partial(attention_kernel, scale, reach), out_sha...  9.3 us
    ppermute x2, waiting for transfers between devices, ring_project(): last_ccw = lax.ppermute(second, 'ctx', counter)  8.29 us
  transfers between devices with their start and end apart: 24, of which 10 were waited for; matrix products, arithmetic and copies ran while one was open for 20% of the time, Pallas kernels for 0%

profile of v12, /device:TPU:0, one launch (start us, length us, event | category | flops | bytes accessed | tf_op | source)
XLA Modules:
  0.0 370.4 jit_solution(977229388243810383)
XLA Ops:
  1.9 3.1 collective-permute-start.7
  5.0 51.2 %collective-permute-done.7 = bf16[2,6,768,128]{3,2,1,0:T(8,128)(2,1)S(1)} collective-permute-done((bf16[2,6,768,128]{3,2,1,0:T(8,128)(2,1)S(1)}, bf16[2,6,768,128]{3,2,1,0:T(8,128)(2,1)S(1)}, u32[]{:S(2)}, u32[]{:S(2)}) %collective-permute-start.7) | collective-permute-done | bytes 2359328 | tf_op jit(solution)/shard_map/ppermute | solution.py:138
  60.0 48.8 %collective-permute-done.8 = bf16[2,6,768,128]{3,2,1,0:T(8,128)(2,1)} collective-permute-done((bf16[2,6,768,128]{3,2,1,0:T(8,128)(2,1)S(1)}, bf16[2,6,768,128]{3,2,1,0:T(8,128)(2,1)}, u32[]{:S(2)}, u32[]{:S(2)}) %collective-permute-start.8) | collective-permute-done | bytes 2359328 | tf_op jit(solution)/shard_map/ppermute | solution.py:138
  132.7 27.7 %collective-permute-done.9 = bf16[2,6,768,128]{3,2,1,0:T(8,128)(2,1)S(1)} collective-permute-done((bf16[2,6,768,128]{3,2,1,0:T(8,128)(2,1)}, bf16[2,6,768,128]{3,2,1,0:T(8,128)(2,1)S(1)}, u32[]{:S(2)}, u32[]{:S(2)}) %collective-permute-start.9) | collective-permute-done | bytes 2359328 | tf_op jit(solution)/shard_map/ppermute | solution.py:138
  165.5 3.1 fusion.7
  168.6 4.6 %fusion.9 = f32[384,2,6,128]{0,3,2,1:T(8,128)} fusion(bf16[2,6,768,128]{3,2,1,0:T(8,128)(2,1)} %collective-permute-done.4, bf16[384,6144]{1,0:T(8,128)(2,1)S(1)} %constant_dynamic-update-slice_fusion, s32[]{:T(128)S(6)} %select_n.170), kind=kOutput, calls=%fused_computation.13 | convolution fusion | flops 905969664 | bytes 5308420 | tf_op jit(solution)/shard_map/tr,...rd->t...d/dot_general | solution.py:127
  173.2 4.6 %fusion.5 = f32[384,2,6,128]{0,3,2,1:T(8,128)} fusion(bf16[2,6,768,128]{3,2,1,0:T(8,128)(2,1)} %collective-permute-done.5, bf16[384,6144]{1,0:T(8,128)(2,1)S(1)} %constant_dynamic-update-slice_fusion, s32[]{:T(128)S(6)} %select_n.176), kind=kOutput, calls=%fused_computation.9 | convolution fusion | flops 905969664 | bytes 5308420 | tf_op jit(solution)/shard_map/tr,...rd->t...d/dot_general | solution.py:127
  177.7 8.3 %collective-permute-done.10 = bf16[2,6,384,128]{3,2,1,0:T(8,128)(2,1)S(1)} collective-permute-done((bf16[2,6,384,128]{3,2,1,0:T(8,128)(2,1)S(1)}, bf16[2,6,384,128]{3,2,1,0:T(8,128)(2,1)S(1)}, u32[]{:S(2)}, u32[]{:S(2)}) %collective-permute-start.10) | collective-permute-done | bytes 1179680 | tf_op jit(solution)/shard_map/ppermute | solution.py:148
  192.0 4.4 %add_convert_fusion = bf16[384,2,6,128]{0,3,2,1:T(8,128)(2,1)S(1)} fusion(f32[384,2,6,128]{0,3,2,1:T(8,128)S(1)} %fusion.38, f32[384,2,6,128]{0,3,2,1:T(8,128)S(1)} %fusion.40, f32[384,2,6,128]{0,3,2,1:T(8,128)} %fusion.5, f32[384,2,6,128]{0,3,2,1:T(8,128)S(1)} %fusion.7, f32[384,2,6,128]{0,3,2,1:T(8,128)} %fusion.9, f32[384,2,6,128]{0,3,2,1:T(8,128)S(1)} %fusion.11, ...), kind=kOutput, calls=%fused_computation | convolution fusion | flops 911278080 | bytes 23003140 | tf_op jit(solution)/shard_map/tr,...rd->t...d/dot_general | solution.py:127
  197.9 38.7 %collective-permute-done.11 = bf16[6,768,128]{2,1,0:T(8,128)(2,1)} collective-permute-done((bf16[6,768,128]{2,1,0:T(8,128)(2,1)S(1)}, bf16[6,768,128]{2,1,0:T(8,128)(2,1)}, u32[]{:S(2)}, u32[]{:S(2)}) %collective-permute-start.11) | collective-permute-done | bytes 1179680 | tf_op jit(solution)/shard_map/ppermute | solution.py:137
  236.6 4.2 %collective-permute-start.14 = (bf16[6,768,128]{2,1,0:T(8,128)(2,1)}, bf16[6,768,128]{2,1,0:T(8,128)(2,1)}, u32[]{:S(2)}, u32[]{:S(2)}) collective-permute-start(bf16[6,768,128]{2,1,0:T(8,128)(2,1)} %collective-permute-done.12), channel_id=1, source_target_pairs={{0,8},{4,0},{12,4},{20,12},{28,20},{24,28},{16,24},{8,16},{1,9},{5... | collective-permute-start | bytes 3538952 | tf_op jit(solution)/shard_map/ppermute | solution.py:138
  240.9 6.2 %collective-permute-done.20 = bf16[384,2,6,128]{0,3,2,1:T(8,128)(2,1)} collective-permute-done((bf16[384,2,6,128]{0,3,2,1:T(8,128)(2,1)S(1)}, bf16[384,2,6,128]{0,3,2,1:T(8,128)(2,1)}, u32[]{:S(2)}, u32[]{:S(2)}) %collective-permute-start.20) | collective-permute-done | bytes 1179680 | tf_op jit(solution)/shard_map/ppermute | solution.py:104
  248.3 6.6 %collective-permute-start.19 = (bf16[384,2,6,128]{0,3,2,1:T(8,128)(2,1)S(1)}, bf16[384,2,6,128]{0,3,2,1:T(8,128)(2,1)}, u32[]{:S(2)}, u32[]{:S(2)}) collective-permute-start(bf16[384,2,6,128]{0,3,2,1:T(8,128)(2,1)S(1)} %add_convert_fusion), channel_id=1, source_target_pairs={{0,4},{8,12},{16,20},{24,28},{1,5},{9,13},{17,21},{25,29},{2,6},{1... | collective-permute-start | bytes 3538952 | tf_op jit(solution)/shard_map/ppermute | solution.py:162
  264.2 2.8 collective-permute-done.13
  269.0 3.0 fusion
  273.6 16.3 %collective-permute-done.21 = bf16[384,2,6,128]{0,3,2,1:T(8,128)(2,1)} collective-permute-done((bf16[384,2,6,128]{0,3,2,1:T(8,128)(2,1)}, bf16[384,2,6,128]{0,3,2,1:T(8,128)(2,1)}, u32[]{:S(2)}, u32[]{:S(2)}) %collective-permute-start.21) | collective-permute-done | bytes 1179680 | tf_op jit(solution)/shard_map/ppermute | solution.py:164
  298.3 2.5 broadcast_select_fusion.1
  300.8 29.9 %collective-permute-done.15 = bf16[6,768,128]{2,1,0:T(8,128)(2,1)} collective-permute-done((bf16[6,768,128]{2,1,0:T(8,128)(2,1)}, bf16[6,768,128]{2,1,0:T(8,128)(2,1)}, u32[]{:S(2)}, u32[]{:S(2)}) %collective-permute-start.15) | collective-permute-done | bytes 1179680 | tf_op jit(solution)/shard_map/ppermute | solution.py:137
  332.7 2.5 collective-permute-start.17
  344.2 2.9 fusion.19
  347.1 2.4 broadcast_select_fusion
  351.6 2.7 fusion.46
  358.2 2.9 add_convert_fusion.1
  361.1 9.3 %shard_map.46 = bf16[6,384,128]{2,1,0:T(8,128)(2,1)} custom-call(bf16[768,384]{1,0:T(8,128)(2,1)} %bitcast.158, bf16[1536,384]{1,0:T(8,128)(2,1)} %bitcast.133, bf16[1536,384]{1,0:T(8,128)(2,1)} %bitcast.135, bf16[1536,384]{1,0:T(8,128)(2,1)} %bitcast.67.refs_2_.refs_6_, bf16[1536,384]{1,0:T(8,128)(2,1)} %bitcast.137, bf16[1536,384]{1,0:T(8,128)(2,1)} %bitcast.134, ...), custom_call_target="tpu_custom_call" | custom-call | flops 1811939328 | bytes 5898240 | tf_op jit(solution)/shard_map/pallas_call | solution.py:50
  (95 shorter events, 72.5 us)
Async XLA Ops:
  1.9 54.3 %collective-permute-start.7 = (bf16[2,6,768,128]{3,2,1,0:T(8,128)(2,1)S(1)}, bf16[2,6,768,128]{3,2,1,0:T(8,128)(2,1)S(1)}, u32[]{:S(2)}, u32[]{:S(2)}) collective-permute-start(bf16[2,6,768,128]{3,2,1,0:T(8,128)(2,1)S(1)} %slice.25), channel_id=1, source_target_pairs={{0,8},{4,0},{12,4},{20,12},{28,20},{24,28},{16,24},{8,16},{1,9},{5... | collective-permute-start | bytes 7077896 | tf_op jit(solution)/shard_map/ppermute | solution.py:138
  5.0 53.0 %collective-permute-start.3 = (bf16[2,6,768,128]{3,2,1,0:T(8,128)(2,1)S(1)}, bf16[2,6,768,128]{3,2,1,0:T(8,128)(2,1)S(1)}, u32[]{:S(2)}, u32[]{:S(2)}) collective-permute-start(bf16[2,6,768,128]{3,2,1,0:T(8,128)(2,1)S(1)} %slice.25), channel_id=1, source_target_pairs={{0,4},{4,12},{12,20},{20,28},{28,24},{24,16},{16,8},{8,0},{1,5},{5... | collective-permute-start | bytes 7077896 | tf_op jit(solution)/shard_map/ppermute | solution.py:137
  56.2 52.5 %collective-permute-start.8 = (bf16[2,6,768,128]{3,2,1,0:T(8,128)(2,1)S(1)}, bf16[2,6,768,128]{3,2,1,0:T(8,128)(2,1)}, u32[]{:S(2)}, u32[]{:S(2)}) collective-permute-start(bf16[2,6,768,128]{3,2,1,0:T(8,128)(2,1)S(1)} %collective-permute-done.7), channel_id=1, source_target_pairs={{0,8},{4,0},{12,4},{20,12},{28,20},{24,28},{16,24},{8,16},{1,9},{5... | collective-permute-start | bytes 7077896 | tf_op jit(solution)/shard_map/ppermute | solution.py:138
  58.0 52.2 %collective-permute-start.4 = (bf16[2,6,768,128]{3,2,1,0:T(8,128)(2,1)S(1)}, bf16[2,6,768,128]{3,2,1,0:T(8,128)(2,1)}, u32[]{:S(2)}, u32[]{:S(2)}) collective-permute-start(bf16[2,6,768,128]{3,2,1,0:T(8,128)(2,1)S(1)} %collective-permute-done.3), channel_id=1, source_target_pairs={{0,4},{4,12},{12,20},{20,28},{28,24},{24,16},{16,8},{8,0},{1,5},{5... | collective-permute-start | bytes 7077896 | tf_op jit(solution)/shard_map/ppermute | solution.py:137
  58.2 65.0 %collective-permute-start = (bf16[384,1536]{1,0:T(8,128)(2,1)S(1)}, bf16[384,1536]{1,0:T(8,128)(2,1)}, u32[]{:S(2)}, u32[]{:S(2)}) collective-permute-start(bf16[384,1536]{1,0:T(8,128)(2,1)S(1)} %copy-done.7), channel_id=1, source_target_pairs={{0,1},{1,2},{2,3},{3,0},{4,5},{5,6},{6,7},{7,4},{8,9},{9,10},{10,1... | collective-permute-start | bytes 3538952 | tf_op jit(solution)/shard_map/ppermute | solution.py:104
  58.2 66.8 %collective-permute-start.1 = (bf16[384,1536]{1,0:T(8,128)(2,1)S(1)}, bf16[384,1536]{1,0:T(8,128)(2,1)}, u32[]{:S(2)}, u32[]{:S(2)}) collective-permute-start(bf16[384,1536]{1,0:T(8,128)(2,1)S(1)} %copy-done.7), channel_id=1, source_target_pairs={{0,2},{1,3},{2,0},{3,1},{4,6},{5,7},{6,4},{7,5},{8,10},{9,11},{10,... | collective-permute-start | bytes 3538952 | tf_op jit(solution)/shard_map/ppermute | solution.py:104
  108.7 51.7 %collective-permute-start.9 = (bf16[2,6,768,128]{3,2,1,0:T(8,128)(2,1)}, bf16[2,6,768,128]{3,2,1,0:T(8,128)(2,1)S(1)}, u32[]{:S(2)}, u32[]{:S(2)}) collective-permute-start(bf16[2,6,768,128]{3,2,1,0:T(8,128)(2,1)} %collective-permute-done.8), channel_id=1, source_target_pairs={{0,8},{4,0},{12,4},{20,12},{28,20},{24,28},{16,24},{8,16},{1,9},{5... | collective-permute-start | bytes 7077896 | tf_op jit(solution)/shard_map/ppermute | solution.py:138
  110.2 51.5 %collective-permute-start.5 = (bf16[2,6,768,128]{3,2,1,0:T(8,128)(2,1)}, bf16[2,6,768,128]{3,2,1,0:T(8,128)(2,1)}, u32[]{:S(2)}, u32[]{:S(2)}) collective-permute-start(bf16[2,6,768,128]{3,2,1,0:T(8,128)(2,1)} %collective-permute-done.4), channel_id=1, source_target_pairs={{0,4},{4,12},{12,20},{20,28},{28,24},{24,16},{16,8},{8,0},{1,5},{5... | collective-permute-start | bytes 7077896 | tf_op jit(solution)/shard_map/ppermute | solution.py:137
  110.8 15.7 %collective-permute-start.2 = (bf16[384,1536]{1,0:T(8,128)(2,1)S(1)}, bf16[384,1536]{1,0:T(8,128)(2,1)}, u32[]{:S(2)}, u32[]{:S(2)}) collective-permute-start(bf16[384,1536]{1,0:T(8,128)(2,1)S(1)} %copy-done.7), channel_id=1, source_target_pairs={{0,3},{1,0},{2,1},{3,2},{4,7},{5,4},{6,5},{7,6},{8,11},{9,8},{10,9... | collective-permute-start | bytes 3538952 | tf_op jit(solution)/shard_map/ppermute | solution.py:104
  160.5 25.5 %collective-permute-start.10 = (bf16[2,6,384,128]{3,2,1,0:T(8,128)(2,1)S(1)}, bf16[2,6,384,128]{3,2,1,0:T(8,128)(2,1)S(1)}, u32[]{:S(2)}, u32[]{:S(2)}) collective-permute-start(bf16[2,6,384,128]{3,2,1,0:T(8,128)(2,1)S(1)} %slice.27), channel_id=1, source_target_pairs={{0,8},{4,0},{12,4},{20,12},{28,20},{24,28},{16,24},{8,16},{1,9},{5... | collective-permute-start | bytes 3538952 | tf_op jit(solution)/shard_map/ppermute | solution.py:148
  163.1 24.9 %collective-permute-start.6 = (bf16[2,6,384,128]{3,2,1,0:T(8,128)(2,1)S(1)}, bf16[2,6,384,128]{3,2,1,0:T(8,128)(2,1)S(1)}, u32[]{:S(2)}, u32[]{:S(2)}) collective-permute-start(bf16[2,6,384,128]{3,2,1,0:T(8,128)(2,1)S(1)} %slice.26), channel_id=1, source_target_pairs={{0,4},{4,12},{12,20},{20,28},{28,24},{24,16},{16,8},{8,0},{1,5},{5... | collective-permute-start | bytes 3538952 | tf_op jit(solution)/shard_map/ppermute | solution.py:147
  188.0 48.6 %collective-permute-start.12 = (bf16[6,768,128]{2,1,0:T(8,128)(2,1)S(1)}, bf16[6,768,128]{2,1,0:T(8,128)(2,1)}, u32[]{:S(2)}, u32[]{:S(2)}) collective-permute-start(bf16[6,768,128]{2,1,0:T(8,128)(2,1)S(1)} %slice_bitcast_fusion), channel_id=1, source_target_pairs={{0,8},{4,0},{12,4},{20,12},{28,20},{24,28},{16,24},{8,16},{1,9},{5... | collective-permute-start | bytes 3538952 | tf_op jit(solution)/shard_map/ppermute | solution.py:138
  189.6 47.0 %collective-permute-start.11 = (bf16[6,768,128]{2,1,0:T(8,128)(2,1)S(1)}, bf16[6,768,128]{2,1,0:T(8,128)(2,1)}, u32[]{:S(2)}, u32[]{:S(2)}) collective-permute-start(bf16[6,768,128]{2,1,0:T(8,128)(2,1)S(1)} %slice_bitcast_fusion), channel_id=1, source_target_pairs={{0,4},{4,12},{12,20},{20,28},{28,24},{24,16},{16,8},{8,0},{1,5},{5... | collective-permute-start | bytes 3538952 | tf_op jit(solution)/shard_map/ppermute | solution.py:137
  196.3 50.7 %collective-permute-start.20 = (bf16[384,2,6,128]{0,3,2,1:T(8,128)(2,1)S(1)}, bf16[384,2,6,128]{0,3,2,1:T(8,128)(2,1)}, u32[]{:S(2)}, u32[]{:S(2)}) collective-permute-start(bf16[384,2,6,128]{0,3,2,1:T(8,128)(2,1)S(1)} %add_convert_fusion), channel_id=1, source_target_pairs={{0,8},{4,12},{8,16},{12,20},{16,24},{20,28},{24,0},{28,4},{1,9},{5... | collective-permute-start | bytes 3538952 | tf_op jit(solution)/shard_map/ppermute | solution.py:104
  236.6 30.4 %collective-permute-start.13 = (bf16[6,768,128]{2,1,0:T(8,128)(2,1)}, bf16[6,768,128]{2,1,0:T(8,128)(2,1)}, u32[]{:S(2)}, u32[]{:S(2)}) collective-permute-start(bf16[6,768,128]{2,1,0:T(8,128)(2,1)} %collective-permute-done.11), channel_id=1, source_target_pairs={{0,4},{4,12},{12,20},{20,28},{28,24},{24,16},{16,8},{8,0},{1,5},{5... | collective-permute-start | bytes 3538952 | tf_op jit(solution)/shard_map/ppermute | solution.py:137
  236.6 30.4 %collective-permute-start.14 = (bf16[6,768,128]{2,1,0:T(8,128)(2,1)}, bf16[6,768,128]{2,1,0:T(8,128)(2,1)}, u32[]{:S(2)}, u32[]{:S(2)}) collective-permute-start(bf16[6,768,128]{2,1,0:T(8,128)(2,1)} %collective-permute-done.12), channel_id=1, source_target_pairs={{0,8},{4,0},{12,4},{20,12},{28,20},{24,28},{16,24},{8,16},{1,9},{5... | collective-permute-start | bytes 3538952 | tf_op jit(solution)/shard_map/ppermute | solution.py:138
  247.0 42.9 %collective-permute-start.21 = (bf16[384,2,6,128]{0,3,2,1:T(8,128)(2,1)}, bf16[384,2,6,128]{0,3,2,1:T(8,128)(2,1)}, u32[]{:S(2)}, u32[]{:S(2)}) collective-permute-start(bf16[384,2,6,128]{0,3,2,1:T(8,128)(2,1)} %collective-permute-done.20), channel_id=1, source_target_pairs={{4,0},{12,8},{20,16},{28,24},{5,1},{13,9},{21,17},{29,25},{6,2},{1... | collective-permute-start | bytes 3538952 | tf_op jit(solution)/shard_map/ppermute | solution.py:164
  248.3 50.0 %collective-permute-start.19 = (bf16[384,2,6,128]{0,3,2,1:T(8,128)(2,1)S(1)}, bf16[384,2,6,128]{0,3,2,1:T(8,128)(2,1)}, u32[]{:S(2)}, u32[]{:S(2)}) collective-permute-start(bf16[384,2,6,128]{0,3,2,1:T(8,128)(2,1)S(1)} %add_convert_fusion), channel_id=1, source_target_pairs={{0,4},{8,12},{16,20},{24,28},{1,5},{9,13},{17,21},{25,29},{2,6},{1... | collective-permute-start | bytes 3538952 | tf_op jit(solution)/shard_map/ppermute | solution.py:162
  254.9 92.2 %collective-permute-start.22 = (bf16[384,2,6,128]{0,3,2,1:T(8,128)(2,1)}, bf16[384,2,6,128]{0,3,2,1:T(8,128)(2,1)}, u32[]{:S(2)}, u32[]{:S(2)}) collective-permute-start(bf16[384,2,6,128]{0,3,2,1:T(8,128)(2,1)} %collective-permute-done.20), channel_id=1, source_target_pairs={{0,4},{8,12},{16,20},{24,28},{1,5},{9,13},{17,21},{25,29},{2,6},{1... | collective-permute-start | bytes 3538952 | tf_op jit(solution)/shard_map/ppermute | solution.py:163
  267.0 63.8 %collective-permute-start.15 = (bf16[6,768,128]{2,1,0:T(8,128)(2,1)}, bf16[6,768,128]{2,1,0:T(8,128)(2,1)}, u32[]{:S(2)}, u32[]{:S(2)}) collective-permute-start(bf16[6,768,128]{2,1,0:T(8,128)(2,1)} %collective-permute-done.13), channel_id=1, source_target_pairs={{0,4},{4,12},{12,20},{20,28},{28,24},{24,16},{16,8},{8,0},{1,5},{5... | collective-permute-start | bytes 3538952 | tf_op jit(solution)/shard_map/ppermute | solution.py:137
  267.0 68.2 %collective-permute-start.16 = (bf16[6,768,128]{2,1,0:T(8,128)(2,1)}, bf16[6,768,128]{2,1,0:T(8,128)(2,1)}, u32[]{:S(2)}, u32[]{:S(2)}) collective-permute-start(bf16[6,768,128]{2,1,0:T(8,128)(2,1)} %collective-permute-done.14), channel_id=1, source_target_pairs={{0,8},{4,0},{12,4},{20,12},{28,20},{24,28},{16,24},{8,16},{1,9},{5... | collective-permute-start | bytes 3538952 | tf_op jit(solution)/shard_map/ppermute | solution.py:138
  289.9 57.2 %collective-permute-start.23 = (bf16[384,2,6,128]{0,3,2,1:T(8,128)(2,1)}, bf16[384,2,6,128]{0,3,2,1:T(8,128)(2,1)}, u32[]{:S(2)}, u32[]{:S(2)}) collective-permute-start(bf16[384,2,6,128]{0,3,2,1:T(8,128)(2,1)} %collective-permute-done.21), channel_id=1, source_target_pairs={{0,8},{8,16},{16,24},{24,0},{1,9},{9,17},{17,25},{25,1},{2,10},{10... | collective-permute-start | bytes 3538952 | tf_op jit(solution)/shard_map/ppermute | solution.py:165
  332.7 16.8 %collective-permute-start.17 = (bf16[6,384,128]{2,1,0:T(8,128)(2,1)}, bf16[6,384,128]{2,1,0:T(8,128)(2,1)}, u32[]{:S(2)}, u32[]{:S(2)}) collective-permute-start(bf16[6,384,128]{2,1,0:T(8,128)(2,1)} %slice.28), channel_id=1, source_target_pairs={{0,4},{4,12},{12,20},{20,28},{28,24},{24,16},{16,8},{8,0},{1,5},{5... | collective-permute-start | bytes 1769480 | tf_op jit(solution)/shard_map/ppermute | solution.py:147
  337.1 17.2 %collective-permute-start.18 = (bf16[6,384,128]{2,1,0:T(8,128)(2,1)}, bf16[6,384,128]{2,1,0:T(8,128)(2,1)}, u32[]{:S(2)}, u32[]{:S(2)}) collective-permute-start(bf16[6,384,128]{2,1,0:T(8,128)(2,1)} %slice.29), channel_id=1, source_target_pairs={{0,8},{4,0},{12,4},{20,12},{28,20},{24,28},{16,24},{8,16},{1,9},{5... | collective-permute-start | bytes 1769480 | tf_op jit(solution)/shard_map/ppermute | solution.py:148
  (14 other events, 635.8 us)

commit v13 on v10

--- a/solution.py
+++ b/solution.py
@@ -11,26 +11,28 @@
 REACH = 4
 
 
-def attention_kernel(scale, reach, q_ref, *refs):
+def attention_kernel(scale, reach, per_step, size, q_ref, *refs):
     k_refs = refs[:reach]
     v_refs = refs[reach : 2 * reach]
     o_ref = refs[2 * reach]
-    q = q_ref[...].T
-    scores = [jnp.dot(q, k_ref[...], preferred_element_type=jnp.float32) * scale for k_ref in k_refs]
-    top = scores[0].max(axis=-1, keepdims=True)
-    for s in scores[1:]:
-        top = jnp.maximum(top, s.max(axis=-1, keepdims=True))
-    expos = [jnp.exp(s - top) for s in scores]
-    totals = expos[0].sum(axis=-1, keepdims=True)
-    for e in expos[1:]:
-        totals = totals + e.sum(axis=-1, keepdims=True)
-    mixed = None
-    for e, v_ref in zip(expos, v_refs):
-        term = lax.dot_general(
-            e.astype(jnp.bfloat16), v_ref[...], (((1,), (1,)), ((), ())), preferred_element_type=jnp.float32
-        )
-        mixed = term if mixed is None else mixed + term
-    o_ref[0] = (mixed / totals).astype(o_ref.dtype)
+    for head in range(per_step):
+        rows = slice(head * size, (head + 1) * size)
+        q = q_ref[rows, :].T
+        scores = [jnp.dot(q, k_ref[rows, :], preferred_element_type=jnp.float32) * scale for k_ref in k_refs]
+        top = scores[0].max(axis=-1, keepdims=True)
+        for s in scores[1:]:
+            top = jnp.maximum(top, s.max(axis=-1, keepdims=True))
+        expos = [jnp.exp(s - top) for s in scores]
+        totals = expos[0].sum(axis=-1, keepdims=True)
+        for e in expos[1:]:
+            totals = totals + e.sum(axis=-1, keepdims=True)
+        mixed = None
+        for e, v_ref in zip(expos, v_refs):
+            term = lax.dot_general(
+                e.astype(jnp.bfloat16), v_ref[rows, :], (((1,), (1,)), ((), ())), preferred_element_type=jnp.float32
+            )
+            mixed = term if mixed is None else mixed + term
+        o_ref[head] = (mixed / totals).astype(o_ref.dtype)
 
 
 def windowed_attention(queries, blocks, scale):
@@ -38,8 +40,10 @@
     reach = len(blocks)
     q_t = queries.reshape(rows, heads * size).T
     kv_t = [block.reshape(rows, 2 * heads * size).T for block in blocks]
-    q_spec = pl.BlockSpec((size, rows), lambda h: (h, 0))
-    v_spec = pl.BlockSpec((size, rows), lambda h: (h + heads, 0))
+    per_step = 2 if heads % 2 == 0 else 1
+    steps = heads // per_step
+    q_spec = pl.BlockSpec((per_step * size, rows), lambda h: (h, 0))
+    v_spec = pl.BlockSpec((per_step * size, rows), lambda h: (h + steps, 0))
     keys = rows * reach
     cost = pl.CostEstimate(
         flops=4 * rows * keys * size * heads,
@@ -47,11 +51,11 @@
         bytes_accessed=2 * (2 * rows * heads * size + 2 * keys * heads * size),
     )
     out = pl.pallas_call(
-        functools.partial(attention_kernel, scale, reach),
+        functools.partial(attention_kernel, scale, reach, per_step, size),
         out_shape=jax.ShapeDtypeStruct((heads, rows, size), jnp.bfloat16),
-        grid=(heads,),
+        grid=(steps,),
         in_specs=[q_spec] + [q_spec] * reach + [v_spec] * reach,
-        out_specs=pl.BlockSpec((1, rows, size), lambda h: (h, 0, 0)),
+        out_specs=pl.BlockSpec((per_step, rows, size), lambda h: (h, 0, 0)),
         cost_estimate=cost,
     )(q_t, *kv_t, *kv_t)
     return jnp.transpose(out, (1, 0, 2))

time: 356 us -> 355 us (level)
  no operation moved by 1% of the time
where the time goes in v13:
time: 355 us; the launch traced here: 354 us
  waiting for transfers between devices  241 us (68%)
  starting transfers between devices  38.5 us (11%)
  matrix products  32.5 us (9%)
  local copies, waits for them, and re-layouts  18.6 us (5%)
  between operations  9.51 us (3%)
  Pallas kernels  8.87 us (2%)
  other arithmetic  5.31 us (1%)
    ppermute x6, waiting for transfers between devices, ring_project(): going_ccw = lax.ppermute(going_ccw, 'ctx', counter)  125 us
    ppermute x6, waiting for transfers between devices, ring_project(): going_cw = lax.ppermute(going_cw, 'ctx', clockwise)  59.4 us
    dot_general x9, matrix products, partial(): jnp.einsum('tr,...rd->t...d', cols, part, preferred_element_type=jnp.floa...  19.3 us
    ppermute x1, waiting for transfers between devices, earlier_blocks(): lax.ppermute(two_back, 'ctx', [(o, o - 1) for o in range(1, n, 2)])  16.5 us
    ppermute x1, waiting for transfers between devices, earlier_blocks(): two_back_up = lax.ppermute(two_back, 'ctx', evens_up)  15 us
    unnamed x9, matrix products  13.2 us
    ppermute x6, starting transfers between devices, ring_project(): going_ccw = lax.ppermute(going_ccw, 'ctx', counter)  13.1 us
    ppermute x2, waiting for transfers between devices, ring_project(): last_ccw = lax.ppermute(second, 'ctx', counter)  11.1 us
  transfers between devices with their start and end apart: 24, of which 13 were waited for; matrix products, arithmetic and copies ran while one was open for 13% of the time, Pallas kernels for 0%

profile of v13, /device:TPU:0, one launch (start us, length us, event | category | flops | bytes accessed | tf_op | source)
XLA Modules:
  0.0 354.2 jit_solution(5373988961733528206)
XLA Ops:
  0.0 4.3 %copy.5 = bf16[768,3,6,128]{0,3,2,1:T(8,128)(2,1)S(1)} copy(bf16[768,3,6,128]{3,0,2,1:T(8,128)(2,1)} %param.5) | data formatting | bytes 7077888 | tf_op args[1]
  4.5 3.1 collective-permute-start.7
  7.6 51.2 %collective-permute-done.7 = bf16[2,6,768,128]{2,3,1,0:T(8,128)(2,1)S(1)} collective-permute-done((bf16[2,6,768,128]{2,3,1,0:T(8,128)(2,1)S(1)}, bf16[2,6,768,128]{2,3,1,0:T(8,128)(2,1)S(1)}, u32[]{:S(2)}, u32[]{:S(2)}) %collective-permute-start.7) | collective-permute-done | bytes 2359328 | tf_op jit(solution)/shard_map/ppermute | solution.py:139
  64.1 47.2 %collective-permute-done.8 = bf16[2,6,768,128]{2,3,1,0:T(8,128)(2,1)} collective-permute-done((bf16[2,6,768,128]{2,3,1,0:T(8,128)(2,1)S(1)}, bf16[2,6,768,128]{2,3,1,0:T(8,128)(2,1)}, u32[]{:S(2)}, u32[]{:S(2)}) %collective-permute-start.8) | collective-permute-done | bytes 2359328 | tf_op jit(solution)/shard_map/ppermute | solution.py:139
  136.6 26.5 %collective-permute-done.9 = bf16[2,6,768,128]{2,3,1,0:T(8,128)(2,1)} collective-permute-done((bf16[2,6,768,128]{2,3,1,0:T(8,128)(2,1)}, bf16[2,6,768,128]{2,3,1,0:T(8,128)(2,1)}, u32[]{:S(2)}, u32[]{:S(2)}) %collective-permute-start.9) | collective-permute-done | bytes 2359328 | tf_op jit(solution)/shard_map/ppermute | solution.py:139
  169.5 3.1 fusion.6
  172.6 3.1 fusion.8
  175.7 3.1 fusion.4
  178.8 11.1 %collective-permute-done.10 = bf16[2,6,384,128]{2,3,1,0:T(8,128)(2,1)S(1)} collective-permute-done((bf16[2,6,384,128]{2,3,1,0:T(8,128)(2,1)S(1)}, bf16[2,6,384,128]{2,3,1,0:T(8,128)(2,1)S(1)}, u32[]{:S(2)}, u32[]{:S(2)}) %collective-permute-start.10) | collective-permute-done | bytes 1179680 | tf_op jit(solution)/shard_map/ppermute | solution.py:149
  189.9 3.4 collective-permute-done.6
  197.2 4.0 %add_convert_fusion = bf16[384,2,6,128]{0,3,2,1:T(8,128)(2,1)S(1)} fusion(f32[384,2,6,128]{0,3,2,1:T(8,128)S(1)} %fusion.37, f32[384,2,6,128]{0,3,2,1:T(8,128)S(1)} %fusion.39, f32[384,2,6,128]{0,3,2,1:T(8,128)S(1)} %fusion.4, f32[384,2,6,128]{0,3,2,1:T(8,128)S(1)} %fusion.6, f32[384,2,6,128]{0,3,2,1:T(8,128)S(1)} %fusion.8, ...), kind=kOutput, calls=%fused_computation | convolution fusion | flops 911278080 | bytes 23003140 | tf_op jit(solution)/shard_map/tr,...rd->t...d/dot_general | solution.py:130
  202.8 37.5 %collective-permute-done.11 = bf16[6,768,128]{1,2,0:T(8,128)(2,1)} collective-permute-done((bf16[6,768,128]{1,2,0:T(8,128)(2,1)S(1)}, bf16[6,768,128]{1,2,0:T(8,128)(2,1)}, u32[]{:S(2)}, u32[]{:S(2)}) %collective-permute-start.11) | collective-permute-done | bytes 1179680 | tf_op jit(solution)/shard_map/ppermute | solution.py:138
  240.3 3.6 %collective-permute-start.14 = (bf16[6,768,128]{1,2,0:T(8,128)(2,1)}, bf16[6,768,128]{1,2,0:T(8,128)(2,1)}, u32[]{:S(2)}, u32[]{:S(2)}) collective-permute-start(bf16[6,768,128]{1,2,0:T(8,128)(2,1)} %collective-permute-done.12), channel_id=1, source_target_pairs={{0,8},{4,0},{12,4},{20,12},{28,20},{24,28},{16,24},{8,16},{1,9},{5... | collective-permute-start | bytes 3538952 | tf_op jit(solution)/shard_map/ppermute | solution.py:139
  243.9 5.6 %collective-permute-done.20 = bf16[384,2,6,128]{0,3,2,1:T(8,128)(2,1)S(1)} collective-permute-done((bf16[384,2,6,128]{0,3,2,1:T(8,128)(2,1)S(1)}, bf16[384,2,6,128]{0,3,2,1:T(8,128)(2,1)S(1)}, u32[]{:S(2)}, u32[]{:S(2)}) %collective-permute-start.20) | collective-permute-done | bytes 1179680 | tf_op jit(solution)/shard_map/ppermute | solution.py:107
  250.9 5.7 %collective-permute-start.19 = (bf16[384,2,6,128]{0,3,2,1:T(8,128)(2,1)S(1)}, bf16[384,2,6,128]{0,3,2,1:T(8,128)(2,1)S(1)}, u32[]{:S(2)}, u32[]{:S(2)}) collective-permute-start(bf16[384,2,6,128]{0,3,2,1:T(8,128)(2,1)S(1)} %add_convert_fusion), channel_id=1, source_target_pairs={{0,4},{8,12},{16,20},{24,28},{1,5},{9,13},{17,21},{25,29},{2,6},{1... | collective-permute-start | bytes 3538952 | tf_op jit(solution)/shard_map/ppermute | solution.py:163
  258.6 11.3 %collective-permute-done.13 = bf16[6,768,128]{1,2,0:T(8,128)(2,1)} collective-permute-done((bf16[6,768,128]{1,2,0:T(8,128)(2,1)}, bf16[6,768,128]{1,2,0:T(8,128)(2,1)}, u32[]{:S(2)}, u32[]{:S(2)}) %collective-permute-start.13) | collective-permute-done | bytes 1179680 | tf_op jit(solution)/shard_map/ppermute | solution.py:138
  278.2 16.5 %collective-permute-done.21 = bf16[384,2,6,128]{0,3,2,1:T(8,128)(2,1)} collective-permute-done((bf16[384,2,6,128]{0,3,2,1:T(8,128)(2,1)S(1)}, bf16[384,2,6,128]{0,3,2,1:T(8,128)(2,1)}, u32[]{:S(2)}, u32[]{:S(2)}) %collective-permute-start.21) | collective-permute-done | bytes 1179680 | tf_op jit(solution)/shard_map/ppermute | solution.py:165
  300.8 2.5 broadcast_select_fusion.1
  303.3 9.5 %collective-permute-done.15 = bf16[6,768,128]{1,2,0:T(8,128)(2,1)S(1)} collective-permute-done((bf16[6,768,128]{1,2,0:T(8,128)(2,1)}, bf16[6,768,128]{1,2,0:T(8,128)(2,1)S(1)}, u32[]{:S(2)}, u32[]{:S(2)}) %collective-permute-start.15) | collective-permute-done | bytes 1179680 | tf_op jit(solution)/shard_map/ppermute | solution.py:138
  312.9 2.4 collective-permute-start.17
  315.4 4.4 %collective-permute-start.18 = (bf16[6,384,128]{1,2,0:T(8,128)(2,1)S(1)}, bf16[6,384,128]{1,2,0:T(8,128)(2,1)S(1)}, u32[]{:S(2)}, u32[]{:S(2)}) collective-permute-start(bf16[6,384,128]{1,2,0:T(8,128)(2,1)S(1)} %slice.29), channel_id=1, source_target_pairs={{0,8},{4,0},{12,4},{20,12},{28,20},{24,28},{16,24},{8,16},{1,9},{5... | collective-permute-start | bytes 1769480 | tf_op jit(solution)/shard_map/ppermute | solution.py:149
  321.4 15.0 %collective-permute-done.22 = bf16[384,2,6,128]{0,3,2,1:T(8,128)(2,1)S(1)} collective-permute-done((bf16[384,2,6,128]{0,3,2,1:T(8,128)(2,1)S(1)}, bf16[384,2,6,128]{0,3,2,1:T(8,128)(2,1)S(1)}, u32[]{:S(2)}, u32[]{:S(2)}) %collective-permute-start.22) | collective-permute-done | bytes 1179680 | tf_op jit(solution)/shard_map/ppermute | solution.py:164
  337.7 5.0 %collective-permute-done.17 = bf16[6,384,128]{1,2,0:T(8,128)(2,1)S(1)} collective-permute-done((bf16[6,384,128]{1,2,0:T(8,128)(2,1)S(1)}, bf16[6,384,128]{1,2,0:T(8,128)(2,1)S(1)}, u32[]{:S(2)}, u32[]{:S(2)}) %collective-permute-start.17) | collective-permute-done | bytes 589856 | tf_op jit(solution)/shard_map/ppermute | solution.py:148
  345.4 8.9 %shard_map.46 = bf16[6,384,128]{2,1,0:T(8,128)(2,1)} custom-call(bf16[768,384]{1,0:T(8,128)(2,1)} %bitcast.156, bf16[1536,384]{1,0:T(8,128)(2,1)} %bitcast.136, bf16[1536,384]{1,0:T(8,128)(2,1)} %bitcast.138, bf16[1536,384]{1,0:T(8,128)(2,1)} %bitcast.152, bf16[1536,384]{1,0:T(8,128)(2,1)} %bitcast.140, bf16[1536,384]{1,0:T(8,128)(2,1)} %bitcast.137, ...), custom_call_target="tpu_custom_call" | custom-call | flops 1811939328 | bytes 5898240 | tf_op jit(solution)/shard_map/pallas_call | solution.py:53
  (84 shorter events, 56.8 us)
Async XLA Ops:
  4.5 54.3 %collective-permute-start.7 = (bf16[2,6,768,128]{2,3,1,0:T(8,128)(2,1)S(1)}, bf16[2,6,768,128]{2,3,1,0:T(8,128)(2,1)S(1)}, u32[]{:S(2)}, u32[]{:S(2)}) collective-permute-start(bf16[2,6,768,128]{2,3,1,0:T(8,128)(2,1)S(1)} %slice.25), channel_id=1, source_target_pairs={{0,8},{4,0},{12,4},{20,12},{28,20},{24,28},{16,24},{8,16},{1,9},{5... | collective-permute-start | bytes 7077896 | tf_op jit(solution)/shard_map/ppermute | solution.py:139
  7.5 53.0 %collective-permute-start.3 = (bf16[2,6,768,128]{2,3,1,0:T(8,128)(2,1)S(1)}, bf16[2,6,768,128]{2,3,1,0:T(8,128)(2,1)S(1)}, u32[]{:S(2)}, u32[]{:S(2)}) collective-permute-start(bf16[2,6,768,128]{2,3,1,0:T(8,128)(2,1)S(1)} %slice.25), channel_id=1, source_target_pairs={{0,4},{4,12},{12,20},{20,28},{28,24},{24,16},{16,8},{8,0},{1,5},{5... | collective-permute-start | bytes 7077896 | tf_op jit(solution)/shard_map/ppermute | solution.py:138
  58.7 52.5 %collective-permute-start.8 = (bf16[2,6,768,128]{2,3,1,0:T(8,128)(2,1)S(1)}, bf16[2,6,768,128]{2,3,1,0:T(8,128)(2,1)}, u32[]{:S(2)}, u32[]{:S(2)}) collective-permute-start(bf16[2,6,768,128]{2,3,1,0:T(8,128)(2,1)S(1)} %collective-permute-done.7), channel_id=1, source_target_pairs={{0,8},{4,0},{12,4},{20,12},{28,20},{24,28},{16,24},{8,16},{1,9},{5... | collective-permute-start | bytes 7077896 | tf_op jit(solution)/shard_map/ppermute | solution.py:139
  61.9 51.9 %collective-permute-start.4 = (bf16[2,6,768,128]{2,3,1,0:T(8,128)(2,1)S(1)}, bf16[2,6,768,128]{2,3,1,0:T(8,128)(2,1)}, u32[]{:S(2)}, u32[]{:S(2)}) collective-permute-start(bf16[2,6,768,128]{2,3,1,0:T(8,128)(2,1)S(1)} %collective-permute-done.3), channel_id=1, source_target_pairs={{0,4},{4,12},{12,20},{20,28},{28,24},{24,16},{16,8},{8,0},{1,5},{5... | collective-permute-start | bytes 7077896 | tf_op jit(solution)/shard_map/ppermute | solution.py:138
  62.3 64.8 %collective-permute-start = (bf16[384,1536]{1,0:T(8,128)(2,1)}, bf16[384,1536]{1,0:T(8,128)(2,1)}, u32[]{:S(2)}, u32[]{:S(2)}) collective-permute-start(bf16[384,1536]{1,0:T(8,128)(2,1)} %param.4), channel_id=1, source_target_pairs={{0,1},{1,2},{2,3},{3,0},{4,5},{5,6},{6,7},{7,4},{8,9},{9,10},{10,1... | collective-permute-start | bytes 3538952 | tf_op jit(solution)/shard_map/ppermute | solution.py:107
  62.4 66.6 %collective-permute-start.1 = (bf16[384,1536]{1,0:T(8,128)(2,1)}, bf16[384,1536]{1,0:T(8,128)(2,1)}, u32[]{:S(2)}, u32[]{:S(2)}) collective-permute-start(bf16[384,1536]{1,0:T(8,128)(2,1)} %param.4), channel_id=1, source_target_pairs={{0,2},{1,3},{2,0},{3,1},{4,6},{5,7},{6,4},{7,5},{8,10},{9,11},{10,... | collective-permute-start | bytes 3538952 | tf_op jit(solution)/shard_map/ppermute | solution.py:107
  111.3 51.8 %collective-permute-start.9 = (bf16[2,6,768,128]{2,3,1,0:T(8,128)(2,1)}, bf16[2,6,768,128]{2,3,1,0:T(8,128)(2,1)}, u32[]{:S(2)}, u32[]{:S(2)}) collective-permute-start(bf16[2,6,768,128]{2,3,1,0:T(8,128)(2,1)} %collective-permute-done.8), channel_id=1, source_target_pairs={{0,8},{4,0},{12,4},{20,12},{28,20},{24,28},{16,24},{8,16},{1,9},{5... | collective-permute-start | bytes 7077896 | tf_op jit(solution)/shard_map/ppermute | solution.py:139
  113.9 51.9 %collective-permute-start.5 = (bf16[2,6,768,128]{2,3,1,0:T(8,128)(2,1)}, bf16[2,6,768,128]{2,3,1,0:T(8,128)(2,1)}, u32[]{:S(2)}, u32[]{:S(2)}) collective-permute-start(bf16[2,6,768,128]{2,3,1,0:T(8,128)(2,1)} %collective-permute-done.4), channel_id=1, source_target_pairs={{0,4},{4,12},{12,20},{20,28},{28,24},{24,16},{16,8},{8,0},{1,5},{5... | collective-permute-start | bytes 7077896 | tf_op jit(solution)/shard_map/ppermute | solution.py:138
  114.6 15.7 %collective-permute-start.2 = (bf16[384,1536]{1,0:T(8,128)(2,1)}, bf16[384,1536]{1,0:T(8,128)(2,1)}, u32[]{:S(2)}, u32[]{:S(2)}) collective-permute-start(bf16[384,1536]{1,0:T(8,128)(2,1)} %param.4), channel_id=1, source_target_pairs={{0,3},{1,0},{2,1},{3,2},{4,7},{5,4},{6,5},{7,6},{8,11},{9,8},{10,9... | collective-permute-start | bytes 3538952 | tf_op jit(solution)/shard_map/ppermute | solution.py:107
  164.5 25.4 %collective-permute-start.10 = (bf16[2,6,384,128]{2,3,1,0:T(8,128)(2,1)S(1)}, bf16[2,6,384,128]{2,3,1,0:T(8,128)(2,1)S(1)}, u32[]{:S(2)}, u32[]{:S(2)}) collective-permute-start(bf16[2,6,384,128]{2,3,1,0:T(8,128)(2,1)S(1)} %slice.27), channel_id=1, source_target_pairs={{0,8},{4,0},{12,4},{20,12},{28,20},{24,28},{16,24},{8,16},{1,9},{5... | collective-permute-start | bytes 3538952 | tf_op jit(solution)/shard_map/ppermute | solution.py:149
  167.1 26.2 %collective-permute-start.6 = (bf16[2,6,384,128]{2,3,1,0:T(8,128)(2,1)S(1)}, bf16[2,6,384,128]{2,3,1,0:T(8,128)(2,1)S(1)}, u32[]{:S(2)}, u32[]{:S(2)}) collective-permute-start(bf16[2,6,384,128]{2,3,1,0:T(8,128)(2,1)S(1)} %slice.26), channel_id=1, source_target_pairs={{0,4},{4,12},{12,20},{20,28},{28,24},{24,16},{16,8},{8,0},{1,5},{5... | collective-permute-start | bytes 3538952 | tf_op jit(solution)/shard_map/ppermute | solution.py:148
  193.3 47.0 %collective-permute-start.11 = (bf16[6,768,128]{1,2,0:T(8,128)(2,1)S(1)}, bf16[6,768,128]{1,2,0:T(8,128)(2,1)}, u32[]{:S(2)}, u32[]{:S(2)}) collective-permute-start(bf16[6,768,128]{1,2,0:T(8,128)(2,1)S(1)} %slice_bitcast_fusion), channel_id=1, source_target_pairs={{0,4},{4,12},{12,20},{20,28},{28,24},{24,16},{16,8},{8,0},{1,5},{5... | collective-permute-start | bytes 3538952 | tf_op jit(solution)/shard_map/ppermute | solution.py:138
  194.2 46.2 %collective-permute-start.12 = (bf16[6,768,128]{1,2,0:T(8,128)(2,1)S(1)}, bf16[6,768,128]{1,2,0:T(8,128)(2,1)}, u32[]{:S(2)}, u32[]{:S(2)}) collective-permute-start(bf16[6,768,128]{1,2,0:T(8,128)(2,1)S(1)} %slice_bitcast_fusion), channel_id=1, source_target_pairs={{0,8},{4,0},{12,4},{20,12},{28,20},{24,28},{16,24},{8,16},{1,9},{5... | collective-permute-start | bytes 3538952 | tf_op jit(solution)/shard_map/ppermute | solution.py:139
  201.2 48.4 %collective-permute-start.20 = (bf16[384,2,6,128]{0,3,2,1:T(8,128)(2,1)S(1)}, bf16[384,2,6,128]{0,3,2,1:T(8,128)(2,1)S(1)}, u32[]{:S(2)}, u32[]{:S(2)}) collective-permute-start(bf16[384,2,6,128]{0,3,2,1:T(8,128)(2,1)S(1)} %add_convert_fusion), channel_id=1, source_target_pairs={{0,8},{4,12},{8,16},{12,20},{16,24},{20,28},{24,0},{28,4},{1,9},{5... | collective-permute-start | bytes 3538952 | tf_op jit(solution)/shard_map/ppermute | solution.py:107
  240.3 29.5 %collective-permute-start.13 = (bf16[6,768,128]{1,2,0:T(8,128)(2,1)}, bf16[6,768,128]{1,2,0:T(8,128)(2,1)}, u32[]{:S(2)}, u32[]{:S(2)}) collective-permute-start(bf16[6,768,128]{1,2,0:T(8,128)(2,1)} %collective-permute-done.11), channel_id=1, source_target_pairs={{0,4},{4,12},{12,20},{20,28},{28,24},{24,16},{16,8},{8,0},{1,5},{5... | collective-permute-start | bytes 3538952 | tf_op jit(solution)/shard_map/ppermute | solution.py:138
  240.3 29.5 %collective-permute-start.14 = (bf16[6,768,128]{1,2,0:T(8,128)(2,1)}, bf16[6,768,128]{1,2,0:T(8,128)(2,1)}, u32[]{:S(2)}, u32[]{:S(2)}) collective-permute-start(bf16[6,768,128]{1,2,0:T(8,128)(2,1)} %collective-permute-done.12), channel_id=1, source_target_pairs={{0,8},{4,0},{12,4},{20,12},{28,20},{24,28},{16,24},{8,16},{1,9},{5... | collective-permute-start | bytes 3538952 | tf_op jit(solution)/shard_map/ppermute | solution.py:139
  249.6 45.2 %collective-permute-start.21 = (bf16[384,2,6,128]{0,3,2,1:T(8,128)(2,1)S(1)}, bf16[384,2,6,128]{0,3,2,1:T(8,128)(2,1)}, u32[]{:S(2)}, u32[]{:S(2)}) collective-permute-start(bf16[384,2,6,128]{0,3,2,1:T(8,128)(2,1)S(1)} %collective-permute-done.20), channel_id=1, source_target_pairs={{4,0},{12,8},{20,16},{28,24},{5,1},{13,9},{21,17},{29,25},{6,2},{1... | collective-permute-start | bytes 3538952 | tf_op jit(solution)/shard_map/ppermute | solution.py:165
  250.9 49.9 %collective-permute-start.19 = (bf16[384,2,6,128]{0,3,2,1:T(8,128)(2,1)S(1)}, bf16[384,2,6,128]{0,3,2,1:T(8,128)(2,1)S(1)}, u32[]{:S(2)}, u32[]{:S(2)}) collective-permute-start(bf16[384,2,6,128]{0,3,2,1:T(8,128)(2,1)S(1)} %add_convert_fusion), channel_id=1, source_target_pairs={{0,4},{8,12},{16,20},{24,28},{1,5},{9,13},{17,21},{25,29},{2,6},{1... | collective-permute-start | bytes 3538952 | tf_op jit(solution)/shard_map/ppermute | solution.py:163
  269.9 43.0 %collective-permute-start.15 = (bf16[6,768,128]{1,2,0:T(8,128)(2,1)}, bf16[6,768,128]{1,2,0:T(8,128)(2,1)S(1)}, u32[]{:S(2)}, u32[]{:S(2)}) collective-permute-start(bf16[6,768,128]{1,2,0:T(8,128)(2,1)} %collective-permute-done.13), channel_id=1, source_target_pairs={{0,4},{4,12},{12,20},{20,28},{28,24},{24,16},{16,8},{8,0},{1,5},{5... | collective-permute-start | bytes 3538952 | tf_op jit(solution)/shard_map/ppermute | solution.py:138
  269.9 45.4 %collective-permute-start.16 = (bf16[6,768,128]{1,2,0:T(8,128)(2,1)}, bf16[6,768,128]{1,2,0:T(8,128)(2,1)S(1)}, u32[]{:S(2)}, u32[]{:S(2)}) collective-permute-start(bf16[6,768,128]{1,2,0:T(8,128)(2,1)} %collective-permute-done.14), channel_id=1, source_target_pairs={{0,8},{4,0},{12,4},{20,12},{28,20},{24,28},{16,24},{8,16},{1,9},{5... | collective-permute-start | bytes 3538952 | tf_op jit(solution)/shard_map/ppermute | solution.py:139
  274.2 62.3 %collective-permute-start.22 = (bf16[384,2,6,128]{0,3,2,1:T(8,128)(2,1)S(1)}, bf16[384,2,6,128]{0,3,2,1:T(8,128)(2,1)S(1)}, u32[]{:S(2)}, u32[]{:S(2)}) collective-permute-start(bf16[384,2,6,128]{0,3,2,1:T(8,128)(2,1)S(1)} %collective-permute-done.20), channel_id=1, source_target_pairs={{0,4},{8,12},{16,20},{24,28},{1,5},{9,13},{17,21},{25,29},{2,6},{1... | collective-permute-start | bytes 3538952 | tf_op jit(solution)/shard_map/ppermute | solution.py:164
  294.7 41.7 %collective-permute-start.23 = (bf16[384,2,6,128]{0,3,2,1:T(8,128)(2,1)}, bf16[384,2,6,128]{0,3,2,1:T(8,128)(2,1)S(1)}, u32[]{:S(2)}, u32[]{:S(2)}) collective-permute-start(bf16[384,2,6,128]{0,3,2,1:T(8,128)(2,1)} %collective-permute-done.21), channel_id=1, source_target_pairs={{0,8},{8,16},{16,24},{24,0},{1,9},{9,17},{17,25},{25,1},{2,10},{10... | collective-permute-start | bytes 3538952 | tf_op jit(solution)/shard_map/ppermute | solution.py:166
  312.9 29.9 %collective-permute-start.17 = (bf16[6,384,128]{1,2,0:T(8,128)(2,1)S(1)}, bf16[6,384,128]{1,2,0:T(8,128)(2,1)S(1)}, u32[]{:S(2)}, u32[]{:S(2)}) collective-permute-start(bf16[6,384,128]{1,2,0:T(8,128)(2,1)S(1)} %slice.28), channel_id=1, source_target_pairs={{0,4},{4,12},{12,20},{20,28},{28,24},{24,16},{16,8},{8,0},{1,5},{5... | collective-permute-start | bytes 1769480 | tf_op jit(solution)/shard_map/ppermute | solution.py:148
  315.4 27.9 %collective-permute-start.18 = (bf16[6,384,128]{1,2,0:T(8,128)(2,1)S(1)}, bf16[6,384,128]{1,2,0:T(8,128)(2,1)S(1)}, u32[]{:S(2)}, u32[]{:S(2)}) collective-permute-start(bf16[6,384,128]{1,2,0:T(8,128)(2,1)S(1)} %slice.29), channel_id=1, source_target_pairs={{0,8},{4,0},{12,4},{20,12},{28,20},{24,28},{16,24},{8,16},{1,9},{5... | collective-permute-start | bytes 1769480 | tf_op jit(solution)/shard_map/ppermute | solution.py:149
  (12 other events, 626.3 us)

commit v14 on v13

--- a/solution.py
+++ b/solution.py
@@ -40,7 +40,7 @@
     reach = len(blocks)
     q_t = queries.reshape(rows, heads * size).T
     kv_t = [block.reshape(rows, 2 * heads * size).T for block in blocks]
-    per_step = 2 if heads % 2 == 0 else 1
+    per_step = 3 if heads % 3 == 0 else (2 if heads % 2 == 0 else 1)
     steps = heads // per_step
     q_spec = pl.BlockSpec((per_step * size, rows), lambda h: (h, 0))
     v_spec = pl.BlockSpec((per_step * size, rows), lambda h: (h + steps, 0))

time: 355 us -> 355 us (level)
  no operation moved by 1% of the time
where the time goes in v14:
time: 355 us; the launch traced here: 354 us
  waiting for transfers between devices  241 us (68%)
  starting transfers between devices  38.4 us (11%)
  matrix products  32.5 us (9%)
  local copies, waits for them, and re-layouts  18.6 us (5%)
  between operations  9.51 us (3%)
  Pallas kernels  8.95 us (3%)
  other arithmetic  5.31 us (1%)
    ppermute x6, waiting for transfers between devices, ring_project(): going_ccw = lax.ppermute(going_ccw, 'ctx', counter)  125 us
    ppermute x6, waiting for transfers between devices, ring_project(): going_cw = lax.ppermute(going_cw, 'ctx', clockwise)  59.4 us
    dot_general x9, matrix products, partial(): jnp.einsum('tr,...rd->t...d', cols, part, preferred_element_type=jnp.floa...  19.3 us
    ppermute x1, waiting for transfers between devices, earlier_blocks(): lax.ppermute(two_back, 'ctx', [(o, o - 1) for o in range(1, n, 2)])  16.5 us
    ppermute x1, waiting for transfers between devices, earlier_blocks(): two_back_up = lax.ppermute(two_back, 'ctx', evens_up)  15 us
    unnamed x9, matrix products  13.2 us
    ppermute x6, starting transfers between devices, ring_project(): going_ccw = lax.ppermute(going_ccw, 'ctx', counter)  13.1 us
    ppermute x2, waiting for transfers between devices, ring_project(): last_ccw = lax.ppermute(second, 'ctx', counter)  11.1 us
  transfers between devices with their start and end apart: 24, of which 13 were waited for; matrix products, arithmetic and copies ran while one was open for 13% of the time, Pallas kernels for 0%

profile of v14, /device:TPU:0, one launch (start us, length us, event | category | flops | bytes accessed | tf_op | source)
XLA Modules:
  0.0 354.3 jit_solution(4728239626382604353)
XLA Ops:
  0.0 4.3 %copy.5 = bf16[768,3,6,128]{0,3,2,1:T(8,128)(2,1)S(1)} copy(bf16[768,3,6,128]{3,0,2,1:T(8,128)(2,1)} %param.5) | data formatting | bytes 7077888 | tf_op args[1]
  4.5 3.1 collective-permute-start.7
  7.6 51.2 %collective-permute-done.7 = bf16[2,6,768,128]{2,3,1,0:T(8,128)(2,1)S(1)} collective-permute-done((bf16[2,6,768,128]{2,3,1,0:T(8,128)(2,1)S(1)}, bf16[2,6,768,128]{2,3,1,0:T(8,128)(2,1)S(1)}, u32[]{:S(2)}, u32[]{:S(2)}) %collective-permute-start.7) | collective-permute-done | bytes 2359328 | tf_op jit(solution)/shard_map/ppermute | solution.py:139
  64.1 47.2 %collective-permute-done.8 = bf16[2,6,768,128]{2,3,1,0:T(8,128)(2,1)} collective-permute-done((bf16[2,6,768,128]{2,3,1,0:T(8,128)(2,1)S(1)}, bf16[2,6,768,128]{2,3,1,0:T(8,128)(2,1)}, u32[]{:S(2)}, u32[]{:S(2)}) %collective-permute-start.8) | collective-permute-done | bytes 2359328 | tf_op jit(solution)/shard_map/ppermute | solution.py:139
  136.6 26.5 %collective-permute-done.9 = bf16[2,6,768,128]{2,3,1,0:T(8,128)(2,1)} collective-permute-done((bf16[2,6,768,128]{2,3,1,0:T(8,128)(2,1)}, bf16[2,6,768,128]{2,3,1,0:T(8,128)(2,1)}, u32[]{:S(2)}, u32[]{:S(2)}) %collective-permute-start.9) | collective-permute-done | bytes 2359328 | tf_op jit(solution)/shard_map/ppermute | solution.py:139
  169.5 3.1 fusion.6
  172.6 3.1 fusion.8
  175.7 3.1 fusion.4
  178.8 11.1 %collective-permute-done.10 = bf16[2,6,384,128]{2,3,1,0:T(8,128)(2,1)S(1)} collective-permute-done((bf16[2,6,384,128]{2,3,1,0:T(8,128)(2,1)S(1)}, bf16[2,6,384,128]{2,3,1,0:T(8,128)(2,1)S(1)}, u32[]{:S(2)}, u32[]{:S(2)}) %collective-permute-start.10) | collective-permute-done | bytes 1179680 | tf_op jit(solution)/shard_map/ppermute | solution.py:149
  189.9 3.4 collective-permute-done.6
  197.2 4.0 %add_convert_fusion = bf16[384,2,6,128]{0,3,2,1:T(8,128)(2,1)S(1)} fusion(f32[384,2,6,128]{0,3,2,1:T(8,128)S(1)} %fusion.37, f32[384,2,6,128]{0,3,2,1:T(8,128)S(1)} %fusion.39, f32[384,2,6,128]{0,3,2,1:T(8,128)S(1)} %fusion.4, f32[384,2,6,128]{0,3,2,1:T(8,128)S(1)} %fusion.6, f32[384,2,6,128]{0,3,2,1:T(8,128)S(1)} %fusion.8, ...), kind=kOutput, calls=%fused_computation | convolution fusion | flops 911278080 | bytes 23003140 | tf_op jit(solution)/shard_map/tr,...rd->t...d/dot_general | solution.py:130
  202.8 37.5 %collective-permute-done.11 = bf16[6,768,128]{1,2,0:T(8,128)(2,1)} collective-permute-done((bf16[6,768,128]{1,2,0:T(8,128)(2,1)S(1)}, bf16[6,768,128]{1,2,0:T(8,128)(2,1)}, u32[]{:S(2)}, u32[]{:S(2)}) %collective-permute-start.11) | collective-permute-done | bytes 1179680 | tf_op jit(solution)/shard_map/ppermute | solution.py:138
  240.3 3.6 %collective-permute-start.14 = (bf16[6,768,128]{1,2,0:T(8,128)(2,1)}, bf16[6,768,128]{1,2,0:T(8,128)(2,1)}, u32[]{:S(2)}, u32[]{:S(2)}) collective-permute-start(bf16[6,768,128]{1,2,0:T(8,128)(2,1)} %collective-permute-done.12), channel_id=1, source_target_pairs={{0,8},{4,0},{12,4},{20,12},{28,20},{24,28},{16,24},{8,16},{1,9},{5... | collective-permute-start | bytes 3538952 | tf_op jit(solution)/shard_map/ppermute | solution.py:139
  243.9 5.6 %collective-permute-done.20 = bf16[384,2,6,128]{0,3,2,1:T(8,128)(2,1)S(1)} collective-permute-done((bf16[384,2,6,128]{0,3,2,1:T(8,128)(2,1)S(1)}, bf16[384,2,6,128]{0,3,2,1:T(8,128)(2,1)S(1)}, u32[]{:S(2)}, u32[]{:S(2)}) %collective-permute-start.20) | collective-permute-done | bytes 1179680 | tf_op jit(solution)/shard_map/ppermute | solution.py:107
  250.9 5.7 %collective-permute-start.19 = (bf16[384,2,6,128]{0,3,2,1:T(8,128)(2,1)S(1)}, bf16[384,2,6,128]{0,3,2,1:T(8,128)(2,1)S(1)}, u32[]{:S(2)}, u32[]{:S(2)}) collective-permute-start(bf16[384,2,6,128]{0,3,2,1:T(8,128)(2,1)S(1)} %add_convert_fusion), channel_id=1, source_target_pairs={{0,4},{8,12},{16,20},{24,28},{1,5},{9,13},{17,21},{25,29},{2,6},{1... | collective-permute-start | bytes 3538952 | tf_op jit(solution)/shard_map/ppermute | solution.py:163
  258.6 11.3 %collective-permute-done.13 = bf16[6,768,128]{1,2,0:T(8,128)(2,1)} collective-permute-done((bf16[6,768,128]{1,2,0:T(8,128)(2,1)}, bf16[6,768,128]{1,2,0:T(8,128)(2,1)}, u32[]{:S(2)}, u32[]{:S(2)}) %collective-permute-start.13) | collective-permute-done | bytes 1179680 | tf_op jit(solution)/shard_map/ppermute | solution.py:138
  278.2 16.5 %collective-permute-done.21 = bf16[384,2,6,128]{0,3,2,1:T(8,128)(2,1)} collective-permute-done((bf16[384,2,6,128]{0,3,2,1:T(8,128)(2,1)S(1)}, bf16[384,2,6,128]{0,3,2,1:T(8,128)(2,1)}, u32[]{:S(2)}, u32[]{:S(2)}) %collective-permute-start.21) | collective-permute-done | bytes 1179680 | tf_op jit(solution)/shard_map/ppermute | solution.py:165
  300.8 2.5 broadcast_select_fusion.1
  303.3 9.5 %collective-permute-done.15 = bf16[6,768,128]{1,2,0:T(8,128)(2,1)S(1)} collective-permute-done((bf16[6,768,128]{1,2,0:T(8,128)(2,1)}, bf16[6,768,128]{1,2,0:T(8,128)(2,1)S(1)}, u32[]{:S(2)}, u32[]{:S(2)}) %collective-permute-start.15) | collective-permute-done | bytes 1179680 | tf_op jit(solution)/shard_map/ppermute | solution.py:138
  312.9 2.4 collective-permute-start.17
  315.4 4.4 %collective-permute-start.18 = (bf16[6,384,128]{1,2,0:T(8,128)(2,1)S(1)}, bf16[6,384,128]{1,2,0:T(8,128)(2,1)S(1)}, u32[]{:S(2)}, u32[]{:S(2)}) collective-permute-start(bf16[6,384,128]{1,2,0:T(8,128)(2,1)S(1)} %slice.29), channel_id=1, source_target_pairs={{0,8},{4,0},{12,4},{20,12},{28,20},{24,28},{16,24},{8,16},{1,9},{5... | collective-permute-start | bytes 1769480 | tf_op jit(solution)/shard_map/ppermute | solution.py:149
  321.4 15.0 %collective-permute-done.22 = bf16[384,2,6,128]{0,3,2,1:T(8,128)(2,1)S(1)} collective-permute-done((bf16[384,2,6,128]{0,3,2,1:T(8,128)(2,1)S(1)}, bf16[384,2,6,128]{0,3,2,1:T(8,128)(2,1)S(1)}, u32[]{:S(2)}, u32[]{:S(2)}) %collective-permute-start.22) | collective-permute-done | bytes 1179680 | tf_op jit(solution)/shard_map/ppermute | solution.py:164
  337.7 5.0 %collective-permute-done.17 = bf16[6,384,128]{1,2,0:T(8,128)(2,1)S(1)} collective-permute-done((bf16[6,384,128]{1,2,0:T(8,128)(2,1)S(1)}, bf16[6,384,128]{1,2,0:T(8,128)(2,1)S(1)}, u32[]{:S(2)}, u32[]{:S(2)}) %collective-permute-start.17) | collective-permute-done | bytes 589856 | tf_op jit(solution)/shard_map/ppermute | solution.py:148
  345.4 9.0 %shard_map.46 = bf16[6,384,128]{2,1,0:T(8,128)(2,1)} custom-call(bf16[768,384]{1,0:T(8,128)(2,1)} %bitcast.156, bf16[1536,384]{1,0:T(8,128)(2,1)} %bitcast.136, bf16[1536,384]{1,0:T(8,128)(2,1)} %bitcast.138, bf16[1536,384]{1,0:T(8,128)(2,1)} %bitcast.152, bf16[1536,384]{1,0:T(8,128)(2,1)} %bitcast.140, bf16[1536,384]{1,0:T(8,128)(2,1)} %bitcast.137, ...), custom_call_target="tpu_custom_call" | custom-call | flops 1811939328 | bytes 5898240 | tf_op jit(solution)/shard_map/pallas_call | solution.py:53
  (84 shorter events, 56.8 us)
Async XLA Ops:
  4.5 54.3 %collective-permute-start.7 = (bf16[2,6,768,128]{2,3,1,0:T(8,128)(2,1)S(1)}, bf16[2,6,768,128]{2,3,1,0:T(8,128)(2,1)S(1)}, u32[]{:S(2)}, u32[]{:S(2)}) collective-permute-start(bf16[2,6,768,128]{2,3,1,0:T(8,128)(2,1)S(1)} %slice.25), channel_id=1, source_target_pairs={{0,8},{4,0},{12,4},{20,12},{28,20},{24,28},{16,24},{8,16},{1,9},{5... | collective-permute-start | bytes 7077896 | tf_op jit(solution)/shard_map/ppermute | solution.py:139
  7.5 53.0 %collective-permute-start.3 = (bf16[2,6,768,128]{2,3,1,0:T(8,128)(2,1)S(1)}, bf16[2,6,768,128]{2,3,1,0:T(8,128)(2,1)S(1)}, u32[]{:S(2)}, u32[]{:S(2)}) collective-permute-start(bf16[2,6,768,128]{2,3,1,0:T(8,128)(2,1)S(1)} %slice.25), channel_id=1, source_target_pairs={{0,4},{4,12},{12,20},{20,28},{28,24},{24,16},{16,8},{8,0},{1,5},{5... | collective-permute-start | bytes 7077896 | tf_op jit(solution)/shard_map/ppermute | solution.py:138
  58.7 52.5 %collective-permute-start.8 = (bf16[2,6,768,128]{2,3,1,0:T(8,128)(2,1)S(1)}, bf16[2,6,768,128]{2,3,1,0:T(8,128)(2,1)}, u32[]{:S(2)}, u32[]{:S(2)}) collective-permute-start(bf16[2,6,768,128]{2,3,1,0:T(8,128)(2,1)S(1)} %collective-permute-done.7), channel_id=1, source_target_pairs={{0,8},{4,0},{12,4},{20,12},{28,20},{24,28},{16,24},{8,16},{1,9},{5... | collective-permute-start | bytes 7077896 | tf_op jit(solution)/shard_map/ppermute | solution.py:139
  61.9 51.9 %collective-permute-start.4 = (bf16[2,6,768,128]{2,3,1,0:T(8,128)(2,1)S(1)}, bf16[2,6,768,128]{2,3,1,0:T(8,128)(2,1)}, u32[]{:S(2)}, u32[]{:S(2)}) collective-permute-start(bf16[2,6,768,128]{2,3,1,0:T(8,128)(2,1)S(1)} %collective-permute-done.3), channel_id=1, source_target_pairs={{0,4},{4,12},{12,20},{20,28},{28,24},{24,16},{16,8},{8,0},{1,5},{5... | collective-permute-start | bytes 7077896 | tf_op jit(solution)/shard_map/ppermute | solution.py:138
  62.3 64.8 %collective-permute-start = (bf16[384,1536]{1,0:T(8,128)(2,1)}, bf16[384,1536]{1,0:T(8,128)(2,1)}, u32[]{:S(2)}, u32[]{:S(2)}) collective-permute-start(bf16[384,1536]{1,0:T(8,128)(2,1)} %param.4), channel_id=1, source_target_pairs={{0,1},{1,2},{2,3},{3,0},{4,5},{5,6},{6,7},{7,4},{8,9},{9,10},{10,1... | collective-permute-start | bytes 3538952 | tf_op jit(solution)/shard_map/ppermute | solution.py:107
  62.4 66.6 %collective-permute-start.1 = (bf16[384,1536]{1,0:T(8,128)(2,1)}, bf16[384,1536]{1,0:T(8,128)(2,1)}, u32[]{:S(2)}, u32[]{:S(2)}) collective-permute-start(bf16[384,1536]{1,0:T(8,128)(2,1)} %param.4), channel_id=1, source_target_pairs={{0,2},{1,3},{2,0},{3,1},{4,6},{5,7},{6,4},{7,5},{8,10},{9,11},{10,... | collective-permute-start | bytes 3538952 | tf_op jit(solution)/shard_map/ppermute | solution.py:107
  111.3 51.8 %collective-permute-start.9 = (bf16[2,6,768,128]{2,3,1,0:T(8,128)(2,1)}, bf16[2,6,768,128]{2,3,1,0:T(8,128)(2,1)}, u32[]{:S(2)}, u32[]{:S(2)}) collective-permute-start(bf16[2,6,768,128]{2,3,1,0:T(8,128)(2,1)} %collective-permute-done.8), channel_id=1, source_target_pairs={{0,8},{4,0},{12,4},{20,12},{28,20},{24,28},{16,24},{8,16},{1,9},{5... | collective-permute-start | bytes 7077896 | tf_op jit(solution)/shard_map/ppermute | solution.py:139
  113.9 51.9 %collective-permute-start.5 = (bf16[2,6,768,128]{2,3,1,0:T(8,128)(2,1)}, bf16[2,6,768,128]{2,3,1,0:T(8,128)(2,1)}, u32[]{:S(2)}, u32[]{:S(2)}) collective-permute-start(bf16[2,6,768,128]{2,3,1,0:T(8,128)(2,1)} %collective-permute-done.4), channel_id=1, source_target_pairs={{0,4},{4,12},{12,20},{20,28},{28,24},{24,16},{16,8},{8,0},{1,5},{5... | collective-permute-start | bytes 7077896 | tf_op jit(solution)/shard_map/ppermute | solution.py:138
  114.6 15.7 %collective-permute-start.2 = (bf16[384,1536]{1,0:T(8,128)(2,1)}, bf16[384,1536]{1,0:T(8,128)(2,1)}, u32[]{:S(2)}, u32[]{:S(2)}) collective-permute-start(bf16[384,1536]{1,0:T(8,128)(2,1)} %param.4), channel_id=1, source_target_pairs={{0,3},{1,0},{2,1},{3,2},{4,7},{5,4},{6,5},{7,6},{8,11},{9,8},{10,9... | collective-permute-start | bytes 3538952 | tf_op jit(solution)/shard_map/ppermute | solution.py:107
  164.5 25.4 %collective-permute-start.10 = (bf16[2,6,384,128]{2,3,1,0:T(8,128)(2,1)S(1)}, bf16[2,6,384,128]{2,3,1,0:T(8,128)(2,1)S(1)}, u32[]{:S(2)}, u32[]{:S(2)}) collective-permute-start(bf16[2,6,384,128]{2,3,1,0:T(8,128)(2,1)S(1)} %slice.27), channel_id=1, source_target_pairs={{0,8},{4,0},{12,4},{20,12},{28,20},{24,28},{16,24},{8,16},{1,9},{5... | collective-permute-start | bytes 3538952 | tf_op jit(solution)/shard_map/ppermute | solution.py:149
  167.1 26.2 %collective-permute-start.6 = (bf16[2,6,384,128]{2,3,1,0:T(8,128)(2,1)S(1)}, bf16[2,6,384,128]{2,3,1,0:T(8,128)(2,1)S(1)}, u32[]{:S(2)}, u32[]{:S(2)}) collective-permute-start(bf16[2,6,384,128]{2,3,1,0:T(8,128)(2,1)S(1)} %slice.26), channel_id=1, source_target_pairs={{0,4},{4,12},{12,20},{20,28},{28,24},{24,16},{16,8},{8,0},{1,5},{5... | collective-permute-start | bytes 3538952 | tf_op jit(solution)/shard_map/ppermute | solution.py:148
  193.3 47.0 %collective-permute-start.11 = (bf16[6,768,128]{1,2,0:T(8,128)(2,1)S(1)}, bf16[6,768,128]{1,2,0:T(8,128)(2,1)}, u32[]{:S(2)}, u32[]{:S(2)}) collective-permute-start(bf16[6,768,128]{1,2,0:T(8,128)(2,1)S(1)} %slice_bitcast_fusion), channel_id=1, source_target_pairs={{0,4},{4,12},{12,20},{20,28},{28,24},{24,16},{16,8},{8,0},{1,5},{5... | collective-permute-start | bytes 3538952 | tf_op jit(solution)/shard_map/ppermute | solution.py:138
  194.2 46.2 %collective-permute-start.12 = (bf16[6,768,128]{1,2,0:T(8,128)(2,1)S(1)}, bf16[6,768,128]{1,2,0:T(8,128)(2,1)}, u32[]{:S(2)}, u32[]{:S(2)}) collective-permute-start(bf16[6,768,128]{1,2,0:T(8,128)(2,1)S(1)} %slice_bitcast_fusion), channel_id=1, source_target_pairs={{0,8},{4,0},{12,4},{20,12},{28,20},{24,28},{16,24},{8,16},{1,9},{5... | collective-permute-start | bytes 3538952 | tf_op jit(solution)/shard_map/ppermute | solution.py:139
  201.2 48.4 %collective-permute-start.20 = (bf16[384,2,6,128]{0,3,2,1:T(8,128)(2,1)S(1)}, bf16[384,2,6,128]{0,3,2,1:T(8,128)(2,1)S(1)}, u32[]{:S(2)}, u32[]{:S(2)}) collective-permute-start(bf16[384,2,6,128]{0,3,2,1:T(8,128)(2,1)S(1)} %add_convert_fusion), channel_id=1, source_target_pairs={{0,8},{4,12},{8,16},{12,20},{16,24},{20,28},{24,0},{28,4},{1,9},{5... | collective-permute-start | bytes 3538952 | tf_op jit(solution)/shard_map/ppermute | solution.py:107
  240.3 29.5 %collective-permute-start.13 = (bf16[6,768,128]{1,2,0:T(8,128)(2,1)}, bf16[6,768,128]{1,2,0:T(8,128)(2,1)}, u32[]{:S(2)}, u32[]{:S(2)}) collective-permute-start(bf16[6,768,128]{1,2,0:T(8,128)(2,1)} %collective-permute-done.11), channel_id=1, source_target_pairs={{0,4},{4,12},{12,20},{20,28},{28,24},{24,16},{16,8},{8,0},{1,5},{5... | collective-permute-start | bytes 3538952 | tf_op jit(solution)/shard_map/ppermute | solution.py:138
  240.3 29.5 %collective-permute-start.14 = (bf16[6,768,128]{1,2,0:T(8,128)(2,1)}, bf16[6,768,128]{1,2,0:T(8,128)(2,1)}, u32[]{:S(2)}, u32[]{:S(2)}) collective-permute-start(bf16[6,768,128]{1,2,0:T(8,128)(2,1)} %collective-permute-done.12), channel_id=1, source_target_pairs={{0,8},{4,0},{12,4},{20,12},{28,20},{24,28},{16,24},{8,16},{1,9},{5... | collective-permute-start | bytes 3538952 | tf_op jit(solution)/shard_map/ppermute | solution.py:139
  249.6 45.2 %collective-permute-start.21 = (bf16[384,2,6,128]{0,3,2,1:T(8,128)(2,1)S(1)}, bf16[384,2,6,128]{0,3,2,1:T(8,128)(2,1)}, u32[]{:S(2)}, u32[]{:S(2)}) collective-permute-start(bf16[384,2,6,128]{0,3,2,1:T(8,128)(2,1)S(1)} %collective-permute-done.20), channel_id=1, source_target_pairs={{4,0},{12,8},{20,16},{28,24},{5,1},{13,9},{21,17},{29,25},{6,2},{1... | collective-permute-start | bytes 3538952 | tf_op jit(solution)/shard_map/ppermute | solution.py:165
  250.9 49.9 %collective-permute-start.19 = (bf16[384,2,6,128]{0,3,2,1:T(8,128)(2,1)S(1)}, bf16[384,2,6,128]{0,3,2,1:T(8,128)(2,1)S(1)}, u32[]{:S(2)}, u32[]{:S(2)}) collective-permute-start(bf16[384,2,6,128]{0,3,2,1:T(8,128)(2,1)S(1)} %add_convert_fusion), channel_id=1, source_target_pairs={{0,4},{8,12},{16,20},{24,28},{1,5},{9,13},{17,21},{25,29},{2,6},{1... | collective-permute-start | bytes 3538952 | tf_op jit(solution)/shard_map/ppermute | solution.py:163
  269.9 43.0 %collective-permute-start.15 = (bf16[6,768,128]{1,2,0:T(8,128)(2,1)}, bf16[6,768,128]{1,2,0:T(8,128)(2,1)S(1)}, u32[]{:S(2)}, u32[]{:S(2)}) collective-permute-start(bf16[6,768,128]{1,2,0:T(8,128)(2,1)} %collective-permute-done.13), channel_id=1, source_target_pairs={{0,4},{4,12},{12,20},{20,28},{28,24},{24,16},{16,8},{8,0},{1,5},{5... | collective-permute-start | bytes 3538952 | tf_op jit(solution)/shard_map/ppermute | solution.py:138
  269.9 45.4 %collective-permute-start.16 = (bf16[6,768,128]{1,2,0:T(8,128)(2,1)}, bf16[6,768,128]{1,2,0:T(8,128)(2,1)S(1)}, u32[]{:S(2)}, u32[]{:S(2)}) collective-permute-start(bf16[6,768,128]{1,2,0:T(8,128)(2,1)} %collective-permute-done.14), channel_id=1, source_target_pairs={{0,8},{4,0},{12,4},{20,12},{28,20},{24,28},{16,24},{8,16},{1,9},{5... | collective-permute-start | bytes 3538952 | tf_op jit(solution)/shard_map/ppermute | solution.py:139
  274.2 62.3 %collective-permute-start.22 = (bf16[384,2,6,128]{0,3,2,1:T(8,128)(2,1)S(1)}, bf16[384,2,6,128]{0,3,2,1:T(8,128)(2,1)S(1)}, u32[]{:S(2)}, u32[]{:S(2)}) collective-permute-start(bf16[384,2,6,128]{0,3,2,1:T(8,128)(2,1)S(1)} %collective-permute-done.20), channel_id=1, source_target_pairs={{0,4},{8,12},{16,20},{24,28},{1,5},{9,13},{17,21},{25,29},{2,6},{1... | collective-permute-start | bytes 3538952 | tf_op jit(solution)/shard_map/ppermute | solution.py:164
  294.7 41.7 %collective-permute-start.23 = (bf16[384,2,6,128]{0,3,2,1:T(8,128)(2,1)}, bf16[384,2,6,128]{0,3,2,1:T(8,128)(2,1)S(1)}, u32[]{:S(2)}, u32[]{:S(2)}) collective-permute-start(bf16[384,2,6,128]{0,3,2,1:T(8,128)(2,1)} %collective-permute-done.21), channel_id=1, source_target_pairs={{0,8},{8,16},{16,24},{24,0},{1,9},{9,17},{17,25},{25,1},{2,10},{10... | collective-permute-start | bytes 3538952 | tf_op jit(solution)/shard_map/ppermute | solution.py:166
  312.9 29.9 %collective-permute-start.17 = (bf16[6,384,128]{1,2,0:T(8,128)(2,1)S(1)}, bf16[6,384,128]{1,2,0:T(8,128)(2,1)S(1)}, u32[]{:S(2)}, u32[]{:S(2)}) collective-permute-start(bf16[6,384,128]{1,2,0:T(8,128)(2,1)S(1)} %slice.28), channel_id=1, source_target_pairs={{0,4},{4,12},{12,20},{20,28},{28,24},{24,16},{16,8},{8,0},{1,5},{5... | collective-permute-start | bytes 1769480 | tf_op jit(solution)/shard_map/ppermute | solution.py:148
  315.4 27.9 %collective-permute-start.18 = (bf16[6,384,128]{1,2,0:T(8,128)(2,1)S(1)}, bf16[6,384,128]{1,2,0:T(8,128)(2,1)S(1)}, u32[]{:S(2)}, u32[]{:S(2)}) collective-permute-start(bf16[6,384,128]{1,2,0:T(8,128)(2,1)S(1)} %slice.29), channel_id=1, source_target_pairs={{0,8},{4,0},{12,4},{20,12},{28,20},{24,28},{16,24},{8,16},{1,9},{5... | collective-permute-start | bytes 1769480 | tf_op jit(solution)/shard_map/ppermute | solution.py:149
  (12 other events, 626.3 us)

commit v15 on v13

--- a/solution.py
+++ b/solution.py
@@ -159,13 +159,12 @@
         if n % 2 or n < 4 or REACH != 4:
             return [shifted(key_value, "ctx", by) for by in range(1, REACH)]
         two_back = shifted(key_value, "ctx", 2)
+        odd = (me % 2) == 1
         evens_up = [(e, e + 1) for e in range(0, n, 2)]
-        own_up = lax.ppermute(key_value, "ctx", evens_up)
+        across = evens_up + [(o, o - 1) for o in range(1, n, 2)]
+        one_back = lax.ppermute(jnp.where(odd, two_back, key_value), "ctx", across)
         two_back_up = lax.ppermute(two_back, "ctx", evens_up)
-        to_even = lax.ppermute(two_back, "ctx", [(o, o - 1) for o in range(1, n, 2)])
-        three_back = lax.ppermute(to_even, "ctx", [(e, (e + 2) % n) for e in range(0, n, 2)])
-        odd = (me % 2) == 1
-        one_back = jnp.where(odd, own_up, to_even)
+        three_back = lax.ppermute(one_back, "ctx", [(e, (e + 2) % n) for e in range(0, n, 2)])
         three_back = jnp.where(odd, two_back_up, three_back)
         return [one_back, two_back, three_back]
 

time: 355 us -> 354 us (level)
  waiting for transfers between devices: 241 us -> 251 us
  starting transfers between devices: 38.5 us -> 29.9 us
    ppermute x6, waiting for transfers between devices: 59.4 us -> 73.4 us  [ring_project(): going_cw = lax.ppermute(going_cw, 'ctx', clockwise)]
    ppermute x3 -> x2, starting transfers between devices: 8.88 us -> 3.95 us  [the longest x1 2.04 us: earlier_blocks(): one_back = lax.ppermute(jnp.where(odd, two_back, key_value), 'ctx', across)]
    ppermute x2, starting transfers between devices: 5.65 us -> 2.06 us  [ring_project(): last_ccw = lax.ppermute(second, 'ctx', counter)]
    ppermute x3 -> x2, waiting for transfers between devices: 16.5 us -> 15.1 us  [the longest x1 15.1 us: earlier_blocks(): one_back = lax.ppermute(jnp.where(odd, two_back, key_value), 'ctx', across)]
    unnamed x25 -> x27, local copies, waits for them, and re-layouts: 7.62 us -> 7.62 us
  transfers between devices with their start and end apart: 24 -> 23, of which waited for: 13 -> 13; matrix products, arithmetic and copies ran while one was open for 13% -> 12% of each run, Pallas kernels for 0% -> 0%
where the time goes in v15:
time: 354 us; the launch traced here: 353 us
  waiting for transfers between devices  251 us (71%)
  matrix products  32 us (9%)
  starting transfers between devices  29.9 us (8%)
  local copies, waits for them, and re-layouts  18.7 us (5%)
  between operations  9.47 us (3%)
  Pallas kernels  8.87 us (3%)
    ppermute x6, waiting for transfers between devices, ring_project(): going_ccw = lax.ppermute(going_ccw, 'ctx', counter)  125 us
    ppermute x6, waiting for transfers between devices, ring_project(): going_cw = lax.ppermute(going_cw, 'ctx', clockwise)  73.4 us
    dot_general x9, matrix products, partial(): jnp.einsum('tr,...rd->t...d', cols, part, preferred_element_type=jnp.floa...  19.2 us
    ppermute x1, waiting for transfers between devices, earlier_blocks(): one_back = lax.ppermute(jnp.where(odd, two_back, key_value), 'ctx', across)  15.1 us
    ppermute x6, starting transfers between devices, ring_project(): going_ccw = lax.ppermute(going_ccw, 'ctx', counter)  13.1 us
    unnamed x9, matrix products  12.8 us
    ppermute x1, waiting for transfers between devices, earlier_blocks(): two_back_up = lax.ppermute(two_back, 'ctx', evens_up)  12.3 us
    ppermute x2, waiting for transfers between devices, ring_project(): last_ccw = lax.ppermute(second, 'ctx', counter)  11.1 us
  transfers between devices with their start and end apart: 23, of which 13 were waited for; matrix products, arithmetic and copies ran while one was open for 12% of the time, Pallas kernels for 0%

profile of v15, /device:TPU:0, one launch (start us, length us, event | category | flops | bytes accessed | tf_op | source)
XLA Modules:
  0.0 352.7 jit_solution(13126583613423376828)
XLA Ops:
  0.0 4.3 %copy.5 = bf16[768,3,6,128]{0,3,2,1:T(8,128)(2,1)S(1)} copy(bf16[768,3,6,128]{3,0,2,1:T(8,128)(2,1)} %param.5) | data formatting | bytes 7077888 | tf_op args[1]
  4.5 3.1 collective-permute-start.7
  7.6 51.2 %collective-permute-done.7 = bf16[2,6,768,128]{2,3,1,0:T(8,128)(2,1)S(1)} collective-permute-done((bf16[2,6,768,128]{2,3,1,0:T(8,128)(2,1)S(1)}, bf16[2,6,768,128]{2,3,1,0:T(8,128)(2,1)S(1)}, u32[]{:S(2)}, u32[]{:S(2)}) %collective-permute-start.7) | collective-permute-done | bytes 2359328 | tf_op jit(solution)/shard_map/ppermute | solution.py:139
  64.1 47.2 %collective-permute-done.8 = bf16[2,6,768,128]{2,3,1,0:T(8,128)(2,1)} collective-permute-done((bf16[2,6,768,128]{2,3,1,0:T(8,128)(2,1)S(1)}, bf16[2,6,768,128]{2,3,1,0:T(8,128)(2,1)}, u32[]{:S(2)}, u32[]{:S(2)}) %collective-permute-start.8) | collective-permute-done | bytes 2359328 | tf_op jit(solution)/shard_map/ppermute | solution.py:139
  136.6 26.5 %collective-permute-done.9 = bf16[2,6,768,128]{2,3,1,0:T(8,128)(2,1)} collective-permute-done((bf16[2,6,768,128]{2,3,1,0:T(8,128)(2,1)}, bf16[2,6,768,128]{2,3,1,0:T(8,128)(2,1)}, u32[]{:S(2)}, u32[]{:S(2)}) %collective-permute-start.9) | collective-permute-done | bytes 2359328 | tf_op jit(solution)/shard_map/ppermute | solution.py:139
  169.5 3.1 fusion.6
  172.6 3.1 fusion.8
  175.7 3.1 fusion.4
  178.8 11.1 %collective-permute-done.10 = bf16[2,6,384,128]{2,3,1,0:T(8,128)(2,1)S(1)} collective-permute-done((bf16[2,6,384,128]{2,3,1,0:T(8,128)(2,1)S(1)}, bf16[2,6,384,128]{2,3,1,0:T(8,128)(2,1)S(1)}, u32[]{:S(2)}, u32[]{:S(2)}) %collective-permute-start.10) | collective-permute-done | bytes 1179680 | tf_op jit(solution)/shard_map/ppermute | solution.py:149
  189.9 3.4 collective-permute-done.6
  197.1 3.9 %add_convert_fusion = bf16[384,2,6,128]{0,3,2,1:T(8,128)(2,1)S(1)} fusion(f32[384,2,6,128]{0,3,2,1:T(8,128)S(1)} %fusion.37, f32[384,2,6,128]{0,3,2,1:T(8,128)S(1)} %fusion.39, f32[384,2,6,128]{0,3,2,1:T(8,128)S(1)} %fusion.4, f32[384,2,6,128]{0,3,2,1:T(8,128)S(1)} %fusion.6, f32[384,2,6,128]{0,3,2,1:T(8,128)S(1)} %fusion.8, ...), kind=kOutput, calls=%fused_computation | convolution fusion | flops 911278080 | bytes 23003140 | tf_op jit(solution)/shard_map/tr,...rd->t...d/dot_general | solution.py:130
  202.7 37.6 %collective-permute-done.11 = bf16[6,768,128]{1,2,0:T(8,128)(2,1)} collective-permute-done((bf16[6,768,128]{1,2,0:T(8,128)(2,1)S(1)}, bf16[6,768,128]{1,2,0:T(8,128)(2,1)}, u32[]{:S(2)}, u32[]{:S(2)}) %collective-permute-start.11) | collective-permute-done | bytes 1179680 | tf_op jit(solution)/shard_map/ppermute | solution.py:138
  240.3 3.6 %collective-permute-start.14 = (bf16[6,768,128]{1,2,0:T(8,128)(2,1)}, bf16[6,768,128]{1,2,0:T(8,128)(2,1)}, u32[]{:S(2)}, u32[]{:S(2)}) collective-permute-start(bf16[6,768,128]{1,2,0:T(8,128)(2,1)} %collective-permute-done.12), channel_id=1, source_target_pairs={{0,8},{4,0},{12,4},{20,12},{28,20},{24,28},{16,24},{8,16},{1,9},{5... | collective-permute-start | bytes 3538952 | tf_op jit(solution)/shard_map/ppermute | solution.py:139
  243.9 5.6 %collective-permute-done.19 = bf16[384,2,6,128]{0,3,2,1:T(8,128)(2,1)S(1)} collective-permute-done((bf16[384,2,6,128]{0,3,2,1:T(8,128)(2,1)S(1)}, bf16[384,2,6,128]{0,3,2,1:T(8,128)(2,1)S(1)}, u32[]{:S(2)}, u32[]{:S(2)}) %collective-permute-start.19) | collective-permute-done | bytes 1179680 | tf_op jit(solution)/shard_map/ppermute | solution.py:107
  251.7 18.1 %collective-permute-done.13 = bf16[6,768,128]{1,2,0:T(8,128)(2,1)} collective-permute-done((bf16[6,768,128]{1,2,0:T(8,128)(2,1)}, bf16[6,768,128]{1,2,0:T(8,128)(2,1)}, u32[]{:S(2)}, u32[]{:S(2)}) %collective-permute-start.13) | collective-permute-done | bytes 1179680 | tf_op jit(solution)/shard_map/ppermute | solution.py:138
  275.8 2.1 fusion.32
  277.9 15.1 %collective-permute-done.20 = bf16[384,2,6,128]{0,3,2,1:T(8,128)(2,1)S(1)} collective-permute-done((bf16[384,2,6,128]{0,3,2,1:T(8,128)(2,1)S(1)}, bf16[384,2,6,128]{0,3,2,1:T(8,128)(2,1)S(1)}, u32[]{:S(2)}, u32[]{:S(2)}) %collective-permute-start.20) | collective-permute-done | bytes 1179680 | tf_op jit(solution)/shard_map/ppermute | solution.py:165
  294.9 2.1 fusion.29
  299.0 2.1 fusion.23
  301.1 16.5 %collective-permute-done.15 = bf16[6,768,128]{1,2,0:T(8,128)(2,1)S(1)} collective-permute-done((bf16[6,768,128]{1,2,0:T(8,128)(2,1)}, bf16[6,768,128]{1,2,0:T(8,128)(2,1)S(1)}, u32[]{:S(2)}, u32[]{:S(2)}) %collective-permute-start.15) | collective-permute-done | bytes 1179680 | tf_op jit(solution)/shard_map/ppermute | solution.py:138
  317.7 2.4 collective-permute-start.17
  322.6 12.3 %collective-permute-done.21 = bf16[384,2,6,128]{0,3,2,1:T(8,128)(2,1)S(1)} collective-permute-done((bf16[384,2,6,128]{0,3,2,1:T(8,128)(2,1)S(1)}, bf16[384,2,6,128]{0,3,2,1:T(8,128)(2,1)S(1)}, u32[]{:S(2)}, u32[]{:S(2)}) %collective-permute-start.21) | collective-permute-done | bytes 1179680 | tf_op jit(solution)/shard_map/ppermute | solution.py:166
  336.2 5.1 %collective-permute-done.17 = bf16[6,384,128]{1,2,0:T(8,128)(2,1)S(1)} collective-permute-done((bf16[6,384,128]{1,2,0:T(8,128)(2,1)S(1)}, bf16[6,384,128]{1,2,0:T(8,128)(2,1)S(1)}, u32[]{:S(2)}, u32[]{:S(2)}) %collective-permute-start.17) | collective-permute-done | bytes 589856 | tf_op jit(solution)/shard_map/ppermute | solution.py:148
  343.8 8.9 %shard_map.46 = bf16[6,384,128]{2,1,0:T(8,128)(2,1)} custom-call(bf16[768,384]{1,0:T(8,128)(2,1)} %bitcast.156, bf16[1536,384]{1,0:T(8,128)(2,1)} %bitcast.133, bf16[1536,384]{1,0:T(8,128)(2,1)} %bitcast.152, bf16[1536,384]{1,0:T(8,128)(2,1)} %bitcast.138, bf16[1536,384]{1,0:T(8,128)(2,1)} %bitcast.140, bf16[1536,384]{1,0:T(8,128)(2,1)} %bitcast.134, ...), custom_call_target="tpu_custom_call" | custom-call | flops 1811939328 | bytes 5898240 | tf_op jit(solution)/shard_map/pallas_call | solution.py:53
  (84 shorter events, 51.8 us)
Async XLA Ops:
  4.3 115.6 %copy-start.7 = (s32[8]{0:T(128)S(1)}, s32[8]{0:T(128)}, u32[]{:S(2)}) copy-start(s32[8]{0:T(128)} %constant.139.clone) | copy-start | bytes 100
  4.5 54.3 %collective-permute-start.7 = (bf16[2,6,768,128]{2,3,1,0:T(8,128)(2,1)S(1)}, bf16[2,6,768,128]{2,3,1,0:T(8,128)(2,1)S(1)}, u32[]{:S(2)}, u32[]{:S(2)}) collective-permute-start(bf16[2,6,768,128]{2,3,1,0:T(8,128)(2,1)S(1)} %slice.25), channel_id=1, source_target_pairs={{0,8},{4,0},{12,4},{20,12},{28,20},{24,28},{16,24},{8,16},{1,9},{5... | collective-permute-start | bytes 7077896 | tf_op jit(solution)/shard_map/ppermute | solution.py:139
  7.5 53.0 %collective-permute-start.3 = (bf16[2,6,768,128]{2,3,1,0:T(8,128)(2,1)S(1)}, bf16[2,6,768,128]{2,3,1,0:T(8,128)(2,1)S(1)}, u32[]{:S(2)}, u32[]{:S(2)}) collective-permute-start(bf16[2,6,768,128]{2,3,1,0:T(8,128)(2,1)S(1)} %slice.25), channel_id=1, source_target_pairs={{0,4},{4,12},{12,20},{20,28},{28,24},{24,16},{16,8},{8,0},{1,5},{5... | collective-permute-start | bytes 7077896 | tf_op jit(solution)/shard_map/ppermute | solution.py:138
  58.7 52.5 %collective-permute-start.8 = (bf16[2,6,768,128]{2,3,1,0:T(8,128)(2,1)S(1)}, bf16[2,6,768,128]{2,3,1,0:T(8,128)(2,1)}, u32[]{:S(2)}, u32[]{:S(2)}) collective-permute-start(bf16[2,6,768,128]{2,3,1,0:T(8,128)(2,1)S(1)} %collective-permute-done.7), channel_id=1, source_target_pairs={{0,8},{4,0},{12,4},{20,12},{28,20},{24,28},{16,24},{8,16},{1,9},{5... | collective-permute-start | bytes 7077896 | tf_op jit(solution)/shard_map/ppermute | solution.py:139
  61.9 51.9 %collective-permute-start.4 = (bf16[2,6,768,128]{2,3,1,0:T(8,128)(2,1)S(1)}, bf16[2,6,768,128]{2,3,1,0:T(8,128)(2,1)}, u32[]{:S(2)}, u32[]{:S(2)}) collective-permute-start(bf16[2,6,768,128]{2,3,1,0:T(8,128)(2,1)S(1)} %collective-permute-done.3), channel_id=1, source_target_pairs={{0,4},{4,12},{12,20},{20,28},{28,24},{24,16},{16,8},{8,0},{1,5},{5... | collective-permute-start | bytes 7077896 | tf_op jit(solution)/shard_map/ppermute | solution.py:138
  62.3 64.8 %collective-permute-start = (bf16[384,1536]{1,0:T(8,128)(2,1)}, bf16[384,1536]{1,0:T(8,128)(2,1)}, u32[]{:S(2)}, u32[]{:S(2)}) collective-permute-start(bf16[384,1536]{1,0:T(8,128)(2,1)} %param.4), channel_id=1, source_target_pairs={{0,1},{1,2},{2,3},{3,0},{4,5},{5,6},{6,7},{7,4},{8,9},{9,10},{10,1... | collective-permute-start | bytes 3538952 | tf_op jit(solution)/shard_map/ppermute | solution.py:107
  62.4 66.6 %collective-permute-start.1 = (bf16[384,1536]{1,0:T(8,128)(2,1)}, bf16[384,1536]{1,0:T(8,128)(2,1)}, u32[]{:S(2)}, u32[]{:S(2)}) collective-permute-start(bf16[384,1536]{1,0:T(8,128)(2,1)} %param.4), channel_id=1, source_target_pairs={{0,2},{1,3},{2,0},{3,1},{4,6},{5,7},{6,4},{7,5},{8,10},{9,11},{10,... | collective-permute-start | bytes 3538952 | tf_op jit(solution)/shard_map/ppermute | solution.py:107
  111.3 51.8 %collective-permute-start.9 = (bf16[2,6,768,128]{2,3,1,0:T(8,128)(2,1)}, bf16[2,6,768,128]{2,3,1,0:T(8,128)(2,1)}, u32[]{:S(2)}, u32[]{:S(2)}) collective-permute-start(bf16[2,6,768,128]{2,3,1,0:T(8,128)(2,1)} %collective-permute-done.8), channel_id=1, source_target_pairs={{0,8},{4,0},{12,4},{20,12},{28,20},{24,28},{16,24},{8,16},{1,9},{5... | collective-permute-start | bytes 7077896 | tf_op jit(solution)/shard_map/ppermute | solution.py:139
  113.9 51.9 %collective-permute-start.5 = (bf16[2,6,768,128]{2,3,1,0:T(8,128)(2,1)}, bf16[2,6,768,128]{2,3,1,0:T(8,128)(2,1)}, u32[]{:S(2)}, u32[]{:S(2)}) collective-permute-start(bf16[2,6,768,128]{2,3,1,0:T(8,128)(2,1)} %collective-permute-done.4), channel_id=1, source_target_pairs={{0,4},{4,12},{12,20},{20,28},{28,24},{24,16},{16,8},{8,0},{1,5},{5... | collective-permute-start | bytes 7077896 | tf_op jit(solution)/shard_map/ppermute | solution.py:138
  114.6 15.7 %collective-permute-start.2 = (bf16[384,1536]{1,0:T(8,128)(2,1)}, bf16[384,1536]{1,0:T(8,128)(2,1)}, u32[]{:S(2)}, u32[]{:S(2)}) collective-permute-start(bf16[384,1536]{1,0:T(8,128)(2,1)} %param.4), channel_id=1, source_target_pairs={{0,3},{1,0},{2,1},{3,2},{4,7},{5,4},{6,5},{7,6},{8,11},{9,8},{10,9... | collective-permute-start | bytes 3538952 | tf_op jit(solution)/shard_map/ppermute | solution.py:107
  164.5 25.4 %collective-permute-start.10 = (bf16[2,6,384,128]{2,3,1,0:T(8,128)(2,1)S(1)}, bf16[2,6,384,128]{2,3,1,0:T(8,128)(2,1)S(1)}, u32[]{:S(2)}, u32[]{:S(2)}) collective-permute-start(bf16[2,6,384,128]{2,3,1,0:T(8,128)(2,1)S(1)} %slice.27), channel_id=1, source_target_pairs={{0,8},{4,0},{12,4},{20,12},{28,20},{24,28},{16,24},{8,16},{1,9},{5... | collective-permute-start | bytes 3538952 | tf_op jit(solution)/shard_map/ppermute | solution.py:149
  167.1 26.2 %collective-permute-start.6 = (bf16[2,6,384,128]{2,3,1,0:T(8,128)(2,1)S(1)}, bf16[2,6,384,128]{2,3,1,0:T(8,128)(2,1)S(1)}, u32[]{:S(2)}, u32[]{:S(2)}) collective-permute-start(bf16[2,6,384,128]{2,3,1,0:T(8,128)(2,1)S(1)} %slice.26), channel_id=1, source_target_pairs={{0,4},{4,12},{12,20},{20,28},{28,24},{24,16},{16,8},{8,0},{1,5},{5... | collective-permute-start | bytes 3538952 | tf_op jit(solution)/shard_map/ppermute | solution.py:148
  193.3 47.0 %collective-permute-start.11 = (bf16[6,768,128]{1,2,0:T(8,128)(2,1)S(1)}, bf16[6,768,128]{1,2,0:T(8,128)(2,1)}, u32[]{:S(2)}, u32[]{:S(2)}) collective-permute-start(bf16[6,768,128]{1,2,0:T(8,128)(2,1)S(1)} %slice_bitcast_fusion), channel_id=1, source_target_pairs={{0,4},{4,12},{12,20},{20,28},{28,24},{24,16},{16,8},{8,0},{1,5},{5... | collective-permute-start | bytes 3538952 | tf_op jit(solution)/shard_map/ppermute | solution.py:138
  194.2 46.2 %collective-permute-start.12 = (bf16[6,768,128]{1,2,0:T(8,128)(2,1)S(1)}, bf16[6,768,128]{1,2,0:T(8,128)(2,1)}, u32[]{:S(2)}, u32[]{:S(2)}) collective-permute-start(bf16[6,768,128]{1,2,0:T(8,128)(2,1)S(1)} %slice_bitcast_fusion), channel_id=1, source_target_pairs={{0,8},{4,0},{12,4},{20,12},{28,20},{24,28},{16,24},{8,16},{1,9},{5... | collective-permute-start | bytes 3538952 | tf_op jit(solution)/shard_map/ppermute | solution.py:139
  201.1 48.5 %collective-permute-start.19 = (bf16[384,2,6,128]{0,3,2,1:T(8,128)(2,1)S(1)}, bf16[384,2,6,128]{0,3,2,1:T(8,128)(2,1)S(1)}, u32[]{:S(2)}, u32[]{:S(2)}) collective-permute-start(bf16[384,2,6,128]{0,3,2,1:T(8,128)(2,1)S(1)} %add_convert_fusion), channel_id=1, source_target_pairs={{0,8},{4,12},{8,16},{12,20},{16,24},{20,28},{24,0},{28,4},{1,9},{5... | collective-permute-start | bytes 3538952 | tf_op jit(solution)/shard_map/ppermute | solution.py:107
  240.3 29.5 %collective-permute-start.13 = (bf16[6,768,128]{1,2,0:T(8,128)(2,1)}, bf16[6,768,128]{1,2,0:T(8,128)(2,1)}, u32[]{:S(2)}, u32[]{:S(2)}) collective-permute-start(bf16[6,768,128]{1,2,0:T(8,128)(2,1)} %collective-permute-done.11), channel_id=1, source_target_pairs={{0,4},{4,12},{12,20},{20,28},{28,24},{24,16},{16,8},{8,0},{1,5},{5... | collective-permute-start | bytes 3538952 | tf_op jit(solution)/shard_map/ppermute | solution.py:138
  240.3 29.5 %collective-permute-start.14 = (bf16[6,768,128]{1,2,0:T(8,128)(2,1)}, bf16[6,768,128]{1,2,0:T(8,128)(2,1)}, u32[]{:S(2)}, u32[]{:S(2)}) collective-permute-start(bf16[6,768,128]{1,2,0:T(8,128)(2,1)} %collective-permute-done.12), channel_id=1, source_target_pairs={{0,8},{4,0},{12,4},{20,12},{28,20},{24,28},{16,24},{8,16},{1,9},{5... | collective-permute-start | bytes 3538952 | tf_op jit(solution)/shard_map/ppermute | solution.py:139
  249.7 43.2 %collective-permute-start.20 = (bf16[384,2,6,128]{0,3,2,1:T(8,128)(2,1)S(1)}, bf16[384,2,6,128]{0,3,2,1:T(8,128)(2,1)S(1)}, u32[]{:S(2)}, u32[]{:S(2)}) collective-permute-start(bf16[384,2,6,128]{0,3,2,1:T(8,128)(2,1)S(1)} %broadcast_select_fusion.1), channel_id=1, source_target_pairs={{0,4},{8,12},{16,20},{24,28},{4,0},{12,8},{20,16},{28,24},{1,5},{9... | collective-permute-start | bytes 3538952 | tf_op jit(solution)/shard_map/ppermute | solution.py:165
  269.9 47.8 %collective-permute-start.15 = (bf16[6,768,128]{1,2,0:T(8,128)(2,1)}, bf16[6,768,128]{1,2,0:T(8,128)(2,1)S(1)}, u32[]{:S(2)}, u32[]{:S(2)}) collective-permute-start(bf16[6,768,128]{1,2,0:T(8,128)(2,1)} %collective-permute-done.13), channel_id=1, source_target_pairs={{0,4},{4,12},{12,20},{20,28},{28,24},{24,16},{16,8},{8,0},{1,5},{5... | collective-permute-start | bytes 3538952 | tf_op jit(solution)/shard_map/ppermute | solution.py:138
  269.9 50.3 %collective-permute-start.16 = (bf16[6,768,128]{1,2,0:T(8,128)(2,1)}, bf16[6,768,128]{1,2,0:T(8,128)(2,1)S(1)}, u32[]{:S(2)}, u32[]{:S(2)}) collective-permute-start(bf16[6,768,128]{1,2,0:T(8,128)(2,1)} %collective-permute-done.14), channel_id=1, source_target_pairs={{0,8},{4,0},{12,4},{20,12},{28,20},{24,28},{16,24},{8,16},{1,9},{5... | collective-permute-start | bytes 3538952 | tf_op jit(solution)/shard_map/ppermute | solution.py:139
  273.8 61.2 %collective-permute-start.21 = (bf16[384,2,6,128]{0,3,2,1:T(8,128)(2,1)S(1)}, bf16[384,2,6,128]{0,3,2,1:T(8,128)(2,1)S(1)}, u32[]{:S(2)}, u32[]{:S(2)}) collective-permute-start(bf16[384,2,6,128]{0,3,2,1:T(8,128)(2,1)S(1)} %collective-permute-done.19), channel_id=1, source_target_pairs={{0,4},{8,12},{16,20},{24,28},{1,5},{9,13},{17,21},{25,29},{2,6},{1... | collective-permute-start | bytes 3538952 | tf_op jit(solution)/shard_map/ppermute | solution.py:166
  292.9 42.0 %collective-permute-start.22 = (bf16[384,2,6,128]{0,3,2,1:T(8,128)(2,1)S(1)}, bf16[384,2,6,128]{0,3,2,1:T(8,128)(2,1)S(1)}, u32[]{:S(2)}, u32[]{:S(2)}) collective-permute-start(bf16[384,2,6,128]{0,3,2,1:T(8,128)(2,1)S(1)} %collective-permute-done.20), channel_id=1, source_target_pairs={{0,8},{8,16},{16,24},{24,0},{1,9},{9,17},{17,25},{25,1},{2,10},{10... | collective-permute-start | bytes 3538952 | tf_op jit(solution)/shard_map/ppermute | solution.py:167
  317.7 23.6 %collective-permute-start.17 = (bf16[6,384,128]{1,2,0:T(8,128)(2,1)S(1)}, bf16[6,384,128]{1,2,0:T(8,128)(2,1)S(1)}, u32[]{:S(2)}, u32[]{:S(2)}) collective-permute-start(bf16[6,384,128]{1,2,0:T(8,128)(2,1)S(1)} %slice.28), channel_id=1, source_target_pairs={{0,4},{4,12},{12,20},{20,28},{28,24},{24,16},{16,8},{8,0},{1,5},{5... | collective-permute-start | bytes 1769480 | tf_op jit(solution)/shard_map/ppermute | solution.py:148
  320.2 21.6 %collective-permute-start.18 = (bf16[6,384,128]{1,2,0:T(8,128)(2,1)S(1)}, bf16[6,384,128]{1,2,0:T(8,128)(2,1)S(1)}, u32[]{:S(2)}, u32[]{:S(2)}) collective-permute-start(bf16[6,384,128]{1,2,0:T(8,128)(2,1)S(1)} %slice.29), channel_id=1, source_target_pairs={{0,8},{4,0},{12,4},{20,12},{28,20},{24,28},{16,24},{8,16},{1,9},{5... | collective-permute-start | bytes 1769480 | tf_op jit(solution)/shard_map/ppermute | solution.py:149
  (12 other events, 534.1 us)

commit v16 on v15

--- a/solution.py
+++ b/solution.py
@@ -163,9 +163,7 @@
         evens_up = [(e, e + 1) for e in range(0, n, 2)]
         across = evens_up + [(o, o - 1) for o in range(1, n, 2)]
         one_back = lax.ppermute(jnp.where(odd, two_back, key_value), "ctx", across)
-        two_back_up = lax.ppermute(two_back, "ctx", evens_up)
-        three_back = lax.ppermute(one_back, "ctx", [(e, (e + 2) % n) for e in range(0, n, 2)])
-        three_back = jnp.where(odd, two_back_up, three_back)
+        three_back = shifted(two_back, "ctx", 1)
         return [one_back, two_back, three_back]
 
     def on_device(tokens, qkv_weight):

time: 354 us -> 363 us (1.025)
  waiting for transfers between devices: 251 us -> 265 us
    ppermute x4 -> x5, waiting for transfers between devices: 5.62 us -> 59.2 us  [shifted(): lax.ppermute(array, axis, [(i, (i + by) % devices) for i in range(devices)])]
    ppermute x2, waiting for transfers between devices: 8.52 us -> 36.6 us  [ring_project(): last_cw = lax.ppermute(first, 'ctx', clockwise)]
    ppermute x6, waiting for transfers between devices: 125 us -> 101 us  [ring_project(): going_ccw = lax.ppermute(going_ccw, 'ctx', counter)]
    ppermute x6, waiting for transfers between devices: 73.4 us -> 51.1 us  [ring_project(): going_cw = lax.ppermute(going_cw, 'ctx', clockwise)]
    ppermute x1, waiting for transfers between devices: 15.1 us -> 0.01 us  [earlier_blocks(): one_back = lax.ppermute(jnp.where(odd, two_back, key_value), 'ctx', across)]
    ppermute x2 -> x0, waiting for transfers between devices: 12.3 us -> none  [the longest x1 12.3 us: earlier_blocks(): two_back_up = lax.ppermute(two_back, 'ctx', evens_up)]
    ppermute x2, waiting for transfers between devices: 11.1 us -> 17.8 us  [ring_project(): last_ccw = lax.ppermute(second, 'ctx', counter)]
    ppermute x6, starting transfers between devices: 2.07 us -> 7.37 us  [ring_project(): going_cw = lax.ppermute(going_cw, 'ctx', clockwise)]
  transfers between devices with their start and end apart: 23 -> 22, of which waited for: 13 -> 12; matrix products, arithmetic and copies ran while one was open for 12% -> 12% of each run, Pallas kernels for 0% -> 0%
where the time goes in v16:
time: 363 us; the launch traced here: 362 us
  waiting for transfers between devices  265 us (73%)
  matrix products  32.2 us (9%)
  starting transfers between devices  27.4 us (8%)
  local copies, waits for them, and re-layouts  17.4 us (5%)
  between operations  9.45 us (3%)
  Pallas kernels  8.87 us (2%)
    ppermute x6, waiting for transfers between devices, ring_project(): going_ccw = lax.ppermute(going_ccw, 'ctx', counter)  101 us
    ppermute x5, waiting for transfers between devices, shifted(): lax.ppermute(array, axis, [(i, (i + by) % devices) for i in range(devices)])  59.2 us
    ppermute x6, waiting for transfers between devices, ring_project(): going_cw = lax.ppermute(going_cw, 'ctx', clockwise)  51.1 us
    ppermute x2, waiting for transfers between devices, ring_project(): last_cw = lax.ppermute(first, 'ctx', clockwise)  36.6 us
    dot_general x9, matrix products, partial(): jnp.einsum('tr,...rd->t...d', cols, part, preferred_element_type=jnp.floa...  19.2 us
    ppermute x2, waiting for transfers between devices, ring_project(): last_ccw = lax.ppermute(second, 'ctx', counter)  17.8 us
    unnamed x9, matrix products  12.9 us
    pallas_call x1, Pallas kernels, windowed_attention(): pl.pallas_call(functools.partial(attention_kernel, scale, reach, per_step...  8.87 us
  transfers between devices with their start and end apart: 22, of which 12 were waited for; matrix products, arithmetic and copies ran while one was open for 12% of the time, Pallas kernels for 0%

profile of v16, /device:TPU:0, one launch (start us, length us, event | category | flops | bytes accessed | tf_op | source)
XLA Modules:
  0.0 362.2 jit_solution(14280342637211113942)
XLA Ops:
  0.0 4.3 %copy.5 = bf16[768,3,6,128]{0,3,2,1:T(8,128)(2,1)S(1)} copy(bf16[768,3,6,128]{3,0,2,1:T(8,128)(2,1)} %param.5) | data formatting | bytes 7077888 | tf_op args[1]
  4.5 3.1 collective-permute-start.7
  7.6 51.2 %collective-permute-done.7 = bf16[2,6,768,128]{2,3,1,0:T(8,128)(2,1)S(1)} collective-permute-done((bf16[2,6,768,128]{2,3,1,0:T(8,128)(2,1)S(1)}, bf16[2,6,768,128]{2,3,1,0:T(8,128)(2,1)S(1)}, u32[]{:S(2)}, u32[]{:S(2)}) %collective-permute-start.7) | collective-permute-done | bytes 2359328 | tf_op jit(solution)/shard_map/ppermute | solution.py:139
  61.9 49.4 %collective-permute-done.8 = bf16[2,6,768,128]{2,3,1,0:T(8,128)(2,1)} collective-permute-done((bf16[2,6,768,128]{2,3,1,0:T(8,128)(2,1)S(1)}, bf16[2,6,768,128]{2,3,1,0:T(8,128)(2,1)}, u32[]{:S(2)}, u32[]{:S(2)}) %collective-permute-start.8) | collective-permute-done | bytes 2359328 | tf_op jit(solution)/shard_map/ppermute | solution.py:139
  129.5 12.6 %collective-permute-done = bf16[384,1536]{1,0:T(8,128)(2,1)} collective-permute-done((bf16[384,1536]{1,0:T(8,128)(2,1)}, bf16[384,1536]{1,0:T(8,128)(2,1)}, u32[]{:S(2)}, u32[]{:S(2)}) %collective-permute-start) | collective-permute-done | bytes 1179680 | tf_op jit(solution)/shard_map/ppermute | solution.py:107
  145.0 22.0 %collective-permute-done.2 = bf16[384,1536]{1,0:T(8,128)(2,1)} collective-permute-done((bf16[384,1536]{1,0:T(8,128)(2,1)}, bf16[384,1536]{1,0:T(8,128)(2,1)}, u32[]{:S(2)}, u32[]{:S(2)}) %collective-permute-start.2) | collective-permute-done | bytes 1179680 | tf_op jit(solution)/shard_map/ppermute | solution.py:107
  168.4 2.3 slice.27
  178.7 3.1 fusion.6
  181.8 17.0 %collective-permute-done.10 = bf16[2,6,384,128]{2,3,1,0:T(8,128)(2,1)S(1)} collective-permute-done((bf16[2,6,384,128]{2,3,1,0:T(8,128)(2,1)S(1)}, bf16[2,6,384,128]{2,3,1,0:T(8,128)(2,1)S(1)}, u32[]{:S(2)}, u32[]{:S(2)}) %collective-permute-start.10) | collective-permute-done | bytes 1179680 | tf_op jit(solution)/shard_map/ppermute | solution.py:149
  198.9 2.5 collective-permute-done.6
  203.4 3.1 fusion.8
  206.5 3.1 fusion.4
  211.4 18.1 %collective-permute-done.11 = bf16[6,768,128]{1,2,0:T(8,128)(2,1)} collective-permute-done((bf16[6,768,128]{1,2,0:T(8,128)(2,1)S(1)}, bf16[6,768,128]{1,2,0:T(8,128)(2,1)}, u32[]{:S(2)}, u32[]{:S(2)}) %collective-permute-start.11) | collective-permute-done | bytes 1179680 | tf_op jit(solution)/shard_map/ppermute | solution.py:138
  231.6 3.9 %add_convert_fusion = bf16[384,2,6,128]{0,3,2,1:T(8,128)(2,1)S(1)} fusion(f32[384,2,6,128]{0,3,2,1:T(8,128)S(1)} %fusion.37, f32[384,2,6,128]{0,3,2,1:T(8,128)S(1)} %fusion.39, f32[384,2,6,128]{0,3,2,1:T(8,128)S(1)} %fusion.4, f32[384,2,6,128]{0,3,2,1:T(8,128)S(1)} %fusion.6, f32[384,2,6,128]{0,3,2,1:T(8,128)S(1)} %fusion.8, ...), kind=kOutput, calls=%fused_computation | convolution fusion | flops 911278080 | bytes 23003140 | tf_op jit(solution)/shard_map/tr,...rd->t...d/dot_general | solution.py:130
  237.1 20.0 %collective-permute-done.13 = bf16[6,768,128]{1,2,0:T(8,128)(2,1)} collective-permute-done((bf16[6,768,128]{1,2,0:T(8,128)(2,1)}, bf16[6,768,128]{1,2,0:T(8,128)(2,1)}, u32[]{:S(2)}, u32[]{:S(2)}) %collective-permute-start.13) | collective-permute-done | bytes 1179680 | tf_op jit(solution)/shard_map/ppermute | solution.py:138
  257.1 2.1 collective-permute-start.15
  261.4 24.6 %collective-permute-done.19 = bf16[384,2,6,128]{0,3,2,1:T(8,128)(2,1)S(1)} collective-permute-done((bf16[384,2,6,128]{0,3,2,1:T(8,128)(2,1)S(1)}, bf16[384,2,6,128]{0,3,2,1:T(8,128)(2,1)S(1)}, u32[]{:S(2)}, u32[]{:S(2)}) %collective-permute-start.19) | collective-permute-done | bytes 1179680 | tf_op jit(solution)/shard_map/ppermute | solution.py:107
  286.2 3.0 collective-permute-start.20
  289.2 2.1 fusion.32
  291.3 2.1 fusion.29
  293.3 2.1 fusion.26
  295.4 13.0 %collective-permute-done.15 = bf16[6,768,128]{1,2,0:T(8,128)(2,1)S(1)} collective-permute-done((bf16[6,768,128]{1,2,0:T(8,128)(2,1)}, bf16[6,768,128]{1,2,0:T(8,128)(2,1)S(1)}, u32[]{:S(2)}, u32[]{:S(2)}) %collective-permute-start.15) | collective-permute-done | bytes 1179680 | tf_op jit(solution)/shard_map/ppermute | solution.py:138
  314.5 34.1 %collective-permute-done.17 = bf16[6,384,128]{1,2,0:T(8,128)(2,1)S(1)} collective-permute-done((bf16[6,384,128]{1,2,0:T(8,128)(2,1)S(1)}, bf16[6,384,128]{1,2,0:T(8,128)(2,1)S(1)}, u32[]{:S(2)}, u32[]{:S(2)}) %collective-permute-start.17) | collective-permute-done | bytes 589856 | tf_op jit(solution)/shard_map/ppermute | solution.py:148
  353.3 8.9 %shard_map.46 = bf16[6,384,128]{2,1,0:T(8,128)(2,1)} custom-call(bf16[768,384]{1,0:T(8,128)(2,1)} %bitcast.156, bf16[1536,384]{1,0:T(8,128)(2,1)} %bitcast.133, bf16[1536,384]{1,0:T(8,128)(2,1)} %bitcast.150, bf16[1536,384]{1,0:T(8,128)(2,1)} %bitcast.138, bf16[1536,384]{1,0:T(8,128)(2,1)} %bitcast.152, bf16[1536,384]{1,0:T(8,128)(2,1)} %bitcast.134, ...), custom_call_target="tpu_custom_call" | custom-call | flops 1811939328 | bytes 5898240 | tf_op jit(solution)/shard_map/pallas_call | solution.py:53
  (83 shorter events, 45.4 us)
Async XLA Ops:
  4.3 112.8 %copy-start.13 = (s32[8]{0:T(128)S(1)}, s32[8]{0:T(128)}, u32[]{:S(2)}) copy-start(s32[8]{0:T(128)} %constant.138.clone) | copy-start | bytes 100
  4.3 118.0 %copy-start.8 = (s32[8]{0:T(128)S(1)}, s32[8]{0:T(128)}, u32[]{:S(2)}) copy-start(s32[8]{0:T(128)} %constant.139.clone) | copy-start | bytes 100
  4.5 54.3 %collective-permute-start.7 = (bf16[2,6,768,128]{2,3,1,0:T(8,128)(2,1)S(1)}, bf16[2,6,768,128]{2,3,1,0:T(8,128)(2,1)S(1)}, u32[]{:S(2)}, u32[]{:S(2)}) collective-permute-start(bf16[2,6,768,128]{2,3,1,0:T(8,128)(2,1)S(1)} %slice.25), channel_id=1, source_target_pairs={{0,8},{4,0},{12,4},{20,12},{28,20},{24,28},{16,24},{8,16},{1,9},{5... | collective-permute-start | bytes 7077896 | tf_op jit(solution)/shard_map/ppermute | solution.py:139
  7.5 53.0 %collective-permute-start.3 = (bf16[2,6,768,128]{2,3,1,0:T(8,128)(2,1)S(1)}, bf16[2,6,768,128]{2,3,1,0:T(8,128)(2,1)S(1)}, u32[]{:S(2)}, u32[]{:S(2)}) collective-permute-start(bf16[2,6,768,128]{2,3,1,0:T(8,128)(2,1)S(1)} %slice.25), channel_id=1, source_target_pairs={{0,4},{4,12},{12,20},{20,28},{28,24},{24,16},{16,8},{8,0},{1,5},{5... | collective-permute-start | bytes 7077896 | tf_op jit(solution)/shard_map/ppermute | solution.py:138
  58.7 52.5 %collective-permute-start.8 = (bf16[2,6,768,128]{2,3,1,0:T(8,128)(2,1)S(1)}, bf16[2,6,768,128]{2,3,1,0:T(8,128)(2,1)}, u32[]{:S(2)}, u32[]{:S(2)}) collective-permute-start(bf16[2,6,768,128]{2,3,1,0:T(8,128)(2,1)S(1)} %collective-permute-done.7), channel_id=1, source_target_pairs={{0,8},{4,0},{12,4},{20,12},{28,20},{24,28},{16,24},{8,16},{1,9},{5... | collective-permute-start | bytes 7077896 | tf_op jit(solution)/shard_map/ppermute | solution.py:139
  60.5 52.2 %collective-permute-start.4 = (bf16[2,6,768,128]{2,3,1,0:T(8,128)(2,1)S(1)}, bf16[2,6,768,128]{2,3,1,0:T(8,128)(2,1)}, u32[]{:S(2)}, u32[]{:S(2)}) collective-permute-start(bf16[2,6,768,128]{2,3,1,0:T(8,128)(2,1)S(1)} %collective-permute-done.3), channel_id=1, source_target_pairs={{0,4},{4,12},{12,20},{20,28},{28,24},{24,16},{16,8},{8,0},{1,5},{5... | collective-permute-start | bytes 7077896 | tf_op jit(solution)/shard_map/ppermute | solution.py:138
  111.3 57.1 %collective-permute-start.9 = (bf16[2,6,768,128]{2,3,1,0:T(8,128)(2,1)}, bf16[2,6,768,128]{2,3,1,0:T(8,128)(2,1)}, u32[]{:S(2)}, u32[]{:S(2)}) collective-permute-start(bf16[2,6,768,128]{2,3,1,0:T(8,128)(2,1)} %collective-permute-done.8), channel_id=1, source_target_pairs={{0,8},{4,0},{12,4},{20,12},{28,20},{24,28},{16,24},{8,16},{1,9},{5... | collective-permute-start | bytes 7077896 | tf_op jit(solution)/shard_map/ppermute | solution.py:139
  112.8 58.7 %collective-permute-start.5 = (bf16[2,6,768,128]{2,3,1,0:T(8,128)(2,1)}, bf16[2,6,768,128]{2,3,1,0:T(8,128)(2,1)}, u32[]{:S(2)}, u32[]{:S(2)}) collective-permute-start(bf16[2,6,768,128]{2,3,1,0:T(8,128)(2,1)} %collective-permute-done.4), channel_id=1, source_target_pairs={{0,4},{4,12},{12,20},{20,28},{28,24},{24,16},{16,8},{8,0},{1,5},{5... | collective-permute-start | bytes 7077896 | tf_op jit(solution)/shard_map/ppermute | solution.py:138
  114.1 28.0 %collective-permute-start = (bf16[384,1536]{1,0:T(8,128)(2,1)}, bf16[384,1536]{1,0:T(8,128)(2,1)}, u32[]{:S(2)}, u32[]{:S(2)}) collective-permute-start(bf16[384,1536]{1,0:T(8,128)(2,1)} %param.4), channel_id=1, source_target_pairs={{0,1},{1,2},{2,3},{3,0},{4,5},{5,6},{6,7},{7,4},{8,9},{9,10},{10,1... | collective-permute-start | bytes 3538952 | tf_op jit(solution)/shard_map/ppermute | solution.py:107
  114.1 29.4 %collective-permute-start.1 = (bf16[384,1536]{1,0:T(8,128)(2,1)}, bf16[384,1536]{1,0:T(8,128)(2,1)}, u32[]{:S(2)}, u32[]{:S(2)}) collective-permute-start(bf16[384,1536]{1,0:T(8,128)(2,1)} %param.4), channel_id=1, source_target_pairs={{0,2},{1,3},{2,0},{3,1},{4,6},{5,7},{6,4},{7,5},{8,10},{9,11},{10,... | collective-permute-start | bytes 3538952 | tf_op jit(solution)/shard_map/ppermute | solution.py:107
  115.6 51.3 %collective-permute-start.2 = (bf16[384,1536]{1,0:T(8,128)(2,1)}, bf16[384,1536]{1,0:T(8,128)(2,1)}, u32[]{:S(2)}, u32[]{:S(2)}) collective-permute-start(bf16[384,1536]{1,0:T(8,128)(2,1)} %param.4), channel_id=1, source_target_pairs={{0,3},{1,0},{2,1},{3,2},{4,7},{5,4},{6,5},{7,6},{8,11},{9,8},{10,9... | collective-permute-start | bytes 3538952 | tf_op jit(solution)/shard_map/ppermute | solution.py:107
  170.7 28.2 %collective-permute-start.10 = (bf16[2,6,384,128]{2,3,1,0:T(8,128)(2,1)S(1)}, bf16[2,6,384,128]{2,3,1,0:T(8,128)(2,1)S(1)}, u32[]{:S(2)}, u32[]{:S(2)}) collective-permute-start(bf16[2,6,384,128]{2,3,1,0:T(8,128)(2,1)S(1)} %slice.27), channel_id=1, source_target_pairs={{0,8},{4,0},{12,4},{20,12},{28,20},{24,28},{16,24},{8,16},{1,9},{5... | collective-permute-start | bytes 3538952 | tf_op jit(solution)/shard_map/ppermute | solution.py:149
  172.8 28.5 %collective-permute-start.6 = (bf16[2,6,384,128]{2,3,1,0:T(8,128)(2,1)S(1)}, bf16[2,6,384,128]{2,3,1,0:T(8,128)(2,1)S(1)}, u32[]{:S(2)}, u32[]{:S(2)}) collective-permute-start(bf16[2,6,384,128]{2,3,1,0:T(8,128)(2,1)S(1)} %slice.26), channel_id=1, source_target_pairs={{0,4},{4,12},{12,20},{20,28},{28,24},{24,16},{16,8},{8,0},{1,5},{5... | collective-permute-start | bytes 3538952 | tf_op jit(solution)/shard_map/ppermute | solution.py:148
  201.4 28.2 %collective-permute-start.11 = (bf16[6,768,128]{1,2,0:T(8,128)(2,1)S(1)}, bf16[6,768,128]{1,2,0:T(8,128)(2,1)}, u32[]{:S(2)}, u32[]{:S(2)}) collective-permute-start(bf16[6,768,128]{1,2,0:T(8,128)(2,1)S(1)} %slice_bitcast_fusion), channel_id=1, source_target_pairs={{0,4},{4,12},{12,20},{20,28},{28,24},{24,16},{16,8},{8,0},{1,5},{5... | collective-permute-start | bytes 3538952 | tf_op jit(solution)/shard_map/ppermute | solution.py:138
  202.7 28.2 %collective-permute-start.12 = (bf16[6,768,128]{1,2,0:T(8,128)(2,1)S(1)}, bf16[6,768,128]{1,2,0:T(8,128)(2,1)}, u32[]{:S(2)}, u32[]{:S(2)}) collective-permute-start(bf16[6,768,128]{1,2,0:T(8,128)(2,1)S(1)} %slice_bitcast_fusion), channel_id=1, source_target_pairs={{0,8},{4,0},{12,4},{20,12},{28,20},{24,28},{16,24},{8,16},{1,9},{5... | collective-permute-start | bytes 3538952 | tf_op jit(solution)/shard_map/ppermute | solution.py:139
  229.5 27.5 %collective-permute-start.13 = (bf16[6,768,128]{1,2,0:T(8,128)(2,1)}, bf16[6,768,128]{1,2,0:T(8,128)(2,1)}, u32[]{:S(2)}, u32[]{:S(2)}) collective-permute-start(bf16[6,768,128]{1,2,0:T(8,128)(2,1)} %collective-permute-done.11), channel_id=1, source_target_pairs={{0,4},{4,12},{12,20},{20,28},{28,24},{24,16},{16,8},{8,0},{1,5},{5... | collective-permute-start | bytes 3538952 | tf_op jit(solution)/shard_map/ppermute | solution.py:138
  230.8 30.3 %collective-permute-start.14 = (bf16[6,768,128]{1,2,0:T(8,128)(2,1)}, bf16[6,768,128]{1,2,0:T(8,128)(2,1)}, u32[]{:S(2)}, u32[]{:S(2)}) collective-permute-start(bf16[6,768,128]{1,2,0:T(8,128)(2,1)} %collective-permute-done.12), channel_id=1, source_target_pairs={{0,8},{4,0},{12,4},{20,12},{28,20},{24,28},{16,24},{8,16},{1,9},{5... | collective-permute-start | bytes 3538952 | tf_op jit(solution)/shard_map/ppermute | solution.py:139
  235.5 50.5 %collective-permute-start.19 = (bf16[384,2,6,128]{0,3,2,1:T(8,128)(2,1)S(1)}, bf16[384,2,6,128]{0,3,2,1:T(8,128)(2,1)S(1)}, u32[]{:S(2)}, u32[]{:S(2)}) collective-permute-start(bf16[384,2,6,128]{0,3,2,1:T(8,128)(2,1)S(1)} %add_convert_fusion), channel_id=1, source_target_pairs={{0,8},{4,12},{8,16},{12,20},{16,24},{20,28},{24,0},{28,4},{1,9},{5... | collective-permute-start | bytes 3538952 | tf_op jit(solution)/shard_map/ppermute | solution.py:107
  257.1 51.3 %collective-permute-start.15 = (bf16[6,768,128]{1,2,0:T(8,128)(2,1)}, bf16[6,768,128]{1,2,0:T(8,128)(2,1)S(1)}, u32[]{:S(2)}, u32[]{:S(2)}) collective-permute-start(bf16[6,768,128]{1,2,0:T(8,128)(2,1)} %collective-permute-done.13), channel_id=1, source_target_pairs={{0,4},{4,12},{12,20},{20,28},{28,24},{24,16},{16,8},{8,0},{1,5},{5... | collective-permute-start | bytes 3538952 | tf_op jit(solution)/shard_map/ppermute | solution.py:138
  261.2 50.7 %collective-permute-start.16 = (bf16[6,768,128]{1,2,0:T(8,128)(2,1)}, bf16[6,768,128]{1,2,0:T(8,128)(2,1)S(1)}, u32[]{:S(2)}, u32[]{:S(2)}) collective-permute-start(bf16[6,768,128]{1,2,0:T(8,128)(2,1)} %collective-permute-done.14), channel_id=1, source_target_pairs={{0,8},{4,0},{12,4},{20,12},{28,20},{24,28},{16,24},{8,16},{1,9},{5... | collective-permute-start | bytes 3538952 | tf_op jit(solution)/shard_map/ppermute | solution.py:139
  286.2 65.7 %collective-permute-start.20 = (bf16[384,2,6,128]{0,3,2,1:T(8,128)(2,1)S(1)}, bf16[384,2,6,128]{0,3,2,1:T(8,128)(2,1)S(1)}, u32[]{:S(2)}, u32[]{:S(2)}) collective-permute-start(bf16[384,2,6,128]{0,3,2,1:T(8,128)(2,1)S(1)} %broadcast_select_fusion), channel_id=1, source_target_pairs={{0,4},{8,12},{16,20},{24,28},{4,0},{12,8},{20,16},{28,24},{1,5},{9... | collective-permute-start | bytes 3538952 | tf_op jit(solution)/shard_map/ppermute | solution.py:165
  289.1 62.8 %collective-permute-start.21 = (bf16[384,2,6,128]{0,3,2,1:T(8,128)(2,1)S(1)}, bf16[384,2,6,128]{0,3,2,1:T(8,128)(2,1)S(1)}, u32[]{:S(2)}, u32[]{:S(2)}) collective-permute-start(bf16[384,2,6,128]{0,3,2,1:T(8,128)(2,1)S(1)} %collective-permute-done.19), channel_id=1, source_target_pairs={{0,4},{4,8},{8,12},{12,16},{16,20},{20,24},{24,28},{28,0},{1,5},{5... | collective-permute-start | bytes 3538952 | tf_op jit(solution)/shard_map/ppermute | solution.py:107
  308.4 40.2 %collective-permute-start.17 = (bf16[6,384,128]{1,2,0:T(8,128)(2,1)S(1)}, bf16[6,384,128]{1,2,0:T(8,128)(2,1)S(1)}, u32[]{:S(2)}, u32[]{:S(2)}) collective-permute-start(bf16[6,384,128]{1,2,0:T(8,128)(2,1)S(1)} %slice.28), channel_id=1, source_target_pairs={{0,4},{4,12},{12,20},{20,28},{28,24},{24,16},{16,8},{8,0},{1,5},{5... | collective-permute-start | bytes 1769480 | tf_op jit(solution)/shard_map/ppermute | solution.py:148
  312.0 37.9 %collective-permute-start.18 = (bf16[6,384,128]{1,2,0:T(8,128)(2,1)S(1)}, bf16[6,384,128]{1,2,0:T(8,128)(2,1)S(1)}, u32[]{:S(2)}, u32[]{:S(2)}) collective-permute-start(bf16[6,384,128]{1,2,0:T(8,128)(2,1)S(1)} %slice.29), channel_id=1, source_target_pairs={{0,8},{4,0},{12,4},{20,12},{28,20},{24,28},{16,24},{8,16},{1,9},{5... | collective-permute-start | bytes 1769480 | tf_op jit(solution)/shard_map/ppermute | solution.py:149
  (12 other events, 329.6 us)
